TPU v7x, 32 devices: a whole 2x2x4 slice. The times are simulated.
32 devices in a mesh: gx: 4 (over y, x), gy: 2 (over core), gz: 4 (over z).
Axes of the slice: x: 2, y: 2, z: 4, core: 2. Of those that a mesh axis runs over, the one named last changes fastest.
Arguments:
- positions: float32 [3, 4, 4, 8, 128], P(None, 'gx', 'gy', 'gz'), may hold values from 0 to 1
- velocities: float32 [3, 4, 4, 8, 128], P(None, 'gx', 'gy', 'gz'), may hold values from -1.8 to 1.8
- species: int32 [4, 4, 8, 128], P('gx', 'gy', 'gz'), may hold values from 0 to 1
- counts: int32 [4, 4, 8], P('gx', 'gy', 'gz'), may hold values from 32 to 128
Outputs:
- new_positions: float32 [3, 4, 4, 8, 128], P(None, 'gx', 'gy', 'gz')
- new_velocities: float32 [3, 4, 4, 8, 128], P(None, 'gx', 'gy', 'gz')
All inputs are finite; a program needn't handle non-finite values.
Results may differ from a plain program's by a relative error of at most 0.0003.
Values sent between devices are 32-bit elements; how exact they have to be, the bound alone decides.
No kernel may reach another device: no remote copies, remote signals or barrier semaphores. Data moves between devices by JAX's collectives and lax.ppermute only.
A program may use at most 64 MiB of HBM per device.

v0:
```python
import functools

import jax
import jax.numpy as jnp
from jax import lax
from jax.experimental import pallas as pl
from jax.experimental.pallas import tpu as pltpu
from jax.sharding import PartitionSpec as P

time_step = 0.05
half_kick = 0.5 * time_step
LANES = 128
GRANT = 8 * 1024 * 1024
ROOT = 1.3 ** (1.0 / 3.0)
STEPS = (-1, 0, 1)


def neighbours(cells, axis, dim, width):
    count = lax.axis_size(axis)
    size = cells.shape[dim]
    head = lax.slice_in_dim(cells, 0, width, axis=dim)
    tail = lax.slice_in_dim(cells, size - width, size, axis=dim)
    if count == 1:
        return tail, head
    if count == 2 and size == 2 * width:
        other = lax.ppermute(cells, axis, [(0, 1), (1, 0)])
        return (
            lax.slice_in_dim(other, width, size, axis=dim),
            lax.slice_in_dim(other, 0, width, axis=dim),
        )
    below = lax.ppermute(tail, axis, [(i, (i + 1) % count) for i in range(count)])
    above = lax.ppermute(head, axis, [((i + 1) % count, i) for i in range(count)])
    return below, above


def ring_halo(cells, axis, dim, width):
    below, above = neighbours(cells, axis, dim, width)
    return jnp.concatenate([below, cells, above], axis=dim)


def split3(value):
    high = value.astype(jnp.bfloat16).astype(jnp.float32)
    rest = value - high
    middle = rest.astype(jnp.bfloat16).astype(jnp.float32)
    return high, middle, rest - middle


def partner_block(row):
    high, middle, low = split3(row)
    first = jnp.concatenate([high, middle], axis=0).astype(jnp.bfloat16)
    last = jnp.concatenate([low, high], axis=0).astype(jnp.bfloat16)
    return jnp.concatenate([first, first, last], axis=0)


def target_block(row):
    high, middle, low = split3(row)
    stacked = jnp.concatenate([high, high, middle, middle, high, low], axis=0)
    return jnp.transpose(stacked).astype(jnp.bfloat16)


class Grid:
    def __init__(self, own):
        self.own = own
        self.ex, self.ey, self.ez = own[0] + 2, own[1] + 2, own[2] + 4
        self.plane = self.ex * self.ey
        row = lax.broadcasted_iota(jnp.int32, (8, LANES), 0)
        self.row = row
        self.masks = [(row == k).astype(jnp.float32) for k in range(7)]
        self.spatial = self.masks[0] + self.masks[1] + self.masks[2]

    def lanes(self, a, b, layer, count=1):
        base = ((layer * self.ex + a) * self.ey + b) * LANES
        return slice(base, base + count * LANES)

    def placed(self, tile, a, b, c):
        m = self.masks
        shift = (
            (a + 0.5 - 0.5 * self.ex) * m[0]
            + (b + 0.5 - 0.5 * self.ey) * m[1]
            + (m[4] + (c + 0.5 - 0.5 * self.ez) * m[2])
        )
        point = jnp.concatenate([tile, jnp.zeros((4, LANES), jnp.float32)], axis=0)
        point = point * self.spatial + shift
        return point, jnp.sum(point * point, axis=0, keepdims=True)

    def partner(self, tile, a, b, c):
        point, bulk = self.placed(tile, a, b, c)
        scale = tile[3:4]
        block = partner_block(jnp.where(self.row == 3, 1.0 - bulk, point) * scale)
        strength = jnp.where(scale > 1.05, 0.4 / ROOT, 0.3)
        return block, jnp.where(self.row == 3, strength, point)

    def target(self, tile, a, b, c):
        point, bulk = self.placed(tile, a, b, c)
        twice = jnp.where(self.row == 4, 2.0 - bulk, 2.0 * point)
        return point, twice + self.masks[3]


def density_of(grid, left, a, b, sources, skip):
    rows = 64
    sums = []
    for start in range(0, LANES, rows):
        total = jnp.zeros((rows, LANES), jnp.float32)
        for ref, layer, same in sources:
            for p in STEPS:
                near = jnp.dot(
                    left[start : start + rows],
                    ref[:, grid.lanes(a + p, b - 1, layer, 3)],
                    preferred_element_type=jnp.float32,
                )
                for k in range(3):
                    part = jnp.maximum(near[:, k * LANES : (k + 1) * LANES], 0.0)
                    if same and p == 0 and k == 1:
                        i = lax.broadcasted_iota(jnp.int32, (rows, LANES), 0)
                        j = lax.broadcasted_iota(jnp.int32, (rows, LANES), 1)
                        part = jnp.where(i + start == j, 0.0, part)
                    total = total + part * part * part
        sums.append(total)
    return jnp.sum(jnp.transpose(jnp.concatenate(sums, axis=0)), axis=0, keepdims=True)


def own_cells(own):
    return [(a, b, c) for a in range(1, own[0] + 1) for b in range(1, own[1] + 1) for c in range(own[2])]


def inner_density_kernel(own, mid_ref, sum_ref, part_ref, point_ref):
    grid = Grid(own)
    for c in range(own[2]):
        for a in range(grid.ex):
            for b in range(grid.ey):
                lanes = grid.lanes(a, b, c)
                part_ref[:, lanes], point_ref[:, lanes] = grid.partner(mid_ref[a, b, c], a, b, c + 2)
    for place, (a, b, c) in enumerate(own_cells(own)):
        _, row = grid.target(mid_ref[a, b, c], a, b, c + 2)
        layers = [c + r for r in STEPS if 0 <= c + r < own[2]]
        sources = [(part_ref, layer, layer == c) for layer in layers]
        sum_ref[place : place + 1, :] = density_of(grid, target_block(row), a, b, sources, c)


def outer_density_kernel(own, mid_ref, low_ref, high_ref, sum_ref, part_ref, slope_ref, edge_ref, edge_point_ref, far_ref):
    grid = Grid(own)
    cz = own[2]
    for ref, layer, where, c in ((low_ref, 0, 0, 0), (low_ref, 1, 0, 1), (high_ref, 0, 1, cz + 2), (high_ref, 1, 1, cz + 3)):
        edge = c in (1, cz + 2)
        for a in range(grid.ex):
            for b in range(grid.ey):
                lanes = grid.lanes(a, b, where)
                block, point = grid.partner(ref[a, b, layer], a, b, c)
                if edge:
                    edge_ref[:, lanes] = block
                    edge_point_ref[:, lanes] = point
                else:
                    far_ref[:, lanes] = block

    def finish(place, tile, density):
        present = jnp.where(tile[3:4] > 0.5, -0.5, 0.0)
        slope_ref[place : place + 1, :] = present / jnp.sqrt(density + 1.0)

    for a in range(1, own[0] + 1):
        for b in range(1, own[1] + 1):
            first = ((a - 1) * own[1] + b - 1) * (cz + 2)
            for side in (0, 1):
                tile = (low_ref[a, b, 1], high_ref[a, b, 0])[side]
                c = (1, cz + 2)[side]
                _, row = grid.target(tile, a, b, c)
                sources = [(far_ref, side, False), (edge_ref, side, True), (part_ref, (0, cz - 1)[side], False)]
                finish(first + side * (cz + 1), tile, density_of(grid, target_block(row), a, b, sources, c))
            for c in range(cz):
                tile = mid_ref[a, b, c]
                place = ((a - 1) * own[1] + b - 1) * cz + c
                density = sum_ref[place : place + 1, :]
                sources = [(edge_ref, side, False) for side in (0, 1) if c == (0, cz - 1)[side]]
                if sources:
                    _, row = grid.target(tile, a, b, c + 2)
                    density = density + density_of(grid, target_block(row), a, b, sources, c)
                finish(first + 1 + c, tile, density)


def pair_block(grid, scale, slope):
    inverse = jnp.where(scale > 1.05, 0.75 / (ROOT * ROOT), 0.75)
    row = jnp.where(grid.row == 5, 0.75 * scale, jnp.where(grid.row == 6, slope * inverse, 0.0))
    return partner_block(row)


def force_sums(grid, own, spread, mid_ref, slope, part_ref, point_ref, edge_ref, edge_point_ref, pair_ref, place):
    rows = 32
    cz = own[2]
    a, b, c = place
    tile = mid_ref[a, b, c]
    point, row = grid.target(tile, a, b, c + 2)
    solute = tile[3:4] > 1.05
    m = grid.masks
    left = target_block(
        row * jnp.where(solute, 0.8, 0.6)
        + slope(a, b, c + 1) * jnp.where(solute, 1.0 / 0.16, 1.0 / 0.09) * m[5]
        + jnp.where(solute, 1.3 / 0.16, 1.0 / 0.09) * m[6]
    )
    sums = [[] for _ in range(4)]
    for start in range(0, LANES, rows):
        total = [jnp.zeros((rows, LANES), jnp.float32) for _ in range(4)]
        for r in STEPS:
            inner = 0 <= c + r < cz
            ref, value_ref, layer = (
                (part_ref, point_ref, c + r) if inner else (edge_ref, edge_point_ref, int(c + r >= cz))
            )
            for p in spread:
                near = jnp.dot(
                    left[start : start + rows],
                    ref[:, grid.lanes(a + p, b - 1, layer, 3)],
                    preferred_element_type=jnp.float32,
                )
                kappa = jnp.dot(
                    left[start : start + rows],
                    pair_ref[:, grid.lanes(a + p, b - 1, c + r + 1, 3)],
                    preferred_element_type=jnp.float32,
                )
                for k in range(3):
                    lanes = grid.lanes(a + p, b - 1 + k, layer)
                    s = jnp.maximum(near[:, k * LANES : (k + 1) * LANES], 0.0)
                    w = s * (value_ref[3:4, lanes] + s * kappa[:, k * LANES : (k + 1) * LANES])
                    total[3] = total[3] + w
                    for axis in range(3):
                        total[axis] = total[axis] + w * value_ref[axis : axis + 1, lanes]
        for k in range(4):
            sums[k].append(total[k])
    flat = [
        jnp.sum(jnp.transpose(jnp.concatenate(parts, axis=0)), axis=0, keepdims=True) for parts in sums
    ]
    return point, flat


def scale_of(own, mid_ref, low_ref, high_ref, a, b, near):
    if near == 0:
        return low_ref[a, b, 1][3:4]
    if near == own[2] + 1:
        return high_ref[a, b, 0][3:4]
    return mid_ref[a, b, near - 1][3:4]


def column_force_kernel(own, mid_ref, low_ref, high_ref, slope_ref, part_ref, point_ref, edge_ref, edge_point_ref, out_ref, pair_ref):
    grid = Grid(own)

    def slope(a, b, near):
        index = ((a - 1) * grid.ey + b) * (own[2] + 2) + near
        return slope_ref[index : index + 1, :]

    for near in range(own[2] + 2):
        for a in range(1, own[0] + 1):
            for b in range(grid.ey):
                scale = scale_of(own, mid_ref, low_ref, high_ref, a, b, near)
                pair_ref[:, grid.lanes(a, b, near)] = pair_block(grid, scale, slope(a, b, near))
    for place, cell in enumerate(own_cells(own)):
        _, flat = force_sums(
            grid, own, (0,), mid_ref, slope, part_ref, point_ref, edge_ref, edge_point_ref, pair_ref, cell
        )
        for k in range(4):
            out_ref[k, place : place + 1, :] = flat[k]


def force_kernel(own, stage, mid_ref, low_ref, high_ref, slope_ref, part_ref, point_ref, edge_ref, edge_point_ref, column_ref, vel_ref, *refs):
    new_vel_ref, pair_ref = refs[0], refs[-1]
    grid = Grid(own)

    def slope(a, b, near):
        index = (a * grid.ey + b) * (own[2] + 2) + near
        return slope_ref[index : index + 1, :]

    for near in range(own[2] + 2):
        for a in range(grid.ex):
            if own[0] == 1 and a == 1:
                continue
            for b in range(grid.ey):
                scale = scale_of(own, mid_ref, low_ref, high_ref, a, b, near)
                pair_ref[:, grid.lanes(a, b, near)] = pair_block(grid, scale, slope(a, b, near))
    for place, cell in enumerate(own_cells(own)):
        point, flat = force_sums(
            grid, own, (-1, 1), mid_ref, slope, part_ref, point_ref, edge_ref, edge_point_ref, pair_ref, cell
        )
        row = slice(place, place + 1)
        flat = [flat[k] + column_ref[k, row, :] for k in range(4)]
        tile = mid_ref[cell[0], cell[1], cell[2]]
        scale = tile[3:4]
        present = jnp.where(scale > 0.5, -2.0, 0.0)
        kick = half_kick * jnp.where(scale > 1.05, 1.6, 1.0)
        for axis in range(3):
            force = present * (flat[axis] - point[axis : axis + 1] * flat[3])
            speed = vel_ref[axis, row, :] + kick * force
            if stage == "middle":
                speed = speed + kick * force
            new_vel_ref[axis, row, :] = speed
            if stage != "last":
                moved = tile[axis : axis + 1] + time_step * speed
                refs[1][place, axis : axis + 1, :] = moved
                if stage == "middle":
                    refs[2][axis, row, :] = moved
        if stage != "last":
            refs[1][place, 3:4, :] = scale


def on_device(positions, velocities, species, counts):
    cx, cy, cz, slots = positions.shape[1:]
    own = (cx, cy, cz)
    cells = cx * cy * cz
    ex, ey = cx + 2, cy + 2
    present = lax.broadcasted_iota(jnp.int32, species.shape, 3) < counts[..., None]
    scale = jnp.where(present, jnp.where(species == 1, ROOT, 1.0), 0.0)
    location = jnp.concatenate([jnp.moveaxis(positions, 0, 3), scale[..., None, :]], axis=3)
    velocity = velocities.reshape(3, cells, slots)
    vmem = pl.BlockSpec(memory_space=pltpu.VMEM)
    flat_shape = jax.ShapeDtypeStruct((3, cells, slots), jnp.float32)

    def block(layers):
        return jax.ShapeDtypeStruct((48, ex * ey * layers * slots), jnp.bfloat16)

    def points(layers):
        return jax.ShapeDtypeStruct((8, ex * ey * layers * slots), jnp.float32)

    def call(kernel, name, operands, out_shape, scratch, pairs):
        return pl.pallas_call(
            kernel,
            out_shape=out_shape,
            in_specs=[vmem] * len(operands),
            out_specs=[vmem] * len(out_shape),
            scratch_shapes=scratch,
            compiler_params=pltpu.CompilerParams(vmem_limit_bytes=GRANT),
            cost_estimate=pl.CostEstimate(
                flops=pairs * slots * slots * 50, bytes_accessed=pairs * slots * slots * 4, transcendentals=0
            ),
            name=name,
        )(*operands)

    def evaluate(location, velocity, stage):
        mid = ring_halo(ring_halo(location, "gy", 1, 1), "gx", 0, 1)
        low, high = neighbours(mid, "gz", 2, 2)
        sums, part, point = call(
            functools.partial(inner_density_kernel, own),
            "inner_density",
            [mid],
            [jax.ShapeDtypeStruct((cells, slots), jnp.float32), block(cz), points(cz)],
            [],
            cells * 18,
        )
        slopes, edge, edge_point = call(
            functools.partial(outer_density_kernel, own),
            "outer_density",
            [mid, low, high, sums, part],
            [jax.ShapeDtypeStruct((cx * cy * (cz + 2), slots), jnp.float32), block(2), points(2)],
            [pltpu.VMEM(block(2).shape, jnp.bfloat16)],
            cells * 36,
        )
        slopes = ring_halo(slopes.reshape(cx, cy, cz + 2, slots), "gy", 1, 1)
        wide = ring_halo(slopes, "gx", 0, 1).reshape(ex * ey * (cz + 2), slots)
        shared = [part, point, edge, edge_point]
        (column,) = call(
            functools.partial(column_force_kernel, own),
            "column_force",
            [mid, low, high, slopes.reshape(cx * ey * (cz + 2), slots), *shared],
            [jax.ShapeDtypeStruct((4, cells, slots), jnp.float32)],
            [pltpu.VMEM(block(cz + 2).shape, jnp.bfloat16)],
            cells * 9,
        )
        out_shape = [flat_shape]
        if stage != "last":
            out_shape.append(jax.ShapeDtypeStruct((cells, 4, slots), jnp.float32))
        if stage == "middle":
            out_shape.append(flat_shape)
        return call(
            functools.partial(force_kernel, own, stage),
            "force_" + stage,
            [mid, low, high, wide, *shared, column, velocity],
            out_shape,
            [pltpu.VMEM(block(cz + 2).shape, jnp.bfloat16)],
            cells * 18,
        )

    velocity, moved = evaluate(location, velocity, "first")
    velocity, moved, new_positions = evaluate(moved.reshape(location.shape), velocity, "middle")
    (velocity,) = evaluate(moved.reshape(location.shape), velocity, "last")
    return new_positions.reshape(positions.shape), velocity.reshape(positions.shape)


def solution(mesh):
    return jax.shard_map(
        on_device,
        mesh=mesh,
        in_specs=(
            P(None, "gx", "gy", "gz", None),
            P(None, "gx", "gy", "gz", None),
            P("gx", "gy", "gz", None),
            P("gx", "gy", "gz"),
        ),
        out_specs=(P(None, "gx", "gy", "gz", None), P(None, "gx", "gy", "gz", None)),
        check_vma=False,
    )
```

profile of v0, /device:TPU:0, one launch (start us, length us, event | category | flops | bytes accessed | tf_op | source)
XLA Modules:
  0.0 81.7 jit_solution(3259800857625187384)
XLA Ops:
  0.6 0.7 copy.10
  1.3 0.7 copy-done.2
  2.0 0.1 compare_select_fusion.1
  2.1 0.6 collective-permute-start
  2.7 0.8 %collective-permute-done = f32[1,2,2,4,128]{4,3,2,1,0:T(4,128)S(1)} collective-permute-done((f32[1,2,2,4,128]{4,3,2,1,0:T(4,128)S(1)}, f32[1,2,2,4,128]{4,3,2,1,0:T(4,128)S(1)}, u32[]{:S(2)}, u32[]{:S(2)}) %collective-permute-start) | collective-permute-done | bytes 8224 | tf_op jit(solution)/shard_map/ppermute | solution.py:26
  3.5 3.8 %collective-permute-start.2 = (f32[1,4,2,4,128]{4,3,2,1,0:T(4,128)S(1)}, f32[1,4,2,4,128]{4,3,2,1,0:T(4,128)S(1)}, u32[]{:S(2)}, u32[]{:S(2)}) collective-permute-start(f32[1,4,2,4,128]{4,3,2,1,0:T(4,128)S(1)} %pad_maximum_fusion.6), channel_id=1, source_target_pairs={{8,0},{16,8},{24,16},{0,24},{9,1},{17,9},{25,17},{1,25},{10,2},{18... | collective-permute-start | bytes 49160 | tf_op jit(solution)/shard_map/ppermute | solution.py:32
  7.3 0.0 collective-permute-start.1
  7.3 1.4 %collective-permute-done.2 = f32[1,4,2,4,128]{4,3,2,1,0:T(4,128)S(1)} collective-permute-done((f32[1,4,2,4,128]{4,3,2,1,0:T(4,128)S(1)}, f32[1,4,2,4,128]{4,3,2,1,0:T(4,128)S(1)}, u32[]{:S(2)}, u32[]{:S(2)}) %collective-permute-start.2) | collective-permute-done | bytes 16416 | tf_op jit(solution)/shard_map/ppermute | solution.py:32
  8.8 3.2 %collective-permute-done.1 = f32[1,4,2,4,128]{4,3,2,1,0:T(4,128)S(1)} collective-permute-done((f32[1,4,2,4,128]{4,3,2,1,0:T(4,128)S(1)}, f32[1,4,2,4,128]{4,3,2,1,0:T(4,128)S(1)}, u32[]{:S(2)}, u32[]{:S(2)}) %collective-permute-start.1) | collective-permute-done | bytes 16416 | tf_op jit(solution)/shard_map/ppermute | solution.py:31
  12.0 3.7 %collective-permute-start.4 = (f32[3,4,2,4,128]{4,3,2,1,0:T(4,128)S(1)}, f32[3,4,2,4,128]{4,3,2,1,0:T(4,128)S(1)}, u32[]{:S(2)}, u32[]{:S(2)}) collective-permute-start(f32[3,4,2,4,128]{4,3,2,1,0:T(4,128)S(1)} %pad_maximum_fusion.mid_ref), channel_id=1, source_target_pairs={{1,0},{2,1},{3,2},{0,3},{5,4},{6,5},{7,6},{4,7},{9,8},{10,9},{11,1... | collective-permute-start | bytes 147464 | tf_op jit(solution)/shard_map/ppermute | solution.py:32
  15.6 0.0 collective-permute-start.3
  15.6 1.0 %inner_density.3 = (f32[4,128]{1,0:T(4,128)S(1)}, bf16[48,3072]{1,0:T(8,128)(2,1)S(1)}, f32[8,3072]{1,0:T(8,128)S(1)}) custom-call(f32[3,4,2,4,128]{4,3,2,1,0:T(4,128)S(1)} %pad_maximum_fusion.mid_ref), custom_call_target="tpu_custom_call" | custom-call | flops 58982400 | bytes 4718592 | tf_op jit(solution)/shard_map/inner_density/pallas_call | solution.py:319
  16.7 0.7 collective-permute-done.4.high_ref
  17.4 4.1 %collective-permute-done.3.low_ref = f32[3,4,2,4,128]{4,3,2,1,0:T(4,128)S(1)} collective-permute-done((f32[3,4,2,4,128]{4,3,2,1,0:T(4,128)S(1)}, f32[3,4,2,4,128]{4,3,2,1,0:T(4,128)S(1)}, u32[]{:S(2)}, u32[]{:S(2)}) %collective-permute-start.3) | collective-permute-done | bytes 49184 | tf_op jit(solution)/shard_map/ppermute | solution.py:31
  21.5 1.9 %outer_density.3 = (f32[8,128]{1,0:T(8,128)S(1)}, bf16[48,3072]{1,0:T(8,128)(2,1)S(1)}, f32[8,3072]{1,0:T(8,128)S(1)}) custom-call(f32[3,4,2,4,128]{4,3,2,1,0:T(4,128)S(1)} %pad_maximum_fusion.mid_ref, f32[3,4,2,4,128]{4,3,2,1,0:T(4,128)S(1)} %collective-permute-done.3.low_ref, f32[3,4,2,4,128]{4,3,2,1,0:T(4,128)S(1)} %collective-permute-done.4.high_ref, ...), custom_call_target="tpu_custom_call" | custom-call | flops 117964800 | bytes 9437184 | tf_op jit(solution)/shard_map/outer_density/pallas_call | solution.py:319
  23.4 0.1 collective-permute-start.5
  23.5 1.2 %collective-permute-done.5 = f32[1,2,4,128]{3,2,1,0:T(4,128)S(1)} collective-permute-done((f32[1,2,4,128]{3,2,1,0:T(4,128)S(1)}, f32[1,2,4,128]{3,2,1,0:T(4,128)S(1)}, u32[]{:S(2)}, u32[]{:S(2)}) %collective-permute-start.5) | collective-permute-done | bytes 4128 | tf_op jit(solution)/shard_map/ppermute | solution.py:26
  24.6 0.1 collective-permute-start.7
  24.7 2.0 %collective-permute-start.6 = (f32[1,4,4,128]{3,2,1,0:T(4,128)S(1)}, f32[1,4,4,128]{3,2,1,0:T(4,128)S(1)}, u32[]{:S(2)}, u32[]{:S(2)}) collective-permute-start(f32[1,4,4,128]{3,2,1,0:T(4,128)S(1)} %pad_maximum_fusion.10), channel_id=1, source_target_pairs={{0,8},{8,16},{16,24},{24,0},{1,9},{9,17},{17,25},{25,1},{2,10},{10... | collective-permute-start | bytes 24584 | tf_op jit(solution)/shard_map/ppermute | solution.py:31
  26.7 1.4 %column_force.3.column_ref = f32[4,4,128]{2,1,0:T(4,128)S(1)} custom-call(f32[3,4,2,4,128]{4,3,2,1,0:T(4,128)S(1)} %pad_maximum_fusion.mid_ref, f32[3,4,2,4,128]{4,3,2,1,0:T(4,128)S(1)} %collective-permute-done.3.low_ref, f32[3,4,2,4,128]{4,3,2,1,0:T(4,128)S(1)} %collective-permute-done.4.high_ref, f32[16,128]{1,0:T(8,128)S(1)} %bitcast.32, ...), custom_call_target="tpu_custom_call" | custom-call | flops 29491200 | bytes 2359296 | tf_op jit(solution)/shard_map/column_force/pallas_call | solution.py:319
  28.2 0.2 collective-permute-done.7
  28.3 1.0 %collective-permute-done.6 = f32[1,4,4,128]{3,2,1,0:T(4,128)S(1)} collective-permute-done((f32[1,4,4,128]{3,2,1,0:T(4,128)S(1)}, f32[1,4,4,128]{3,2,1,0:T(4,128)S(1)}, u32[]{:S(2)}, u32[]{:S(2)}) %collective-permute-start.6) | collective-permute-done | bytes 8224 | tf_op jit(solution)/shard_map/ppermute | solution.py:31
  29.3 0.7 copy-done
  30.0 2.6 %force_first.1 = (f32[3,4,128]{2,1,0:T(4,128)S(1)}, f32[4,4,128]{2,1,0:T(4,128)S(1)}) custom-call(f32[3,4,2,4,128]{4,3,2,1,0:T(4,128)S(1)} %pad_maximum_fusion.mid_ref, f32[3,4,2,4,128]{4,3,2,1,0:T(4,128)S(1)} %collective-permute-done.3.low_ref, f32[3,4,2,4,128]{4,3,2,1,0:T(4,128)S(1)} %collective-permute-done.4.high_ref, f32[48,128]{1,0:T(8,128)S(1)} %bitcast.24, ...), custom_call_target="tpu_custom_call" | custom-call | flops 58982400 | bytes 4718592 | tf_op jit(solution)/shard_map/force_first/pallas_call | solution.py:319
  32.6 0.1 collective-permute-start.8
  32.7 1.2 %collective-permute-done.8 = f32[1,2,2,4,128]{4,3,2,1,0:T(4,128)S(1)} collective-permute-done((f32[1,2,2,4,128]{4,3,2,1,0:T(4,128)S(1)}, f32[1,2,2,4,128]{4,3,2,1,0:T(4,128)S(1)}, u32[]{:S(2)}, u32[]{:S(2)}) %collective-permute-start.8) | collective-permute-done | bytes 8224 | tf_op jit(solution)/shard_map/ppermute | solution.py:26
  33.9 1.1 %collective-permute-start.10 = (f32[1,4,2,4,128]{4,3,2,1,0:T(4,128)S(1)}, f32[1,4,2,4,128]{4,3,2,1,0:T(4,128)S(1)}, u32[]{:S(2)}, u32[]{:S(2)}) collective-permute-start(f32[1,4,2,4,128]{4,3,2,1,0:T(4,128)S(1)} %pad_maximum_fusion.7), channel_id=1, source_target_pairs={{8,0},{16,8},{24,16},{0,24},{9,1},{17,9},{25,17},{1,25},{10,2},{18... | collective-permute-start | bytes 49160 | tf_op jit(solution)/shard_map/ppermute | solution.py:32
  34.9 1.0 %collective-permute-start.9 = (f32[1,4,2,4,128]{4,3,2,1,0:T(4,128)S(1)}, f32[1,4,2,4,128]{4,3,2,1,0:T(4,128)S(1)}, u32[]{:S(2)}, u32[]{:S(2)}) collective-permute-start(f32[1,4,2,4,128]{4,3,2,1,0:T(4,128)S(1)} %pad_maximum_fusion.7), channel_id=1, source_target_pairs={{0,8},{8,16},{16,24},{24,0},{1,9},{9,17},{17,25},{25,1},{2,10},{10... | collective-permute-start | bytes 49160 | tf_op jit(solution)/shard_map/ppermute | solution.py:31
  36.0 1.7 %collective-permute-done.10 = f32[1,4,2,4,128]{4,3,2,1,0:T(4,128)S(1)} collective-permute-done((f32[1,4,2,4,128]{4,3,2,1,0:T(4,128)S(1)}, f32[1,4,2,4,128]{4,3,2,1,0:T(4,128)S(1)}, u32[]{:S(2)}, u32[]{:S(2)}) %collective-permute-start.10) | collective-permute-done | bytes 16416 | tf_op jit(solution)/shard_map/ppermute | solution.py:32
  37.7 1.9 %collective-permute-done.9 = f32[1,4,2,4,128]{4,3,2,1,0:T(4,128)S(1)} collective-permute-done((f32[1,4,2,4,128]{4,3,2,1,0:T(4,128)S(1)}, f32[1,4,2,4,128]{4,3,2,1,0:T(4,128)S(1)}, u32[]{:S(2)}, u32[]{:S(2)}) %collective-permute-start.9) | collective-permute-done | bytes 16416 | tf_op jit(solution)/shard_map/ppermute | solution.py:31
  39.6 0.1 collective-permute-start.12
  39.7 2.0 %collective-permute-start.11 = (f32[3,4,2,4,128]{4,3,2,1,0:T(4,128)S(1)}, f32[3,4,2,4,128]{4,3,2,1,0:T(4,128)S(1)}, u32[]{:S(2)}, u32[]{:S(2)}) collective-permute-start(f32[3,4,2,4,128]{4,3,2,1,0:T(4,128)S(1)} %pad_maximum_fusion.1.mid_ref), channel_id=1, source_target_pairs={{0,1},{1,2},{2,3},{3,0},{4,5},{5,6},{6,7},{7,4},{8,9},{9,10},{10,1... | collective-permute-start | bytes 147464 | tf_op jit(solution)/shard_map/ppermute | solution.py:31
  41.7 1.0 %inner_density.4 = (f32[4,128]{1,0:T(4,128)S(1)}, bf16[48,3072]{1,0:T(8,128)(2,1)S(1)}, f32[8,3072]{1,0:T(8,128)S(1)}) custom-call(f32[3,4,2,4,128]{4,3,2,1,0:T(4,128)S(1)} %pad_maximum_fusion.1.mid_ref), custom_call_target="tpu_custom_call" | custom-call | flops 58982400 | bytes 4718592 | tf_op jit(solution)/shard_map/inner_density/pallas_call | solution.py:319
  42.7 1.2 %collective-permute-done.12.high_ref = f32[3,4,2,4,128]{4,3,2,1,0:T(4,128)S(1)} collective-permute-done((f32[3,4,2,4,128]{4,3,2,1,0:T(4,128)S(1)}, f32[3,4,2,4,128]{4,3,2,1,0:T(4,128)S(1)}, u32[]{:S(2)}, u32[]{:S(2)}) %collective-permute-start.12) | collective-permute-done | bytes 49184 | tf_op jit(solution)/shard_map/ppermute | solution.py:32
  43.9 1.7 %collective-permute-done.11.low_ref = f32[3,4,2,4,128]{4,3,2,1,0:T(4,128)S(1)} collective-permute-done((f32[3,4,2,4,128]{4,3,2,1,0:T(4,128)S(1)}, f32[3,4,2,4,128]{4,3,2,1,0:T(4,128)S(1)}, u32[]{:S(2)}, u32[]{:S(2)}) %collective-permute-start.11) | collective-permute-done | bytes 49184 | tf_op jit(solution)/shard_map/ppermute | solution.py:31
  45.6 1.9 %outer_density.4 = (f32[8,128]{1,0:T(8,128)S(1)}, bf16[48,3072]{1,0:T(8,128)(2,1)S(1)}, f32[8,3072]{1,0:T(8,128)S(1)}) custom-call(f32[3,4,2,4,128]{4,3,2,1,0:T(4,128)S(1)} %pad_maximum_fusion.1.mid_ref, f32[3,4,2,4,128]{4,3,2,1,0:T(4,128)S(1)} %collective-permute-done.11.low_ref, f32[3,4,2,4,128]{4,3,2,1,0:T(4,128)S(1)} %collective-permute-done.12.high_ref, ...), custom_call_target="tpu_custom_call" | custom-call | flops 117964800 | bytes 9437184 | tf_op jit(solution)/shard_map/outer_density/pallas_call | solution.py:319
  47.5 0.1 collective-permute-start.13
  47.6 1.2 %collective-permute-done.13 = f32[1,2,4,128]{3,2,1,0:T(4,128)S(1)} collective-permute-done((f32[1,2,4,128]{3,2,1,0:T(4,128)S(1)}, f32[1,2,4,128]{3,2,1,0:T(4,128)S(1)}, u32[]{:S(2)}, u32[]{:S(2)}) %collective-permute-start.13) | collective-permute-done | bytes 4128 | tf_op jit(solution)/shard_map/ppermute | solution.py:26
  48.7 0.3 collective-permute-start.15
  49.0 1.8 %collective-permute-start.14 = (f32[1,4,4,128]{3,2,1,0:T(4,128)S(1)}, f32[1,4,4,128]{3,2,1,0:T(4,128)S(1)}, u32[]{:S(2)}, u32[]{:S(2)}) collective-permute-start(f32[1,4,4,128]{3,2,1,0:T(4,128)S(1)} %pad_maximum_fusion.11), channel_id=1, source_target_pairs={{0,8},{8,16},{16,24},{24,0},{1,9},{9,17},{17,25},{25,1},{2,10},{10... | collective-permute-start | bytes 24584 | tf_op jit(solution)/shard_map/ppermute | solution.py:31
  50.8 1.4 %column_force.4.column_ref = f32[4,4,128]{2,1,0:T(4,128)S(1)} custom-call(f32[3,4,2,4,128]{4,3,2,1,0:T(4,128)S(1)} %pad_maximum_fusion.1.mid_ref, f32[3,4,2,4,128]{4,3,2,1,0:T(4,128)S(1)} %collective-permute-done.11.low_ref, f32[3,4,2,4,128]{4,3,2,1,0:T(4,128)S(1)} %collective-permute-done.12.high_ref, f32[16,128]{1,0:T(8,128)S(1)} %bitcast.33, ...), custom_call_target="tpu_custom_call" | custom-call | flops 29491200 | bytes 2359296 | tf_op jit(solution)/shard_map/column_force/pallas_call | solution.py:319
  52.2 0.2 collective-permute-done.15
  52.4 1.1 %collective-permute-done.14 = f32[1,4,4,128]{3,2,1,0:T(4,128)S(1)} collective-permute-done((f32[1,4,4,128]{3,2,1,0:T(4,128)S(1)}, f32[1,4,4,128]{3,2,1,0:T(4,128)S(1)}, u32[]{:S(2)}, u32[]{:S(2)}) %collective-permute-start.14) | collective-permute-done | bytes 8224 | tf_op jit(solution)/shard_map/ppermute | solution.py:31
  53.6 3.2 %force_middle.1 = (f32[3,4,128]{2,1,0:T(4,128)S(1)}, f32[4,4,128]{2,1,0:T(4,128)S(1)}, f32[3,4,128]{2,1,0:T(4,128)}) custom-call(f32[3,4,2,4,128]{4,3,2,1,0:T(4,128)S(1)} %pad_maximum_fusion.1.mid_ref, f32[3,4,2,4,128]{4,3,2,1,0:T(4,128)S(1)} %collective-permute-done.11.low_ref, f32[3,4,2,4,128]{4,3,2,1,0:T(4,128)S(1)} %collective-permute-done.12.high_ref, ...), custom_call_target="tpu_custom_call" | custom-call | flops 58982400 | bytes 4718592 | tf_op jit(solution)/shard_map/force_middle/pallas_call | solution.py:319
  56.8 0.0 collective-permute-start.16
  56.8 1.2 %collective-permute-done.16 = f32[1,2,2,4,128]{4,3,2,1,0:T(4,128)S(1)} collective-permute-done((f32[1,2,2,4,128]{4,3,2,1,0:T(4,128)S(1)}, f32[1,2,2,4,128]{4,3,2,1,0:T(4,128)S(1)}, u32[]{:S(2)}, u32[]{:S(2)}) %collective-permute-start.16) | collective-permute-done | bytes 8224 | tf_op jit(solution)/shard_map/ppermute | solution.py:26
  58.0 1.9 %collective-permute-start.18 = (f32[1,4,2,4,128]{4,3,2,1,0:T(4,128)S(1)}, f32[1,4,2,4,128]{4,3,2,1,0:T(4,128)S(1)}, u32[]{:S(2)}, u32[]{:S(2)}) collective-permute-start(f32[1,4,2,4,128]{4,3,2,1,0:T(4,128)S(1)} %pad_maximum_fusion.8), channel_id=1, source_target_pairs={{8,0},{16,8},{24,16},{0,24},{9,1},{17,9},{25,17},{1,25},{10,2},{18... | collective-permute-start | bytes 49160 | tf_op jit(solution)/shard_map/ppermute | solution.py:32
  59.9 0.2 collective-permute-start.17
  60.1 1.7 %collective-permute-done.18 = f32[1,4,2,4,128]{4,3,2,1,0:T(4,128)S(1)} collective-permute-done((f32[1,4,2,4,128]{4,3,2,1,0:T(4,128)S(1)}, f32[1,4,2,4,128]{4,3,2,1,0:T(4,128)S(1)}, u32[]{:S(2)}, u32[]{:S(2)}) %collective-permute-start.18) | collective-permute-done | bytes 16416 | tf_op jit(solution)/shard_map/ppermute | solution.py:32
  61.8 2.7 %collective-permute-done.17 = f32[1,4,2,4,128]{4,3,2,1,0:T(4,128)S(1)} collective-permute-done((f32[1,4,2,4,128]{4,3,2,1,0:T(4,128)S(1)}, f32[1,4,2,4,128]{4,3,2,1,0:T(4,128)S(1)}, u32[]{:S(2)}, u32[]{:S(2)}) %collective-permute-start.17) | collective-permute-done | bytes 16416 | tf_op jit(solution)/shard_map/ppermute | solution.py:31
  64.5 0.1 collective-permute-start.20
  64.6 2.0 %collective-permute-start.19 = (f32[3,4,2,4,128]{4,3,2,1,0:T(4,128)S(1)}, f32[3,4,2,4,128]{4,3,2,1,0:T(4,128)S(1)}, u32[]{:S(2)}, u32[]{:S(2)}) collective-permute-start(f32[3,4,2,4,128]{4,3,2,1,0:T(4,128)S(1)} %pad_maximum_fusion.2.mid_ref), channel_id=1, source_target_pairs={{0,1},{1,2},{2,3},{3,0},{4,5},{5,6},{6,7},{7,4},{8,9},{9,10},{10,1... | collective-permute-start | bytes 147464 | tf_op jit(solution)/shard_map/ppermute | solution.py:31
  66.6 1.0 %inner_density.5 = (f32[4,128]{1,0:T(4,128)S(1)}, bf16[48,3072]{1,0:T(8,128)(2,1)S(1)}, f32[8,3072]{1,0:T(8,128)S(1)}) custom-call(f32[3,4,2,4,128]{4,3,2,1,0:T(4,128)S(1)} %pad_maximum_fusion.2.mid_ref), custom_call_target="tpu_custom_call" | custom-call | flops 58982400 | bytes 4718592 | tf_op jit(solution)/shard_map/inner_density/pallas_call | solution.py:319
  67.6 1.3 %collective-permute-done.20.high_ref = f32[3,4,2,4,128]{4,3,2,1,0:T(4,128)S(1)} collective-permute-done((f32[3,4,2,4,128]{4,3,2,1,0:T(4,128)S(1)}, f32[3,4,2,4,128]{4,3,2,1,0:T(4,128)S(1)}, u32[]{:S(2)}, u32[]{:S(2)}) %collective-permute-start.20) | collective-permute-done | bytes 49184 | tf_op jit(solution)/shard_map/ppermute | solution.py:32
  68.9 1.6 %collective-permute-done.19.low_ref = f32[3,4,2,4,128]{4,3,2,1,0:T(4,128)S(1)} collective-permute-done((f32[3,4,2,4,128]{4,3,2,1,0:T(4,128)S(1)}, f32[3,4,2,4,128]{4,3,2,1,0:T(4,128)S(1)}, u32[]{:S(2)}, u32[]{:S(2)}) %collective-permute-start.19) | collective-permute-done | bytes 49184 | tf_op jit(solution)/shard_map/ppermute | solution.py:31
  70.5 1.9 %outer_density.5 = (f32[8,128]{1,0:T(8,128)S(1)}, bf16[48,3072]{1,0:T(8,128)(2,1)S(1)}, f32[8,3072]{1,0:T(8,128)S(1)}) custom-call(f32[3,4,2,4,128]{4,3,2,1,0:T(4,128)S(1)} %pad_maximum_fusion.2.mid_ref, f32[3,4,2,4,128]{4,3,2,1,0:T(4,128)S(1)} %collective-permute-done.19.low_ref, f32[3,4,2,4,128]{4,3,2,1,0:T(4,128)S(1)} %collective-permute-done.20.high_ref, ...), custom_call_target="tpu_custom_call" | custom-call | flops 117964800 | bytes 9437184 | tf_op jit(solution)/shard_map/outer_density/pallas_call | solution.py:319
  72.4 0.1 collective-permute-start.21
  72.5 1.2 %collective-permute-done.21 = f32[1,2,4,128]{3,2,1,0:T(4,128)S(1)} collective-permute-done((f32[1,2,4,128]{3,2,1,0:T(4,128)S(1)}, f32[1,2,4,128]{3,2,1,0:T(4,128)S(1)}, u32[]{:S(2)}, u32[]{:S(2)}) %collective-permute-start.21) | collective-permute-done | bytes 4128 | tf_op jit(solution)/shard_map/ppermute | solution.py:26
  73.6 0.3 collective-permute-start.23
  74.0 1.8 %collective-permute-start.22 = (f32[1,4,4,128]{3,2,1,0:T(4,128)S(1)}, f32[1,4,4,128]{3,2,1,0:T(4,128)S(1)}, u32[]{:S(2)}, u32[]{:S(2)}) collective-permute-start(f32[1,4,4,128]{3,2,1,0:T(4,128)S(1)} %pad_maximum_fusion.12), channel_id=1, source_target_pairs={{0,8},{8,16},{16,24},{24,0},{1,9},{9,17},{17,25},{25,1},{2,10},{10... | collective-permute-start | bytes 24584 | tf_op jit(solution)/shard_map/ppermute | solution.py:31
  75.7 1.4 %column_force.5.column_ref = f32[4,4,128]{2,1,0:T(4,128)S(1)} custom-call(f32[3,4,2,4,128]{4,3,2,1,0:T(4,128)S(1)} %pad_maximum_fusion.2.mid_ref, f32[3,4,2,4,128]{4,3,2,1,0:T(4,128)S(1)} %collective-permute-done.19.low_ref, f32[3,4,2,4,128]{4,3,2,1,0:T(4,128)S(1)} %collective-permute-done.20.high_ref, f32[16,128]{1,0:T(8,128)S(1)} %bitcast.34, ...), custom_call_target="tpu_custom_call" | custom-call | flops 29491200 | bytes 2359296 | tf_op jit(solution)/shard_map/column_force/pallas_call | solution.py:319
  77.2 0.2 collective-permute-done.23
  77.3 1.2 %collective-permute-done.22 = f32[1,4,4,128]{3,2,1,0:T(4,128)S(1)} collective-permute-done((f32[1,4,4,128]{3,2,1,0:T(4,128)S(1)}, f32[1,4,4,128]{3,2,1,0:T(4,128)S(1)}, u32[]{:S(2)}, u32[]{:S(2)}) %collective-permute-start.22) | collective-permute-done | bytes 8224 | tf_op jit(solution)/shard_map/ppermute | solution.py:31
  78.5 3.2 %force_last.1 = f32[3,4,128]{2,1,0:T(4,128)} custom-call(f32[3,4,2,4,128]{4,3,2,1,0:T(4,128)S(1)} %pad_maximum_fusion.2.mid_ref, f32[3,4,2,4,128]{4,3,2,1,0:T(4,128)S(1)} %collective-permute-done.19.low_ref, f32[3,4,2,4,128]{4,3,2,1,0:T(4,128)S(1)} %collective-permute-done.20.high_ref, f32[48,128]{1,0:T(8,128)S(1)} %bitcast.25, ...), custom_call_target="tpu_custom_call" | custom-call | flops 58982400 | bytes 4718592 | tf_op jit(solution)/shard_map/force_last/pallas_call | solution.py:319
  (23 shorter events, 0.1 us)
Async XLA Ops:
  0.6 0.7 copy-start.1
  1.3 0.7 copy-start.2
  2.1 1.4 %collective-permute-start = (f32[1,2,2,4,128]{4,3,2,1,0:T(4,128)S(1)}, f32[1,2,2,4,128]{4,3,2,1,0:T(4,128)S(1)}, u32[]{:S(2)}, u32[]{:S(2)}) collective-permute-start(f32[1,2,2,4,128]{4,3,2,1,0:T(4,128)S(1)} %pad_maximum_fusion.9), channel_id=1, source_target_pairs={{0,4},{4,0},{1,5},{5,1},{2,6},{6,2},{3,7},{7,3},{8,12},{12,8},{9,1... | collective-permute-start | bytes 24584 | tf_op jit(solution)/shard_map/ppermute | solution.py:26
  3.5 5.3 %collective-permute-start.2 = (f32[1,4,2,4,128]{4,3,2,1,0:T(4,128)S(1)}, f32[1,4,2,4,128]{4,3,2,1,0:T(4,128)S(1)}, u32[]{:S(2)}, u32[]{:S(2)}) collective-permute-start(f32[1,4,2,4,128]{4,3,2,1,0:T(4,128)S(1)} %pad_maximum_fusion.6), channel_id=1, source_target_pairs={{8,0},{16,8},{24,16},{0,24},{9,1},{17,9},{25,17},{1,25},{10,2},{18... | collective-permute-start | bytes 49160 | tf_op jit(solution)/shard_map/ppermute | solution.py:32
  7.3 4.6 %collective-permute-start.1 = (f32[1,4,2,4,128]{4,3,2,1,0:T(4,128)S(1)}, f32[1,4,2,4,128]{4,3,2,1,0:T(4,128)S(1)}, u32[]{:S(2)}, u32[]{:S(2)}) collective-permute-start(f32[1,4,2,4,128]{4,3,2,1,0:T(4,128)S(1)} %pad_maximum_fusion.6), channel_id=1, source_target_pairs={{0,8},{8,16},{16,24},{24,0},{1,9},{9,17},{17,25},{25,1},{2,10},{10... | collective-permute-start | bytes 49160 | tf_op jit(solution)/shard_map/ppermute | solution.py:31
  12.0 5.4 %collective-permute-start.4 = (f32[3,4,2,4,128]{4,3,2,1,0:T(4,128)S(1)}, f32[3,4,2,4,128]{4,3,2,1,0:T(4,128)S(1)}, u32[]{:S(2)}, u32[]{:S(2)}) collective-permute-start(f32[3,4,2,4,128]{4,3,2,1,0:T(4,128)S(1)} %pad_maximum_fusion.mid_ref), channel_id=1, source_target_pairs={{1,0},{2,1},{3,2},{0,3},{5,4},{6,5},{7,6},{4,7},{9,8},{10,9},{11,1... | collective-permute-start | bytes 147464 | tf_op jit(solution)/shard_map/ppermute | solution.py:32
  15.6 5.9 %collective-permute-start.3 = (f32[3,4,2,4,128]{4,3,2,1,0:T(4,128)S(1)}, f32[3,4,2,4,128]{4,3,2,1,0:T(4,128)S(1)}, u32[]{:S(2)}, u32[]{:S(2)}) collective-permute-start(f32[3,4,2,4,128]{4,3,2,1,0:T(4,128)S(1)} %pad_maximum_fusion.mid_ref), channel_id=1, source_target_pairs={{0,1},{1,2},{2,3},{3,0},{4,5},{5,6},{6,7},{7,4},{8,9},{9,10},{10,1... | collective-permute-start | bytes 147464 | tf_op jit(solution)/shard_map/ppermute | solution.py:31
  23.4 1.2 %collective-permute-start.5 = (f32[1,2,4,128]{3,2,1,0:T(4,128)S(1)}, f32[1,2,4,128]{3,2,1,0:T(4,128)S(1)}, u32[]{:S(2)}, u32[]{:S(2)}) collective-permute-start(f32[1,2,4,128]{3,2,1,0:T(4,128)S(1)} %bitcast.35), channel_id=1, source_target_pairs={{0,4},{4,0},{1,5},{5,1},{2,6},{6,2},{3,7},{7,3},{8,12},{12,8},{9,1... | collective-permute-start | bytes 12296 | tf_op jit(solution)/shard_map/ppermute | solution.py:26
  24.6 3.7 %collective-permute-start.7 = (f32[1,4,4,128]{3,2,1,0:T(4,128)S(1)}, f32[1,4,4,128]{3,2,1,0:T(4,128)S(1)}, u32[]{:S(2)}, u32[]{:S(2)}) collective-permute-start(f32[1,4,4,128]{3,2,1,0:T(4,128)S(1)} %pad_maximum_fusion.10), channel_id=1, source_target_pairs={{8,0},{16,8},{24,16},{0,24},{9,1},{17,9},{25,17},{1,25},{10,2},{18... | collective-permute-start | bytes 24584 | tf_op jit(solution)/shard_map/ppermute | solution.py:32
  24.7 4.6 %collective-permute-start.6 = (f32[1,4,4,128]{3,2,1,0:T(4,128)S(1)}, f32[1,4,4,128]{3,2,1,0:T(4,128)S(1)}, u32[]{:S(2)}, u32[]{:S(2)}) collective-permute-start(f32[1,4,4,128]{3,2,1,0:T(4,128)S(1)} %pad_maximum_fusion.10), channel_id=1, source_target_pairs={{0,8},{8,16},{16,24},{24,0},{1,9},{9,17},{17,25},{25,1},{2,10},{10... | collective-permute-start | bytes 24584 | tf_op jit(solution)/shard_map/ppermute | solution.py:31
  29.3 0.7 copy-start
  32.6 1.2 %collective-permute-start.8 = (f32[1,2,2,4,128]{4,3,2,1,0:T(4,128)S(1)}, f32[1,2,2,4,128]{4,3,2,1,0:T(4,128)S(1)}, u32[]{:S(2)}, u32[]{:S(2)}) collective-permute-start(f32[1,2,2,4,128]{4,3,2,1,0:T(4,128)S(1)} %bitcast.29), channel_id=1, source_target_pairs={{0,4},{4,0},{1,5},{5,1},{2,6},{6,2},{3,7},{7,3},{8,12},{12,8},{9,1... | collective-permute-start | bytes 24584 | tf_op jit(solution)/shard_map/ppermute | solution.py:26
  33.9 3.8 %collective-permute-start.10 = (f32[1,4,2,4,128]{4,3,2,1,0:T(4,128)S(1)}, f32[1,4,2,4,128]{4,3,2,1,0:T(4,128)S(1)}, u32[]{:S(2)}, u32[]{:S(2)}) collective-permute-start(f32[1,4,2,4,128]{4,3,2,1,0:T(4,128)S(1)} %pad_maximum_fusion.7), channel_id=1, source_target_pairs={{8,0},{16,8},{24,16},{0,24},{9,1},{17,9},{25,17},{1,25},{10,2},{18... | collective-permute-start | bytes 49160 | tf_op jit(solution)/shard_map/ppermute | solution.py:32
  34.9 4.6 %collective-permute-start.9 = (f32[1,4,2,4,128]{4,3,2,1,0:T(4,128)S(1)}, f32[1,4,2,4,128]{4,3,2,1,0:T(4,128)S(1)}, u32[]{:S(2)}, u32[]{:S(2)}) collective-permute-start(f32[1,4,2,4,128]{4,3,2,1,0:T(4,128)S(1)} %pad_maximum_fusion.7), channel_id=1, source_target_pairs={{0,8},{8,16},{16,24},{24,0},{1,9},{9,17},{17,25},{25,1},{2,10},{10... | collective-permute-start | bytes 49160 | tf_op jit(solution)/shard_map/ppermute | solution.py:31
  39.6 4.3 %collective-permute-start.12 = (f32[3,4,2,4,128]{4,3,2,1,0:T(4,128)S(1)}, f32[3,4,2,4,128]{4,3,2,1,0:T(4,128)S(1)}, u32[]{:S(2)}, u32[]{:S(2)}) collective-permute-start(f32[3,4,2,4,128]{4,3,2,1,0:T(4,128)S(1)} %pad_maximum_fusion.1.mid_ref), channel_id=1, source_target_pairs={{1,0},{2,1},{3,2},{0,3},{5,4},{6,5},{7,6},{4,7},{9,8},{10,9},{11,1... | collective-permute-start | bytes 147464 | tf_op jit(solution)/shard_map/ppermute | solution.py:32
  39.7 5.9 %collective-permute-start.11 = (f32[3,4,2,4,128]{4,3,2,1,0:T(4,128)S(1)}, f32[3,4,2,4,128]{4,3,2,1,0:T(4,128)S(1)}, u32[]{:S(2)}, u32[]{:S(2)}) collective-permute-start(f32[3,4,2,4,128]{4,3,2,1,0:T(4,128)S(1)} %pad_maximum_fusion.1.mid_ref), channel_id=1, source_target_pairs={{0,1},{1,2},{2,3},{3,0},{4,5},{5,6},{6,7},{7,4},{8,9},{9,10},{10,1... | collective-permute-start | bytes 147464 | tf_op jit(solution)/shard_map/ppermute | solution.py:31
  47.5 1.2 %collective-permute-start.13 = (f32[1,2,4,128]{3,2,1,0:T(4,128)S(1)}, f32[1,2,4,128]{3,2,1,0:T(4,128)S(1)}, u32[]{:S(2)}, u32[]{:S(2)}) collective-permute-start(f32[1,2,4,128]{3,2,1,0:T(4,128)S(1)} %bitcast.38), channel_id=1, source_target_pairs={{0,4},{4,0},{1,5},{5,1},{2,6},{6,2},{3,7},{7,3},{8,12},{12,8},{9,1... | collective-permute-start | bytes 12296 | tf_op jit(solution)/shard_map/ppermute | solution.py:26
  48.7 3.7 %collective-permute-start.15 = (f32[1,4,4,128]{3,2,1,0:T(4,128)S(1)}, f32[1,4,4,128]{3,2,1,0:T(4,128)S(1)}, u32[]{:S(2)}, u32[]{:S(2)}) collective-permute-start(f32[1,4,4,128]{3,2,1,0:T(4,128)S(1)} %pad_maximum_fusion.11), channel_id=1, source_target_pairs={{8,0},{16,8},{24,16},{0,24},{9,1},{17,9},{25,17},{1,25},{10,2},{18... | collective-permute-start | bytes 24584 | tf_op jit(solution)/shard_map/ppermute | solution.py:32
  49.0 4.6 %collective-permute-start.14 = (f32[1,4,4,128]{3,2,1,0:T(4,128)S(1)}, f32[1,4,4,128]{3,2,1,0:T(4,128)S(1)}, u32[]{:S(2)}, u32[]{:S(2)}) collective-permute-start(f32[1,4,4,128]{3,2,1,0:T(4,128)S(1)} %pad_maximum_fusion.11), channel_id=1, source_target_pairs={{0,8},{8,16},{16,24},{24,0},{1,9},{9,17},{17,25},{25,1},{2,10},{10... | collective-permute-start | bytes 24584 | tf_op jit(solution)/shard_map/ppermute | solution.py:31
  56.8 1.2 %collective-permute-start.16 = (f32[1,2,2,4,128]{4,3,2,1,0:T(4,128)S(1)}, f32[1,2,2,4,128]{4,3,2,1,0:T(4,128)S(1)}, u32[]{:S(2)}, u32[]{:S(2)}) collective-permute-start(f32[1,2,2,4,128]{4,3,2,1,0:T(4,128)S(1)} %bitcast.26), channel_id=1, source_target_pairs={{0,4},{4,0},{1,5},{5,1},{2,6},{6,2},{3,7},{7,3},{8,12},{12,8},{9,1... | collective-permute-start | bytes 24584 | tf_op jit(solution)/shard_map/ppermute | solution.py:26
  58.0 3.8 %collective-permute-start.18 = (f32[1,4,2,4,128]{4,3,2,1,0:T(4,128)S(1)}, f32[1,4,2,4,128]{4,3,2,1,0:T(4,128)S(1)}, u32[]{:S(2)}, u32[]{:S(2)}) collective-permute-start(f32[1,4,2,4,128]{4,3,2,1,0:T(4,128)S(1)} %pad_maximum_fusion.8), channel_id=1, source_target_pairs={{8,0},{16,8},{24,16},{0,24},{9,1},{17,9},{25,17},{1,25},{10,2},{18... | collective-permute-start | bytes 49160 | tf_op jit(solution)/shard_map/ppermute | solution.py:32
  59.9 4.6 %collective-permute-start.17 = (f32[1,4,2,4,128]{4,3,2,1,0:T(4,128)S(1)}, f32[1,4,2,4,128]{4,3,2,1,0:T(4,128)S(1)}, u32[]{:S(2)}, u32[]{:S(2)}) collective-permute-start(f32[1,4,2,4,128]{4,3,2,1,0:T(4,128)S(1)} %pad_maximum_fusion.8), channel_id=1, source_target_pairs={{0,8},{8,16},{16,24},{24,0},{1,9},{9,17},{17,25},{25,1},{2,10},{10... | collective-permute-start | bytes 49160 | tf_op jit(solution)/shard_map/ppermute | solution.py:31
  64.5 4.4 %collective-permute-start.20 = (f32[3,4,2,4,128]{4,3,2,1,0:T(4,128)S(1)}, f32[3,4,2,4,128]{4,3,2,1,0:T(4,128)S(1)}, u32[]{:S(2)}, u32[]{:S(2)}) collective-permute-start(f32[3,4,2,4,128]{4,3,2,1,0:T(4,128)S(1)} %pad_maximum_fusion.2.mid_ref), channel_id=1, source_target_pairs={{1,0},{2,1},{3,2},{0,3},{5,4},{6,5},{7,6},{4,7},{9,8},{10,9},{11,1... | collective-permute-start | bytes 147464 | tf_op jit(solution)/shard_map/ppermute | solution.py:32
  64.6 5.9 %collective-permute-start.19 = (f32[3,4,2,4,128]{4,3,2,1,0:T(4,128)S(1)}, f32[3,4,2,4,128]{4,3,2,1,0:T(4,128)S(1)}, u32[]{:S(2)}, u32[]{:S(2)}) collective-permute-start(f32[3,4,2,4,128]{4,3,2,1,0:T(4,128)S(1)} %pad_maximum_fusion.2.mid_ref), channel_id=1, source_target_pairs={{0,1},{1,2},{2,3},{3,0},{4,5},{5,6},{6,7},{7,4},{8,9},{9,10},{10,1... | collective-permute-start | bytes 147464 | tf_op jit(solution)/shard_map/ppermute | solution.py:31
  72.4 1.2 %collective-permute-start.21 = (f32[1,2,4,128]{3,2,1,0:T(4,128)S(1)}, f32[1,2,4,128]{3,2,1,0:T(4,128)S(1)}, u32[]{:S(2)}, u32[]{:S(2)}) collective-permute-start(f32[1,2,4,128]{3,2,1,0:T(4,128)S(1)} %bitcast.41), channel_id=1, source_target_pairs={{0,4},{4,0},{1,5},{5,1},{2,6},{6,2},{3,7},{7,3},{8,12},{12,8},{9,1... | collective-permute-start | bytes 12296 | tf_op jit(solution)/shard_map/ppermute | solution.py:26
  73.6 3.7 %collective-permute-start.23 = (f32[1,4,4,128]{3,2,1,0:T(4,128)S(1)}, f32[1,4,4,128]{3,2,1,0:T(4,128)S(1)}, u32[]{:S(2)}, u32[]{:S(2)}) collective-permute-start(f32[1,4,4,128]{3,2,1,0:T(4,128)S(1)} %pad_maximum_fusion.12), channel_id=1, source_target_pairs={{8,0},{16,8},{24,16},{0,24},{9,1},{17,9},{25,17},{1,25},{10,2},{18... | collective-permute-start | bytes 24584 | tf_op jit(solution)/shard_map/ppermute | solution.py:32
  74.0 4.5 %collective-permute-start.22 = (f32[1,4,4,128]{3,2,1,0:T(4,128)S(1)}, f32[1,4,4,128]{3,2,1,0:T(4,128)S(1)}, u32[]{:S(2)}, u32[]{:S(2)}) collective-permute-start(f32[1,4,4,128]{3,2,1,0:T(4,128)S(1)} %pad_maximum_fusion.12), channel_id=1, source_target_pairs={{0,8},{8,16},{16,24},{24,0},{1,9},{9,17},{17,25},{25,1},{2,10},{10... | collective-permute-start | bytes 24584 | tf_op jit(solution)/shard_map/ppermute | solution.py:31
where the time goes:
time: 82 us; the launch traced here: 81.7 us
  waiting for transfers between devices  33.9 us (41%)
  starting transfers between devices  22.8 us (28%)
  Pallas kernels  22 us (27%)
  local copies, waits for them, and re-layouts  2.07 us (3%)
    pallas_call x12, Pallas kernels, call(): pl.pallas_call(kernel, out_shape=out_shape, in_specs=[vmem] * len(operand...  22 us
    ppermute x9, waiting for transfers between devices, neighbours(): lax.ppermute(tail, axis, [(i, (i + 1) % count) for i in range(count)])  18.6 us
    ppermute x9, starting transfers between devices, neighbours(): lax.ppermute(head, axis, [((i + 1) % count, i) for i in range(count)])  11.2 us
    ppermute x9, starting transfers between devices, neighbours(): lax.ppermute(tail, axis, [(i, (i + 1) % count) for i in range(count)])  10.8 us
    ppermute x9, waiting for transfers between devices, neighbours(): lax.ppermute(head, axis, [((i + 1) % count, i) for i in range(count)])  8.69 us
    ppermute x6, waiting for transfers between devices, neighbours(): other = lax.ppermute(cells, axis, [(0, 1), (1, 0)])  6.62 us
    unnamed x7, local copies, waits for them, and re-layouts  2.06 us
  transfers between devices with their start and end apart: 24, of which 24 were waited for; matrix products, arithmetic and copies ran while one was open for 0% of the time, Pallas kernels for 9%

commit v1 on v0

v1 whole, which is shorter than its diff:
```python
import functools

import jax
import jax.numpy as jnp
from jax import lax
from jax.experimental import pallas as pl
from jax.experimental.pallas import tpu as pltpu
from jax.sharding import PartitionSpec as P

time_step = 0.05
half_kick = 0.5 * time_step
LANES = 128
GRANT = 8 * 1024 * 1024
ROOT = 1.3 ** (1.0 / 3.0)
STEPS = (-1, 0, 1)


def neighbours(cells, axis, dim, width):
    count = lax.axis_size(axis)
    size = cells.shape[dim]
    head = lax.slice_in_dim(cells, 0, width, axis=dim)
    tail = lax.slice_in_dim(cells, size - width, size, axis=dim)
    if count == 1:
        return tail, head
    if count == 2 and size == 2 * width:
        other = lax.ppermute(cells, axis, [(0, 1), (1, 0)])
        return (
            lax.slice_in_dim(other, width, size, axis=dim),
            lax.slice_in_dim(other, 0, width, axis=dim),
        )
    below = lax.ppermute(tail, axis, [(i, (i + 1) % count) for i in range(count)])
    above = lax.ppermute(head, axis, [((i + 1) % count, i) for i in range(count)])
    return below, above


def ring_halo(cells, axis, dim, width):
    below, above = neighbours(cells, axis, dim, width)
    return jnp.concatenate([below, cells, above], axis=dim)


def split3(value):
    high = value.astype(jnp.bfloat16).astype(jnp.float32)
    rest = value - high
    middle = rest.astype(jnp.bfloat16).astype(jnp.float32)
    return high, middle, rest - middle


def partner_block(row):
    high, middle, low = split3(row)
    first = jnp.concatenate([high, middle], axis=0).astype(jnp.bfloat16)
    last = jnp.concatenate([low, high], axis=0).astype(jnp.bfloat16)
    return jnp.concatenate([first, first, last], axis=0)


def target_block(row):
    high, middle, low = split3(row)
    stacked = jnp.concatenate([high, high, middle, middle, high, low], axis=0)
    return jnp.transpose(stacked).astype(jnp.bfloat16)


class Grid:
    def __init__(self, own):
        self.cx, self.cy, self.cz = own
        self.ex, self.ey, self.ez = own[0] + 2, own[1] + 2, own[2] + 4
        row = lax.broadcasted_iota(jnp.int32, (8, LANES), 0)
        self.row = row
        self.masks = [(row == k).astype(jnp.float32) for k in range(7)]
        self.spatial = self.masks[0] + self.masks[1] + self.masks[2]

    def own_targets(self):
        return [
            (a, b, c)
            for a in range(1, self.cx + 1)
            for b in range(1, self.cy + 1)
            for c in range(2, self.cz + 2)
        ]

    def edge_targets(self):
        return [
            (a, b, c)
            for a in range(1, self.cx + 1)
            for b in range(1, self.cy + 1)
            for c in (1, self.cz + 2)
        ]

    def slope_row(self, a, b, c):
        return ((a - 1) * self.cy + b - 1) * (self.cz + 2) + c - 1

    def layer(self, c):
        if c in (0, self.ez - 1):
            return "far", int(c > 0)
        if c in (1, self.ez - 2):
            return "edge", int(c > 1)
        return "own", c - 2

    def own_y(self, layer, a, b):
        first, last = max(b - 1, 1), min(b + 1, self.cy)
        return ((layer * self.ex + a) * self.cy + first - 1) * LANES, first, last - first + 1

    def ghost_y(self, side, a, c):
        return ((side * self.ex + a) * self.ez + c) * LANES

    def sides(self, b):
        return [side for side in (0, 1) if b == (1, self.cy)[side]]

    def placed(self, tile, a, b, c):
        m = self.masks
        shift = (
            (a + 0.5 - 0.5 * self.ex) * m[0]
            + (b + 0.5 - 0.5 * self.ey) * m[1]
            + (m[4] + (c + 0.5 - 0.5 * self.ez) * m[2])
        )
        point = jnp.concatenate([tile, jnp.zeros((4, LANES), jnp.float32)], axis=0)
        point = point * self.spatial + shift
        return point, jnp.sum(point * point, axis=0, keepdims=True)

    def partner(self, tile, a, b, c):
        point, bulk = self.placed(tile, a, b, c)
        scale = tile[3:4]
        block = partner_block(jnp.where(self.row == 3, 1.0 - bulk, point) * scale)
        strength = jnp.where(scale > 1.05, 0.4 / ROOT, 0.3)
        return block, jnp.where(self.row == 3, strength, point)

    def target(self, tile, a, b, c):
        point, bulk = self.placed(tile, a, b, c)
        twice = jnp.where(self.row == 4, 2.0 - bulk, 2.0 * point)
        return point, twice + self.masks[3]


def density_of(left_ref, place, sources):
    rows = 64
    sums = []
    for start in range(0, LANES, rows):
        total = jnp.zeros((rows, LANES), jnp.float32)
        for ref, first, count, same in sources:
            near = jnp.dot(
                left_ref[place, start : start + rows, :],
                ref[:, first : first + count * LANES],
                preferred_element_type=jnp.float32,
            )
            for k in range(count):
                part = jnp.maximum(near[:, k * LANES : (k + 1) * LANES], 0.0)
                if k == same:
                    i = lax.broadcasted_iota(jnp.int32, (rows, LANES), 0)
                    j = lax.broadcasted_iota(jnp.int32, (rows, LANES), 1)
                    part = jnp.where(i + start == j, 0.0, part)
                total = total + part * part * part
        sums.append(total)
    return jnp.sum(jnp.transpose(jnp.concatenate(sums, axis=0)), axis=0, keepdims=True)


def own_y_sources(grid, refs, target, layers):
    a, b, c = target
    sources = []
    for r in STEPS:
        which, layer = grid.layer(c + r)
        if which not in layers:
            continue
        for p in STEPS:
            first, start, count = grid.own_y(layer, a + p, b)
            same = b - start if (p == 0 and r == 0) else -1
            sources.append((refs[which], first, count, same))
    return sources


def inner_density_kernel(own, mid_ref, sum_ref, part_ref, point_ref, left_ref):
    grid = Grid(own)
    for c in range(2, grid.cz + 2):
        for a in range(grid.ex):
            for b in range(1, grid.cy + 1):
                first = ((c - 2) * grid.ex + a) * grid.cy * LANES + (b - 1) * LANES
                lanes = slice(first, first + LANES)
                part_ref[:, lanes], point_ref[:, lanes] = grid.partner(mid_ref[a, b - 1, c - 2], a, b, c)
    for place, target in enumerate(grid.own_targets()):
        a, b, c = target
        _, row = grid.target(mid_ref[a, b - 1, c - 2], a, b, c)
        left_ref[place] = target_block(row)
        sources = own_y_sources(grid, {"own": part_ref}, target, ("own",))
        sum_ref[place : place + 1, :] = density_of(left_ref, place, sources)


def outer_density_kernel(own, low_ref, high_ref, inner_ref, part_ref, left_ref, sum_ref, edge_ref, edge_point_ref, edge_left_ref, far_ref):
    grid = Grid(own)

    def tile_of(a, b, c):
        return low_ref[a, b - 1, c] if c < 2 else high_ref[a, b - 1, c - grid.cz - 2]

    for c in (0, 1, grid.ez - 2, grid.ez - 1):
        which, layer = grid.layer(c)
        for a in range(grid.ex):
            for b in range(1, grid.cy + 1):
                first = ((layer * grid.ex + a) * grid.cy + b - 1) * LANES
                lanes = slice(first, first + LANES)
                block, point = grid.partner(tile_of(a, b, c), a, b, c)
                if which == "edge":
                    edge_ref[:, lanes] = block
                    edge_point_ref[:, lanes] = point
                else:
                    far_ref[:, lanes] = block
    refs = {"own": part_ref, "edge": edge_ref, "far": far_ref}
    for place, target in enumerate(grid.edge_targets()):
        _, row = grid.target(tile_of(*target), *target)
        edge_left_ref[place] = target_block(row)
        sources = own_y_sources(grid, refs, target, ("own", "edge", "far"))
        where = grid.slope_row(*target)
        sum_ref[where : where + 1, :] = density_of(edge_left_ref, place, sources)
    for place, target in enumerate(grid.own_targets()):
        where = grid.slope_row(*target)
        density = inner_ref[place : place + 1, :]
        sources = own_y_sources(grid, refs, target, ("edge",))
        if sources:
            density = density + density_of(left_ref, place, sources)
        sum_ref[where : where + 1, :] = density


def last_density_kernel(own, mid_ref, low_ref, high_ref, below_ref, above_ref, sum_ref, left_ref, edge_left_ref, slope_ref, ghost_ref, ghost_point_ref):
    grid = Grid(own)
    for side, ref in enumerate((below_ref, above_ref)):
        for a in range(grid.ex):
            for c in range(grid.ez):
                first = grid.ghost_y(side, a, c)
                lanes = slice(first, first + LANES)
                ghost_ref[:, lanes], ghost_point_ref[:, lanes] = grid.partner(
                    ref[a, 0, c], a, (0, grid.ey - 1)[side], c
                )
    groups = ((grid.own_targets(), left_ref), (grid.edge_targets(), edge_left_ref))
    for targets, rows_ref in groups:
        for place, target in enumerate(targets):
            a, b, c = target
            if c < 2:
                tile = low_ref[a, b - 1, c]
            elif c >= grid.cz + 2:
                tile = high_ref[a, b - 1, c - grid.cz - 2]
            else:
                tile = mid_ref[a, b - 1, c - 2]
            where = grid.slope_row(a, b, c)
            density = sum_ref[where : where + 1, :]
            sources = [
                (ghost_ref, grid.ghost_y(side, a + p, c - 1), 3, -1) for side in grid.sides(b) for p in STEPS
            ]
            if sources:
                density = density + density_of(rows_ref, place, sources)
            present = jnp.where(tile[3:4] > 0.5, -0.5, 0.0)
            slope_ref[where : where + 1, :] = present / jnp.sqrt(density + 1.0)


def pair_block(grid, scale, slope):
    inverse = jnp.where(scale > 1.05, 0.75 / (ROOT * ROOT), 0.75)
    row = jnp.where(grid.row == 5, 0.75 * scale, jnp.where(grid.row == 6, slope * inverse, 0.0))
    return partner_block(row)


def force_of(left_ref, place, sources):
    rows = 32
    sums = [[] for _ in range(4)]
    for start in range(0, LANES, rows):
        total = [jnp.zeros((rows, LANES), jnp.float32) for _ in range(4)]
        for ref, value_ref, first, pair_ref, pair_first, count in sources:
            left = left_ref[place, start : start + rows, :]
            near = jnp.dot(left, ref[:, first : first + count * LANES], preferred_element_type=jnp.float32)
            kappa = jnp.dot(
                left, pair_ref[:, pair_first : pair_first + count * LANES], preferred_element_type=jnp.float32
            )
            for k in range(count):
                part = slice(k * LANES, (k + 1) * LANES)
                lanes = slice(first + k * LANES, first + (k + 1) * LANES)
                s = jnp.maximum(near[:, part], 0.0)
                w = s * (value_ref[3:4, lanes] + s * kappa[:, part])
                total[3] = total[3] + w
                for axis in range(3):
                    total[axis] = total[axis] + w * value_ref[axis : axis + 1, lanes]
        for k in range(4):
            sums[k].append(total[k])
    return [
        jnp.sum(jnp.transpose(jnp.concatenate(parts, axis=0)), axis=0, keepdims=True) for parts in sums
    ]


def own_y_force(grid, columns, scale, slope, left_ref, own_refs, edge_refs, pair_ref, result):
    where = {}
    for c in range(1, grid.ez - 1):
        for a in columns:
            for b in range(1, grid.cy + 1):
                first = where[(a, b, c)] = len(where) * LANES
                pair_ref[:, first : first + LANES] = pair_block(grid, scale(a, b, c), slope(a, b, c))
    refs = {"own": own_refs, "edge": edge_refs}
    for place, (a, b, c) in enumerate(grid.own_targets()):
        sources = []
        for r in STEPS:
            which, layer = grid.layer(c + r)
            for p in STEPS:
                if a + p in columns:
                    first, start, count = grid.own_y(layer, a + p, b)
                    sources.append((*refs[which], first, pair_ref, where[(a + p, start, c + r)], count))
        result(place, force_of(left_ref, place, sources))


def scale_reader(grid, mid_ref, low_ref, high_ref):
    def scale(a, b, c):
        if c < 2:
            return low_ref[a, b - 1, c][3:4]
        if c >= grid.cz + 2:
            return high_ref[a, b - 1, c - grid.cz - 2][3:4]
        return mid_ref[a, b - 1, c - 2][3:4]

    return scale


def column_force_kernel(own, mid_ref, low_ref, high_ref, slope_ref, part_ref, point_ref, edge_ref, edge_point_ref, out_ref, left_ref, pair_ref):
    grid = Grid(own)
    m = grid.masks

    def slope(a, b, c):
        where = grid.slope_row(a, b, c)
        return slope_ref[where : where + 1, :]

    for place, (a, b, c) in enumerate(grid.own_targets()):
        tile = mid_ref[a, b - 1, c - 2]
        _, row = grid.target(tile, a, b, c)
        solute = tile[3:4] > 1.05
        left_ref[place] = target_block(
            row * jnp.where(solute, 0.8, 0.6)
            + slope(a, b, c) * jnp.where(solute, 1.0 / 0.16, 1.0 / 0.09) * m[5]
            + jnp.where(solute, 1.3 / 0.16, 1.0 / 0.09) * m[6]
        )

    def result(place, flat):
        for k in range(4):
            out_ref[k, place : place + 1, :] = flat[k]

    scale = scale_reader(grid, mid_ref, low_ref, high_ref)
    columns = range(1, grid.cx + 1)
    own_y_force(
        grid, columns, scale, slope, left_ref, (part_ref, point_ref), (edge_ref, edge_point_ref), pair_ref, result
    )


def side_force_kernel(own, mid_ref, low_ref, high_ref, slope_ref, part_ref, point_ref, edge_ref, edge_point_ref, column_ref, left_ref, out_ref, pair_ref):
    grid = Grid(own)

    def slope(a, b, c):
        where = grid.slope_row(a + 1, b, c)
        return slope_ref[where : where + 1, :]

    def result(place, flat):
        for k in range(4):
            out_ref[k, place : place + 1, :] = flat[k] + column_ref[k, place : place + 1, :]

    scale = scale_reader(grid, mid_ref, low_ref, high_ref)
    columns = (0, grid.ex - 1)
    own_y_force(
        grid, columns, scale, slope, left_ref, (part_ref, point_ref), (edge_ref, edge_point_ref), pair_ref, result
    )


def last_force_kernel(own, stage, mid_ref, below_ref, above_ref, slope_below_ref, slope_above_ref, ghost_ref, ghost_point_ref, column_ref, left_ref, vel_ref, *refs):
    new_vel_ref, new_loc_ref, pair_ref = refs
    grid = Grid(own)
    near_z = grid.cz + 2
    for side in (0, 1):
        cells_ref, slope_ref = ((below_ref, slope_below_ref), (above_ref, slope_above_ref))[side]
        for a in range(grid.ex):
            for c in range(near_z):
                first = ((side * grid.ex + a) * near_z + c) * LANES
                where = a * near_z + c
                pair_ref[:, first : first + LANES] = pair_block(
                    grid, cells_ref[a, 0, c + 1][3:4], slope_ref[where : where + 1, :]
                )
    for place, (a, b, c) in enumerate(grid.own_targets()):
        sources = [
            (
                ghost_ref,
                ghost_point_ref,
                grid.ghost_y(side, a + p, c - 1),
                pair_ref,
                ((side * grid.ex + a + p) * near_z + c - 2) * LANES,
                3,
            )
            for side in grid.sides(b)
            for p in STEPS
        ]
        row = slice(place, place + 1)
        flat = [column_ref[k, row, :] for k in range(4)]
        if sources:
            flat = [old + new for old, new in zip(flat, force_of(left_ref, place, sources))]
        tile = mid_ref[a, b - 1, c - 2]
        point, _ = grid.placed(tile, a, b, c)
        scale = tile[3:4]
        present = jnp.where(scale > 0.5, -2.0, 0.0)
        kick = half_kick * jnp.where(scale > 1.05, 1.6, 1.0)
        for axis in range(3):
            force = present * (flat[axis] - point[axis : axis + 1] * flat[3])
            speed = vel_ref[axis, row, :] + kick * force
            if stage == "middle":
                speed = speed + kick * force
            new_vel_ref[axis, row, :] = speed
            if stage == "last":
                new_loc_ref[axis, row, :] = tile[axis : axis + 1]
            else:
                new_loc_ref[place, axis : axis + 1, :] = tile[axis : axis + 1] + time_step * speed
        if stage != "last":
            new_loc_ref[place, 3:4, :] = scale


def on_device(positions, velocities, species, counts):
    cx, cy, cz, slots = positions.shape[1:]
    own = (cx, cy, cz)
    cells = cx * cy * cz
    ex, ez = cx + 2, cz + 4
    near = cz + 2
    present = lax.broadcasted_iota(jnp.int32, species.shape, 3) < counts[..., None]
    scale = jnp.where(present, jnp.where(species == 1, ROOT, 1.0), 0.0)
    location = jnp.concatenate([jnp.moveaxis(positions, 0, 3), scale[..., None, :]], axis=3)
    velocity = velocities.reshape(3, cells, slots)
    vmem = pl.BlockSpec(memory_space=pltpu.VMEM)
    flat_shape = jax.ShapeDtypeStruct((3, cells, slots), jnp.float32)

    def block(count):
        return jax.ShapeDtypeStruct((48, count * slots), jnp.bfloat16)

    def points(count):
        return jax.ShapeDtypeStruct((8, count * slots), jnp.float32)

    def rows(count):
        return jax.ShapeDtypeStruct((count, slots), jnp.float32)

    def lefts(count):
        return jax.ShapeDtypeStruct((count, slots, 48), jnp.bfloat16)

    def call(kernel, name, operands, out_shape, pairs, scratch=None):
        return pl.pallas_call(
            kernel,
            out_shape=out_shape,
            in_specs=[vmem] * len(operands),
            out_specs=[vmem] * len(out_shape),
            scratch_shapes=[] if scratch is None else [pltpu.VMEM(scratch.shape, scratch.dtype)],
            compiler_params=pltpu.CompilerParams(vmem_limit_bytes=GRANT),
            cost_estimate=pl.CostEstimate(
                flops=pairs * slots * slots * 50, bytes_accessed=pairs * slots * slots * 4, transcendentals=0
            ),
            name=name,
        )(*operands)

    def evaluate(location, velocity, stage):
        mid = ring_halo(location, "gx", 0, 1)
        low, high = neighbours(mid, "gz", 2, 2)
        tall = jnp.concatenate([low, mid, high], axis=2)
        inner, part, point, left = call(
            functools.partial(inner_density_kernel, own),
            "inner_density",
            [mid],
            [rows(cells), block(ex * cy * cz), points(ex * cy * cz), lefts(cells)],
            cells * 12,
        )
        tall, inner = lax.optimization_barrier((tall, inner))
        below, above = neighbours(tall, "gy", 1, 1)
        sums, edge, edge_point, edge_left = call(
            functools.partial(outer_density_kernel, own),
            "outer_density",
            [low, high, inner, part, left],
            [rows(cx * cy * near), block(ex * cy * 2), points(ex * cy * 2), lefts(cx * cy * 2)],
            cells * 24,
            block(ex * cy * 2),
        )
        slopes, ghost, ghost_point = call(
            functools.partial(last_density_kernel, own),
            "last_density",
            [mid, low, high, below, above, sums, left, edge_left],
            [rows(cx * cy * near), block(2 * ex * ez), points(2 * ex * ez)],
            cells * 18,
        )
        wide = ring_halo(slopes.reshape(cx, cy, near, slots), "gx", 0, 1)
        shared = [part, point, edge, edge_point]
        column, left = call(
            functools.partial(column_force_kernel, own),
            "column_force",
            [mid, low, high, slopes, *shared],
            [jax.ShapeDtypeStruct((4, cells, slots), jnp.float32), lefts(cells)],
            cells * 6,
            block(cx * cy * near),
        )
        wide, column = lax.optimization_barrier((wide, column))
        slope_below, slope_above = neighbours(wide, "gy", 1, 1)
        (column,) = call(
            functools.partial(side_force_kernel, own),
            "side_force",
            [mid, low, high, wide.reshape(ex * cy * near, slots), *shared, column, left],
            [jax.ShapeDtypeStruct((4, cells, slots), jnp.float32)],
            cells * 12,
            block(2 * cy * near),
        )
        moved = flat_shape if stage == "last" else jax.ShapeDtypeStruct((cells, 4, slots), jnp.float32)
        return call(
            functools.partial(last_force_kernel, own, stage),
            "force_" + stage,
            [
                mid,
                below,
                above,
                slope_below.reshape(ex * near, slots),
                slope_above.reshape(ex * near, slots),
                ghost,
                ghost_point,
                column,
                left,
                velocity,
            ],
            [flat_shape, moved],
            cells * 9,
            block(2 * ex * near),
        )

    velocity, moved = evaluate(location, velocity, "first")
    velocity, moved = evaluate(moved.reshape(location.shape), velocity, "middle")
    velocity, new_positions = evaluate(moved.reshape(location.shape), velocity, "last")
    return new_positions.reshape(positions.shape), velocity.reshape(positions.shape)


def solution(mesh):
    return jax.shard_map(
        on_device,
        mesh=mesh,
        in_specs=(
            P(None, "gx", "gy", "gz", None),
            P(None, "gx", "gy", "gz", None),
            P("gx", "gy", "gz", None),
            P("gx", "gy", "gz"),
        ),
        out_specs=(P(None, "gx", "gy", "gz", None), P(None, "gx", "gy", "gz", None)),
        check_vma=False,
    )
```

time: 82 us -> 75.8 us (0.924)
  waiting for transfers between devices: 33.9 us -> 28 us
    ppermute x6, waiting for transfers between devices: 6.62 us -> 0.1 us  [neighbours(): other = lax.ppermute(cells, axis, [(0, 1), (1, 0)])]
    pallas_call x12 -> x18, Pallas kernels: 22 us -> 21.9 us  [call(): pl.pallas_call(kernel, out_shape=out_shape, in_specs=[vmem] * len(operand...]
  transfers between devices with their start and end apart: 24 -> 24, of which waited for: 24 -> 18; matrix products, arithmetic and copies ran while one was open for 0% -> 0% of each run, Pallas kernels for 9% -> 19%
where the time goes in v1:
time: 75.8 us; the launch traced here: 75.5 us
  waiting for transfers between devices  28 us (37%)
  starting transfers between devices  22.4 us (30%)
  Pallas kernels  21.9 us (29%)
  local copies, waits for them, and re-layouts  2.15 us (3%)
  between operations  0.91 us (1%)
    pallas_call x18, Pallas kernels, call(): pl.pallas_call(kernel, out_shape=out_shape, in_specs=[vmem] * len(operand...  21.9 us
    ppermute x9, waiting for transfers between devices, neighbours(): lax.ppermute(tail, axis, [(i, (i + 1) % count) for i in range(count)])  18.5 us
    ppermute x9, starting transfers between devices, neighbours(): lax.ppermute(head, axis, [((i + 1) % count, i) for i in range(count)])  11.3 us
    ppermute x9, starting transfers between devices, neighbours(): lax.ppermute(tail, axis, [(i, (i + 1) % count) for i in range(count)])  10.9 us
    ppermute x9, waiting for transfers between devices, neighbours(): lax.ppermute(head, axis, [((i + 1) % count, i) for i in range(count)])  9.43 us
    unnamed x7, local copies, waits for them, and re-layouts  2.05 us
  transfers between devices with their start and end apart: 24, of which 18 were waited for; matrix products, arithmetic and copies ran while one was open for 0% of the time, Pallas kernels for 19%

profile of v1, /device:TPU:0, one launch (start us, length us, event | category | flops | bytes accessed | tf_op | source)
XLA Modules:
  0.0 75.5 jit_solution(6268482905167361391)
XLA Ops:
  0.6 0.7 copy.22
  1.3 0.7 copy-done.2
  2.0 0.1 compare_select_fusion.1
  2.1 4.0 %collective-permute-start.1 = (f32[1,2,2,4,128]{4,3,2,1,0:T(4,128)S(1)}, f32[1,2,2,4,128]{4,3,2,1,0:T(4,128)S(1)}, u32[]{:S(2)}, u32[]{:S(2)}) collective-permute-start(f32[1,2,2,4,128]{4,3,2,1,0:T(4,128)S(1)} %pad_maximum_fusion.9), channel_id=1, source_target_pairs={{8,0},{16,8},{24,16},{0,24},{9,1},{17,9},{25,17},{1,25},{10,2},{18... | collective-permute-start | bytes 24584 | tf_op jit(solution)/shard_map/ppermute | solution.py:32
  6.1 0.0 collective-permute-start
  6.1 1.4 %collective-permute-done.1 = f32[1,2,2,4,128]{4,3,2,1,0:T(4,128)S(1)} collective-permute-done((f32[1,2,2,4,128]{4,3,2,1,0:T(4,128)S(1)}, f32[1,2,2,4,128]{4,3,2,1,0:T(4,128)S(1)}, u32[]{:S(2)}, u32[]{:S(2)}) %collective-permute-start.1) | collective-permute-done | bytes 8224 | tf_op jit(solution)/shard_map/ppermute | solution.py:32
  7.4 3.2 %collective-permute-done = f32[1,2,2,4,128]{4,3,2,1,0:T(4,128)S(1)} collective-permute-done((f32[1,2,2,4,128]{4,3,2,1,0:T(4,128)S(1)}, f32[1,2,2,4,128]{4,3,2,1,0:T(4,128)S(1)}, u32[]{:S(2)}, u32[]{:S(2)}) %collective-permute-start) | collective-permute-done | bytes 8224 | tf_op jit(solution)/shard_map/ppermute | solution.py:31
  10.6 3.7 %collective-permute-start.3 = (f32[3,2,2,4,128]{4,3,2,1,0:T(4,128)S(1)}, f32[3,2,2,4,128]{4,3,2,1,0:T(4,128)S(1)}, u32[]{:S(2)}, u32[]{:S(2)}) collective-permute-start(f32[3,2,2,4,128]{4,3,2,1,0:T(4,128)S(1)} %pad_maximum_fusion.3.mid_ref), channel_id=1, source_target_pairs={{1,0},{2,1},{3,2},{0,3},{5,4},{6,5},{7,6},{4,7},{9,8},{10,9},{11,1... | collective-permute-start | bytes 73736 | tf_op jit(solution)/shard_map/ppermute | solution.py:32
  14.3 0.8 %inner_density.3 = (f32[4,128]{1,0:T(4,128)S(1)}, bf16[48,1536]{1,0:T(8,128)(2,1)S(1)}, f32[8,1536]{1,0:T(8,128)S(1)}, bf16[4,128,48]{2,1,0:T(8,128)(2,1)S(1)}) custom-call(f32[3,2,2,4,128]{4,3,2,1,0:T(4,128)S(1)} %pad_maximum_fusion.3.mid_ref), custom_call_target="tpu_custom_call" | custom-call | flops 39321600 | bytes 3145728 | tf_op jit(solution)/shard_map/inner_density/pallas_call | solution.py:431
  15.1 0.7 collective-permute-done.3.high_ref
  15.8 4.1 %collective-permute-done.2.low_ref = f32[3,2,2,4,128]{4,3,2,1,0:T(4,128)S(1)} collective-permute-done((f32[3,2,2,4,128]{4,3,2,1,0:T(4,128)S(1)}, f32[3,2,2,4,128]{4,3,2,1,0:T(4,128)S(1)}, u32[]{:S(2)}, u32[]{:S(2)}) %collective-permute-start.2) | collective-permute-done | bytes 24608 | tf_op jit(solution)/shard_map/ppermute | solution.py:31
  19.9 0.1 collective-permute-start.4
  20.0 1.2 %outer_density.3 = (f32[8,128]{1,0:T(8,128)S(1)}, bf16[48,1536]{1,0:T(8,128)(2,1)S(1)}, f32[8,1536]{1,0:T(8,128)S(1)}, bf16[4,128,48]{2,1,0:T(8,128)(2,1)S(1)}) custom-call(f32[3,2,2,4,128]{4,3,2,1,0:T(4,128)S(1)} %collective-permute-done.2.low_ref, f32[3,2,2,4,128]{4,3,2,1,0:T(4,128)S(1)} %collective-permute-done.3.high_ref, ...), custom_call_target="tpu_custom_call" | custom-call | flops 78643200 | bytes 6291456 | tf_op jit(solution)/shard_map/outer_density/pallas_call | solution.py:431
  21.2 0.0 collective-permute-done.4
  21.3 1.0 %last_density.3 = (f32[8,128]{1,0:T(8,128)S(1)}, bf16[48,4608]{1,0:T(8,128)(2,1)S(1)}, f32[8,4608]{1,0:T(8,128)S(1)}) custom-call(f32[3,2,2,4,128]{4,3,2,1,0:T(4,128)S(1)} %pad_maximum_fusion.3.mid_ref, f32[3,2,2,4,128]{4,3,2,1,0:T(4,128)S(1)} %collective-permute-done.2.low_ref, f32[3,2,2,4,128]{4,3,2,1,0:T(4,128)S(1)} %collective-permute-done.3.high_ref, ...), custom_call_target="tpu_custom_call" | custom-call | flops 58982400 | bytes 4718592 | tf_op jit(solution)/shard_map/last_density/pallas_call | solution.py:431
  22.3 0.1 collective-permute-start.6
  22.3 2.0 %collective-permute-start.5 = (f32[1,2,4,128]{3,2,0,1:T(4,128)S(1)}, f32[1,2,4,128]{3,2,0,1:T(4,128)S(1)}, u32[]{:S(2)}, u32[]{:S(2)}) collective-permute-start(f32[1,2,4,128]{3,2,0,1:T(4,128)S(1)} %bitcast.50), channel_id=1, source_target_pairs={{0,8},{8,16},{16,24},{24,0},{1,9},{9,17},{17,25},{25,1},{2,10},{10... | collective-permute-start | bytes 12296 | tf_op jit(solution)/shard_map/ppermute | solution.py:31
  24.3 1.0 %column_force.3 = (f32[4,4,128]{2,1,0:T(4,128)S(1)}, bf16[4,128,48]{2,1,0:T(8,128)(2,1)S(1)}) custom-call(f32[3,2,2,4,128]{4,3,2,1,0:T(4,128)S(1)} %pad_maximum_fusion.3.mid_ref, f32[3,2,2,4,128]{4,3,2,1,0:T(4,128)S(1)} %collective-permute-done.2.low_ref, f32[3,2,2,4,128]{4,3,2,1,0:T(4,128)S(1)} %collective-permute-done.3.high_ref, ...), custom_call_target="tpu_custom_call" | custom-call | flops 19660800 | bytes 1572864 | tf_op jit(solution)/shard_map/column_force/pallas_call | solution.py:431
  25.4 0.5 collective-permute-done.6
  25.9 1.0 %collective-permute-done.5 = f32[1,2,4,128]{3,2,0,1:T(4,128)S(1)} collective-permute-done((f32[1,2,4,128]{3,2,0,1:T(4,128)S(1)}, f32[1,2,4,128]{3,2,0,1:T(4,128)S(1)}, u32[]{:S(2)}, u32[]{:S(2)}) %collective-permute-start.5) | collective-permute-done | bytes 4128 | tf_op jit(solution)/shard_map/ppermute | solution.py:31
  26.9 1.7 %side_force.3.column_ref = f32[4,4,128]{2,1,0:T(4,128)S(1)} custom-call(f32[3,2,2,4,128]{4,3,2,1,0:T(4,128)S(1)} %pad_maximum_fusion.3.mid_ref, f32[3,2,2,4,128]{4,3,2,1,0:T(4,128)S(1)} %collective-permute-done.2.low_ref, f32[3,2,2,4,128]{4,3,2,1,0:T(4,128)S(1)} %collective-permute-done.3.high_ref, f32[24,128]{1,0:T(8,128)S(1)} %bitcast.38, ...), custom_call_target="tpu_custom_call" | custom-call | flops 39321600 | bytes 3145728 | tf_op jit(solution)/shard_map/side_force/pallas_call | solution.py:431
  28.7 0.0 copy-start
  28.7 0.7 copy-done
  29.4 1.4 %force_first.1 = (f32[3,4,128]{2,1,0:T(4,128)S(1)}, f32[4,4,128]{2,1,0:T(4,128)S(1)}) custom-call(f32[3,2,2,4,128]{4,3,2,1,0:T(4,128)S(1)} %pad_maximum_fusion.3.mid_ref, f32[3,1,6,4,128]{4,3,2,1,0:T(4,128)S(1)} %get-tuple-element.123.below_ref, f32[3,1,6,4,128]{4,3,2,1,0:T(4,128)S(1)} %get-tuple-element.122.above_ref, ...), custom_call_target="tpu_custom_call" | custom-call | flops 29491200 | bytes 2359296 | tf_op jit(solution)/shard_map/force_first/pallas_call | solution.py:431
  30.8 1.1 %collective-permute-start.9 = (f32[1,2,2,4,128]{4,3,2,1,0:T(4,128)S(1)}, f32[1,2,2,4,128]{4,3,2,1,0:T(4,128)S(1)}, u32[]{:S(2)}, u32[]{:S(2)}) collective-permute-start(f32[1,2,2,4,128]{4,3,2,1,0:T(4,128)S(1)} %bitcast.45), channel_id=1, source_target_pairs={{8,0},{16,8},{24,16},{0,24},{9,1},{17,9},{25,17},{1,25},{10,2},{18... | collective-permute-start | bytes 24584 | tf_op jit(solution)/shard_map/ppermute | solution.py:32
  31.8 1.0 %collective-permute-start.8 = (f32[1,2,2,4,128]{4,3,2,1,0:T(4,128)S(1)}, f32[1,2,2,4,128]{4,3,2,1,0:T(4,128)S(1)}, u32[]{:S(2)}, u32[]{:S(2)}) collective-permute-start(f32[1,2,2,4,128]{4,3,2,1,0:T(4,128)S(1)} %bitcast.46), channel_id=1, source_target_pairs={{0,8},{8,16},{16,24},{24,0},{1,9},{9,17},{17,25},{25,1},{2,10},{10... | collective-permute-start | bytes 24584 | tf_op jit(solution)/shard_map/ppermute | solution.py:31
  32.8 1.6 %collective-permute-done.9 = f32[1,2,2,4,128]{4,3,2,1,0:T(4,128)S(1)} collective-permute-done((f32[1,2,2,4,128]{4,3,2,1,0:T(4,128)S(1)}, f32[1,2,2,4,128]{4,3,2,1,0:T(4,128)S(1)}, u32[]{:S(2)}, u32[]{:S(2)}) %collective-permute-start.9) | collective-permute-done | bytes 8224 | tf_op jit(solution)/shard_map/ppermute | solution.py:32
  34.5 1.9 %collective-permute-done.8 = f32[1,2,2,4,128]{4,3,2,1,0:T(4,128)S(1)} collective-permute-done((f32[1,2,2,4,128]{4,3,2,1,0:T(4,128)S(1)}, f32[1,2,2,4,128]{4,3,2,1,0:T(4,128)S(1)}, u32[]{:S(2)}, u32[]{:S(2)}) %collective-permute-start.8) | collective-permute-done | bytes 8224 | tf_op jit(solution)/shard_map/ppermute | solution.py:31
  36.4 0.1 collective-permute-start.11
  36.4 2.0 %collective-permute-start.10 = (f32[3,2,2,4,128]{4,3,2,1,0:T(4,128)S(1)}, f32[3,2,2,4,128]{4,3,2,1,0:T(4,128)S(1)}, u32[]{:S(2)}, u32[]{:S(2)}) collective-permute-start(f32[3,2,2,4,128]{4,3,2,1,0:T(4,128)S(1)} %pad_maximum_fusion.4.mid_ref), channel_id=1, source_target_pairs={{0,1},{1,2},{2,3},{3,0},{4,5},{5,6},{6,7},{7,4},{8,9},{9,10},{10,1... | collective-permute-start | bytes 73736 | tf_op jit(solution)/shard_map/ppermute | solution.py:31
  38.4 0.8 %inner_density.4 = (f32[4,128]{1,0:T(4,128)S(1)}, bf16[48,1536]{1,0:T(8,128)(2,1)S(1)}, f32[8,1536]{1,0:T(8,128)S(1)}, bf16[4,128,48]{2,1,0:T(8,128)(2,1)S(1)}) custom-call(f32[3,2,2,4,128]{4,3,2,1,0:T(4,128)S(1)} %pad_maximum_fusion.4.mid_ref), custom_call_target="tpu_custom_call" | custom-call | flops 39321600 | bytes 3145728 | tf_op jit(solution)/shard_map/inner_density/pallas_call | solution.py:431
  39.2 1.2 %collective-permute-done.11.high_ref = f32[3,2,2,4,128]{4,3,2,1,0:T(4,128)S(1)} collective-permute-done((f32[3,2,2,4,128]{4,3,2,1,0:T(4,128)S(1)}, f32[3,2,2,4,128]{4,3,2,1,0:T(4,128)S(1)}, u32[]{:S(2)}, u32[]{:S(2)}) %collective-permute-start.11) | collective-permute-done | bytes 24608 | tf_op jit(solution)/shard_map/ppermute | solution.py:32
  40.5 1.7 %collective-permute-done.10.low_ref = f32[3,2,2,4,128]{4,3,2,1,0:T(4,128)S(1)} collective-permute-done((f32[3,2,2,4,128]{4,3,2,1,0:T(4,128)S(1)}, f32[3,2,2,4,128]{4,3,2,1,0:T(4,128)S(1)}, u32[]{:S(2)}, u32[]{:S(2)}) %collective-permute-start.10) | collective-permute-done | bytes 24608 | tf_op jit(solution)/shard_map/ppermute | solution.py:31
  42.1 0.1 collective-permute-start.12
  42.2 1.2 %outer_density.4 = (f32[8,128]{1,0:T(8,128)S(1)}, bf16[48,1536]{1,0:T(8,128)(2,1)S(1)}, f32[8,1536]{1,0:T(8,128)S(1)}, bf16[4,128,48]{2,1,0:T(8,128)(2,1)S(1)}) custom-call(f32[3,2,2,4,128]{4,3,2,1,0:T(4,128)S(1)} %collective-permute-done.10.low_ref, f32[3,2,2,4,128]{4,3,2,1,0:T(4,128)S(1)} %collective-permute-done.11.high_ref, ...), custom_call_target="tpu_custom_call" | custom-call | flops 78643200 | bytes 6291456 | tf_op jit(solution)/shard_map/outer_density/pallas_call | solution.py:431
  43.4 0.0 collective-permute-done.12
  43.5 1.0 %last_density.4 = (f32[8,128]{1,0:T(8,128)S(1)}, bf16[48,4608]{1,0:T(8,128)(2,1)S(1)}, f32[8,4608]{1,0:T(8,128)S(1)}) custom-call(f32[3,2,2,4,128]{4,3,2,1,0:T(4,128)S(1)} %pad_maximum_fusion.4.mid_ref, f32[3,2,2,4,128]{4,3,2,1,0:T(4,128)S(1)} %collective-permute-done.10.low_ref, f32[3,2,2,4,128]{4,3,2,1,0:T(4,128)S(1)} %collective-permute-done.11.high_ref, ...), custom_call_target="tpu_custom_call" | custom-call | flops 58982400 | bytes 4718592 | tf_op jit(solution)/shard_map/last_density/pallas_call | solution.py:431
  44.5 0.2 collective-permute-start.14
  44.6 1.9 %collective-permute-start.13 = (f32[1,2,4,128]{3,2,0,1:T(4,128)S(1)}, f32[1,2,4,128]{3,2,0,1:T(4,128)S(1)}, u32[]{:S(2)}, u32[]{:S(2)}) collective-permute-start(f32[1,2,4,128]{3,2,0,1:T(4,128)S(1)} %bitcast.53), channel_id=1, source_target_pairs={{0,8},{8,16},{16,24},{24,0},{1,9},{9,17},{17,25},{25,1},{2,10},{10... | collective-permute-start | bytes 12296 | tf_op jit(solution)/shard_map/ppermute | solution.py:31
  46.5 1.0 %column_force.4 = (f32[4,4,128]{2,1,0:T(4,128)S(1)}, bf16[4,128,48]{2,1,0:T(8,128)(2,1)S(1)}) custom-call(f32[3,2,2,4,128]{4,3,2,1,0:T(4,128)S(1)} %pad_maximum_fusion.4.mid_ref, f32[3,2,2,4,128]{4,3,2,1,0:T(4,128)S(1)} %collective-permute-done.10.low_ref, f32[3,2,2,4,128]{4,3,2,1,0:T(4,128)S(1)} %collective-permute-done.11.high_ref, ...), custom_call_target="tpu_custom_call" | custom-call | flops 19660800 | bytes 1572864 | tf_op jit(solution)/shard_map/column_force/pallas_call | solution.py:431
  47.6 0.5 collective-permute-done.14
  48.1 1.1 %collective-permute-done.13 = f32[1,2,4,128]{3,2,0,1:T(4,128)S(1)} collective-permute-done((f32[1,2,4,128]{3,2,0,1:T(4,128)S(1)}, f32[1,2,4,128]{3,2,0,1:T(4,128)S(1)}, u32[]{:S(2)}, u32[]{:S(2)}) %collective-permute-start.13) | collective-permute-done | bytes 4128 | tf_op jit(solution)/shard_map/ppermute | solution.py:31
  49.3 1.7 %side_force.4.column_ref = f32[4,4,128]{2,1,0:T(4,128)S(1)} custom-call(f32[3,2,2,4,128]{4,3,2,1,0:T(4,128)S(1)} %pad_maximum_fusion.4.mid_ref, f32[3,2,2,4,128]{4,3,2,1,0:T(4,128)S(1)} %collective-permute-done.10.low_ref, f32[3,2,2,4,128]{4,3,2,1,0:T(4,128)S(1)} %collective-permute-done.11.high_ref, f32[24,128]{1,0:T(8,128)S(1)} %bitcast.39, ...), custom_call_target="tpu_custom_call" | custom-call | flops 39321600 | bytes 3145728 | tf_op jit(solution)/shard_map/side_force/pallas_call | solution.py:431
  51.1 1.3 %force_middle.1 = (f32[3,4,128]{2,1,0:T(4,128)S(1)}, f32[4,4,128]{2,1,0:T(4,128)S(1)}) custom-call(f32[3,2,2,4,128]{4,3,2,1,0:T(4,128)S(1)} %pad_maximum_fusion.4.mid_ref, f32[3,1,6,4,128]{4,3,2,1,0:T(4,128)S(1)} %get-tuple-element.121.below_ref, f32[3,1,6,4,128]{4,3,2,1,0:T(4,128)S(1)} %get-tuple-element.120.above_ref, ...), custom_call_target="tpu_custom_call" | custom-call | flops 29491200 | bytes 2359296 | tf_op jit(solution)/shard_map/force_middle/pallas_call | solution.py:431
  52.4 1.9 %collective-permute-start.17 = (f32[1,2,2,4,128]{4,3,2,1,0:T(4,128)S(1)}, f32[1,2,2,4,128]{4,3,2,1,0:T(4,128)S(1)}, u32[]{:S(2)}, u32[]{:S(2)}) collective-permute-start(f32[1,2,2,4,128]{4,3,2,1,0:T(4,128)S(1)} %bitcast.41), channel_id=1, source_target_pairs={{8,0},{16,8},{24,16},{0,24},{9,1},{17,9},{25,17},{1,25},{10,2},{18... | collective-permute-start | bytes 24584 | tf_op jit(solution)/shard_map/ppermute | solution.py:32
  54.3 0.2 collective-permute-start.16
  54.5 1.6 %collective-permute-done.17 = f32[1,2,2,4,128]{4,3,2,1,0:T(4,128)S(1)} collective-permute-done((f32[1,2,2,4,128]{4,3,2,1,0:T(4,128)S(1)}, f32[1,2,2,4,128]{4,3,2,1,0:T(4,128)S(1)}, u32[]{:S(2)}, u32[]{:S(2)}) %collective-permute-start.17) | collective-permute-done | bytes 8224 | tf_op jit(solution)/shard_map/ppermute | solution.py:32
  56.1 2.7 %collective-permute-done.16 = f32[1,2,2,4,128]{4,3,2,1,0:T(4,128)S(1)} collective-permute-done((f32[1,2,2,4,128]{4,3,2,1,0:T(4,128)S(1)}, f32[1,2,2,4,128]{4,3,2,1,0:T(4,128)S(1)}, u32[]{:S(2)}, u32[]{:S(2)}) %collective-permute-start.16) | collective-permute-done | bytes 8224 | tf_op jit(solution)/shard_map/ppermute | solution.py:31
  58.9 0.1 collective-permute-start.19
  59.0 2.0 %collective-permute-start.18 = (f32[3,2,2,4,128]{4,3,2,1,0:T(4,128)S(1)}, f32[3,2,2,4,128]{4,3,2,1,0:T(4,128)S(1)}, u32[]{:S(2)}, u32[]{:S(2)}) collective-permute-start(f32[3,2,2,4,128]{4,3,2,1,0:T(4,128)S(1)} %pad_maximum_fusion.5.mid_ref), channel_id=1, source_target_pairs={{0,1},{1,2},{2,3},{3,0},{4,5},{5,6},{6,7},{7,4},{8,9},{9,10},{10,1... | collective-permute-start | bytes 73736 | tf_op jit(solution)/shard_map/ppermute | solution.py:31
  61.0 0.8 %inner_density.5 = (f32[4,128]{1,0:T(4,128)S(1)}, bf16[48,1536]{1,0:T(8,128)(2,1)S(1)}, f32[8,1536]{1,0:T(8,128)S(1)}, bf16[4,128,48]{2,1,0:T(8,128)(2,1)S(1)}) custom-call(f32[3,2,2,4,128]{4,3,2,1,0:T(4,128)S(1)} %pad_maximum_fusion.5.mid_ref), custom_call_target="tpu_custom_call" | custom-call | flops 39321600 | bytes 3145728 | tf_op jit(solution)/shard_map/inner_density/pallas_call | solution.py:431
  61.7 1.2 %collective-permute-done.19.high_ref = f32[3,2,2,4,128]{4,3,2,1,0:T(4,128)S(1)} collective-permute-done((f32[3,2,2,4,128]{4,3,2,1,0:T(4,128)S(1)}, f32[3,2,2,4,128]{4,3,2,1,0:T(4,128)S(1)}, u32[]{:S(2)}, u32[]{:S(2)}) %collective-permute-start.19) | collective-permute-done | bytes 24608 | tf_op jit(solution)/shard_map/ppermute | solution.py:32
  63.0 1.6 %collective-permute-done.18.low_ref = f32[3,2,2,4,128]{4,3,2,1,0:T(4,128)S(1)} collective-permute-done((f32[3,2,2,4,128]{4,3,2,1,0:T(4,128)S(1)}, f32[3,2,2,4,128]{4,3,2,1,0:T(4,128)S(1)}, u32[]{:S(2)}, u32[]{:S(2)}) %collective-permute-start.18) | collective-permute-done | bytes 24608 | tf_op jit(solution)/shard_map/ppermute | solution.py:31
  64.6 0.1 collective-permute-start.20
  64.7 1.2 %outer_density.5 = (f32[8,128]{1,0:T(8,128)S(1)}, bf16[48,1536]{1,0:T(8,128)(2,1)S(1)}, f32[8,1536]{1,0:T(8,128)S(1)}, bf16[4,128,48]{2,1,0:T(8,128)(2,1)S(1)}) custom-call(f32[3,2,2,4,128]{4,3,2,1,0:T(4,128)S(1)} %collective-permute-done.18.low_ref, f32[3,2,2,4,128]{4,3,2,1,0:T(4,128)S(1)} %collective-permute-done.19.high_ref, ...), custom_call_target="tpu_custom_call" | custom-call | flops 78643200 | bytes 6291456 | tf_op jit(solution)/shard_map/outer_density/pallas_call | solution.py:431
  65.9 0.0 collective-permute-done.20
  66.0 1.0 %last_density.5 = (f32[8,128]{1,0:T(8,128)S(1)}, bf16[48,4608]{1,0:T(8,128)(2,1)S(1)}, f32[8,4608]{1,0:T(8,128)S(1)}) custom-call(f32[3,2,2,4,128]{4,3,2,1,0:T(4,128)S(1)} %pad_maximum_fusion.5.mid_ref, f32[3,2,2,4,128]{4,3,2,1,0:T(4,128)S(1)} %collective-permute-done.18.low_ref, f32[3,2,2,4,128]{4,3,2,1,0:T(4,128)S(1)} %collective-permute-done.19.high_ref, ...), custom_call_target="tpu_custom_call" | custom-call | flops 58982400 | bytes 4718592 | tf_op jit(solution)/shard_map/last_density/pallas_call | solution.py:431
  67.0 0.3 collective-permute-start.22
  67.3 1.8 %collective-permute-start.21 = (f32[1,2,4,128]{3,2,0,1:T(4,128)S(1)}, f32[1,2,4,128]{3,2,0,1:T(4,128)S(1)}, u32[]{:S(2)}, u32[]{:S(2)}) collective-permute-start(f32[1,2,4,128]{3,2,0,1:T(4,128)S(1)} %bitcast.56), channel_id=1, source_target_pairs={{0,8},{8,16},{16,24},{24,0},{1,9},{9,17},{17,25},{25,1},{2,10},{10... | collective-permute-start | bytes 12296 | tf_op jit(solution)/shard_map/ppermute | solution.py:31
  69.0 1.0 %column_force.5 = (f32[4,4,128]{2,1,0:T(4,128)S(1)}, bf16[4,128,48]{2,1,0:T(8,128)(2,1)S(1)}) custom-call(f32[3,2,2,4,128]{4,3,2,1,0:T(4,128)S(1)} %pad_maximum_fusion.5.mid_ref, f32[3,2,2,4,128]{4,3,2,1,0:T(4,128)S(1)} %collective-permute-done.18.low_ref, f32[3,2,2,4,128]{4,3,2,1,0:T(4,128)S(1)} %collective-permute-done.19.high_ref, ...), custom_call_target="tpu_custom_call" | custom-call | flops 19660800 | bytes 1572864 | tf_op jit(solution)/shard_map/column_force/pallas_call | solution.py:431
  70.1 0.5 collective-permute-done.22
  70.6 1.1 %collective-permute-done.21 = f32[1,2,4,128]{3,2,0,1:T(4,128)S(1)} collective-permute-done((f32[1,2,4,128]{3,2,0,1:T(4,128)S(1)}, f32[1,2,4,128]{3,2,0,1:T(4,128)S(1)}, u32[]{:S(2)}, u32[]{:S(2)}) %collective-permute-start.21) | collective-permute-done | bytes 4128 | tf_op jit(solution)/shard_map/ppermute | solution.py:31
  71.8 1.7 %side_force.5.column_ref = f32[4,4,128]{2,1,0:T(4,128)S(1)} custom-call(f32[3,2,2,4,128]{4,3,2,1,0:T(4,128)S(1)} %pad_maximum_fusion.5.mid_ref, f32[3,2,2,4,128]{4,3,2,1,0:T(4,128)S(1)} %collective-permute-done.18.low_ref, f32[3,2,2,4,128]{4,3,2,1,0:T(4,128)S(1)} %collective-permute-done.19.high_ref, f32[24,128]{1,0:T(8,128)S(1)} %bitcast.40, ...), custom_call_target="tpu_custom_call" | custom-call | flops 39321600 | bytes 3145728 | tf_op jit(solution)/shard_map/side_force/pallas_call | solution.py:431
  73.6 1.9 %force_last.1 = (f32[3,4,128]{2,1,0:T(4,128)}, f32[3,4,128]{2,1,0:T(4,128)}) custom-call(f32[3,2,2,4,128]{4,3,2,1,0:T(4,128)S(1)} %pad_maximum_fusion.5.mid_ref, f32[3,1,6,4,128]{4,3,2,1,0:T(4,128)S(1)} %get-tuple-element.119.below_ref, f32[3,1,6,4,128]{4,3,2,1,0:T(4,128)S(1)} %get-tuple-element.118.above_ref, f32[12,128]{1,0:T(8,128)S(1)} %reshape.78.slope_below_ref, ...), custom_call_target="tpu_custom_call" | custom-call | flops 29491200 | bytes 2359296 | tf_op jit(solution)/shard_map/force_last/pallas_call | solution.py:431
  (35 shorter events, 0.2 us)
Async XLA Ops:
  0.6 0.7 copy-start.1
  1.3 0.7 copy-start.2
  2.1 5.3 %collective-permute-start.1 = (f32[1,2,2,4,128]{4,3,2,1,0:T(4,128)S(1)}, f32[1,2,2,4,128]{4,3,2,1,0:T(4,128)S(1)}, u32[]{:S(2)}, u32[]{:S(2)}) collective-permute-start(f32[1,2,2,4,128]{4,3,2,1,0:T(4,128)S(1)} %pad_maximum_fusion.9), channel_id=1, source_target_pairs={{8,0},{16,8},{24,16},{0,24},{9,1},{17,9},{25,17},{1,25},{10,2},{18... | collective-permute-start | bytes 24584 | tf_op jit(solution)/shard_map/ppermute | solution.py:32
  6.1 4.5 %collective-permute-start = (f32[1,2,2,4,128]{4,3,2,1,0:T(4,128)S(1)}, f32[1,2,2,4,128]{4,3,2,1,0:T(4,128)S(1)}, u32[]{:S(2)}, u32[]{:S(2)}) collective-permute-start(f32[1,2,2,4,128]{4,3,2,1,0:T(4,128)S(1)} %pad_maximum_fusion.9), channel_id=1, source_target_pairs={{0,8},{8,16},{16,24},{24,0},{1,9},{9,17},{17,25},{25,1},{2,10},{10... | collective-permute-start | bytes 24584 | tf_op jit(solution)/shard_map/ppermute | solution.py:31
  10.6 5.2 %collective-permute-start.3 = (f32[3,2,2,4,128]{4,3,2,1,0:T(4,128)S(1)}, f32[3,2,2,4,128]{4,3,2,1,0:T(4,128)S(1)}, u32[]{:S(2)}, u32[]{:S(2)}) collective-permute-start(f32[3,2,2,4,128]{4,3,2,1,0:T(4,128)S(1)} %pad_maximum_fusion.3.mid_ref), channel_id=1, source_target_pairs={{1,0},{2,1},{3,2},{0,3},{5,4},{6,5},{7,6},{4,7},{9,8},{10,9},{11,1... | collective-permute-start | bytes 73736 | tf_op jit(solution)/shard_map/ppermute | solution.py:32
  14.3 5.6 %collective-permute-start.2 = (f32[3,2,2,4,128]{4,3,2,1,0:T(4,128)S(1)}, f32[3,2,2,4,128]{4,3,2,1,0:T(4,128)S(1)}, u32[]{:S(2)}, u32[]{:S(2)}) collective-permute-start(f32[3,2,2,4,128]{4,3,2,1,0:T(4,128)S(1)} %pad_maximum_fusion.3.mid_ref), channel_id=1, source_target_pairs={{0,1},{1,2},{2,3},{3,0},{4,5},{5,6},{6,7},{7,4},{8,9},{9,10},{10,1... | collective-permute-start | bytes 73736 | tf_op jit(solution)/shard_map/ppermute | solution.py:31
  19.9 1.3 %collective-permute-start.4 = (f32[3,2,6,4,128]{4,3,2,1,0:T(4,128)S(1)}, f32[3,2,6,4,128]{4,3,2,1,0:T(4,128)S(1)}, u32[]{:S(2)}, u32[]{:S(2)}) collective-permute-start(f32[3,2,6,4,128]{4,3,2,1,0:T(4,128)S(1)} %pad_maximum_fusion), channel_id=1, source_target_pairs={{0,4},{4,0},{1,5},{5,1},{2,6},{6,2},{3,7},{7,3},{8,12},{12,8},{9,1... | collective-permute-start | bytes 221192 | tf_op jit(solution)/shard_map/ppermute | solution.py:26
  22.3 3.7 %collective-permute-start.6 = (f32[1,2,4,128]{3,2,0,1:T(4,128)S(1)}, f32[1,2,4,128]{3,2,0,1:T(4,128)S(1)}, u32[]{:S(2)}, u32[]{:S(2)}) collective-permute-start(f32[1,2,4,128]{3,2,0,1:T(4,128)S(1)} %bitcast.49), channel_id=1, source_target_pairs={{8,0},{16,8},{24,16},{0,24},{9,1},{17,9},{25,17},{1,25},{10,2},{18... | collective-permute-start | bytes 12296 | tf_op jit(solution)/shard_map/ppermute | solution.py:32
  22.3 4.6 %collective-permute-start.5 = (f32[1,2,4,128]{3,2,0,1:T(4,128)S(1)}, f32[1,2,4,128]{3,2,0,1:T(4,128)S(1)}, u32[]{:S(2)}, u32[]{:S(2)}) collective-permute-start(f32[1,2,4,128]{3,2,0,1:T(4,128)S(1)} %bitcast.50), channel_id=1, source_target_pairs={{0,8},{8,16},{16,24},{24,0},{1,9},{9,17},{17,25},{25,1},{2,10},{10... | collective-permute-start | bytes 12296 | tf_op jit(solution)/shard_map/ppermute | solution.py:31
  26.9 1.8 %collective-permute-start.7 = (f32[3,2,4,128]{3,2,0,1:T(4,128)S(1)}, f32[3,2,4,128]{3,2,0,1:T(4,128)S(1)}, u32[]{:S(2)}, u32[]{:S(2)}) collective-permute-start(f32[3,2,4,128]{3,2,0,1:T(4,128)S(1)} %pad_maximum_fusion.6), channel_id=1, source_target_pairs={{0,4},{4,0},{1,5},{5,1},{2,6},{6,2},{3,7},{7,3},{8,12},{12,8},{9,1... | collective-permute-start | bytes 36872 | tf_op jit(solution)/shard_map/ppermute | solution.py:26
  28.7 0.7 copy-start
  30.8 3.7 %collective-permute-start.9 = (f32[1,2,2,4,128]{4,3,2,1,0:T(4,128)S(1)}, f32[1,2,2,4,128]{4,3,2,1,0:T(4,128)S(1)}, u32[]{:S(2)}, u32[]{:S(2)}) collective-permute-start(f32[1,2,2,4,128]{4,3,2,1,0:T(4,128)S(1)} %bitcast.45), channel_id=1, source_target_pairs={{8,0},{16,8},{24,16},{0,24},{9,1},{17,9},{25,17},{1,25},{10,2},{18... | collective-permute-start | bytes 24584 | tf_op jit(solution)/shard_map/ppermute | solution.py:32
  31.8 4.5 %collective-permute-start.8 = (f32[1,2,2,4,128]{4,3,2,1,0:T(4,128)S(1)}, f32[1,2,2,4,128]{4,3,2,1,0:T(4,128)S(1)}, u32[]{:S(2)}, u32[]{:S(2)}) collective-permute-start(f32[1,2,2,4,128]{4,3,2,1,0:T(4,128)S(1)} %bitcast.46), channel_id=1, source_target_pairs={{0,8},{8,16},{16,24},{24,0},{1,9},{9,17},{17,25},{25,1},{2,10},{10... | collective-permute-start | bytes 24584 | tf_op jit(solution)/shard_map/ppermute | solution.py:31
  36.4 4.1 %collective-permute-start.11 = (f32[3,2,2,4,128]{4,3,2,1,0:T(4,128)S(1)}, f32[3,2,2,4,128]{4,3,2,1,0:T(4,128)S(1)}, u32[]{:S(2)}, u32[]{:S(2)}) collective-permute-start(f32[3,2,2,4,128]{4,3,2,1,0:T(4,128)S(1)} %pad_maximum_fusion.4.mid_ref), channel_id=1, source_target_pairs={{1,0},{2,1},{3,2},{0,3},{5,4},{6,5},{7,6},{4,7},{9,8},{10,9},{11,1... | collective-permute-start | bytes 73736 | tf_op jit(solution)/shard_map/ppermute | solution.py:32
  36.4 5.7 %collective-permute-start.10 = (f32[3,2,2,4,128]{4,3,2,1,0:T(4,128)S(1)}, f32[3,2,2,4,128]{4,3,2,1,0:T(4,128)S(1)}, u32[]{:S(2)}, u32[]{:S(2)}) collective-permute-start(f32[3,2,2,4,128]{4,3,2,1,0:T(4,128)S(1)} %pad_maximum_fusion.4.mid_ref), channel_id=1, source_target_pairs={{0,1},{1,2},{2,3},{3,0},{4,5},{5,6},{6,7},{7,4},{8,9},{9,10},{10,1... | collective-permute-start | bytes 73736 | tf_op jit(solution)/shard_map/ppermute | solution.py:31
  42.1 1.3 %collective-permute-start.12 = (f32[3,2,6,4,128]{4,3,2,1,0:T(4,128)S(1)}, f32[3,2,6,4,128]{4,3,2,1,0:T(4,128)S(1)}, u32[]{:S(2)}, u32[]{:S(2)}) collective-permute-start(f32[3,2,6,4,128]{4,3,2,1,0:T(4,128)S(1)} %pad_maximum_fusion.1), channel_id=1, source_target_pairs={{0,4},{4,0},{1,5},{5,1},{2,6},{6,2},{3,7},{7,3},{8,12},{12,8},{9,1... | collective-permute-start | bytes 221192 | tf_op jit(solution)/shard_map/ppermute | solution.py:26
  44.5 3.7 %collective-permute-start.14 = (f32[1,2,4,128]{3,2,0,1:T(4,128)S(1)}, f32[1,2,4,128]{3,2,0,1:T(4,128)S(1)}, u32[]{:S(2)}, u32[]{:S(2)}) collective-permute-start(f32[1,2,4,128]{3,2,0,1:T(4,128)S(1)} %bitcast.52), channel_id=1, source_target_pairs={{8,0},{16,8},{24,16},{0,24},{9,1},{17,9},{25,17},{1,25},{10,2},{18... | collective-permute-start | bytes 12296 | tf_op jit(solution)/shard_map/ppermute | solution.py:32
  44.6 4.6 %collective-permute-start.13 = (f32[1,2,4,128]{3,2,0,1:T(4,128)S(1)}, f32[1,2,4,128]{3,2,0,1:T(4,128)S(1)}, u32[]{:S(2)}, u32[]{:S(2)}) collective-permute-start(f32[1,2,4,128]{3,2,0,1:T(4,128)S(1)} %bitcast.53), channel_id=1, source_target_pairs={{0,8},{8,16},{16,24},{24,0},{1,9},{9,17},{17,25},{25,1},{2,10},{10... | collective-permute-start | bytes 12296 | tf_op jit(solution)/shard_map/ppermute | solution.py:31
  49.3 1.8 %collective-permute-start.15 = (f32[3,2,4,128]{3,2,0,1:T(4,128)S(1)}, f32[3,2,4,128]{3,2,0,1:T(4,128)S(1)}, u32[]{:S(2)}, u32[]{:S(2)}) collective-permute-start(f32[3,2,4,128]{3,2,0,1:T(4,128)S(1)} %pad_maximum_fusion.7), channel_id=1, source_target_pairs={{0,4},{4,0},{1,5},{5,1},{2,6},{6,2},{3,7},{7,3},{8,12},{12,8},{9,1... | collective-permute-start | bytes 36872 | tf_op jit(solution)/shard_map/ppermute | solution.py:26
  52.4 3.7 %collective-permute-start.17 = (f32[1,2,2,4,128]{4,3,2,1,0:T(4,128)S(1)}, f32[1,2,2,4,128]{4,3,2,1,0:T(4,128)S(1)}, u32[]{:S(2)}, u32[]{:S(2)}) collective-permute-start(f32[1,2,2,4,128]{4,3,2,1,0:T(4,128)S(1)} %bitcast.41), channel_id=1, source_target_pairs={{8,0},{16,8},{24,16},{0,24},{9,1},{17,9},{25,17},{1,25},{10,2},{18... | collective-permute-start | bytes 24584 | tf_op jit(solution)/shard_map/ppermute | solution.py:32
  54.3 4.5 %collective-permute-start.16 = (f32[1,2,2,4,128]{4,3,2,1,0:T(4,128)S(1)}, f32[1,2,2,4,128]{4,3,2,1,0:T(4,128)S(1)}, u32[]{:S(2)}, u32[]{:S(2)}) collective-permute-start(f32[1,2,2,4,128]{4,3,2,1,0:T(4,128)S(1)} %bitcast.42), channel_id=1, source_target_pairs={{0,8},{8,16},{16,24},{24,0},{1,9},{9,17},{17,25},{25,1},{2,10},{10... | collective-permute-start | bytes 24584 | tf_op jit(solution)/shard_map/ppermute | solution.py:31
  58.9 4.1 %collective-permute-start.19 = (f32[3,2,2,4,128]{4,3,2,1,0:T(4,128)S(1)}, f32[3,2,2,4,128]{4,3,2,1,0:T(4,128)S(1)}, u32[]{:S(2)}, u32[]{:S(2)}) collective-permute-start(f32[3,2,2,4,128]{4,3,2,1,0:T(4,128)S(1)} %pad_maximum_fusion.5.mid_ref), channel_id=1, source_target_pairs={{1,0},{2,1},{3,2},{0,3},{5,4},{6,5},{7,6},{4,7},{9,8},{10,9},{11,1... | collective-permute-start | bytes 73736 | tf_op jit(solution)/shard_map/ppermute | solution.py:32
  59.0 5.7 %collective-permute-start.18 = (f32[3,2,2,4,128]{4,3,2,1,0:T(4,128)S(1)}, f32[3,2,2,4,128]{4,3,2,1,0:T(4,128)S(1)}, u32[]{:S(2)}, u32[]{:S(2)}) collective-permute-start(f32[3,2,2,4,128]{4,3,2,1,0:T(4,128)S(1)} %pad_maximum_fusion.5.mid_ref), channel_id=1, source_target_pairs={{0,1},{1,2},{2,3},{3,0},{4,5},{5,6},{6,7},{7,4},{8,9},{9,10},{10,1... | collective-permute-start | bytes 73736 | tf_op jit(solution)/shard_map/ppermute | solution.py:31
  64.6 1.3 %collective-permute-start.20 = (f32[3,2,6,4,128]{4,3,2,1,0:T(4,128)S(1)}, f32[3,2,6,4,128]{4,3,2,1,0:T(4,128)S(1)}, u32[]{:S(2)}, u32[]{:S(2)}) collective-permute-start(f32[3,2,6,4,128]{4,3,2,1,0:T(4,128)S(1)} %pad_maximum_fusion.2), channel_id=1, source_target_pairs={{0,4},{4,0},{1,5},{5,1},{2,6},{6,2},{3,7},{7,3},{8,12},{12,8},{9,1... | collective-permute-start | bytes 221192 | tf_op jit(solution)/shard_map/ppermute | solution.py:26
  67.0 3.7 %collective-permute-start.22 = (f32[1,2,4,128]{3,2,0,1:T(4,128)S(1)}, f32[1,2,4,128]{3,2,0,1:T(4,128)S(1)}, u32[]{:S(2)}, u32[]{:S(2)}) collective-permute-start(f32[1,2,4,128]{3,2,0,1:T(4,128)S(1)} %bitcast.55), channel_id=1, source_target_pairs={{8,0},{16,8},{24,16},{0,24},{9,1},{17,9},{25,17},{1,25},{10,2},{18... | collective-permute-start | bytes 12296 | tf_op jit(solution)/shard_map/ppermute | solution.py:32
  67.3 4.5 %collective-permute-start.21 = (f32[1,2,4,128]{3,2,0,1:T(4,128)S(1)}, f32[1,2,4,128]{3,2,0,1:T(4,128)S(1)}, u32[]{:S(2)}, u32[]{:S(2)}) collective-permute-start(f32[1,2,4,128]{3,2,0,1:T(4,128)S(1)} %bitcast.56), channel_id=1, source_target_pairs={{0,8},{8,16},{16,24},{24,0},{1,9},{9,17},{17,25},{25,1},{2,10},{10... | collective-permute-start | bytes 12296 | tf_op jit(solution)/shard_map/ppermute | solution.py:31
  71.8 1.8 %collective-permute-start.23 = (f32[3,2,4,128]{3,2,0,1:T(4,128)S(1)}, f32[3,2,4,128]{3,2,0,1:T(4,128)S(1)}, u32[]{:S(2)}, u32[]{:S(2)}) collective-permute-start(f32[3,2,4,128]{3,2,0,1:T(4,128)S(1)} %pad_maximum_fusion.8), channel_id=1, source_target_pairs={{0,4},{4,0},{1,5},{5,1},{2,6},{6,2},{3,7},{7,3},{8,12},{12,8},{9,1... | collective-permute-start | bytes 36872 | tf_op jit(solution)/shard_map/ppermute | solution.py:26

commit v2 on v1

v2 whole, which is shorter than its diff:
```python
import functools

import jax
import jax.numpy as jnp
from jax import lax
from jax.experimental import pallas as pl
from jax.experimental.pallas import tpu as pltpu
from jax.sharding import PartitionSpec as P

time_step = 0.05
half_kick = 0.5 * time_step
LANES = 128
GRANT = 8 * 1024 * 1024
ROOT = 1.3 ** (1.0 / 3.0)
STEPS = (-1, 0, 1)
SETS = ("own", "edge", "gown", "gedge")


def neighbours(cells, axis, dim, width):
    count = lax.axis_size(axis)
    size = cells.shape[dim]
    head = lax.slice_in_dim(cells, 0, width, axis=dim)
    tail = lax.slice_in_dim(cells, size - width, size, axis=dim)
    if count == 1:
        return tail, head
    if count == 2 and size == 2 * width:
        other = lax.ppermute(cells, axis, [(0, 1), (1, 0)])
        return (
            lax.slice_in_dim(other, width, size, axis=dim),
            lax.slice_in_dim(other, 0, width, axis=dim),
        )
    below = lax.ppermute(tail, axis, [(i, (i + 1) % count) for i in range(count)])
    above = lax.ppermute(head, axis, [((i + 1) % count, i) for i in range(count)])
    return below, above


def ring_halo(cells, axis, dim, width):
    below, above = neighbours(cells, axis, dim, width)
    return jnp.concatenate([below, cells, above], axis=dim)


def split3(value):
    high = value.astype(jnp.bfloat16).astype(jnp.float32)
    rest = value - high
    middle = rest.astype(jnp.bfloat16).astype(jnp.float32)
    return high, middle, rest - middle


def partner_block(row):
    high, middle, low = split3(row)
    first = jnp.concatenate([high, middle], axis=0).astype(jnp.bfloat16)
    last = jnp.concatenate([low, high], axis=0).astype(jnp.bfloat16)
    return jnp.concatenate([first, first, last], axis=0)


def target_block(row):
    high, middle, low = split3(row)
    stacked = jnp.concatenate([high, high, middle, middle, high, low], axis=0)
    return jnp.transpose(stacked).astype(jnp.bfloat16)


class Grid:
    def __init__(self, own):
        self.cx, self.cy, self.cz = own
        self.ex, self.ey, self.ez = own[0] + 2, own[1] + 2, own[2] + 4
        row = lax.broadcasted_iota(jnp.int32, (8, LANES), 0)
        self.row = row
        self.masks = [(row == k).astype(jnp.float32) for k in range(7)]
        self.spatial = self.masks[0] + self.masks[1] + self.masks[2]
        self.inner = range(1, self.cx + 1)
        self.outer = (0, self.ex - 1)

    def own_targets(self):
        return [(a, b, c) for a in self.inner for b in range(1, self.cy + 1) for c in range(2, self.cz + 2)]

    def edge_targets(self):
        return [(a, b, c) for a in self.inner for b in range(1, self.cy + 1) for c in (1, self.cz + 2)]

    def slope_row(self, a, b, c):
        return ((a - 1) * self.cy + b - 1) * (self.cz + 2) + c - 1

    def place(self, a, b, c):
        if c in (0, self.ez - 1):
            which, layer = "far", int(c > 0)
        elif c in (1, self.ez - 2):
            which, layer = "edge", int(c > 1)
        else:
            which, layer = "own", c - 2
        if 1 <= b <= self.cy:
            return which, (layer * self.ex + a) * self.cy + b - 1
        layers = self.cz if which == "own" else 2
        column = self.outer.index(a) if a in self.outer else a + 1
        return "g" + which, (int(b > 0) * layers + layer) * self.ex + column

    def cells_of(self, which, columns=None):
        columns = range(self.ex) if columns is None else columns
        rows = (0, self.ey - 1) if which[0] == "g" else range(1, self.cy + 1)
        layers = {"n": range(2, self.cz + 2), "e": (1, self.ez - 2), "r": (0, self.ez - 1)}[
            "n" if which.endswith("own") else "e" if which.endswith("edge") else "r"
        ]
        return [(a, b, c) for c in layers for a in columns for b in rows]

    def sources(self, target, sets, columns=None):
        found = {}
        for p in STEPS:
            for q in STEPS:
                for r in STEPS:
                    a, b, c = target[0] + p, target[1] + q, target[2] + r
                    which, index = self.place(a, b, c)
                    if which in sets and (columns is None or a in columns):
                        found.setdefault(which, []).append((index, p == q == r == 0))
        runs = []
        for which in sets:
            entries = sorted(found.get(which, []))
            while entries:
                length = 1
                while length < len(entries) and entries[length][0] == entries[0][0] + length:
                    length += 1
                count = min(length, 2 if length % 2 == 0 else 3)
                same = [k for k in range(count) if entries[k][1]]
                runs.append((which, entries[0][0], count, same[0] if same else -1))
                entries = entries[count:]
        return runs

    def placed(self, tile, a, b, c):
        m = self.masks
        shift = (
            (a + 0.5 - 0.5 * self.ex) * m[0]
            + (b + 0.5 - 0.5 * self.ey) * m[1]
            + (m[4] + (c + 0.5 - 0.5 * self.ez) * m[2])
        )
        point = jnp.concatenate([tile, jnp.zeros((4, LANES), jnp.float32)], axis=0)
        point = point * self.spatial + shift
        return point, jnp.sum(point * point, axis=0, keepdims=True)

    def put_partner(self, tile, cell, refs, point_refs=None):
        which, index = self.place(*cell)
        lanes = slice(index * LANES, (index + 1) * LANES)
        point, bulk = self.placed(tile, *cell)
        scale = tile[3:4]
        refs[which][:, lanes] = partner_block(jnp.where(self.row == 3, 1.0 - bulk, point) * scale)
        if point_refs is not None:
            strength = jnp.where(scale > 1.05, 0.4 / ROOT, 0.3)
            point_refs[which][:, lanes] = jnp.where(
                self.row == 3, strength, jnp.where(self.row == 4, scale, point)
            )

    def target(self, tile, a, b, c):
        point, bulk = self.placed(tile, a, b, c)
        twice = jnp.where(self.row == 4, 2.0 - bulk, 2.0 * point)
        return twice + self.masks[3]


def across(total):
    return jnp.sum(jnp.transpose(total), axis=0, keepdims=True)


def add_density(grid, left_ref, place, runs, refs, before, after):
    rows = 64
    for start in range(0, LANES, rows):
        chunk = slice(start, start + rows)
        total = before(chunk)
        for which, first, count, same in runs:
            near = jnp.dot(
                left_ref[place, chunk, :],
                refs[which][:, first * LANES : (first + count) * LANES],
                preferred_element_type=jnp.float32,
            )
            for k in range(count):
                part = jnp.maximum(near[:, k * LANES : (k + 1) * LANES], 0.0)
                if k == same:
                    i = lax.broadcasted_iota(jnp.int32, (rows, LANES), 0)
                    j = lax.broadcasted_iota(jnp.int32, (rows, LANES), 1)
                    part = jnp.where(i + start == j, 0.0, part)
                cube = part * part * part
                total = cube if total is None else total + cube
        after(chunk, total)


def store_to(ref, place):
    def after(chunk, total):
        ref[place, chunk, :] = total

    return after


def nothing(chunk):
    return None


def prepare_kernel(pos_hbm, vel_hbm, species_hbm, counts_hbm, loc_ref, out_ref, pos_ref, vel_ref, species_ref, counts_ref, arrived):
    copies = [
        pltpu.make_async_copy(source, target, arrived.at[k])
        for k, (source, target) in enumerate(
            ((pos_hbm, pos_ref), (vel_hbm, vel_ref), (species_hbm, species_ref), (counts_hbm, counts_ref))
        )
    ]
    for copy in copies:
        copy.start()
    for copy in copies:
        copy.wait()
    cx, cy, cz = pos_ref.shape[1:4]
    slot = lax.broadcasted_iota(jnp.int32, (1, LANES), 1)
    for a in range(cx):
        for b in range(cy):
            for c in range(cz):
                place = (a * cy + b) * cz + c
                one = slice(c, c + 1)
                for axis in range(3):
                    loc_ref[a, b, c, axis : axis + 1, :] = pos_ref[axis, a, b, one, :]
                    out_ref[axis, place : place + 1, :] = vel_ref[axis, a, b, one, :]
                kind = jnp.where(species_ref[a, b, one, :] == 1, ROOT, 1.0)
                count = jnp.broadcast_to(counts_ref[a, b : b + 1, one], (1, LANES))
                loc_ref[a, b, c, 3:4, :] = jnp.where(slot < count, kind, 0.0)


def inner_density_kernel(own, mid_ref, below_ref, above_ref, sum_ref, part_ref, point_ref, ghost_ref, ghost_point_ref, left_ref):
    grid = Grid(own)
    refs = {"own": part_ref, "gown": ghost_ref}
    point_refs = {"own": point_ref, "gown": ghost_point_ref}
    for a, b, c in grid.cells_of("own"):
        grid.put_partner(mid_ref[a, b - 1, c - 2], (a, b, c), refs, point_refs)
    for a, b, c in grid.cells_of("gown"):
        tile = (below_ref if b == 0 else above_ref)[a, 0, c - 2]
        grid.put_partner(tile, (a, b, c), refs, point_refs)
    for place, (a, b, c) in enumerate(grid.own_targets()):
        left_ref[place] = target_block(grid.target(mid_ref[a, b - 1, c - 2], a, b, c))
        runs = grid.sources((a, b, c), ("own", "gown"))
        add_density(grid, left_ref, place, runs, refs, nothing, store_to(sum_ref, place))


def outer_density_kernel(own, low_ref, high_ref, inner_ref, part_ref, ghost_ref, left_ref, own_sum_ref, edge_sum_ref, edge_ref, edge_point_ref, edge_left_ref, far_ref):
    grid = Grid(own)
    refs = {"own": part_ref, "gown": ghost_ref, "edge": edge_ref, "far": far_ref}

    def tile_of(a, b, c):
        return low_ref[a, b - 1, c] if c < 2 else high_ref[a, b - 1, c - grid.cz - 2]

    for cell in grid.cells_of("edge"):
        grid.put_partner(tile_of(*cell), cell, refs, {"edge": edge_point_ref})
    for cell in grid.cells_of("far"):
        grid.put_partner(tile_of(*cell), cell, refs)
    for place, cell in enumerate(grid.edge_targets()):
        edge_left_ref[place] = target_block(grid.target(tile_of(*cell), *cell))
        runs = grid.sources(cell, ("own", "gown", "edge", "far"))
        add_density(grid, edge_left_ref, place, runs, refs, nothing, store_to(edge_sum_ref, place))
    for place, cell in enumerate(grid.own_targets()):
        runs = grid.sources(cell, ("edge",))
        before = lambda chunk, place=place: inner_ref[place, chunk, :]
        add_density(grid, left_ref, place, runs, refs, before, store_to(own_sum_ref, place))


def last_density_kernel(own, mid_ref, low_ref, high_ref, below_ref, above_ref, own_sum_ref, edge_sum_ref, left_ref, edge_left_ref, slope_ref, weight_ref, ghost_ref, ghost_point_ref, far_ref):
    grid = Grid(own)
    refs = {"gedge": ghost_ref, "gfar": far_ref}
    for which in ("gedge", "gfar"):
        for a, b, c in grid.cells_of(which):
            tile = (below_ref if b == 0 else above_ref)[a, 0, c if c < 2 else c - grid.cz]
            grid.put_partner(tile, (a, b, c), refs, {"gedge": ghost_point_ref} if which == "gedge" else None)
    groups = ((grid.own_targets(), own_sum_ref, left_ref), (grid.edge_targets(), edge_sum_ref, edge_left_ref))
    for targets, sum_ref, rows_ref in groups:
        for place, (a, b, c) in enumerate(targets):
            if c < 2:
                tile = low_ref[a, b - 1, c]
            elif c >= grid.cz + 2:
                tile = high_ref[a, b - 1, c - grid.cz - 2]
            else:
                tile = mid_ref[a, b - 1, c - 2]
            runs = grid.sources((a, b, c), ("gedge", "gfar"))
            parts = []
            before = lambda chunk, place=place, sum_ref=sum_ref: sum_ref[place, chunk, :]
            add_density(grid, rows_ref, place, runs, refs, before, lambda chunk, total: parts.append(total))
            density = across(jnp.concatenate(parts, axis=0))
            scale = tile[3:4]
            slope = jnp.where(scale > 0.5, -0.5, 0.0) / jnp.sqrt(density + 1.0)
            where = grid.slope_row(a, b, c)
            slope_ref[where : where + 1, :] = slope
            weight_ref[where : where + 1, :] = slope * jnp.where(scale > 1.05, 0.75 / (ROOT * ROOT), 0.75)


def put_pair(grid, cell, point_refs, pair_refs, weight):
    which, index = grid.place(*cell)
    lanes = slice(index * LANES, (index + 1) * LANES)
    scale = point_refs[which][4:5, lanes]
    row = jnp.where(grid.row == 5, 0.75 * scale, jnp.where(grid.row == 6, weight, 0.0))
    high = row.astype(jnp.bfloat16).astype(jnp.float32)
    first = jnp.concatenate([high, row - high], axis=0).astype(jnp.bfloat16)
    last = jnp.concatenate([jnp.zeros((8, LANES), jnp.float32), high], axis=0).astype(jnp.bfloat16)
    pair_refs[which][:, lanes] = jnp.concatenate([first, first, last], axis=0)


def add_force(left_ref, place, runs, refs, point_refs, pair_refs, before, after):
    rows = 32
    for start in range(0, LANES, rows):
        chunk = slice(start, start + rows)
        total = before(chunk)
        left = left_ref[place, chunk, :]
        for which, first, count, _ in runs:
            span = slice(first * LANES, (first + count) * LANES)
            near = jnp.dot(left, refs[which][:, span], preferred_element_type=jnp.float32)
            kappa = jnp.dot(left, pair_refs[which][:, span], preferred_element_type=jnp.float32)
            value_ref = point_refs[which]
            for k in range(count):
                part = slice(k * LANES, (k + 1) * LANES)
                lanes = slice((first + k) * LANES, (first + k + 1) * LANES)
                s = jnp.maximum(near[:, part], 0.0)
                w = s * (value_ref[3:4, lanes] + s * kappa[:, part])
                new = [w * value_ref[axis : axis + 1, lanes] for axis in range(3)] + [w]
                total = new if total is None else [old + more for old, more in zip(total, new)]
        after(chunk, total)


def store_four(ref, place):
    def after(chunk, total):
        for k in range(4):
            ref[k, place, chunk, :] = total[k]

    return after


def load_four(ref, place):
    def before(chunk):
        return [ref[k, place, chunk, :] for k in range(4)]

    return before


def row_of(ref, index):
    return ref[index : index + 1, :]


def column_force_kernel(own, *all_refs):
    mid_ref, slope_ref, weight_ref, below_ref, above_ref = all_refs[:5]
    refs = dict(zip(SETS, all_refs[5:9]))
    point_refs = dict(zip(SETS, all_refs[9:13]))
    out_ref, left_ref = all_refs[13:15]
    pair_refs = dict(zip(SETS, all_refs[15:]))
    grid = Grid(own)
    m = grid.masks
    near = grid.cz + 2
    for which in SETS:
        for a, b, c in grid.cells_of(which, grid.inner):
            if which[0] == "g":
                weight = row_of(below_ref if b == 0 else above_ref, (a - 1) * near + c - 1)
            else:
                weight = row_of(weight_ref, grid.slope_row(a, b, c))
            put_pair(grid, (a, b, c), point_refs, pair_refs, weight)
    for place, (a, b, c) in enumerate(grid.own_targets()):
        tile = mid_ref[a, b - 1, c - 2]
        solute = tile[3:4] > 1.05
        left_ref[place] = target_block(
            grid.target(tile, a, b, c) * jnp.where(solute, 0.8, 0.6)
            + row_of(slope_ref, grid.slope_row(a, b, c)) * jnp.where(solute, 1.0 / 0.16, 1.0 / 0.09) * m[5]
            + jnp.where(solute, 1.3 / 0.16, 1.0 / 0.09) * m[6]
        )
        runs = grid.sources((a, b, c), SETS, grid.inner)
        add_force(left_ref, place, runs, refs, point_refs, pair_refs, nothing, store_four(out_ref, place))


def side_force_kernel(own, below_ref, above_ref, part_ref, edge_ref, point_ref, edge_point_ref, column_ref, left_ref, out_ref, pair_ref, edge_pair_ref):
    grid = Grid(own)
    refs = {"own": part_ref, "edge": edge_ref}
    point_refs = {"own": point_ref, "edge": edge_point_ref}
    pair_refs = {"own": pair_ref, "edge": edge_pair_ref}
    for which in refs:
        for a, b, c in grid.cells_of(which, grid.outer):
            weight = row_of(below_ref if a == 0 else above_ref, grid.slope_row(1, b, c))
            put_pair(grid, (a, b, c), point_refs, pair_refs, weight)
    for place, cell in enumerate(grid.own_targets()):
        runs = grid.sources(cell, tuple(refs), grid.outer)
        before, after = load_four(column_ref, place), store_four(out_ref, place)
        add_force(left_ref, place, runs, refs, point_refs, pair_refs, before, after)


def last_force_kernel(own, stage, mid_ref, below_ref, above_ref, ghost_ref, ghost_edge_ref, ghost_point_ref, ghost_edge_point_ref, column_ref, left_ref, vel_ref, *out_refs):
    new_vel_ref, new_loc_ref, pair_ref, edge_pair_ref = out_refs
    grid = Grid(own)
    near = grid.cz + 2
    refs = {"gown": ghost_ref, "gedge": ghost_edge_ref}
    point_refs = {"gown": ghost_point_ref, "gedge": ghost_edge_point_ref}
    pair_refs = {"gown": pair_ref, "gedge": edge_pair_ref}
    for which in refs:
        for a, b, c in grid.cells_of(which, grid.outer):
            weight = row_of(below_ref if b == 0 else above_ref, int(a > 0) * near + c - 1)
            put_pair(grid, (a, b, c), point_refs, pair_refs, weight)
    for place, (a, b, c) in enumerate(grid.own_targets()):
        parts = []
        runs = grid.sources((a, b, c), tuple(refs), grid.outer)
        after = lambda chunk, total: parts.append(total)
        add_force(left_ref, place, runs, refs, point_refs, pair_refs, load_four(column_ref, place), after)
        flat = [across(jnp.concatenate([part[k] for part in parts], axis=0)) for k in range(4)]
        row = slice(place, place + 1)
        tile = mid_ref[a, b - 1, c - 2]
        point, _ = grid.placed(tile, a, b, c)
        scale = tile[3:4]
        present = jnp.where(scale > 0.5, -2.0, 0.0)
        kick = half_kick * jnp.where(scale > 1.05, 1.6, 1.0)
        for axis in range(3):
            force = present * (flat[axis] - point[axis : axis + 1] * flat[3])
            speed = vel_ref[axis, row, :] + kick * force
            if stage == "middle":
                speed = speed + kick * force
            new_vel_ref[axis, row, :] = speed
            if stage == "last":
                new_loc_ref[axis, row, :] = tile[axis : axis + 1]
            else:
                new_loc_ref[place, axis : axis + 1, :] = tile[axis : axis + 1] + time_step * speed
        if stage != "last":
            new_loc_ref[place, 3:4, :] = scale


def on_device(positions, velocities, species, counts):
    cx, cy, cz, slots = positions.shape[1:]
    own = (cx, cy, cz)
    cells = cx * cy * cz
    ex, near = cx + 2, cz + 2
    vmem = pl.BlockSpec(memory_space=pltpu.VMEM)
    flat_shape = jax.ShapeDtypeStruct((3, cells, slots), jnp.float32)
    sizes = {"own": ex * cy * cz, "edge": ex * cy * 2, "gown": 2 * ex * cz, "gedge": 2 * ex * 2}

    def block(which):
        return jax.ShapeDtypeStruct((48, sizes[which] * slots), jnp.bfloat16)

    def points(which):
        return jax.ShapeDtypeStruct((8, sizes[which] * slots), jnp.float32)

    def sums(*count):
        return jax.ShapeDtypeStruct((*count, slots, slots), jnp.float32)

    def rows(count):
        return jax.ShapeDtypeStruct((count, slots), jnp.float32)

    def lefts(count):
        return jax.ShapeDtypeStruct((count, slots, 48), jnp.bfloat16)

    def call(kernel, name, operands, out_shape, pairs, scratch=()):
        return pl.pallas_call(
            kernel,
            out_shape=out_shape,
            in_specs=[vmem] * len(operands),
            out_specs=[vmem] * len(out_shape),
            scratch_shapes=[pltpu.VMEM(item.shape, item.dtype) for item in scratch],
            compiler_params=pltpu.CompilerParams(vmem_limit_bytes=GRANT),
            cost_estimate=pl.CostEstimate(
                flops=pairs * slots * slots * 50, bytes_accessed=pairs * slots * slots * 4, transcendentals=0
            ),
            name=name,
        )(*operands)

    def evaluate(location, velocity, stage):
        mid = ring_halo(location, "gx", 0, 1)
        mid_below, mid_above = neighbours(mid, "gy", 1, 1)
        low, high = neighbours(mid, "gz", 2, 2)
        inner, part, point, ghost, ghost_point, left = call(
            functools.partial(inner_density_kernel, own),
            "inner_density",
            [mid, mid_below, mid_above],
            [sums(cells), block("own"), points("own"), block("gown"), points("gown"), lefts(cells)],
            cells * 18,
        )
        tall, inner = lax.optimization_barrier((jnp.concatenate([low, high], axis=2), inner))
        below, above = neighbours(tall, "gy", 1, 1)
        own_sum, edge_sum, edge, edge_point, edge_left = call(
            functools.partial(outer_density_kernel, own),
            "outer_density",
            [low, high, inner, part, ghost, left],
            [sums(cells), sums(cx * cy * 2), block("edge"), points("edge"), lefts(cx * cy * 2)],
            cells * 27,
            [block("edge")],
        )
        slopes, weights, ghost_edge, ghost_edge_point = call(
            functools.partial(last_density_kernel, own),
            "last_density",
            [mid, low, high, below, above, own_sum, edge_sum, left, edge_left],
            [rows(cx * cy * near), rows(cx * cy * near), block("gedge"), points("gedge")],
            cells * 9,
            [block("gedge")],
        )
        weights = weights.reshape(cx, cy, near, slots)
        weight_below, weight_above = neighbours(weights, "gy", 1, 1)
        side_below, side_above = neighbours(weights, "gx", 0, 1)
        column, left = call(
            functools.partial(column_force_kernel, own),
            "column_force",
            [
                mid,
                slopes,
                weights.reshape(cx * cy * near, slots),
                weight_below.reshape(cx * near, slots),
                weight_above.reshape(cx * near, slots),
                *(part, edge, ghost, ghost_edge),
                *(point, edge_point, ghost_point, ghost_edge_point),
            ],
            [sums(4, cells), lefts(cells)],
            cells * 9,
            [block(which) for which in SETS],
        )
        sides, column = lax.optimization_barrier((jnp.concatenate([side_below, side_above], axis=0), column))
        corner_below, corner_above = neighbours(sides, "gy", 1, 1)
        (column,) = call(
            functools.partial(side_force_kernel, own),
            "side_force",
            [
                side_below.reshape(cy * near, slots),
                side_above.reshape(cy * near, slots),
                *(part, edge, point, edge_point, column, left),
            ],
            [sums(4, cells)],
            cells * 12,
            [block("own"), block("edge")],
        )
        moved = flat_shape if stage == "last" else jax.ShapeDtypeStruct((cells, 4, slots), jnp.float32)
        return call(
            functools.partial(last_force_kernel, own, stage),
            "force_" + stage,
            [
                mid,
                corner_below.reshape(2 * near, slots),
                corner_above.reshape(2 * near, slots),
                *(ghost, ghost_edge, ghost_point, ghost_edge_point, column, left, velocity),
            ],
            [flat_shape, moved],
            cells * 6,
            [block("gown"), block("gedge")],
        )

    arrays = [pltpu.with_memory_space_constraint(x, pltpu.HBM) for x in (positions, velocities, species, counts)]
    location, velocity = pl.pallas_call(
        prepare_kernel,
        out_shape=[jax.ShapeDtypeStruct((cx, cy, cz, 4, slots), jnp.float32), flat_shape],
        in_specs=[pl.BlockSpec(memory_space=pltpu.HBM)] * 4,
        out_specs=[vmem] * 2,
        scratch_shapes=[pltpu.VMEM(array.shape, array.dtype) for array in arrays] + [pltpu.SemaphoreType.DMA((4,))],
        compiler_params=pltpu.CompilerParams(vmem_limit_bytes=GRANT),
        name="prepare",
    )(*arrays)
    velocity, moved = evaluate(location, velocity, "first")
    velocity, moved = evaluate(moved.reshape(location.shape), velocity, "middle")
    velocity, new_positions = evaluate(moved.reshape(location.shape), velocity, "last")
    return new_positions.reshape(positions.shape), velocity.reshape(positions.shape)


def solution(mesh):
    return jax.shard_map(
        on_device,
        mesh=mesh,
        in_specs=(
            P(None, "gx", "gy", "gz", None),
            P(None, "gx", "gy", "gz", None),
            P("gx", "gy", "gz", None),
            P("gx", "gy", "gz"),
        ),
        out_specs=(P(None, "gx", "gy", "gz", None), P(None, "gx", "gy", "gz", None)),
        check_vma=False,
    )
```

time: 75.8 us -> 74 us (0.976)
  local copies, waits for them, and re-layouts: 2.15 us -> 0.06 us
  starting transfers between devices: 22.4 us -> 24.4 us
  waiting for transfers between devices: 28 us -> 26.2 us
    ppermute x9, waiting for transfers between devices: 9.43 us -> 7.18 us  [neighbours(): lax.ppermute(head, axis, [((i + 1) % count, i) for i in range(count)])]
    unnamed x7 -> x2, local copies, waits for them, and re-layouts: 2.05 us -> 0.01 us
    ppermute x6 -> x12, starting transfers between devices: 0.22 us -> 2.03 us  [neighbours(): other = lax.ppermute(cells, axis, [(0, 1), (1, 0)])]
    ppermute x9, starting transfers between devices: 10.9 us -> 12 us  [neighbours(): lax.ppermute(tail, axis, [(i, (i + 1) % count) for i in range(count)])]
    ppermute x9, starting transfers between devices: 11.3 us -> 10.4 us  [neighbours(): lax.ppermute(head, axis, [((i + 1) % count, i) for i in range(count)])]
    pallas_call x0 -> x1, Pallas kernels: none -> 0.84 us  [on_device(): pl.pallas_call(prepare_kernel, out_shape=[jax.ShapeDtypeStruct((cx, cy, c...]
  transfers between devices with their start and end apart: 24 -> 30, of which waited for: 18 -> 18; matrix products, arithmetic and copies ran while one was open for 0% -> 0% of each run, Pallas kernels for 19% -> 21%
where the time goes in v2:
time: 74 us; the launch traced here: 73.8 us
  waiting for transfers between devices  26.2 us (35%)
  starting transfers between devices  24.4 us (33%)
  Pallas kernels  22 us (30%)
  between operations  0.95 us (1%)
    pallas_call x18, Pallas kernels, call(): pl.pallas_call(kernel, out_shape=out_shape, in_specs=[vmem] * len(operand...  21.2 us
    ppermute x9, waiting for transfers between devices, neighbours(): lax.ppermute(tail, axis, [(i, (i + 1) % count) for i in range(count)])  19 us
    ppermute x9, starting transfers between devices, neighbours(): lax.ppermute(tail, axis, [(i, (i + 1) % count) for i in range(count)])  12 us
    ppermute x9, starting transfers between devices, neighbours(): lax.ppermute(head, axis, [((i + 1) % count, i) for i in range(count)])  10.4 us
    ppermute x9, waiting for transfers between devices, neighbours(): lax.ppermute(head, axis, [((i + 1) % count, i) for i in range(count)])  7.18 us
    ppermute x12, starting transfers between devices, neighbours(): other = lax.ppermute(cells, axis, [(0, 1), (1, 0)])  2.03 us
  transfers between devices with their start and end apart: 30, of which 18 were waited for; matrix products, arithmetic and copies ran while one was open for 0% of the time, Pallas kernels for 21%

profile of v2, /device:TPU:0, one launch (start us, length us, event | category | flops | bytes accessed | tf_op | source)
XLA Modules:
  0.0 73.8 jit_solution(11617722117334170013)
XLA Ops:
  0.6 0.8 %prepare.1 = (f32[1,2,2,4,128]{4,3,2,1,0:T(4,128)S(1)}, f32[3,4,128]{2,1,0:T(4,128)S(1)}) custom-call(f32[3,1,2,2,128]{4,3,2,1,0:T(2,128)} %pos_hbm.1, f32[3,1,2,2,128]{4,3,2,1,0:T(2,128)} %vel_hbm.1, s32[1,2,2,128]{3,2,1,0:T(2,128)} %species_hbm.1, s32[1,2,2]{2,1,0:T(2,128)} %counts_hbm.1), custom_call_target="tpu_custom_call" | custom-call | tf_op jit(solution)/shard_map/prepare/pallas_call | solution.py:528
  1.5 3.0 %collective-permute-start = (f32[1,2,2,4,128]{4,3,2,1,0:T(4,128)S(1)}, f32[1,2,2,4,128]{4,3,2,1,0:T(4,128)S(1)}, u32[]{:S(2)}, u32[]{:S(2)}) collective-permute-start(f32[1,2,2,4,128]{4,3,2,1,0:T(4,128)S(1)} %get-tuple-element.73), channel_id=1, source_target_pairs={{0,8},{8,16},{16,24},{24,0},{1,9},{9,17},{17,25},{25,1},{2,10},{10... | collective-permute-start | bytes 24584 | tf_op jit(solution)/shard_map/ppermute | solution.py:32
  4.5 1.0 %collective-permute-start.1 = (f32[1,2,2,4,128]{4,3,2,1,0:T(4,128)S(1)}, f32[1,2,2,4,128]{4,3,2,1,0:T(4,128)S(1)}, u32[]{:S(2)}, u32[]{:S(2)}) collective-permute-start(f32[1,2,2,4,128]{4,3,2,1,0:T(4,128)S(1)} %get-tuple-element.73), channel_id=1, source_target_pairs={{8,0},{16,8},{24,16},{0,24},{9,1},{17,9},{25,17},{1,25},{10,2},{18... | collective-permute-start | bytes 24584 | tf_op jit(solution)/shard_map/ppermute | solution.py:33
  5.5 1.6 %collective-permute-done = f32[1,2,2,4,128]{4,3,2,1,0:T(4,128)S(1)} collective-permute-done((f32[1,2,2,4,128]{4,3,2,1,0:T(4,128)S(1)}, f32[1,2,2,4,128]{4,3,2,1,0:T(4,128)S(1)}, u32[]{:S(2)}, u32[]{:S(2)}) %collective-permute-start) | collective-permute-done | bytes 8224 | tf_op jit(solution)/shard_map/ppermute | solution.py:32
  7.1 1.1 %collective-permute-done.1 = f32[1,2,2,4,128]{4,3,2,1,0:T(4,128)S(1)} collective-permute-done((f32[1,2,2,4,128]{4,3,2,1,0:T(4,128)S(1)}, f32[1,2,2,4,128]{4,3,2,1,0:T(4,128)S(1)}, u32[]{:S(2)}, u32[]{:S(2)}) %collective-permute-start.1) | collective-permute-done | bytes 8224 | tf_op jit(solution)/shard_map/ppermute | solution.py:33
  8.2 0.0 collective-permute-start.4
  8.2 3.6 %collective-permute-start.3 = (f32[3,2,2,4,128]{4,3,2,1,0:T(4,128)S(1)}, f32[3,2,2,4,128]{4,3,2,1,0:T(4,128)S(1)}, u32[]{:S(2)}, u32[]{:S(2)}) collective-permute-start(f32[3,2,2,4,128]{4,3,2,1,0:T(4,128)S(1)} %constant_dynamic-update-slice_fusion.mid_ref.all_refs_0_), channel_id=1, source_target_pairs={{1,0},{2,1},{3,2},{0,3},{5,4},{6,5},{7,6},{4,7},{9,8},{10,9},{11,1... | collective-permute-start | bytes 73736 | tf_op jit(solution)/shard_map/ppermute | solution.py:33
  11.8 0.0 collective-permute-start.2
  11.8 1.0 %inner_density.3 = (f32[4,128,128]{2,1,0:T(8,128)S(1)}, bf16[48,1536]{1,0:T(8,128)(2,1)S(1)}, f32[8,1536]{1,0:T(8,128)S(1)}, bf16[48,1536]{1,0:T(8,128)(2,1)S(1)...) custom-call(f32[3,2,2,4,128]{4,3,2,1,0:T(4,128)S(1)} %constant_dynamic-update-slice_fusion.mid_ref.all_refs_0_, ...), custom_call_target="tpu_custom_call" | custom-call | flops 58982400 | bytes 4718592 | tf_op jit(solution)/shard_map/inner_density/pallas_call | solution.py:437
  12.7 0.5 collective-permute-done.3.high_ref
  13.3 4.1 %collective-permute-done.2.low_ref = f32[3,2,2,4,128]{4,3,2,1,0:T(4,128)S(1)} collective-permute-done((f32[3,2,2,4,128]{4,3,2,1,0:T(4,128)S(1)}, f32[3,2,2,4,128]{4,3,2,1,0:T(4,128)S(1)}, u32[]{:S(2)}, u32[]{:S(2)}) %collective-permute-start.2) | collective-permute-done | bytes 24608 | tf_op jit(solution)/shard_map/ppermute | solution.py:32
  17.4 0.1 collective-permute-start.5
  17.5 1.3 %outer_density.3 = (f32[4,128,128]{2,1,0:T(8,128)S(1)}, f32[4,128,128]{2,1,0:T(8,128)S(1)}, bf16[48,1536]{1,0:T(8,128)(2,1)S(1)}, f32[8,1536]{1,0:T(8,128)S(1)}, bf16[4,128,48]{2,1,0:T(8,128)(2,1)S(1)}) custom-call(f32[3,2,2,4,128]{4,3,2,1,0:T(4,128)S(1)} %collective-permute-done.2.low_ref, f32[3,2,2,4,128]{4,3,2,1,0:T(4,128)S(1)} %collective-permute-done.3.high_ref, ...), custom_call_target="tpu_custom_call" | custom-call | flops 88473600 | bytes 7077888 | tf_op jit(solution)/shard_map/outer_density/pallas_call | solution.py:437
  18.8 0.6 last_density.3
  19.5 0.6 collective-permute-start.8
  20.0 2.3 %collective-permute-start.7 = (f32[1,2,4,128]{3,2,1,0:T(4,128)S(1)}, f32[1,2,4,128]{3,2,1,0:T(4,128)S(1)}, u32[]{:S(2)}, u32[]{:S(2)}) collective-permute-start(f32[1,2,4,128]{3,2,1,0:T(4,128)S(1)} %bitcast.54), channel_id=1, source_target_pairs={{8,0},{16,8},{24,16},{0,24},{9,1},{17,9},{25,17},{1,25},{10,2},{18... | collective-permute-start | bytes 12296 | tf_op jit(solution)/shard_map/ppermute | solution.py:33
  22.3 0.1 collective-permute-start.6
  22.4 1.3 %column_force.3 = (f32[4,4,128,128]{3,2,1,0:T(8,128)S(1)}, bf16[4,128,48]{2,1,0:T(8,128)(2,1)S(1)}) custom-call(f32[3,2,2,4,128]{4,3,2,1,0:T(4,128)S(1)} %constant_dynamic-update-slice_fusion.mid_ref.all_refs_0_, f32[8,128]{1,0:T(8,128)S(1)} %get-tuple-element.84.all_refs_1_, f32[8,128]{1,0:T(8,128)S(1)} %get-tuple-element.83.all_refs_2_, ...), custom_call_target="tpu_custom_call" | custom-call | flops 29491200 | bytes 2359296 | tf_op jit(solution)/shard_map/column_force/pallas_call | solution.py:437
  23.8 0.2 collective-permute-done.7
  24.0 2.9 %collective-permute-done.6 = f32[1,2,4,128]{3,2,1,0:T(4,128)S(1)} collective-permute-done((f32[1,2,4,128]{3,2,1,0:T(4,128)S(1)}, f32[1,2,4,128]{3,2,1,0:T(4,128)S(1)}, u32[]{:S(2)}, u32[]{:S(2)}) %collective-permute-start.6) | collective-permute-done | bytes 4128 | tf_op jit(solution)/shard_map/ppermute | solution.py:32
  26.9 1.6 %side_force.3.column_ref = f32[4,4,128,128]{3,2,1,0:T(8,128)S(1)} custom-call(f32[8,128]{1,0:T(8,128)S(1)} %bitcast.38, f32[8,128]{1,0:T(8,128)S(1)} %bitcast.35, bf16[48,1536]{1,0:T(8,128)(2,1)S(1)} %get-tuple-element.77.part_ref.all_refs_5_, bf16[48,1536]{1,0:T(8,128)(2,1)S(1)} %get-tuple-element.85.all_refs_6_.edge_ref, ...), custom_call_target="tpu_custom_call" | custom-call | flops 39321600 | bytes 3145728 | tf_op jit(solution)/shard_map/side_force/pallas_call | solution.py:437
  28.5 1.0 %force_first.1 = (f32[3,4,128]{2,1,0:T(4,128)S(1)}, f32[4,4,128]{2,1,0:T(4,128)S(1)}) custom-call(f32[3,2,2,4,128]{4,3,2,1,0:T(4,128)S(1)} %constant_dynamic-update-slice_fusion.mid_ref.all_refs_0_, f32[8,128]{1,0:T(8,128)S(1)} %bitcast.42, f32[8,128]{1,0:T(8,128)S(1)} %bitcast.41, bf16[48,1536]{1,0:T(8,128)(2,1)S(1)} %get-tuple-element.78.ghost_ref.all_refs_7_, ...), custom_call_target="tpu_custom_call" | custom-call | flops 19660800 | bytes 1572864 | tf_op jit(solution)/shard_map/force_first/pallas_call | solution.py:437
  29.5 0.2 collective-permute-start.11
  29.7 1.9 %collective-permute-start.10 = (f32[1,2,2,4,128]{4,3,2,1,0:T(4,128)S(1)}, f32[1,2,2,4,128]{4,3,2,1,0:T(4,128)S(1)}, u32[]{:S(2)}, u32[]{:S(2)}) collective-permute-start(f32[1,2,2,4,128]{4,3,2,1,0:T(4,128)S(1)} %bitcast.48), channel_id=1, source_target_pairs={{0,8},{8,16},{16,24},{24,0},{1,9},{9,17},{17,25},{25,1},{2,10},{10... | collective-permute-start | bytes 24584 | tf_op jit(solution)/shard_map/ppermute | solution.py:32
  31.6 1.6 %collective-permute-done.11 = f32[1,2,2,4,128]{4,3,2,1,0:T(4,128)S(1)} collective-permute-done((f32[1,2,2,4,128]{4,3,2,1,0:T(4,128)S(1)}, f32[1,2,2,4,128]{4,3,2,1,0:T(4,128)S(1)}, u32[]{:S(2)}, u32[]{:S(2)}) %collective-permute-start.11) | collective-permute-done | bytes 8224 | tf_op jit(solution)/shard_map/ppermute | solution.py:33
  33.2 1.0 %collective-permute-done.10 = f32[1,2,2,4,128]{4,3,2,1,0:T(4,128)S(1)} collective-permute-done((f32[1,2,2,4,128]{4,3,2,1,0:T(4,128)S(1)}, f32[1,2,2,4,128]{4,3,2,1,0:T(4,128)S(1)}, u32[]{:S(2)}, u32[]{:S(2)}) %collective-permute-start.10) | collective-permute-done | bytes 8224 | tf_op jit(solution)/shard_map/ppermute | solution.py:32
  34.3 0.1 collective-permute-start.14
  34.4 0.1 collective-permute-start.13
  34.5 2.0 %collective-permute-start.12 = (f32[3,2,2,4,128]{4,3,2,1,0:T(4,128)S(1)}, f32[3,2,2,4,128]{4,3,2,1,0:T(4,128)S(1)}, u32[]{:S(2)}, u32[]{:S(2)}) collective-permute-start(f32[3,2,2,4,128]{4,3,2,1,0:T(4,128)S(1)} %pad_maximum_fusion.3.mid_ref.all_refs_0_), channel_id=1, source_target_pairs={{0,1},{1,2},{2,3},{3,0},{4,5},{5,6},{6,7},{7,4},{8,9},{9,10},{10,1... | collective-permute-start | bytes 73736 | tf_op jit(solution)/shard_map/ppermute | solution.py:32
  36.5 1.0 %inner_density.4 = (f32[4,128,128]{2,1,0:T(8,128)S(1)}, bf16[48,1536]{1,0:T(8,128)(2,1)S(1)}, f32[8,1536]{1,0:T(8,128)S(1)}, bf16[48,1536]{1,0:T(8,128)(2,1)S(1)...) custom-call(f32[3,2,2,4,128]{4,3,2,1,0:T(4,128)S(1)} %pad_maximum_fusion.3.mid_ref.all_refs_0_, ...), custom_call_target="tpu_custom_call" | custom-call | flops 58982400 | bytes 4718592 | tf_op jit(solution)/shard_map/inner_density/pallas_call | solution.py:437
  37.4 0.8 %collective-permute-done.13.high_ref = f32[3,2,2,4,128]{4,3,2,1,0:T(4,128)S(1)} collective-permute-done((f32[3,2,2,4,128]{4,3,2,1,0:T(4,128)S(1)}, f32[3,2,2,4,128]{4,3,2,1,0:T(4,128)S(1)}, u32[]{:S(2)}, u32[]{:S(2)}) %collective-permute-start.13) | collective-permute-done | bytes 24608 | tf_op jit(solution)/shard_map/ppermute | solution.py:33
  38.3 1.9 %collective-permute-done.12.low_ref = f32[3,2,2,4,128]{4,3,2,1,0:T(4,128)S(1)} collective-permute-done((f32[3,2,2,4,128]{4,3,2,1,0:T(4,128)S(1)}, f32[3,2,2,4,128]{4,3,2,1,0:T(4,128)S(1)}, u32[]{:S(2)}, u32[]{:S(2)}) %collective-permute-start.12) | collective-permute-done | bytes 24608 | tf_op jit(solution)/shard_map/ppermute | solution.py:32
  40.1 0.1 collective-permute-start.15
  40.2 1.3 %outer_density.4 = (f32[4,128,128]{2,1,0:T(8,128)S(1)}, f32[4,128,128]{2,1,0:T(8,128)S(1)}, bf16[48,1536]{1,0:T(8,128)(2,1)S(1)}, f32[8,1536]{1,0:T(8,128)S(1)}, bf16[4,128,48]{2,1,0:T(8,128)(2,1)S(1)}) custom-call(f32[3,2,2,4,128]{4,3,2,1,0:T(4,128)S(1)} %collective-permute-done.12.low_ref, f32[3,2,2,4,128]{4,3,2,1,0:T(4,128)S(1)} %collective-permute-done.13.high_ref, ...), custom_call_target="tpu_custom_call" | custom-call | flops 88473600 | bytes 7077888 | tf_op jit(solution)/shard_map/outer_density/pallas_call | solution.py:437
  41.5 0.6 last_density.4
  42.2 0.6 collective-permute-start.18
  42.8 1.9 %collective-permute-start.17 = (f32[1,2,4,128]{3,2,1,0:T(4,128)S(1)}, f32[1,2,4,128]{3,2,1,0:T(4,128)S(1)}, u32[]{:S(2)}, u32[]{:S(2)}) collective-permute-start(f32[1,2,4,128]{3,2,1,0:T(4,128)S(1)} %bitcast.57), channel_id=1, source_target_pairs={{8,0},{16,8},{24,16},{0,24},{9,1},{17,9},{25,17},{1,25},{10,2},{18... | collective-permute-start | bytes 12296 | tf_op jit(solution)/shard_map/ppermute | solution.py:33
  44.7 0.1 collective-permute-start.16
  44.8 1.3 %column_force.4 = (f32[4,4,128,128]{3,2,1,0:T(8,128)S(1)}, bf16[4,128,48]{2,1,0:T(8,128)(2,1)S(1)}) custom-call(f32[3,2,2,4,128]{4,3,2,1,0:T(4,128)S(1)} %pad_maximum_fusion.3.mid_ref.all_refs_0_, f32[8,128]{1,0:T(8,128)S(1)} %get-tuple-element.107.all_refs_1_, f32[8,128]{1,0:T(8,128)S(1)} %get-tuple-element.106.all_refs_2_, ...), custom_call_target="tpu_custom_call" | custom-call | flops 29491200 | bytes 2359296 | tf_op jit(solution)/shard_map/column_force/pallas_call | solution.py:437
  46.1 0.2 collective-permute-done.17
  46.4 2.8 %collective-permute-done.16 = f32[1,2,4,128]{3,2,1,0:T(4,128)S(1)} collective-permute-done((f32[1,2,4,128]{3,2,1,0:T(4,128)S(1)}, f32[1,2,4,128]{3,2,1,0:T(4,128)S(1)}, u32[]{:S(2)}, u32[]{:S(2)}) %collective-permute-start.16) | collective-permute-done | bytes 4128 | tf_op jit(solution)/shard_map/ppermute | solution.py:32
  49.2 1.6 %side_force.4.column_ref = f32[4,4,128,128]{3,2,1,0:T(8,128)S(1)} custom-call(f32[8,128]{1,0:T(8,128)S(1)} %bitcast.39, f32[8,128]{1,0:T(8,128)S(1)} %bitcast.36, bf16[48,1536]{1,0:T(8,128)(2,1)S(1)} %get-tuple-element.100.part_ref.all_refs_5_, bf16[48,1536]{1,0:T(8,128)(2,1)S(1)} %get-tuple-element.108.all_refs_6_.edge_ref, ...), custom_call_target="tpu_custom_call" | custom-call | flops 39321600 | bytes 3145728 | tf_op jit(solution)/shard_map/side_force/pallas_call | solution.py:437
  50.8 1.0 %force_middle.1 = (f32[3,4,128]{2,1,0:T(4,128)S(1)}, f32[4,4,128]{2,1,0:T(4,128)S(1)}) custom-call(f32[3,2,2,4,128]{4,3,2,1,0:T(4,128)S(1)} %pad_maximum_fusion.3.mid_ref.all_refs_0_, f32[8,128]{1,0:T(8,128)S(1)} %bitcast.44, f32[8,128]{1,0:T(8,128)S(1)} %bitcast.43, bf16[48,1536]{1,0:T(8,128)(2,1)S(1)} %get-tuple-element.101.ghost_ref.all_refs_7_, ...), custom_call_target="tpu_custom_call" | custom-call | flops 19660800 | bytes 1572864 | tf_op jit(solution)/shard_map/force_middle/pallas_call | solution.py:437
  51.9 0.1 collective-permute-start.21
  52.0 1.9 %collective-permute-start.20 = (f32[1,2,2,4,128]{4,3,2,1,0:T(4,128)S(1)}, f32[1,2,2,4,128]{4,3,2,1,0:T(4,128)S(1)}, u32[]{:S(2)}, u32[]{:S(2)}) collective-permute-start(f32[1,2,2,4,128]{4,3,2,1,0:T(4,128)S(1)} %bitcast.51), channel_id=1, source_target_pairs={{0,8},{8,16},{16,24},{24,0},{1,9},{9,17},{17,25},{25,1},{2,10},{10... | collective-permute-start | bytes 24584 | tf_op jit(solution)/shard_map/ppermute | solution.py:32
  53.9 1.6 %collective-permute-done.21 = f32[1,2,2,4,128]{4,3,2,1,0:T(4,128)S(1)} collective-permute-done((f32[1,2,2,4,128]{4,3,2,1,0:T(4,128)S(1)}, f32[1,2,2,4,128]{4,3,2,1,0:T(4,128)S(1)}, u32[]{:S(2)}, u32[]{:S(2)}) %collective-permute-start.21) | collective-permute-done | bytes 8224 | tf_op jit(solution)/shard_map/ppermute | solution.py:33
  55.6 1.0 %collective-permute-done.20 = f32[1,2,2,4,128]{4,3,2,1,0:T(4,128)S(1)} collective-permute-done((f32[1,2,2,4,128]{4,3,2,1,0:T(4,128)S(1)}, f32[1,2,2,4,128]{4,3,2,1,0:T(4,128)S(1)}, u32[]{:S(2)}, u32[]{:S(2)}) %collective-permute-start.20) | collective-permute-done | bytes 8224 | tf_op jit(solution)/shard_map/ppermute | solution.py:32
  56.5 0.1 collective-permute-start.24
  56.6 0.2 collective-permute-start.23
  56.8 1.9 %collective-permute-start.22 = (f32[3,2,2,4,128]{4,3,2,1,0:T(4,128)S(1)}, f32[3,2,2,4,128]{4,3,2,1,0:T(4,128)S(1)}, u32[]{:S(2)}, u32[]{:S(2)}) collective-permute-start(f32[3,2,2,4,128]{4,3,2,1,0:T(4,128)S(1)} %pad_maximum_fusion.4.mid_ref.all_refs_0_), channel_id=1, source_target_pairs={{0,1},{1,2},{2,3},{3,0},{4,5},{5,6},{6,7},{7,4},{8,9},{9,10},{10,1... | collective-permute-start | bytes 73736 | tf_op jit(solution)/shard_map/ppermute | solution.py:32
  58.7 1.0 %inner_density.5 = (f32[4,128,128]{2,1,0:T(8,128)S(1)}, bf16[48,1536]{1,0:T(8,128)(2,1)S(1)}, f32[8,1536]{1,0:T(8,128)S(1)}, bf16[48,1536]{1,0:T(8,128)(2,1)S(1)...) custom-call(f32[3,2,2,4,128]{4,3,2,1,0:T(4,128)S(1)} %pad_maximum_fusion.4.mid_ref.all_refs_0_, ...), custom_call_target="tpu_custom_call" | custom-call | flops 58982400 | bytes 4718592 | tf_op jit(solution)/shard_map/inner_density/pallas_call | solution.py:437
  59.7 0.8 %collective-permute-done.23.high_ref = f32[3,2,2,4,128]{4,3,2,1,0:T(4,128)S(1)} collective-permute-done((f32[3,2,2,4,128]{4,3,2,1,0:T(4,128)S(1)}, f32[3,2,2,4,128]{4,3,2,1,0:T(4,128)S(1)}, u32[]{:S(2)}, u32[]{:S(2)}) %collective-permute-start.23) | collective-permute-done | bytes 24608 | tf_op jit(solution)/shard_map/ppermute | solution.py:33
  60.5 1.9 %collective-permute-done.22.low_ref = f32[3,2,2,4,128]{4,3,2,1,0:T(4,128)S(1)} collective-permute-done((f32[3,2,2,4,128]{4,3,2,1,0:T(4,128)S(1)}, f32[3,2,2,4,128]{4,3,2,1,0:T(4,128)S(1)}, u32[]{:S(2)}, u32[]{:S(2)}) %collective-permute-start.22) | collective-permute-done | bytes 24608 | tf_op jit(solution)/shard_map/ppermute | solution.py:32
  62.4 0.1 collective-permute-start.25
  62.5 1.3 %outer_density.5 = (f32[4,128,128]{2,1,0:T(8,128)S(1)}, f32[4,128,128]{2,1,0:T(8,128)S(1)}, bf16[48,1536]{1,0:T(8,128)(2,1)S(1)}, f32[8,1536]{1,0:T(8,128)S(1)}, bf16[4,128,48]{2,1,0:T(8,128)(2,1)S(1)}) custom-call(f32[3,2,2,4,128]{4,3,2,1,0:T(4,128)S(1)} %collective-permute-done.22.low_ref, f32[3,2,2,4,128]{4,3,2,1,0:T(4,128)S(1)} %collective-permute-done.23.high_ref, ...), custom_call_target="tpu_custom_call" | custom-call | flops 88473600 | bytes 7077888 | tf_op jit(solution)/shard_map/outer_density/pallas_call | solution.py:437
  63.8 0.6 last_density.5
  64.5 0.6 collective-permute-start.28
  65.0 1.0 %collective-permute-start.27 = (f32[1,2,4,128]{3,2,1,0:T(4,128)S(1)}, f32[1,2,4,128]{3,2,1,0:T(4,128)S(1)}, u32[]{:S(2)}, u32[]{:S(2)}) collective-permute-start(f32[1,2,4,128]{3,2,1,0:T(4,128)S(1)} %bitcast.60), channel_id=1, source_target_pairs={{8,0},{16,8},{24,16},{0,24},{9,1},{17,9},{25,17},{1,25},{10,2},{18... | collective-permute-start | bytes 12296 | tf_op jit(solution)/shard_map/ppermute | solution.py:33
  66.0 1.0 %collective-permute-start.26 = (f32[1,2,4,128]{3,2,1,0:T(4,128)S(1)}, f32[1,2,4,128]{3,2,1,0:T(4,128)S(1)}, u32[]{:S(2)}, u32[]{:S(2)}) collective-permute-start(f32[1,2,4,128]{3,2,1,0:T(4,128)S(1)} %bitcast.61), channel_id=1, source_target_pairs={{0,8},{8,16},{16,24},{24,0},{1,9},{9,17},{17,25},{25,1},{2,10},{10... | collective-permute-start | bytes 12296 | tf_op jit(solution)/shard_map/ppermute | solution.py:32
  67.1 1.3 %column_force.5 = (f32[4,4,128,128]{3,2,1,0:T(8,128)S(1)}, bf16[4,128,48]{2,1,0:T(8,128)(2,1)S(1)}) custom-call(f32[3,2,2,4,128]{4,3,2,1,0:T(4,128)S(1)} %pad_maximum_fusion.4.mid_ref.all_refs_0_, f32[8,128]{1,0:T(8,128)S(1)} %get-tuple-element.130.all_refs_1_, f32[8,128]{1,0:T(8,128)S(1)} %get-tuple-element.129.all_refs_2_, ...), custom_call_target="tpu_custom_call" | custom-call | flops 29491200 | bytes 2359296 | tf_op jit(solution)/shard_map/column_force/pallas_call | solution.py:437
  68.4 0.2 collective-permute-done.27
  68.6 1.9 %collective-permute-done.26 = f32[1,2,4,128]{3,2,1,0:T(4,128)S(1)} collective-permute-done((f32[1,2,4,128]{3,2,1,0:T(4,128)S(1)}, f32[1,2,4,128]{3,2,1,0:T(4,128)S(1)}, u32[]{:S(2)}, u32[]{:S(2)}) %collective-permute-start.26) | collective-permute-done | bytes 4128 | tf_op jit(solution)/shard_map/ppermute | solution.py:32
  70.5 1.6 %side_force.5.column_ref = f32[4,4,128,128]{3,2,1,0:T(8,128)S(1)} custom-call(f32[8,128]{1,0:T(8,128)S(1)} %bitcast.40, f32[8,128]{1,0:T(8,128)S(1)} %bitcast.37, bf16[48,1536]{1,0:T(8,128)(2,1)S(1)} %get-tuple-element.123.part_ref.all_refs_5_, bf16[48,1536]{1,0:T(8,128)(2,1)S(1)} %get-tuple-element.131.all_refs_6_.edge_ref, ...), custom_call_target="tpu_custom_call" | custom-call | flops 39321600 | bytes 3145728 | tf_op jit(solution)/shard_map/side_force/pallas_call | solution.py:437
  72.2 1.6 %force_last.1 = (f32[3,4,128]{2,1,0:T(4,128)}, f32[3,4,128]{2,1,0:T(4,128)}) custom-call(f32[3,2,2,4,128]{4,3,2,1,0:T(4,128)S(1)} %pad_maximum_fusion.4.mid_ref.all_refs_0_, f32[8,128]{1,0:T(8,128)S(1)} %bitcast.46, f32[8,128]{1,0:T(8,128)S(1)} %bitcast.45, bf16[48,1536]{1,0:T(8,128)(2,1)S(1)} %get-tuple-element.124.ghost_ref.all_refs_7_, ...), custom_call_target="tpu_custom_call" | custom-call | flops 19660800 | bytes 1572864 | tf_op jit(solution)/shard_map/force_last/pallas_call | solution.py:437
  (38 shorter events, 0.2 us)
Async XLA Ops:
  1.5 5.6 %collective-permute-start = (f32[1,2,2,4,128]{4,3,2,1,0:T(4,128)S(1)}, f32[1,2,2,4,128]{4,3,2,1,0:T(4,128)S(1)}, u32[]{:S(2)}, u32[]{:S(2)}) collective-permute-start(f32[1,2,2,4,128]{4,3,2,1,0:T(4,128)S(1)} %get-tuple-element.73), channel_id=1, source_target_pairs={{0,8},{8,16},{16,24},{24,0},{1,9},{9,17},{17,25},{25,1},{2,10},{10... | collective-permute-start | bytes 24584 | tf_op jit(solution)/shard_map/ppermute | solution.py:32
  4.5 3.7 %collective-permute-start.1 = (f32[1,2,2,4,128]{4,3,2,1,0:T(4,128)S(1)}, f32[1,2,2,4,128]{4,3,2,1,0:T(4,128)S(1)}, u32[]{:S(2)}, u32[]{:S(2)}) collective-permute-start(f32[1,2,2,4,128]{4,3,2,1,0:T(4,128)S(1)} %get-tuple-element.73), channel_id=1, source_target_pairs={{8,0},{16,8},{24,16},{0,24},{9,1},{17,9},{25,17},{1,25},{10,2},{18... | collective-permute-start | bytes 24584 | tf_op jit(solution)/shard_map/ppermute | solution.py:33
  8.2 3.6 %collective-permute-start.4 = (f32[3,2,2,4,128]{4,3,2,1,0:T(4,128)S(1)}, f32[3,2,2,4,128]{4,3,2,1,0:T(4,128)S(1)}, u32[]{:S(2)}, u32[]{:S(2)}) collective-permute-start(f32[3,2,2,4,128]{4,3,2,1,0:T(4,128)S(1)} %constant_dynamic-update-slice_fusion.mid_ref.all_refs_0_), channel_id=1, source_target_pairs={{0,4},{4,0},{1,5},{5,1},{2,6},{6,2},{3,7},{7,3},{8,12},{12,8},{9,1... | collective-permute-start | bytes 73736 | tf_op jit(solution)/shard_map/ppermute | solution.py:27
  8.2 5.1 %collective-permute-start.3 = (f32[3,2,2,4,128]{4,3,2,1,0:T(4,128)S(1)}, f32[3,2,2,4,128]{4,3,2,1,0:T(4,128)S(1)}, u32[]{:S(2)}, u32[]{:S(2)}) collective-permute-start(f32[3,2,2,4,128]{4,3,2,1,0:T(4,128)S(1)} %constant_dynamic-update-slice_fusion.mid_ref.all_refs_0_), channel_id=1, source_target_pairs={{1,0},{2,1},{3,2},{0,3},{5,4},{6,5},{7,6},{4,7},{9,8},{10,9},{11,1... | collective-permute-start | bytes 73736 | tf_op jit(solution)/shard_map/ppermute | solution.py:33
  11.8 5.6 %collective-permute-start.2 = (f32[3,2,2,4,128]{4,3,2,1,0:T(4,128)S(1)}, f32[3,2,2,4,128]{4,3,2,1,0:T(4,128)S(1)}, u32[]{:S(2)}, u32[]{:S(2)}) collective-permute-start(f32[3,2,2,4,128]{4,3,2,1,0:T(4,128)S(1)} %constant_dynamic-update-slice_fusion.mid_ref.all_refs_0_), channel_id=1, source_target_pairs={{0,1},{1,2},{2,3},{3,0},{4,5},{5,6},{6,7},{7,4},{8,9},{9,10},{10,1... | collective-permute-start | bytes 73736 | tf_op jit(solution)/shard_map/ppermute | solution.py:32
  17.4 1.4 %collective-permute-start.5 = (f32[3,2,4,4,128]{4,3,2,1,0:T(4,128)S(1)}, f32[3,2,4,4,128]{4,3,2,1,0:T(4,128)S(1)}, u32[]{:S(2)}, u32[]{:S(2)}) collective-permute-start(f32[3,2,4,4,128]{4,3,2,1,0:T(4,128)S(1)} %pad_maximum_fusion), channel_id=1, source_target_pairs={{0,4},{4,0},{1,5},{5,1},{2,6},{6,2},{3,7},{7,3},{8,12},{12,8},{9,1... | collective-permute-start | bytes 147464 | tf_op jit(solution)/shard_map/ppermute | solution.py:27
  19.5 3.0 %collective-permute-start.8 = (f32[1,2,4,128]{3,2,1,0:T(4,128)S(1)}, f32[1,2,4,128]{3,2,1,0:T(4,128)S(1)}, u32[]{:S(2)}, u32[]{:S(2)}) collective-permute-start(f32[1,2,4,128]{3,2,1,0:T(4,128)S(1)} %bitcast.53), channel_id=1, source_target_pairs={{0,4},{4,0},{1,5},{5,1},{2,6},{6,2},{3,7},{7,3},{8,12},{12,8},{9,1... | collective-permute-start | bytes 12296 | tf_op jit(solution)/shard_map/ppermute | solution.py:27
  20.0 4.0 %collective-permute-start.7 = (f32[1,2,4,128]{3,2,1,0:T(4,128)S(1)}, f32[1,2,4,128]{3,2,1,0:T(4,128)S(1)}, u32[]{:S(2)}, u32[]{:S(2)}) collective-permute-start(f32[1,2,4,128]{3,2,1,0:T(4,128)S(1)} %bitcast.54), channel_id=1, source_target_pairs={{8,0},{16,8},{24,16},{0,24},{9,1},{17,9},{25,17},{1,25},{10,2},{18... | collective-permute-start | bytes 12296 | tf_op jit(solution)/shard_map/ppermute | solution.py:33
  22.3 4.5 %collective-permute-start.6 = (f32[1,2,4,128]{3,2,1,0:T(4,128)S(1)}, f32[1,2,4,128]{3,2,1,0:T(4,128)S(1)}, u32[]{:S(2)}, u32[]{:S(2)}) collective-permute-start(f32[1,2,4,128]{3,2,1,0:T(4,128)S(1)} %bitcast.55), channel_id=1, source_target_pairs={{0,8},{8,16},{16,24},{24,0},{1,9},{9,17},{17,25},{25,1},{2,10},{10... | collective-permute-start | bytes 12296 | tf_op jit(solution)/shard_map/ppermute | solution.py:32
  26.9 1.6 %collective-permute-start.9 = (f32[2,2,4,128]{3,2,1,0:T(4,128)S(1)}, f32[2,2,4,128]{3,2,1,0:T(4,128)S(1)}, u32[]{:S(2)}, u32[]{:S(2)}) collective-permute-start(f32[2,2,4,128]{3,2,1,0:T(4,128)S(1)} %pad_maximum_fusion.5), channel_id=1, source_target_pairs={{0,4},{4,0},{1,5},{5,1},{2,6},{6,2},{3,7},{7,3},{8,12},{12,8},{9,1... | collective-permute-start | bytes 24584 | tf_op jit(solution)/shard_map/ppermute | solution.py:27
  29.5 3.7 %collective-permute-start.11 = (f32[1,2,2,4,128]{4,3,2,1,0:T(4,128)S(1)}, f32[1,2,2,4,128]{4,3,2,1,0:T(4,128)S(1)}, u32[]{:S(2)}, u32[]{:S(2)}) collective-permute-start(f32[1,2,2,4,128]{4,3,2,1,0:T(4,128)S(1)} %bitcast.47), channel_id=1, source_target_pairs={{8,0},{16,8},{24,16},{0,24},{9,1},{17,9},{25,17},{1,25},{10,2},{18... | collective-permute-start | bytes 24584 | tf_op jit(solution)/shard_map/ppermute | solution.py:33
  29.7 4.6 %collective-permute-start.10 = (f32[1,2,2,4,128]{4,3,2,1,0:T(4,128)S(1)}, f32[1,2,2,4,128]{4,3,2,1,0:T(4,128)S(1)}, u32[]{:S(2)}, u32[]{:S(2)}) collective-permute-start(f32[1,2,2,4,128]{4,3,2,1,0:T(4,128)S(1)} %bitcast.48), channel_id=1, source_target_pairs={{0,8},{8,16},{16,24},{24,0},{1,9},{9,17},{17,25},{25,1},{2,10},{10... | collective-permute-start | bytes 24584 | tf_op jit(solution)/shard_map/ppermute | solution.py:32
  34.3 2.2 %collective-permute-start.14 = (f32[3,2,2,4,128]{4,3,2,1,0:T(4,128)S(1)}, f32[3,2,2,4,128]{4,3,2,1,0:T(4,128)S(1)}, u32[]{:S(2)}, u32[]{:S(2)}) collective-permute-start(f32[3,2,2,4,128]{4,3,2,1,0:T(4,128)S(1)} %pad_maximum_fusion.3.mid_ref.all_refs_0_), channel_id=1, source_target_pairs={{0,4},{4,0},{1,5},{5,1},{2,6},{6,2},{3,7},{7,3},{8,12},{12,8},{9,1... | collective-permute-start | bytes 73736 | tf_op jit(solution)/shard_map/ppermute | solution.py:27
  34.4 3.9 %collective-permute-start.13 = (f32[3,2,2,4,128]{4,3,2,1,0:T(4,128)S(1)}, f32[3,2,2,4,128]{4,3,2,1,0:T(4,128)S(1)}, u32[]{:S(2)}, u32[]{:S(2)}) collective-permute-start(f32[3,2,2,4,128]{4,3,2,1,0:T(4,128)S(1)} %pad_maximum_fusion.3.mid_ref.all_refs_0_), channel_id=1, source_target_pairs={{1,0},{2,1},{3,2},{0,3},{5,4},{6,5},{7,6},{4,7},{9,8},{10,9},{11,1... | collective-permute-start | bytes 73736 | tf_op jit(solution)/shard_map/ppermute | solution.py:33
  34.5 5.6 %collective-permute-start.12 = (f32[3,2,2,4,128]{4,3,2,1,0:T(4,128)S(1)}, f32[3,2,2,4,128]{4,3,2,1,0:T(4,128)S(1)}, u32[]{:S(2)}, u32[]{:S(2)}) collective-permute-start(f32[3,2,2,4,128]{4,3,2,1,0:T(4,128)S(1)} %pad_maximum_fusion.3.mid_ref.all_refs_0_), channel_id=1, source_target_pairs={{0,1},{1,2},{2,3},{3,0},{4,5},{5,6},{6,7},{7,4},{8,9},{9,10},{10,1... | collective-permute-start | bytes 73736 | tf_op jit(solution)/shard_map/ppermute | solution.py:32
  40.1 1.4 %collective-permute-start.15 = (f32[3,2,4,4,128]{4,3,2,1,0:T(4,128)S(1)}, f32[3,2,4,4,128]{4,3,2,1,0:T(4,128)S(1)}, u32[]{:S(2)}, u32[]{:S(2)}) collective-permute-start(f32[3,2,4,4,128]{4,3,2,1,0:T(4,128)S(1)} %pad_maximum_fusion.1), channel_id=1, source_target_pairs={{0,4},{4,0},{1,5},{5,1},{2,6},{6,2},{3,7},{7,3},{8,12},{12,8},{9,1... | collective-permute-start | bytes 147464 | tf_op jit(solution)/shard_map/ppermute | solution.py:27
  42.2 2.6 %collective-permute-start.18 = (f32[1,2,4,128]{3,2,1,0:T(4,128)S(1)}, f32[1,2,4,128]{3,2,1,0:T(4,128)S(1)}, u32[]{:S(2)}, u32[]{:S(2)}) collective-permute-start(f32[1,2,4,128]{3,2,1,0:T(4,128)S(1)} %bitcast.56), channel_id=1, source_target_pairs={{0,4},{4,0},{1,5},{5,1},{2,6},{6,2},{3,7},{7,3},{8,12},{12,8},{9,1... | collective-permute-start | bytes 12296 | tf_op jit(solution)/shard_map/ppermute | solution.py:27
  42.8 3.6 %collective-permute-start.17 = (f32[1,2,4,128]{3,2,1,0:T(4,128)S(1)}, f32[1,2,4,128]{3,2,1,0:T(4,128)S(1)}, u32[]{:S(2)}, u32[]{:S(2)}) collective-permute-start(f32[1,2,4,128]{3,2,1,0:T(4,128)S(1)} %bitcast.57), channel_id=1, source_target_pairs={{8,0},{16,8},{24,16},{0,24},{9,1},{17,9},{25,17},{1,25},{10,2},{18... | collective-permute-start | bytes 12296 | tf_op jit(solution)/shard_map/ppermute | solution.py:33
  44.7 4.5 %collective-permute-start.16 = (f32[1,2,4,128]{3,2,1,0:T(4,128)S(1)}, f32[1,2,4,128]{3,2,1,0:T(4,128)S(1)}, u32[]{:S(2)}, u32[]{:S(2)}) collective-permute-start(f32[1,2,4,128]{3,2,1,0:T(4,128)S(1)} %bitcast.58), channel_id=1, source_target_pairs={{0,8},{8,16},{16,24},{24,0},{1,9},{9,17},{17,25},{25,1},{2,10},{10... | collective-permute-start | bytes 12296 | tf_op jit(solution)/shard_map/ppermute | solution.py:32
  49.2 1.6 %collective-permute-start.19 = (f32[2,2,4,128]{3,2,1,0:T(4,128)S(1)}, f32[2,2,4,128]{3,2,1,0:T(4,128)S(1)}, u32[]{:S(2)}, u32[]{:S(2)}) collective-permute-start(f32[2,2,4,128]{3,2,1,0:T(4,128)S(1)} %pad_maximum_fusion.6), channel_id=1, source_target_pairs={{0,4},{4,0},{1,5},{5,1},{2,6},{6,2},{3,7},{7,3},{8,12},{12,8},{9,1... | collective-permute-start | bytes 24584 | tf_op jit(solution)/shard_map/ppermute | solution.py:27
  51.9 3.7 %collective-permute-start.21 = (f32[1,2,2,4,128]{4,3,2,1,0:T(4,128)S(1)}, f32[1,2,2,4,128]{4,3,2,1,0:T(4,128)S(1)}, u32[]{:S(2)}, u32[]{:S(2)}) collective-permute-start(f32[1,2,2,4,128]{4,3,2,1,0:T(4,128)S(1)} %bitcast.50), channel_id=1, source_target_pairs={{8,0},{16,8},{24,16},{0,24},{9,1},{17,9},{25,17},{1,25},{10,2},{18... | collective-permute-start | bytes 24584 | tf_op jit(solution)/shard_map/ppermute | solution.py:33
  52.0 4.5 %collective-permute-start.20 = (f32[1,2,2,4,128]{4,3,2,1,0:T(4,128)S(1)}, f32[1,2,2,4,128]{4,3,2,1,0:T(4,128)S(1)}, u32[]{:S(2)}, u32[]{:S(2)}) collective-permute-start(f32[1,2,2,4,128]{4,3,2,1,0:T(4,128)S(1)} %bitcast.51), channel_id=1, source_target_pairs={{0,8},{8,16},{16,24},{24,0},{1,9},{9,17},{17,25},{25,1},{2,10},{10... | collective-permute-start | bytes 24584 | tf_op jit(solution)/shard_map/ppermute | solution.py:32
  56.5 2.2 %collective-permute-start.24 = (f32[3,2,2,4,128]{4,3,2,1,0:T(4,128)S(1)}, f32[3,2,2,4,128]{4,3,2,1,0:T(4,128)S(1)}, u32[]{:S(2)}, u32[]{:S(2)}) collective-permute-start(f32[3,2,2,4,128]{4,3,2,1,0:T(4,128)S(1)} %pad_maximum_fusion.4.mid_ref.all_refs_0_), channel_id=1, source_target_pairs={{0,4},{4,0},{1,5},{5,1},{2,6},{6,2},{3,7},{7,3},{8,12},{12,8},{9,1... | collective-permute-start | bytes 73736 | tf_op jit(solution)/shard_map/ppermute | solution.py:27
  56.6 3.9 %collective-permute-start.23 = (f32[3,2,2,4,128]{4,3,2,1,0:T(4,128)S(1)}, f32[3,2,2,4,128]{4,3,2,1,0:T(4,128)S(1)}, u32[]{:S(2)}, u32[]{:S(2)}) collective-permute-start(f32[3,2,2,4,128]{4,3,2,1,0:T(4,128)S(1)} %pad_maximum_fusion.4.mid_ref.all_refs_0_), channel_id=1, source_target_pairs={{1,0},{2,1},{3,2},{0,3},{5,4},{6,5},{7,6},{4,7},{9,8},{10,9},{11,1... | collective-permute-start | bytes 73736 | tf_op jit(solution)/shard_map/ppermute | solution.py:33
  56.8 5.6 %collective-permute-start.22 = (f32[3,2,2,4,128]{4,3,2,1,0:T(4,128)S(1)}, f32[3,2,2,4,128]{4,3,2,1,0:T(4,128)S(1)}, u32[]{:S(2)}, u32[]{:S(2)}) collective-permute-start(f32[3,2,2,4,128]{4,3,2,1,0:T(4,128)S(1)} %pad_maximum_fusion.4.mid_ref.all_refs_0_), channel_id=1, source_target_pairs={{0,1},{1,2},{2,3},{3,0},{4,5},{5,6},{6,7},{7,4},{8,9},{9,10},{10,1... | collective-permute-start | bytes 73736 | tf_op jit(solution)/shard_map/ppermute | solution.py:32
  62.4 1.4 %collective-permute-start.25 = (f32[3,2,4,4,128]{4,3,2,1,0:T(4,128)S(1)}, f32[3,2,4,4,128]{4,3,2,1,0:T(4,128)S(1)}, u32[]{:S(2)}, u32[]{:S(2)}) collective-permute-start(f32[3,2,4,4,128]{4,3,2,1,0:T(4,128)S(1)} %pad_maximum_fusion.2), channel_id=1, source_target_pairs={{0,4},{4,0},{1,5},{5,1},{2,6},{6,2},{3,7},{7,3},{8,12},{12,8},{9,1... | collective-permute-start | bytes 147464 | tf_op jit(solution)/shard_map/ppermute | solution.py:27
  64.5 2.6 %collective-permute-start.28 = (f32[1,2,4,128]{3,2,1,0:T(4,128)S(1)}, f32[1,2,4,128]{3,2,1,0:T(4,128)S(1)}, u32[]{:S(2)}, u32[]{:S(2)}) collective-permute-start(f32[1,2,4,128]{3,2,1,0:T(4,128)S(1)} %bitcast.59), channel_id=1, source_target_pairs={{0,4},{4,0},{1,5},{5,1},{2,6},{6,2},{3,7},{7,3},{8,12},{12,8},{9,1... | collective-permute-start | bytes 12296 | tf_op jit(solution)/shard_map/ppermute | solution.py:27
  65.0 3.6 %collective-permute-start.27 = (f32[1,2,4,128]{3,2,1,0:T(4,128)S(1)}, f32[1,2,4,128]{3,2,1,0:T(4,128)S(1)}, u32[]{:S(2)}, u32[]{:S(2)}) collective-permute-start(f32[1,2,4,128]{3,2,1,0:T(4,128)S(1)} %bitcast.60), channel_id=1, source_target_pairs={{8,0},{16,8},{24,16},{0,24},{9,1},{17,9},{25,17},{1,25},{10,2},{18... | collective-permute-start | bytes 12296 | tf_op jit(solution)/shard_map/ppermute | solution.py:33
  66.0 4.5 %collective-permute-start.26 = (f32[1,2,4,128]{3,2,1,0:T(4,128)S(1)}, f32[1,2,4,128]{3,2,1,0:T(4,128)S(1)}, u32[]{:S(2)}, u32[]{:S(2)}) collective-permute-start(f32[1,2,4,128]{3,2,1,0:T(4,128)S(1)} %bitcast.61), channel_id=1, source_target_pairs={{0,8},{8,16},{16,24},{24,0},{1,9},{9,17},{17,25},{25,1},{2,10},{10... | collective-permute-start | bytes 12296 | tf_op jit(solution)/shard_map/ppermute | solution.py:32
  70.5 1.6 %collective-permute-start.29 = (f32[2,2,4,128]{3,2,1,0:T(4,128)S(1)}, f32[2,2,4,128]{3,2,1,0:T(4,128)S(1)}, u32[]{:S(2)}, u32[]{:S(2)}) collective-permute-start(f32[2,2,4,128]{3,2,1,0:T(4,128)S(1)} %pad_maximum_fusion.7), channel_id=1, source_target_pairs={{0,4},{4,0},{1,5},{5,1},{2,6},{6,2},{3,7},{7,3},{8,12},{12,8},{9,1... | collective-permute-start | bytes 24584 | tf_op jit(solution)/shard_map/ppermute | solution.py:27

commit v3 on v2

--- a/solution.py
+++ b/solution.py
@@ -6,6 +6,7 @@
 from jax.experimental import pallas as pl
 from jax.experimental.pallas import tpu as pltpu
 from jax.sharding import PartitionSpec as P
+
 
 time_step = 0.05
 half_kick = 0.5 * time_step
@@ -155,8 +156,8 @@
     return jnp.sum(jnp.transpose(total), axis=0, keepdims=True)
 
 
-def add_density(grid, left_ref, place, runs, refs, before, after):
-    rows = 64
+def add_density(left_ref, place, runs, refs, before, after):
+    rows = 128
     for start in range(0, LANES, rows):
         chunk = slice(start, start + rows)
         total = before(chunk)
@@ -226,7 +227,7 @@
     for place, (a, b, c) in enumerate(grid.own_targets()):
         left_ref[place] = target_block(grid.target(mid_ref[a, b - 1, c - 2], a, b, c))
         runs = grid.sources((a, b, c), ("own", "gown"))
-        add_density(grid, left_ref, place, runs, refs, nothing, store_to(sum_ref, place))
+        add_density(left_ref, place, runs, refs, nothing, store_to(sum_ref, place))
 
 
 def outer_density_kernel(own, low_ref, high_ref, inner_ref, part_ref, ghost_ref, left_ref, own_sum_ref, edge_sum_ref, edge_ref, edge_point_ref, edge_left_ref, far_ref):
@@ -243,11 +244,11 @@
     for place, cell in enumerate(grid.edge_targets()):
         edge_left_ref[place] = target_block(grid.target(tile_of(*cell), *cell))
         runs = grid.sources(cell, ("own", "gown", "edge", "far"))
-        add_density(grid, edge_left_ref, place, runs, refs, nothing, store_to(edge_sum_ref, place))
+        add_density(edge_left_ref, place, runs, refs, nothing, store_to(edge_sum_ref, place))
     for place, cell in enumerate(grid.own_targets()):
         runs = grid.sources(cell, ("edge",))
         before = lambda chunk, place=place: inner_ref[place, chunk, :]
-        add_density(grid, left_ref, place, runs, refs, before, store_to(own_sum_ref, place))
+        add_density(left_ref, place, runs, refs, before, store_to(own_sum_ref, place))
 
 
 def last_density_kernel(own, mid_ref, low_ref, high_ref, below_ref, above_ref, own_sum_ref, edge_sum_ref, left_ref, edge_left_ref, slope_ref, weight_ref, ghost_ref, ghost_point_ref, far_ref):
@@ -269,7 +270,7 @@
             runs = grid.sources((a, b, c), ("gedge", "gfar"))
             parts = []
             before = lambda chunk, place=place, sum_ref=sum_ref: sum_ref[place, chunk, :]
-            add_density(grid, rows_ref, place, runs, refs, before, lambda chunk, total: parts.append(total))
+            add_density(rows_ref, place, runs, refs, before, lambda chunk, total: parts.append(total))
             density = across(jnp.concatenate(parts, axis=0))
             scale = tile[3:4]
             slope = jnp.where(scale > 0.5, -0.5, 0.0) / jnp.sqrt(density + 1.0)
@@ -290,7 +291,7 @@
 
 
 def add_force(left_ref, place, runs, refs, point_refs, pair_refs, before, after):
-    rows = 32
+    rows = 128
     for start in range(0, LANES, rows):
         chunk = slice(start, start + rows)
         total = before(chunk)
@@ -433,7 +434,7 @@
     def lefts(count):
         return jax.ShapeDtypeStruct((count, slots, 48), jnp.bfloat16)
 
-    def call(kernel, name, operands, out_shape, pairs, scratch=()):
+    def call(kernel, operands, out_shape, pairs, scratch=()):
         return pl.pallas_call(
             kernel,
             out_shape=out_shape,
@@ -444,7 +445,6 @@
             cost_estimate=pl.CostEstimate(
                 flops=pairs * slots * slots * 50, bytes_accessed=pairs * slots * slots * 4, transcendentals=0
             ),
-            name=name,
         )(*operands)
 
     def evaluate(location, velocity, stage):
@@ -453,7 +453,6 @@
         low, high = neighbours(mid, "gz", 2, 2)
         inner, part, point, ghost, ghost_point, left = call(
             functools.partial(inner_density_kernel, own),
-            "inner_density",
             [mid, mid_below, mid_above],
             [sums(cells), block("own"), points("own"), block("gown"), points("gown"), lefts(cells)],
             cells * 18,
@@ -462,7 +461,6 @@
         below, above = neighbours(tall, "gy", 1, 1)
         own_sum, edge_sum, edge, edge_point, edge_left = call(
             functools.partial(outer_density_kernel, own),
-            "outer_density",
             [low, high, inner, part, ghost, left],
             [sums(cells), sums(cx * cy * 2), block("edge"), points("edge"), lefts(cx * cy * 2)],
             cells * 27,
@@ -470,18 +468,16 @@
         )
         slopes, weights, ghost_edge, ghost_edge_point = call(
             functools.partial(last_density_kernel, own),
-            "last_density",
             [mid, low, high, below, above, own_sum, edge_sum, left, edge_left],
             [rows(cx * cy * near), rows(cx * cy * near), block("gedge"), points("gedge")],
             cells * 9,
             [block("gedge")],
         )
         weights = weights.reshape(cx, cy, near, slots)
+        side_below, side_above = neighbours(weights, "gx", 0, 1)
         weight_below, weight_above = neighbours(weights, "gy", 1, 1)
-        side_below, side_above = neighbours(weights, "gx", 0, 1)
         column, left = call(
             functools.partial(column_force_kernel, own),
-            "column_force",
             [
                 mid,
                 slopes,
@@ -499,7 +495,6 @@
         corner_below, corner_above = neighbours(sides, "gy", 1, 1)
         (column,) = call(
             functools.partial(side_force_kernel, own),
-            "side_force",
             [
                 side_below.reshape(cy * near, slots),
                 side_above.reshape(cy * near, slots),
@@ -512,7 +507,6 @@
         moved = flat_shape if stage == "last" else jax.ShapeDtypeStruct((cells, 4, slots), jnp.float32)
         return call(
             functools.partial(last_force_kernel, own, stage),
-            "force_" + stage,
             [
                 mid,
                 corner_below.reshape(2 * near, slots),
@@ -534,9 +528,10 @@
         compiler_params=pltpu.CompilerParams(vmem_limit_bytes=GRANT),
         name="prepare",
     )(*arrays)
-    velocity, moved = evaluate(location, velocity, "first")
-    velocity, moved = evaluate(moved.reshape(location.shape), velocity, "middle")
-    velocity, new_positions = evaluate(moved.reshape(location.shape), velocity, "last")
+    for stage in ("first", "middle", "last"):
+        velocity, moved = evaluate(location.reshape(cx, cy, cz, 4, slots), velocity, stage)
+        location = moved
+    new_positions = moved
     return new_positions.reshape(positions.shape), velocity.reshape(positions.shape)
 
 

time: 74 us -> 73.9 us (level)
  no operation moved by 1% of the time
where the time goes in v3:
time: 73.9 us; the launch traced here: 73.7 us
  waiting for transfers between devices  26.4 us (36%)
  starting transfers between devices  24.4 us (33%)
  Pallas kernels  21.8 us (29%)
  between operations  0.94 us (1%)
    pallas_call x18, Pallas kernels, call(): pl.pallas_call(kernel, out_shape=out_shape, in_specs=[vmem] * len(operand...  21 us
    ppermute x9, waiting for transfers between devices, neighbours(): lax.ppermute(tail, axis, [(i, (i + 1) % count) for i in range(count)])  19 us
    ppermute x9, starting transfers between devices, neighbours(): lax.ppermute(tail, axis, [(i, (i + 1) % count) for i in range(count)])  12 us
    ppermute x9, starting transfers between devices, neighbours(): lax.ppermute(head, axis, [((i + 1) % count, i) for i in range(count)])  10.4 us
    ppermute x9, waiting for transfers between devices, neighbours(): lax.ppermute(head, axis, [((i + 1) % count, i) for i in range(count)])  7.3 us
    ppermute x12, starting transfers between devices, neighbours(): other = lax.ppermute(cells, axis, [(0, 1), (1, 0)])  2.03 us
  transfers between devices with their start and end apart: 30, of which 18 were waited for; matrix products, arithmetic and copies ran while one was open for 0% of the time, Pallas kernels for 21%

profile of v3, /device:TPU:0, one launch (start us, length us, event | category | flops | bytes accessed | tf_op | source)
XLA Modules:
  0.0 73.7 jit_solution(14202514861175826417)
XLA Ops:
  0.6 0.8 %prepare.1 = (f32[1,2,2,4,128]{4,3,2,1,0:T(4,128)S(1)}, f32[3,4,128]{2,1,0:T(4,128)S(1)}) custom-call(f32[3,1,2,2,128]{4,3,2,1,0:T(2,128)} %pos_hbm.1, f32[3,1,2,2,128]{4,3,2,1,0:T(2,128)} %vel_hbm.1, s32[1,2,2,128]{3,2,1,0:T(2,128)} %species_hbm.1, s32[1,2,2]{2,1,0:T(2,128)} %counts_hbm.1), custom_call_target="tpu_custom_call" | custom-call | tf_op jit(solution)/shard_map/prepare/pallas_call | solution.py:522
  1.5 3.0 %collective-permute-start = (f32[1,2,2,4,128]{4,3,2,1,0:T(4,128)S(1)}, f32[1,2,2,4,128]{4,3,2,1,0:T(4,128)S(1)}, u32[]{:S(2)}, u32[]{:S(2)}) collective-permute-start(f32[1,2,2,4,128]{4,3,2,1,0:T(4,128)S(1)} %get-tuple-element.73), channel_id=1, source_target_pairs={{0,8},{8,16},{16,24},{24,0},{1,9},{9,17},{17,25},{25,1},{2,10},{10... | collective-permute-start | bytes 24584 | tf_op jit(solution)/shard_map/ppermute | solution.py:33
  4.5 1.0 %collective-permute-start.1 = (f32[1,2,2,4,128]{4,3,2,1,0:T(4,128)S(1)}, f32[1,2,2,4,128]{4,3,2,1,0:T(4,128)S(1)}, u32[]{:S(2)}, u32[]{:S(2)}) collective-permute-start(f32[1,2,2,4,128]{4,3,2,1,0:T(4,128)S(1)} %get-tuple-element.73), channel_id=1, source_target_pairs={{8,0},{16,8},{24,16},{0,24},{9,1},{17,9},{25,17},{1,25},{10,2},{18... | collective-permute-start | bytes 24584 | tf_op jit(solution)/shard_map/ppermute | solution.py:34
  5.5 1.6 %collective-permute-done = f32[1,2,2,4,128]{4,3,2,1,0:T(4,128)S(1)} collective-permute-done((f32[1,2,2,4,128]{4,3,2,1,0:T(4,128)S(1)}, f32[1,2,2,4,128]{4,3,2,1,0:T(4,128)S(1)}, u32[]{:S(2)}, u32[]{:S(2)}) %collective-permute-start) | collective-permute-done | bytes 8224 | tf_op jit(solution)/shard_map/ppermute | solution.py:33
  7.1 1.1 %collective-permute-done.1 = f32[1,2,2,4,128]{4,3,2,1,0:T(4,128)S(1)} collective-permute-done((f32[1,2,2,4,128]{4,3,2,1,0:T(4,128)S(1)}, f32[1,2,2,4,128]{4,3,2,1,0:T(4,128)S(1)}, u32[]{:S(2)}, u32[]{:S(2)}) %collective-permute-start.1) | collective-permute-done | bytes 8224 | tf_op jit(solution)/shard_map/ppermute | solution.py:34
  8.2 3.6 %collective-permute-start.3 = (f32[3,2,2,4,128]{4,3,2,1,0:T(4,128)S(1)}, f32[3,2,2,4,128]{4,3,2,1,0:T(4,128)S(1)}, u32[]{:S(2)}, u32[]{:S(2)}) collective-permute-start(f32[3,2,2,4,128]{4,3,2,1,0:T(4,128)S(1)} %constant_dynamic-update-slice_fusion.mid_ref.all_refs_0_), channel_id=1, source_target_pairs={{1,0},{2,1},{3,2},{0,3},{5,4},{6,5},{7,6},{4,7},{9,8},{10,9},{11,1... | collective-permute-start | bytes 73736 | tf_op jit(solution)/shard_map/ppermute | solution.py:34
  11.8 1.0 %shard_map.59 = (f32[4,128,128]{2,1,0:T(8,128)S(1)}, bf16[48,1536]{1,0:T(8,128)(2,1)S(1)}, f32[8,1536]{1,0:T(8,128)S(1)}, bf16[48,1536]{1,0:T(8,128)(2,1)S(1)}, ...) custom-call(f32[3,2,2,4,128]{4,3,2,1,0:T(4,128)S(1)} %constant_dynamic-update-slice_fusion.mid_ref.all_refs_0_, ...), custom_call_target="tpu_custom_call" | custom-call | flops 58982400 | bytes 4718592 | tf_op jit(solution)/shard_map/pallas_call | solution.py:438
  12.8 0.5 collective-permute-done.3.high_ref
  13.3 4.1 %collective-permute-done.2.low_ref = f32[3,2,2,4,128]{4,3,2,1,0:T(4,128)S(1)} collective-permute-done((f32[3,2,2,4,128]{4,3,2,1,0:T(4,128)S(1)}, f32[3,2,2,4,128]{4,3,2,1,0:T(4,128)S(1)}, u32[]{:S(2)}, u32[]{:S(2)}) %collective-permute-start.2) | collective-permute-done | bytes 24608 | tf_op jit(solution)/shard_map/ppermute | solution.py:33
  17.4 0.1 collective-permute-start.5
  17.5 1.3 %shard_map.60 = (f32[4,128,128]{2,1,0:T(8,128)S(1)}, f32[4,128,128]{2,1,0:T(8,128)S(1)}, bf16[48,1536]{1,0:T(8,128)(2,1)S(1)}, f32[8,1536]{1,0:T(8,128)S(1)}, bf16[4,128,48]{2,1,0:T(8,128)(2,1)S(1)}) custom-call(f32[3,2,2,4,128]{4,3,2,1,0:T(4,128)S(1)} %collective-permute-done.2.low_ref, f32[3,2,2,4,128]{4,3,2,1,0:T(4,128)S(1)} %collective-permute-done.3.high_ref, ...), custom_call_target="tpu_custom_call" | custom-call | flops 88473600 | bytes 7077888 | tf_op jit(solution)/shard_map/pallas_call | solution.py:438
  18.8 0.0 collective-permute-done.5
  18.8 0.6 shard_map.61
  19.5 0.6 collective-permute-start.8
  20.0 2.3 %collective-permute-start.7 = (f32[1,2,4,128]{3,2,1,0:T(4,128)S(1)}, f32[1,2,4,128]{3,2,1,0:T(4,128)S(1)}, u32[]{:S(2)}, u32[]{:S(2)}) collective-permute-start(f32[1,2,4,128]{3,2,1,0:T(4,128)S(1)} %bitcast.54), channel_id=1, source_target_pairs={{8,0},{16,8},{24,16},{0,24},{9,1},{17,9},{25,17},{1,25},{10,2},{18... | collective-permute-start | bytes 12296 | tf_op jit(solution)/shard_map/ppermute | solution.py:34
  22.4 0.1 collective-permute-start.6
  22.4 1.3 %shard_map.62 = (f32[4,4,128,128]{3,2,1,0:T(8,128)S(1)}, bf16[4,128,48]{2,1,0:T(8,128)(2,1)S(1)}) custom-call(f32[3,2,2,4,128]{4,3,2,1,0:T(4,128)S(1)} %constant_dynamic-update-slice_fusion.mid_ref.all_refs_0_, f32[8,128]{1,0:T(8,128)S(1)} %get-tuple-element.84.all_refs_1_, f32[8,128]{1,0:T(8,128)S(1)} %get-tuple-element.83.all_refs_2_, ...), custom_call_target="tpu_custom_call" | custom-call | flops 29491200 | bytes 2359296 | tf_op jit(solution)/shard_map/pallas_call | solution.py:438
  23.7 0.3 collective-permute-done.7
  24.0 2.9 %collective-permute-done.6 = f32[1,2,4,128]{3,2,1,0:T(4,128)S(1)} collective-permute-done((f32[1,2,4,128]{3,2,1,0:T(4,128)S(1)}, f32[1,2,4,128]{3,2,1,0:T(4,128)S(1)}, u32[]{:S(2)}, u32[]{:S(2)}) %collective-permute-start.6) | collective-permute-done | bytes 4128 | tf_op jit(solution)/shard_map/ppermute | solution.py:33
  26.9 0.0 collective-permute-start.9
  26.9 1.6 %shard_map.63.column_ref = f32[4,4,128,128]{3,2,1,0:T(8,128)S(1)} custom-call(f32[8,128]{1,0:T(8,128)S(1)} %bitcast.38, f32[8,128]{1,0:T(8,128)S(1)} %bitcast.35, bf16[48,1536]{1,0:T(8,128)(2,1)S(1)} %get-tuple-element.77.part_ref.all_refs_5_, bf16[48,1536]{1,0:T(8,128)(2,1)S(1)} %get-tuple-element.85.all_refs_6_.edge_ref, ...), custom_call_target="tpu_custom_call" | custom-call | flops 39321600 | bytes 3145728 | tf_op jit(solution)/shard_map/pallas_call | solution.py:438
  28.5 1.0 %shard_map.64 = (f32[3,4,128]{2,1,0:T(4,128)S(1)}, f32[4,4,128]{2,1,0:T(4,128)S(1)}) custom-call(f32[3,2,2,4,128]{4,3,2,1,0:T(4,128)S(1)} %constant_dynamic-update-slice_fusion.mid_ref.all_refs_0_, f32[8,128]{1,0:T(8,128)S(1)} %bitcast.42, f32[8,128]{1,0:T(8,128)S(1)} %bitcast.41, bf16[48,1536]{1,0:T(8,128)(2,1)S(1)} %get-tuple-element.78.ghost_ref.all_refs_7_, ...), custom_call_target="tpu_custom_call" | custom-call | flops 19660800 | bytes 1572864 | tf_op jit(solution)/shard_map/pallas_call | solution.py:438
  29.5 0.1 collective-permute-start.11
  29.6 1.9 %collective-permute-start.10 = (f32[1,2,2,4,128]{4,3,2,1,0:T(4,128)S(1)}, f32[1,2,2,4,128]{4,3,2,1,0:T(4,128)S(1)}, u32[]{:S(2)}, u32[]{:S(2)}) collective-permute-start(f32[1,2,2,4,128]{4,3,2,1,0:T(4,128)S(1)} %bitcast.48), channel_id=1, source_target_pairs={{0,8},{8,16},{16,24},{24,0},{1,9},{9,17},{17,25},{25,1},{2,10},{10... | collective-permute-start | bytes 24584 | tf_op jit(solution)/shard_map/ppermute | solution.py:33
  31.6 1.6 %collective-permute-done.11 = f32[1,2,2,4,128]{4,3,2,1,0:T(4,128)S(1)} collective-permute-done((f32[1,2,2,4,128]{4,3,2,1,0:T(4,128)S(1)}, f32[1,2,2,4,128]{4,3,2,1,0:T(4,128)S(1)}, u32[]{:S(2)}, u32[]{:S(2)}) %collective-permute-start.11) | collective-permute-done | bytes 8224 | tf_op jit(solution)/shard_map/ppermute | solution.py:34
  33.2 1.0 %collective-permute-done.10 = f32[1,2,2,4,128]{4,3,2,1,0:T(4,128)S(1)} collective-permute-done((f32[1,2,2,4,128]{4,3,2,1,0:T(4,128)S(1)}, f32[1,2,2,4,128]{4,3,2,1,0:T(4,128)S(1)}, u32[]{:S(2)}, u32[]{:S(2)}) %collective-permute-start.10) | collective-permute-done | bytes 8224 | tf_op jit(solution)/shard_map/ppermute | solution.py:33
  34.2 0.1 collective-permute-start.14
  34.3 0.1 collective-permute-start.13
  34.4 2.0 %collective-permute-start.12 = (f32[3,2,2,4,128]{4,3,2,1,0:T(4,128)S(1)}, f32[3,2,2,4,128]{4,3,2,1,0:T(4,128)S(1)}, u32[]{:S(2)}, u32[]{:S(2)}) collective-permute-start(f32[3,2,2,4,128]{4,3,2,1,0:T(4,128)S(1)} %pad_maximum_fusion.3.mid_ref.all_refs_0_), channel_id=1, source_target_pairs={{0,1},{1,2},{2,3},{3,0},{4,5},{5,6},{6,7},{7,4},{8,9},{9,10},{10,1... | collective-permute-start | bytes 73736 | tf_op jit(solution)/shard_map/ppermute | solution.py:33
  36.4 1.0 %shard_map.65 = (f32[4,128,128]{2,1,0:T(8,128)S(1)}, bf16[48,1536]{1,0:T(8,128)(2,1)S(1)}, f32[8,1536]{1,0:T(8,128)S(1)}, bf16[48,1536]{1,0:T(8,128)(2,1)S(1)}, ...) custom-call(f32[3,2,2,4,128]{4,3,2,1,0:T(4,128)S(1)} %pad_maximum_fusion.3.mid_ref.all_refs_0_, ...), custom_call_target="tpu_custom_call" | custom-call | flops 58982400 | bytes 4718592 | tf_op jit(solution)/shard_map/pallas_call | solution.py:438
  37.4 0.8 %collective-permute-done.13.high_ref = f32[3,2,2,4,128]{4,3,2,1,0:T(4,128)S(1)} collective-permute-done((f32[3,2,2,4,128]{4,3,2,1,0:T(4,128)S(1)}, f32[3,2,2,4,128]{4,3,2,1,0:T(4,128)S(1)}, u32[]{:S(2)}, u32[]{:S(2)}) %collective-permute-start.13) | collective-permute-done | bytes 24608 | tf_op jit(solution)/shard_map/ppermute | solution.py:34
  38.2 1.9 %collective-permute-done.12.low_ref = f32[3,2,2,4,128]{4,3,2,1,0:T(4,128)S(1)} collective-permute-done((f32[3,2,2,4,128]{4,3,2,1,0:T(4,128)S(1)}, f32[3,2,2,4,128]{4,3,2,1,0:T(4,128)S(1)}, u32[]{:S(2)}, u32[]{:S(2)}) %collective-permute-start.12) | collective-permute-done | bytes 24608 | tf_op jit(solution)/shard_map/ppermute | solution.py:33
  40.1 0.1 collective-permute-start.15
  40.2 1.3 %shard_map.66 = (f32[4,128,128]{2,1,0:T(8,128)S(1)}, f32[4,128,128]{2,1,0:T(8,128)S(1)}, bf16[48,1536]{1,0:T(8,128)(2,1)S(1)}, f32[8,1536]{1,0:T(8,128)S(1)}, bf16[4,128,48]{2,1,0:T(8,128)(2,1)S(1)}) custom-call(f32[3,2,2,4,128]{4,3,2,1,0:T(4,128)S(1)} %collective-permute-done.12.low_ref, f32[3,2,2,4,128]{4,3,2,1,0:T(4,128)S(1)} %collective-permute-done.13.high_ref, ...), custom_call_target="tpu_custom_call" | custom-call | flops 88473600 | bytes 7077888 | tf_op jit(solution)/shard_map/pallas_call | solution.py:438
  41.5 0.7 shard_map.67
  42.1 0.6 collective-permute-start.18
  42.7 1.9 %collective-permute-start.17 = (f32[1,2,4,128]{3,2,1,0:T(4,128)S(1)}, f32[1,2,4,128]{3,2,1,0:T(4,128)S(1)}, u32[]{:S(2)}, u32[]{:S(2)}) collective-permute-start(f32[1,2,4,128]{3,2,1,0:T(4,128)S(1)} %bitcast.57), channel_id=1, source_target_pairs={{8,0},{16,8},{24,16},{0,24},{9,1},{17,9},{25,17},{1,25},{10,2},{18... | collective-permute-start | bytes 12296 | tf_op jit(solution)/shard_map/ppermute | solution.py:34
  44.6 0.1 collective-permute-start.16
  44.7 1.3 %shard_map.68 = (f32[4,4,128,128]{3,2,1,0:T(8,128)S(1)}, bf16[4,128,48]{2,1,0:T(8,128)(2,1)S(1)}) custom-call(f32[3,2,2,4,128]{4,3,2,1,0:T(4,128)S(1)} %pad_maximum_fusion.3.mid_ref.all_refs_0_, f32[8,128]{1,0:T(8,128)S(1)} %get-tuple-element.107.all_refs_1_, f32[8,128]{1,0:T(8,128)S(1)} %get-tuple-element.106.all_refs_2_, ...), custom_call_target="tpu_custom_call" | custom-call | flops 29491200 | bytes 2359296 | tf_op jit(solution)/shard_map/pallas_call | solution.py:438
  46.0 0.3 collective-permute-done.17
  46.3 2.8 %collective-permute-done.16 = f32[1,2,4,128]{3,2,1,0:T(4,128)S(1)} collective-permute-done((f32[1,2,4,128]{3,2,1,0:T(4,128)S(1)}, f32[1,2,4,128]{3,2,1,0:T(4,128)S(1)}, u32[]{:S(2)}, u32[]{:S(2)}) %collective-permute-start.16) | collective-permute-done | bytes 4128 | tf_op jit(solution)/shard_map/ppermute | solution.py:33
  49.2 1.6 %shard_map.69.column_ref = f32[4,4,128,128]{3,2,1,0:T(8,128)S(1)} custom-call(f32[8,128]{1,0:T(8,128)S(1)} %bitcast.39, f32[8,128]{1,0:T(8,128)S(1)} %bitcast.36, bf16[48,1536]{1,0:T(8,128)(2,1)S(1)} %get-tuple-element.100.part_ref.all_refs_5_, bf16[48,1536]{1,0:T(8,128)(2,1)S(1)} %get-tuple-element.108.all_refs_6_.edge_ref, ...), custom_call_target="tpu_custom_call" | custom-call | flops 39321600 | bytes 3145728 | tf_op jit(solution)/shard_map/pallas_call | solution.py:438
  50.8 1.0 %shard_map.70 = (f32[3,4,128]{2,1,0:T(4,128)S(1)}, f32[4,4,128]{2,1,0:T(4,128)S(1)}) custom-call(f32[3,2,2,4,128]{4,3,2,1,0:T(4,128)S(1)} %pad_maximum_fusion.3.mid_ref.all_refs_0_, f32[8,128]{1,0:T(8,128)S(1)} %bitcast.44, f32[8,128]{1,0:T(8,128)S(1)} %bitcast.43, bf16[48,1536]{1,0:T(8,128)(2,1)S(1)} %get-tuple-element.101.ghost_ref.all_refs_7_, ...), custom_call_target="tpu_custom_call" | custom-call | flops 19660800 | bytes 1572864 | tf_op jit(solution)/shard_map/pallas_call | solution.py:438
  51.8 0.1 collective-permute-start.21
  51.9 1.9 %collective-permute-start.20 = (f32[1,2,2,4,128]{4,3,2,1,0:T(4,128)S(1)}, f32[1,2,2,4,128]{4,3,2,1,0:T(4,128)S(1)}, u32[]{:S(2)}, u32[]{:S(2)}) collective-permute-start(f32[1,2,2,4,128]{4,3,2,1,0:T(4,128)S(1)} %bitcast.51), channel_id=1, source_target_pairs={{0,8},{8,16},{16,24},{24,0},{1,9},{9,17},{17,25},{25,1},{2,10},{10... | collective-permute-start | bytes 24584 | tf_op jit(solution)/shard_map/ppermute | solution.py:33
  53.9 1.6 %collective-permute-done.21 = f32[1,2,2,4,128]{4,3,2,1,0:T(4,128)S(1)} collective-permute-done((f32[1,2,2,4,128]{4,3,2,1,0:T(4,128)S(1)}, f32[1,2,2,4,128]{4,3,2,1,0:T(4,128)S(1)}, u32[]{:S(2)}, u32[]{:S(2)}) %collective-permute-start.21) | collective-permute-done | bytes 8224 | tf_op jit(solution)/shard_map/ppermute | solution.py:34
  55.5 1.0 %collective-permute-done.20 = f32[1,2,2,4,128]{4,3,2,1,0:T(4,128)S(1)} collective-permute-done((f32[1,2,2,4,128]{4,3,2,1,0:T(4,128)S(1)}, f32[1,2,2,4,128]{4,3,2,1,0:T(4,128)S(1)}, u32[]{:S(2)}, u32[]{:S(2)}) %collective-permute-start.20) | collective-permute-done | bytes 8224 | tf_op jit(solution)/shard_map/ppermute | solution.py:33
  56.5 0.1 collective-permute-start.24
  56.6 0.2 collective-permute-start.23
  56.7 1.9 %collective-permute-start.22 = (f32[3,2,2,4,128]{4,3,2,1,0:T(4,128)S(1)}, f32[3,2,2,4,128]{4,3,2,1,0:T(4,128)S(1)}, u32[]{:S(2)}, u32[]{:S(2)}) collective-permute-start(f32[3,2,2,4,128]{4,3,2,1,0:T(4,128)S(1)} %pad_maximum_fusion.4.mid_ref.all_refs_0_), channel_id=1, source_target_pairs={{0,1},{1,2},{2,3},{3,0},{4,5},{5,6},{6,7},{7,4},{8,9},{9,10},{10,1... | collective-permute-start | bytes 73736 | tf_op jit(solution)/shard_map/ppermute | solution.py:33
  58.6 1.0 %shard_map.71 = (f32[4,128,128]{2,1,0:T(8,128)S(1)}, bf16[48,1536]{1,0:T(8,128)(2,1)S(1)}, f32[8,1536]{1,0:T(8,128)S(1)}, bf16[48,1536]{1,0:T(8,128)(2,1)S(1)}, ...) custom-call(f32[3,2,2,4,128]{4,3,2,1,0:T(4,128)S(1)} %pad_maximum_fusion.4.mid_ref.all_refs_0_, ...), custom_call_target="tpu_custom_call" | custom-call | flops 58982400 | bytes 4718592 | tf_op jit(solution)/shard_map/pallas_call | solution.py:438
  59.6 0.8 %collective-permute-done.23.high_ref = f32[3,2,2,4,128]{4,3,2,1,0:T(4,128)S(1)} collective-permute-done((f32[3,2,2,4,128]{4,3,2,1,0:T(4,128)S(1)}, f32[3,2,2,4,128]{4,3,2,1,0:T(4,128)S(1)}, u32[]{:S(2)}, u32[]{:S(2)}) %collective-permute-start.23) | collective-permute-done | bytes 24608 | tf_op jit(solution)/shard_map/ppermute | solution.py:34
  60.4 1.9 %collective-permute-done.22.low_ref = f32[3,2,2,4,128]{4,3,2,1,0:T(4,128)S(1)} collective-permute-done((f32[3,2,2,4,128]{4,3,2,1,0:T(4,128)S(1)}, f32[3,2,2,4,128]{4,3,2,1,0:T(4,128)S(1)}, u32[]{:S(2)}, u32[]{:S(2)}) %collective-permute-start.22) | collective-permute-done | bytes 24608 | tf_op jit(solution)/shard_map/ppermute | solution.py:33
  62.4 0.1 collective-permute-start.25
  62.4 1.3 %shard_map.72 = (f32[4,128,128]{2,1,0:T(8,128)S(1)}, f32[4,128,128]{2,1,0:T(8,128)S(1)}, bf16[48,1536]{1,0:T(8,128)(2,1)S(1)}, f32[8,1536]{1,0:T(8,128)S(1)}, bf16[4,128,48]{2,1,0:T(8,128)(2,1)S(1)}) custom-call(f32[3,2,2,4,128]{4,3,2,1,0:T(4,128)S(1)} %collective-permute-done.22.low_ref, f32[3,2,2,4,128]{4,3,2,1,0:T(4,128)S(1)} %collective-permute-done.23.high_ref, ...), custom_call_target="tpu_custom_call" | custom-call | flops 88473600 | bytes 7077888 | tf_op jit(solution)/shard_map/pallas_call | solution.py:438
  63.8 0.6 shard_map.73
  64.4 0.6 collective-permute-start.28
  65.0 1.0 %collective-permute-start.27 = (f32[1,2,4,128]{3,2,1,0:T(4,128)S(1)}, f32[1,2,4,128]{3,2,1,0:T(4,128)S(1)}, u32[]{:S(2)}, u32[]{:S(2)}) collective-permute-start(f32[1,2,4,128]{3,2,1,0:T(4,128)S(1)} %bitcast.60), channel_id=1, source_target_pairs={{8,0},{16,8},{24,16},{0,24},{9,1},{17,9},{25,17},{1,25},{10,2},{18... | collective-permute-start | bytes 12296 | tf_op jit(solution)/shard_map/ppermute | solution.py:34
  65.9 1.1 %collective-permute-start.26 = (f32[1,2,4,128]{3,2,1,0:T(4,128)S(1)}, f32[1,2,4,128]{3,2,1,0:T(4,128)S(1)}, u32[]{:S(2)}, u32[]{:S(2)}) collective-permute-start(f32[1,2,4,128]{3,2,1,0:T(4,128)S(1)} %bitcast.61), channel_id=1, source_target_pairs={{0,8},{8,16},{16,24},{24,0},{1,9},{9,17},{17,25},{25,1},{2,10},{10... | collective-permute-start | bytes 12296 | tf_op jit(solution)/shard_map/ppermute | solution.py:33
  67.0 1.3 %shard_map.74 = (f32[4,4,128,128]{3,2,1,0:T(8,128)S(1)}, bf16[4,128,48]{2,1,0:T(8,128)(2,1)S(1)}) custom-call(f32[3,2,2,4,128]{4,3,2,1,0:T(4,128)S(1)} %pad_maximum_fusion.4.mid_ref.all_refs_0_, f32[8,128]{1,0:T(8,128)S(1)} %get-tuple-element.130.all_refs_1_, f32[8,128]{1,0:T(8,128)S(1)} %get-tuple-element.129.all_refs_2_, ...), custom_call_target="tpu_custom_call" | custom-call | flops 29491200 | bytes 2359296 | tf_op jit(solution)/shard_map/pallas_call | solution.py:438
  68.3 0.3 collective-permute-done.27
  68.6 1.9 %collective-permute-done.26 = f32[1,2,4,128]{3,2,1,0:T(4,128)S(1)} collective-permute-done((f32[1,2,4,128]{3,2,1,0:T(4,128)S(1)}, f32[1,2,4,128]{3,2,1,0:T(4,128)S(1)}, u32[]{:S(2)}, u32[]{:S(2)}) %collective-permute-start.26) | collective-permute-done | bytes 4128 | tf_op jit(solution)/shard_map/ppermute | solution.py:33
  70.5 1.6 %shard_map.75.column_ref = f32[4,4,128,128]{3,2,1,0:T(8,128)S(1)} custom-call(f32[8,128]{1,0:T(8,128)S(1)} %bitcast.40, f32[8,128]{1,0:T(8,128)S(1)} %bitcast.37, bf16[48,1536]{1,0:T(8,128)(2,1)S(1)} %get-tuple-element.123.part_ref.all_refs_5_, bf16[48,1536]{1,0:T(8,128)(2,1)S(1)} %get-tuple-element.131.all_refs_6_.edge_ref, ...), custom_call_target="tpu_custom_call" | custom-call | flops 39321600 | bytes 3145728 | tf_op jit(solution)/shard_map/pallas_call | solution.py:438
  72.1 1.6 %shard_map.76 = (f32[3,4,128]{2,1,0:T(4,128)}, f32[3,4,128]{2,1,0:T(4,128)}) custom-call(f32[3,2,2,4,128]{4,3,2,1,0:T(4,128)S(1)} %pad_maximum_fusion.4.mid_ref.all_refs_0_, f32[8,128]{1,0:T(8,128)S(1)} %bitcast.46, f32[8,128]{1,0:T(8,128)S(1)} %bitcast.45, bf16[48,1536]{1,0:T(8,128)(2,1)S(1)} %get-tuple-element.124.ghost_ref.all_refs_7_, ...), custom_call_target="tpu_custom_call" | custom-call | flops 19660800 | bytes 1572864 | tf_op jit(solution)/shard_map/pallas_call | solution.py:438
  (38 shorter events, 0.2 us)
Async XLA Ops:
  1.5 5.6 %collective-permute-start = (f32[1,2,2,4,128]{4,3,2,1,0:T(4,128)S(1)}, f32[1,2,2,4,128]{4,3,2,1,0:T(4,128)S(1)}, u32[]{:S(2)}, u32[]{:S(2)}) collective-permute-start(f32[1,2,2,4,128]{4,3,2,1,0:T(4,128)S(1)} %get-tuple-element.73), channel_id=1, source_target_pairs={{0,8},{8,16},{16,24},{24,0},{1,9},{9,17},{17,25},{25,1},{2,10},{10... | collective-permute-start | bytes 24584 | tf_op jit(solution)/shard_map/ppermute | solution.py:33
  4.5 3.7 %collective-permute-start.1 = (f32[1,2,2,4,128]{4,3,2,1,0:T(4,128)S(1)}, f32[1,2,2,4,128]{4,3,2,1,0:T(4,128)S(1)}, u32[]{:S(2)}, u32[]{:S(2)}) collective-permute-start(f32[1,2,2,4,128]{4,3,2,1,0:T(4,128)S(1)} %get-tuple-element.73), channel_id=1, source_target_pairs={{8,0},{16,8},{24,16},{0,24},{9,1},{17,9},{25,17},{1,25},{10,2},{18... | collective-permute-start | bytes 24584 | tf_op jit(solution)/shard_map/ppermute | solution.py:34
  8.2 3.6 %collective-permute-start.4 = (f32[3,2,2,4,128]{4,3,2,1,0:T(4,128)S(1)}, f32[3,2,2,4,128]{4,3,2,1,0:T(4,128)S(1)}, u32[]{:S(2)}, u32[]{:S(2)}) collective-permute-start(f32[3,2,2,4,128]{4,3,2,1,0:T(4,128)S(1)} %constant_dynamic-update-slice_fusion.mid_ref.all_refs_0_), channel_id=1, source_target_pairs={{0,4},{4,0},{1,5},{5,1},{2,6},{6,2},{3,7},{7,3},{8,12},{12,8},{9,1... | collective-permute-start | bytes 73736 | tf_op jit(solution)/shard_map/ppermute | solution.py:28
  8.2 5.1 %collective-permute-start.3 = (f32[3,2,2,4,128]{4,3,2,1,0:T(4,128)S(1)}, f32[3,2,2,4,128]{4,3,2,1,0:T(4,128)S(1)}, u32[]{:S(2)}, u32[]{:S(2)}) collective-permute-start(f32[3,2,2,4,128]{4,3,2,1,0:T(4,128)S(1)} %constant_dynamic-update-slice_fusion.mid_ref.all_refs_0_), channel_id=1, source_target_pairs={{1,0},{2,1},{3,2},{0,3},{5,4},{6,5},{7,6},{4,7},{9,8},{10,9},{11,1... | collective-permute-start | bytes 73736 | tf_op jit(solution)/shard_map/ppermute | solution.py:34
  11.8 5.6 %collective-permute-start.2 = (f32[3,2,2,4,128]{4,3,2,1,0:T(4,128)S(1)}, f32[3,2,2,4,128]{4,3,2,1,0:T(4,128)S(1)}, u32[]{:S(2)}, u32[]{:S(2)}) collective-permute-start(f32[3,2,2,4,128]{4,3,2,1,0:T(4,128)S(1)} %constant_dynamic-update-slice_fusion.mid_ref.all_refs_0_), channel_id=1, source_target_pairs={{0,1},{1,2},{2,3},{3,0},{4,5},{5,6},{6,7},{7,4},{8,9},{9,10},{10,1... | collective-permute-start | bytes 73736 | tf_op jit(solution)/shard_map/ppermute | solution.py:33
  17.4 1.4 %collective-permute-start.5 = (f32[3,2,4,4,128]{4,3,2,1,0:T(4,128)S(1)}, f32[3,2,4,4,128]{4,3,2,1,0:T(4,128)S(1)}, u32[]{:S(2)}, u32[]{:S(2)}) collective-permute-start(f32[3,2,4,4,128]{4,3,2,1,0:T(4,128)S(1)} %pad_maximum_fusion), channel_id=1, source_target_pairs={{0,4},{4,0},{1,5},{5,1},{2,6},{6,2},{3,7},{7,3},{8,12},{12,8},{9,1... | collective-permute-start | bytes 147464 | tf_op jit(solution)/shard_map/ppermute | solution.py:28
  19.5 3.0 %collective-permute-start.8 = (f32[1,2,4,128]{3,2,1,0:T(4,128)S(1)}, f32[1,2,4,128]{3,2,1,0:T(4,128)S(1)}, u32[]{:S(2)}, u32[]{:S(2)}) collective-permute-start(f32[1,2,4,128]{3,2,1,0:T(4,128)S(1)} %bitcast.53), channel_id=1, source_target_pairs={{0,4},{4,0},{1,5},{5,1},{2,6},{6,2},{3,7},{7,3},{8,12},{12,8},{9,1... | collective-permute-start | bytes 12296 | tf_op jit(solution)/shard_map/ppermute | solution.py:28
  20.0 4.0 %collective-permute-start.7 = (f32[1,2,4,128]{3,2,1,0:T(4,128)S(1)}, f32[1,2,4,128]{3,2,1,0:T(4,128)S(1)}, u32[]{:S(2)}, u32[]{:S(2)}) collective-permute-start(f32[1,2,4,128]{3,2,1,0:T(4,128)S(1)} %bitcast.54), channel_id=1, source_target_pairs={{8,0},{16,8},{24,16},{0,24},{9,1},{17,9},{25,17},{1,25},{10,2},{18... | collective-permute-start | bytes 12296 | tf_op jit(solution)/shard_map/ppermute | solution.py:34
  22.4 4.5 %collective-permute-start.6 = (f32[1,2,4,128]{3,2,1,0:T(4,128)S(1)}, f32[1,2,4,128]{3,2,1,0:T(4,128)S(1)}, u32[]{:S(2)}, u32[]{:S(2)}) collective-permute-start(f32[1,2,4,128]{3,2,1,0:T(4,128)S(1)} %bitcast.55), channel_id=1, source_target_pairs={{0,8},{8,16},{16,24},{24,0},{1,9},{9,17},{17,25},{25,1},{2,10},{10... | collective-permute-start | bytes 12296 | tf_op jit(solution)/shard_map/ppermute | solution.py:33
  26.9 1.6 %collective-permute-start.9 = (f32[2,2,4,128]{3,2,1,0:T(4,128)S(1)}, f32[2,2,4,128]{3,2,1,0:T(4,128)S(1)}, u32[]{:S(2)}, u32[]{:S(2)}) collective-permute-start(f32[2,2,4,128]{3,2,1,0:T(4,128)S(1)} %pad_maximum_fusion.5), channel_id=1, source_target_pairs={{0,4},{4,0},{1,5},{5,1},{2,6},{6,2},{3,7},{7,3},{8,12},{12,8},{9,1... | collective-permute-start | bytes 24584 | tf_op jit(solution)/shard_map/ppermute | solution.py:28
  29.5 3.7 %collective-permute-start.11 = (f32[1,2,2,4,128]{4,3,2,1,0:T(4,128)S(1)}, f32[1,2,2,4,128]{4,3,2,1,0:T(4,128)S(1)}, u32[]{:S(2)}, u32[]{:S(2)}) collective-permute-start(f32[1,2,2,4,128]{4,3,2,1,0:T(4,128)S(1)} %bitcast.47), channel_id=1, source_target_pairs={{8,0},{16,8},{24,16},{0,24},{9,1},{17,9},{25,17},{1,25},{10,2},{18... | collective-permute-start | bytes 24584 | tf_op jit(solution)/shard_map/ppermute | solution.py:34
  29.6 4.6 %collective-permute-start.10 = (f32[1,2,2,4,128]{4,3,2,1,0:T(4,128)S(1)}, f32[1,2,2,4,128]{4,3,2,1,0:T(4,128)S(1)}, u32[]{:S(2)}, u32[]{:S(2)}) collective-permute-start(f32[1,2,2,4,128]{4,3,2,1,0:T(4,128)S(1)} %bitcast.48), channel_id=1, source_target_pairs={{0,8},{8,16},{16,24},{24,0},{1,9},{9,17},{17,25},{25,1},{2,10},{10... | collective-permute-start | bytes 24584 | tf_op jit(solution)/shard_map/ppermute | solution.py:33
  34.2 2.2 %collective-permute-start.14 = (f32[3,2,2,4,128]{4,3,2,1,0:T(4,128)S(1)}, f32[3,2,2,4,128]{4,3,2,1,0:T(4,128)S(1)}, u32[]{:S(2)}, u32[]{:S(2)}) collective-permute-start(f32[3,2,2,4,128]{4,3,2,1,0:T(4,128)S(1)} %pad_maximum_fusion.3.mid_ref.all_refs_0_), channel_id=1, source_target_pairs={{0,4},{4,0},{1,5},{5,1},{2,6},{6,2},{3,7},{7,3},{8,12},{12,8},{9,1... | collective-permute-start | bytes 73736 | tf_op jit(solution)/shard_map/ppermute | solution.py:28
  34.3 3.9 %collective-permute-start.13 = (f32[3,2,2,4,128]{4,3,2,1,0:T(4,128)S(1)}, f32[3,2,2,4,128]{4,3,2,1,0:T(4,128)S(1)}, u32[]{:S(2)}, u32[]{:S(2)}) collective-permute-start(f32[3,2,2,4,128]{4,3,2,1,0:T(4,128)S(1)} %pad_maximum_fusion.3.mid_ref.all_refs_0_), channel_id=1, source_target_pairs={{1,0},{2,1},{3,2},{0,3},{5,4},{6,5},{7,6},{4,7},{9,8},{10,9},{11,1... | collective-permute-start | bytes 73736 | tf_op jit(solution)/shard_map/ppermute | solution.py:34
  34.4 5.6 %collective-permute-start.12 = (f32[3,2,2,4,128]{4,3,2,1,0:T(4,128)S(1)}, f32[3,2,2,4,128]{4,3,2,1,0:T(4,128)S(1)}, u32[]{:S(2)}, u32[]{:S(2)}) collective-permute-start(f32[3,2,2,4,128]{4,3,2,1,0:T(4,128)S(1)} %pad_maximum_fusion.3.mid_ref.all_refs_0_), channel_id=1, source_target_pairs={{0,1},{1,2},{2,3},{3,0},{4,5},{5,6},{6,7},{7,4},{8,9},{9,10},{10,1... | collective-permute-start | bytes 73736 | tf_op jit(solution)/shard_map/ppermute | solution.py:33
  40.1 1.4 %collective-permute-start.15 = (f32[3,2,4,4,128]{4,3,2,1,0:T(4,128)S(1)}, f32[3,2,4,4,128]{4,3,2,1,0:T(4,128)S(1)}, u32[]{:S(2)}, u32[]{:S(2)}) collective-permute-start(f32[3,2,4,4,128]{4,3,2,1,0:T(4,128)S(1)} %pad_maximum_fusion.1), channel_id=1, source_target_pairs={{0,4},{4,0},{1,5},{5,1},{2,6},{6,2},{3,7},{7,3},{8,12},{12,8},{9,1... | collective-permute-start | bytes 147464 | tf_op jit(solution)/shard_map/ppermute | solution.py:28
  42.1 2.6 %collective-permute-start.18 = (f32[1,2,4,128]{3,2,1,0:T(4,128)S(1)}, f32[1,2,4,128]{3,2,1,0:T(4,128)S(1)}, u32[]{:S(2)}, u32[]{:S(2)}) collective-permute-start(f32[1,2,4,128]{3,2,1,0:T(4,128)S(1)} %bitcast.56), channel_id=1, source_target_pairs={{0,4},{4,0},{1,5},{5,1},{2,6},{6,2},{3,7},{7,3},{8,12},{12,8},{9,1... | collective-permute-start | bytes 12296 | tf_op jit(solution)/shard_map/ppermute | solution.py:28
  42.7 3.6 %collective-permute-start.17 = (f32[1,2,4,128]{3,2,1,0:T(4,128)S(1)}, f32[1,2,4,128]{3,2,1,0:T(4,128)S(1)}, u32[]{:S(2)}, u32[]{:S(2)}) collective-permute-start(f32[1,2,4,128]{3,2,1,0:T(4,128)S(1)} %bitcast.57), channel_id=1, source_target_pairs={{8,0},{16,8},{24,16},{0,24},{9,1},{17,9},{25,17},{1,25},{10,2},{18... | collective-permute-start | bytes 12296 | tf_op jit(solution)/shard_map/ppermute | solution.py:34
  44.6 4.5 %collective-permute-start.16 = (f32[1,2,4,128]{3,2,1,0:T(4,128)S(1)}, f32[1,2,4,128]{3,2,1,0:T(4,128)S(1)}, u32[]{:S(2)}, u32[]{:S(2)}) collective-permute-start(f32[1,2,4,128]{3,2,1,0:T(4,128)S(1)} %bitcast.58), channel_id=1, source_target_pairs={{0,8},{8,16},{16,24},{24,0},{1,9},{9,17},{17,25},{25,1},{2,10},{10... | collective-permute-start | bytes 12296 | tf_op jit(solution)/shard_map/ppermute | solution.py:33
  49.2 1.6 %collective-permute-start.19 = (f32[2,2,4,128]{3,2,1,0:T(4,128)S(1)}, f32[2,2,4,128]{3,2,1,0:T(4,128)S(1)}, u32[]{:S(2)}, u32[]{:S(2)}) collective-permute-start(f32[2,2,4,128]{3,2,1,0:T(4,128)S(1)} %pad_maximum_fusion.6), channel_id=1, source_target_pairs={{0,4},{4,0},{1,5},{5,1},{2,6},{6,2},{3,7},{7,3},{8,12},{12,8},{9,1... | collective-permute-start | bytes 24584 | tf_op jit(solution)/shard_map/ppermute | solution.py:28
  51.8 3.7 %collective-permute-start.21 = (f32[1,2,2,4,128]{4,3,2,1,0:T(4,128)S(1)}, f32[1,2,2,4,128]{4,3,2,1,0:T(4,128)S(1)}, u32[]{:S(2)}, u32[]{:S(2)}) collective-permute-start(f32[1,2,2,4,128]{4,3,2,1,0:T(4,128)S(1)} %bitcast.50), channel_id=1, source_target_pairs={{8,0},{16,8},{24,16},{0,24},{9,1},{17,9},{25,17},{1,25},{10,2},{18... | collective-permute-start | bytes 24584 | tf_op jit(solution)/shard_map/ppermute | solution.py:34
  51.9 4.5 %collective-permute-start.20 = (f32[1,2,2,4,128]{4,3,2,1,0:T(4,128)S(1)}, f32[1,2,2,4,128]{4,3,2,1,0:T(4,128)S(1)}, u32[]{:S(2)}, u32[]{:S(2)}) collective-permute-start(f32[1,2,2,4,128]{4,3,2,1,0:T(4,128)S(1)} %bitcast.51), channel_id=1, source_target_pairs={{0,8},{8,16},{16,24},{24,0},{1,9},{9,17},{17,25},{25,1},{2,10},{10... | collective-permute-start | bytes 24584 | tf_op jit(solution)/shard_map/ppermute | solution.py:33
  56.5 2.2 %collective-permute-start.24 = (f32[3,2,2,4,128]{4,3,2,1,0:T(4,128)S(1)}, f32[3,2,2,4,128]{4,3,2,1,0:T(4,128)S(1)}, u32[]{:S(2)}, u32[]{:S(2)}) collective-permute-start(f32[3,2,2,4,128]{4,3,2,1,0:T(4,128)S(1)} %pad_maximum_fusion.4.mid_ref.all_refs_0_), channel_id=1, source_target_pairs={{0,4},{4,0},{1,5},{5,1},{2,6},{6,2},{3,7},{7,3},{8,12},{12,8},{9,1... | collective-permute-start | bytes 73736 | tf_op jit(solution)/shard_map/ppermute | solution.py:28
  56.6 3.9 %collective-permute-start.23 = (f32[3,2,2,4,128]{4,3,2,1,0:T(4,128)S(1)}, f32[3,2,2,4,128]{4,3,2,1,0:T(4,128)S(1)}, u32[]{:S(2)}, u32[]{:S(2)}) collective-permute-start(f32[3,2,2,4,128]{4,3,2,1,0:T(4,128)S(1)} %pad_maximum_fusion.4.mid_ref.all_refs_0_), channel_id=1, source_target_pairs={{1,0},{2,1},{3,2},{0,3},{5,4},{6,5},{7,6},{4,7},{9,8},{10,9},{11,1... | collective-permute-start | bytes 73736 | tf_op jit(solution)/shard_map/ppermute | solution.py:34
  56.7 5.6 %collective-permute-start.22 = (f32[3,2,2,4,128]{4,3,2,1,0:T(4,128)S(1)}, f32[3,2,2,4,128]{4,3,2,1,0:T(4,128)S(1)}, u32[]{:S(2)}, u32[]{:S(2)}) collective-permute-start(f32[3,2,2,4,128]{4,3,2,1,0:T(4,128)S(1)} %pad_maximum_fusion.4.mid_ref.all_refs_0_), channel_id=1, source_target_pairs={{0,1},{1,2},{2,3},{3,0},{4,5},{5,6},{6,7},{7,4},{8,9},{9,10},{10,1... | collective-permute-start | bytes 73736 | tf_op jit(solution)/shard_map/ppermute | solution.py:33
  62.4 1.4 %collective-permute-start.25 = (f32[3,2,4,4,128]{4,3,2,1,0:T(4,128)S(1)}, f32[3,2,4,4,128]{4,3,2,1,0:T(4,128)S(1)}, u32[]{:S(2)}, u32[]{:S(2)}) collective-permute-start(f32[3,2,4,4,128]{4,3,2,1,0:T(4,128)S(1)} %pad_maximum_fusion.2), channel_id=1, source_target_pairs={{0,4},{4,0},{1,5},{5,1},{2,6},{6,2},{3,7},{7,3},{8,12},{12,8},{9,1... | collective-permute-start | bytes 147464 | tf_op jit(solution)/shard_map/ppermute | solution.py:28
  64.4 2.6 %collective-permute-start.28 = (f32[1,2,4,128]{3,2,1,0:T(4,128)S(1)}, f32[1,2,4,128]{3,2,1,0:T(4,128)S(1)}, u32[]{:S(2)}, u32[]{:S(2)}) collective-permute-start(f32[1,2,4,128]{3,2,1,0:T(4,128)S(1)} %bitcast.59), channel_id=1, source_target_pairs={{0,4},{4,0},{1,5},{5,1},{2,6},{6,2},{3,7},{7,3},{8,12},{12,8},{9,1... | collective-permute-start | bytes 12296 | tf_op jit(solution)/shard_map/ppermute | solution.py:28
  65.0 3.6 %collective-permute-start.27 = (f32[1,2,4,128]{3,2,1,0:T(4,128)S(1)}, f32[1,2,4,128]{3,2,1,0:T(4,128)S(1)}, u32[]{:S(2)}, u32[]{:S(2)}) collective-permute-start(f32[1,2,4,128]{3,2,1,0:T(4,128)S(1)} %bitcast.60), channel_id=1, source_target_pairs={{8,0},{16,8},{24,16},{0,24},{9,1},{17,9},{25,17},{1,25},{10,2},{18... | collective-permute-start | bytes 12296 | tf_op jit(solution)/shard_map/ppermute | solution.py:34
  65.9 4.5 %collective-permute-start.26 = (f32[1,2,4,128]{3,2,1,0:T(4,128)S(1)}, f32[1,2,4,128]{3,2,1,0:T(4,128)S(1)}, u32[]{:S(2)}, u32[]{:S(2)}) collective-permute-start(f32[1,2,4,128]{3,2,1,0:T(4,128)S(1)} %bitcast.61), channel_id=1, source_target_pairs={{0,8},{8,16},{16,24},{24,0},{1,9},{9,17},{17,25},{25,1},{2,10},{10... | collective-permute-start | bytes 12296 | tf_op jit(solution)/shard_map/ppermute | solution.py:33
  70.5 1.6 %collective-permute-start.29 = (f32[2,2,4,128]{3,2,1,0:T(4,128)S(1)}, f32[2,2,4,128]{3,2,1,0:T(4,128)S(1)}, u32[]{:S(2)}, u32[]{:S(2)}) collective-permute-start(f32[2,2,4,128]{3,2,1,0:T(4,128)S(1)} %pad_maximum_fusion.7), channel_id=1, source_target_pairs={{0,4},{4,0},{1,5},{5,1},{2,6},{6,2},{3,7},{7,3},{8,12},{12,8},{9,1... | collective-permute-start | bytes 24584 | tf_op jit(solution)/shard_map/ppermute | solution.py:28

commit v4 on v3

--- a/solution.py
+++ b/solution.py
@@ -17,7 +17,7 @@
 SETS = ("own", "edge", "gown", "gedge")
 
 
-def neighbours(cells, axis, dim, width):
+def neighbours(cells, axis, dim, width, even=None):
     count = lax.axis_size(axis)
     size = cells.shape[dim]
     head = lax.slice_in_dim(cells, 0, width, axis=dim)
@@ -30,13 +30,19 @@
             lax.slice_in_dim(other, width, size, axis=dim),
             lax.slice_in_dim(other, 0, width, axis=dim),
         )
-    below = lax.ppermute(tail, axis, [(i, (i + 1) % count) for i in range(count)])
-    above = lax.ppermute(head, axis, [((i + 1) % count, i) for i in range(count)])
-    return below, above
-
-
-def ring_halo(cells, axis, dim, width):
-    below, above = neighbours(cells, axis, dim, width)
+    if count % 2:
+        below = lax.ppermute(tail, axis, [(i, (i + 1) % count) for i in range(count)])
+        above = lax.ppermute(head, axis, [((i + 1) % count, i) for i in range(count)])
+        return below, above
+    even = lax.axis_index(axis) % 2 == 0 if even is None else even
+    first, second = (cells, cells) if size == width else (jnp.where(even, tail, head), jnp.where(even, head, tail))
+    first = lax.ppermute(first, axis, [(i, i ^ 1) for i in range(count)])
+    second = lax.ppermute(second, axis, [(i, (i - 1 if i % 2 == 0 else i + 1) % count) for i in range(count)])
+    return jnp.where(even, second, first), jnp.where(even, first, second)
+
+
+def ring_halo(cells, axis, dim, width, even=None):
+    below, above = neighbours(cells, axis, dim, width, even)
     return jnp.concatenate([below, cells, above], axis=dim)
 
 
@@ -447,10 +453,12 @@
             ),
         )(*operands)
 
+    even = {axis: lax.optimization_barrier(lax.axis_index(axis) % 2 == 0) for axis in ("gx", "gz")}
+
     def evaluate(location, velocity, stage):
-        mid = ring_halo(location, "gx", 0, 1)
+        mid = ring_halo(location, "gx", 0, 1, even["gx"])
         mid_below, mid_above = neighbours(mid, "gy", 1, 1)
-        low, high = neighbours(mid, "gz", 2, 2)
+        low, high = neighbours(mid, "gz", 2, 2, even["gz"])
         inner, part, point, ghost, ghost_point, left = call(
             functools.partial(inner_density_kernel, own),
             [mid, mid_below, mid_above],
@@ -474,7 +482,7 @@
             [block("gedge")],
         )
         weights = weights.reshape(cx, cy, near, slots)
-        side_below, side_above = neighbours(weights, "gx", 0, 1)
+        side_below, side_above = neighbours(weights, "gx", 0, 1, even["gx"])
         weight_below, weight_above = neighbours(weights, "gy", 1, 1)
         column, left = call(
             functools.partial(column_force_kernel, own),

time: 73.9 us -> 77.9 us (1.054)
  starting transfers between devices: 24.4 us -> 29.6 us
  waiting for transfers between devices: 26.4 us -> 24.9 us
    ppermute x18, starting transfers between devices: 22.4 us -> 29.1 us  [the longest x9 19.3 us: neighbours(): lax.ppermute(second, axis, [(i, (i - 1 if i % 2 == 0 else i + 1) % count)...]
    ppermute x12, starting transfers between devices: 2.03 us -> 0.44 us  [neighbours(): other = lax.ppermute(cells, axis, [(0, 1), (1, 0)])]
    ppermute x18, waiting for transfers between devices: 26.3 us -> 24.8 us  [the longest x9 18.5 us: neighbours(): lax.ppermute(second, axis, [(i, (i - 1 if i % 2 == 0 else i + 1) % count)...]
  transfers between devices with their start and end apart: 30 -> 30, of which waited for: 18 -> 17; matrix products, arithmetic and copies ran while one was open for 0% -> 0% of each run, Pallas kernels for 21% -> 11%
where the time goes in v4:
time: 77.9 us; the launch traced here: 77.7 us
  starting transfers between devices  29.6 us (38%)
  waiting for transfers between devices  24.9 us (32%)
  Pallas kernels  22 us (28%)
  between operations  1.04 us (1%)
    pallas_call x18, Pallas kernels, call(): pl.pallas_call(kernel, out_shape=out_shape, in_specs=[vmem] * len(operand...  21.2 us
    ppermute x9, starting transfers between devices, neighbours(): lax.ppermute(second, axis, [(i, (i - 1 if i % 2 == 0 else i + 1) % count)...  19.3 us
    ppermute x9, waiting for transfers between devices, neighbours(): lax.ppermute(second, axis, [(i, (i - 1 if i % 2 == 0 else i + 1) % count)...  18.5 us
    ppermute x9, starting transfers between devices, neighbours(): first = lax.ppermute(first, axis, [(i, i ^ 1) for i in range(count)])  9.87 us
    ppermute x9, waiting for transfers between devices, neighbours(): first = lax.ppermute(first, axis, [(i, i ^ 1) for i in range(count)])  6.33 us
  transfers between devices with their start and end apart: 30, of which 17 were waited for; matrix products, arithmetic and copies ran while one was open for 0% of the time, Pallas kernels for 11%

profile of v4, /device:TPU:0, one launch (start us, length us, event | category | flops | bytes accessed | tf_op | source)
XLA Modules:
  0.0 77.7 jit_solution(6509215419381502213)
XLA Ops:
  0.6 0.8 %prepare.1 = (f32[1,2,2,4,128]{4,3,2,1,0:T(4,128)S(1)}, f32[3,4,128]{2,1,0:T(4,128)S(1)}) custom-call(f32[3,1,2,2,128]{4,3,2,1,0:T(2,128)} %pos_hbm.1, f32[3,1,2,2,128]{4,3,2,1,0:T(2,128)} %vel_hbm.1, s32[1,2,2,128]{3,2,1,0:T(2,128)} %species_hbm.1, s32[1,2,2]{2,1,0:T(2,128)} %counts_hbm.1), custom_call_target="tpu_custom_call" | custom-call | tf_op jit(solution)/shard_map/prepare/pallas_call | solution.py:530
  1.5 3.0 %collective-permute-start.1 = (f32[1,2,2,4,128]{4,3,2,1,0:T(4,128)S(1)}, f32[1,2,2,4,128]{4,3,2,1,0:T(4,128)S(1)}, u32[]{:S(2)}, u32[]{:S(2)}) collective-permute-start(f32[1,2,2,4,128]{4,3,2,1,0:T(4,128)S(1)} %get-tuple-element.73), channel_id=1, source_target_pairs={{0,8},{8,0},{16,24},{24,16},{1,9},{9,1},{17,25},{25,17},{2,10},{10... | collective-permute-start | bytes 24584 | tf_op jit(solution)/shard_map/ppermute | solution.py:39
  4.5 1.5 %collective-permute-start = (f32[1,2,2,4,128]{4,3,2,1,0:T(4,128)S(1)}, f32[1,2,2,4,128]{4,3,2,1,0:T(4,128)S(1)}, u32[]{:S(2)}, u32[]{:S(2)}) collective-permute-start(f32[1,2,2,4,128]{4,3,2,1,0:T(4,128)S(1)} %get-tuple-element.73), channel_id=1, source_target_pairs={{0,24},{8,16},{16,8},{24,0},{1,25},{9,17},{17,9},{25,1},{2,26},{10... | collective-permute-start | bytes 24584 | tf_op jit(solution)/shard_map/ppermute | solution.py:40
  6.0 0.1 collective-permute-done.1
  6.1 2.9 %collective-permute-done = f32[1,2,2,4,128]{4,3,2,1,0:T(4,128)S(1)} collective-permute-done((f32[1,2,2,4,128]{4,3,2,1,0:T(4,128)S(1)}, f32[1,2,2,4,128]{4,3,2,1,0:T(4,128)S(1)}, u32[]{:S(2)}, u32[]{:S(2)}) %collective-permute-start) | collective-permute-done | bytes 8224 | tf_op jit(solution)/shard_map/ppermute | solution.py:40
  9.1 1.6 %collective-permute-start.3 = (f32[3,2,2,4,128]{4,3,2,1,0:T(4,128)S(1)}, f32[3,2,2,4,128]{4,3,2,1,0:T(4,128)S(1)}, u32[]{:S(2)}, u32[]{:S(2)}) collective-permute-start(f32[3,2,2,4,128]{4,3,2,1,0:T(4,128)S(1)} %pad_maximum_fusion.3.mid_ref.all_refs_0_), channel_id=1, source_target_pairs={{0,1},{1,0},{2,3},{3,2},{4,5},{5,4},{6,7},{7,6},{8,9},{9,8},{10,11... | collective-permute-start | bytes 73736 | tf_op jit(solution)/shard_map/ppermute | solution.py:39
  10.7 2.5 %collective-permute-start.2 = (f32[3,2,2,4,128]{4,3,2,1,0:T(4,128)S(1)}, f32[3,2,2,4,128]{4,3,2,1,0:T(4,128)S(1)}, u32[]{:S(2)}, u32[]{:S(2)}) collective-permute-start(f32[3,2,2,4,128]{4,3,2,1,0:T(4,128)S(1)} %pad_maximum_fusion.3.mid_ref.all_refs_0_), channel_id=1, source_target_pairs={{0,3},{1,2},{2,1},{3,0},{4,7},{5,6},{6,5},{7,4},{8,11},{9,10},{10,... | collective-permute-start | bytes 73736 | tf_op jit(solution)/shard_map/ppermute | solution.py:40
  13.2 3.1 %collective-permute-done.2 = f32[3,2,2,4,128]{4,3,2,1,0:T(4,128)S(1)} collective-permute-done((f32[3,2,2,4,128]{4,3,2,1,0:T(4,128)S(1)}, f32[3,2,2,4,128]{4,3,2,1,0:T(4,128)S(1)}, u32[]{:S(2)}, u32[]{:S(2)}) %collective-permute-start.2) | collective-permute-done | bytes 24608 | tf_op jit(solution)/shard_map/ppermute | solution.py:40
  16.4 1.0 %shard_map.59 = (f32[4,128,128]{2,1,0:T(8,128)S(1)}, bf16[48,1536]{1,0:T(8,128)(2,1)S(1)}, f32[8,1536]{1,0:T(8,128)S(1)}, bf16[48,1536]{1,0:T(8,128)(2,1)S(1)}, ...) custom-call(f32[3,2,2,4,128]{4,3,2,1,0:T(4,128)S(1)} %pad_maximum_fusion.3.mid_ref.all_refs_0_, ...), custom_call_target="tpu_custom_call" | custom-call | flops 58982400 | bytes 4718592 | tf_op jit(solution)/shard_map/pallas_call | solution.py:444
  17.4 0.1 collective-permute-start.5
  17.4 1.3 %shard_map.60 = (f32[4,128,128]{2,1,0:T(8,128)S(1)}, f32[4,128,128]{2,1,0:T(8,128)S(1)}, bf16[48,1536]{1,0:T(8,128)(2,1)S(1)}, f32[8,1536]{1,0:T(8,128)S(1)}, bf16[4,128,48]{2,1,0:T(8,128)(2,1)S(1)}) custom-call(f32[3,2,2,4,128]{4,3,2,1,0:T(4,128)S(1)} %bitcast.81, f32[3,2,2,4,128]{4,3,2,1,0:T(4,128)S(1)} %bitcast.78, ...), custom_call_target="tpu_custom_call" | custom-call | flops 88473600 | bytes 7077888 | tf_op jit(solution)/shard_map/pallas_call | solution.py:444
  18.8 0.6 shard_map.61
  19.4 0.6 collective-permute-start.7
  20.0 2.4 %collective-permute-start.6 = (f32[1,2,4,128]{3,2,1,0:T(4,128)S(1)}, f32[1,2,4,128]{3,2,1,0:T(4,128)S(1)}, u32[]{:S(2)}, u32[]{:S(2)}) collective-permute-start(f32[1,2,4,128]{3,2,1,0:T(4,128)S(1)} %bitcast.117), channel_id=1, source_target_pairs={{0,24},{8,16},{16,8},{24,0},{1,25},{9,17},{17,9},{25,1},{2,26},{10... | collective-permute-start | bytes 12296 | tf_op jit(solution)/shard_map/ppermute | solution.py:40
  22.5 0.0 collective-permute-start.8
  22.5 0.6 collective-permute-done.7
  23.1 1.4 %collective-permute-done.6 = f32[1,2,4,128]{3,2,1,0:T(4,128)S(1)} collective-permute-done((f32[1,2,4,128]{3,2,1,0:T(4,128)S(1)}, f32[1,2,4,128]{3,2,1,0:T(4,128)S(1)}, u32[]{:S(2)}, u32[]{:S(2)}) %collective-permute-start.6) | collective-permute-done | bytes 4128 | tf_op jit(solution)/shard_map/ppermute | solution.py:40
  24.5 0.0 collective-permute-done.8
  24.6 1.3 %shard_map.62 = (f32[4,4,128,128]{3,2,1,0:T(8,128)S(1)}, bf16[4,128,48]{2,1,0:T(8,128)(2,1)S(1)}) custom-call(f32[3,2,2,4,128]{4,3,2,1,0:T(4,128)S(1)} %pad_maximum_fusion.3.mid_ref.all_refs_0_, f32[8,128]{1,0:T(8,128)S(1)} %get-tuple-element.84.all_refs_1_, f32[8,128]{1,0:T(8,128)S(1)} %get-tuple-element.83.all_refs_2_, ...), custom_call_target="tpu_custom_call" | custom-call | flops 29491200 | bytes 2359296 | tf_op jit(solution)/shard_map/pallas_call | solution.py:444
  25.9 0.1 collective-permute-start.9
  26.0 1.6 %shard_map.63.column_ref = f32[4,4,128,128]{3,2,1,0:T(8,128)S(1)} custom-call(f32[8,128]{1,0:T(8,128)S(1)} %bitcast.94, f32[8,128]{1,0:T(8,128)S(1)} %bitcast.96, bf16[48,1536]{1,0:T(8,128)(2,1)S(1)} %get-tuple-element.77.part_ref.all_refs_5_, bf16[48,1536]{1,0:T(8,128)(2,1)S(1)} %get-tuple-element.85.all_refs_6_.edge_ref, ...), custom_call_target="tpu_custom_call" | custom-call | flops 39321600 | bytes 3145728 | tf_op jit(solution)/shard_map/pallas_call | solution.py:444
  27.6 1.0 %shard_map.64 = (f32[3,4,128]{2,1,0:T(4,128)S(1)}, f32[4,4,128]{2,1,0:T(4,128)S(1)}) custom-call(f32[3,2,2,4,128]{4,3,2,1,0:T(4,128)S(1)} %pad_maximum_fusion.3.mid_ref.all_refs_0_, f32[8,128]{1,0:T(8,128)S(1)} %bitcast.102, f32[8,128]{1,0:T(8,128)S(1)} %bitcast.101, bf16[48,1536]{1,0:T(8,128)(2,1)S(1)} %get-tuple-element.78.ghost_ref.all_refs_7_, ...), custom_call_target="tpu_custom_call" | custom-call | flops 19660800 | bytes 1572864 | tf_op jit(solution)/shard_map/pallas_call | solution.py:444
  28.6 1.5 %collective-permute-start.11 = (f32[1,2,2,4,128]{4,3,2,1,0:T(4,128)S(1)}, f32[1,2,2,4,128]{4,3,2,1,0:T(4,128)S(1)}, u32[]{:S(2)}, u32[]{:S(2)}) collective-permute-start(f32[1,2,2,4,128]{4,3,2,1,0:T(4,128)S(1)} %bitcast.107), channel_id=1, source_target_pairs={{0,8},{8,0},{16,24},{24,16},{1,9},{9,1},{17,25},{25,17},{2,10},{10... | collective-permute-start | bytes 24584 | tf_op jit(solution)/shard_map/ppermute | solution.py:39
  30.1 1.5 %collective-permute-start.10 = (f32[1,2,2,4,128]{4,3,2,1,0:T(4,128)S(1)}, f32[1,2,2,4,128]{4,3,2,1,0:T(4,128)S(1)}, u32[]{:S(2)}, u32[]{:S(2)}) collective-permute-start(f32[1,2,2,4,128]{4,3,2,1,0:T(4,128)S(1)} %bitcast.108), channel_id=1, source_target_pairs={{0,24},{8,16},{16,8},{24,0},{1,25},{9,17},{17,9},{25,1},{2,26},{10... | collective-permute-start | bytes 24584 | tf_op jit(solution)/shard_map/ppermute | solution.py:40
  31.6 0.7 collective-permute-done.11
  32.3 2.4 %collective-permute-done.10 = f32[1,2,2,4,128]{4,3,2,1,0:T(4,128)S(1)} collective-permute-done((f32[1,2,2,4,128]{4,3,2,1,0:T(4,128)S(1)}, f32[1,2,2,4,128]{4,3,2,1,0:T(4,128)S(1)}, u32[]{:S(2)}, u32[]{:S(2)}) %collective-permute-start.10) | collective-permute-done | bytes 8224 | tf_op jit(solution)/shard_map/ppermute | solution.py:40
  34.7 0.1 collective-permute-start.13
  34.8 2.5 %collective-permute-start.12 = (f32[3,2,2,4,128]{4,3,2,1,0:T(4,128)S(1)}, f32[3,2,2,4,128]{4,3,2,1,0:T(4,128)S(1)}, u32[]{:S(2)}, u32[]{:S(2)}) collective-permute-start(f32[3,2,2,4,128]{4,3,2,1,0:T(4,128)S(1)} %pad_maximum_fusion.4.mid_ref.all_refs_0_), channel_id=1, source_target_pairs={{0,3},{1,2},{2,1},{3,0},{4,7},{5,6},{6,5},{7,4},{8,11},{9,10},{10,... | collective-permute-start | bytes 73736 | tf_op jit(solution)/shard_map/ppermute | solution.py:40
  37.3 1.5 %collective-permute-done.13 = f32[3,2,2,4,128]{4,3,2,1,0:T(4,128)S(1)} collective-permute-done((f32[3,2,2,4,128]{4,3,2,1,0:T(4,128)S(1)}, f32[3,2,2,4,128]{4,3,2,1,0:T(4,128)S(1)}, u32[]{:S(2)}, u32[]{:S(2)}) %collective-permute-start.13) | collective-permute-done | bytes 24608 | tf_op jit(solution)/shard_map/ppermute | solution.py:39
  38.8 1.6 %collective-permute-done.12 = f32[3,2,2,4,128]{4,3,2,1,0:T(4,128)S(1)} collective-permute-done((f32[3,2,2,4,128]{4,3,2,1,0:T(4,128)S(1)}, f32[3,2,2,4,128]{4,3,2,1,0:T(4,128)S(1)}, u32[]{:S(2)}, u32[]{:S(2)}) %collective-permute-start.12) | collective-permute-done | bytes 24608 | tf_op jit(solution)/shard_map/ppermute | solution.py:40
  40.5 1.0 %shard_map.65 = (f32[4,128,128]{2,1,0:T(8,128)S(1)}, bf16[48,1536]{1,0:T(8,128)(2,1)S(1)}, f32[8,1536]{1,0:T(8,128)S(1)}, bf16[48,1536]{1,0:T(8,128)(2,1)S(1)}, ...) custom-call(f32[3,2,2,4,128]{4,3,2,1,0:T(4,128)S(1)} %pad_maximum_fusion.4.mid_ref.all_refs_0_, ...), custom_call_target="tpu_custom_call" | custom-call | flops 58982400 | bytes 4718592 | tf_op jit(solution)/shard_map/pallas_call | solution.py:444
  41.5 0.1 collective-permute-start.15
  41.6 1.3 %shard_map.66 = (f32[4,128,128]{2,1,0:T(8,128)S(1)}, f32[4,128,128]{2,1,0:T(8,128)S(1)}, bf16[48,1536]{1,0:T(8,128)(2,1)S(1)}, f32[8,1536]{1,0:T(8,128)S(1)}, bf16[4,128,48]{2,1,0:T(8,128)(2,1)S(1)}) custom-call(f32[3,2,2,4,128]{4,3,2,1,0:T(4,128)S(1)} %bitcast.87, f32[3,2,2,4,128]{4,3,2,1,0:T(4,128)S(1)} %bitcast.84, ...), custom_call_target="tpu_custom_call" | custom-call | flops 88473600 | bytes 7077888 | tf_op jit(solution)/shard_map/pallas_call | solution.py:444
  42.9 0.6 shard_map.67
  43.5 0.6 collective-permute-start.17
  44.2 2.4 %collective-permute-start.16 = (f32[1,2,4,128]{3,2,1,0:T(4,128)S(1)}, f32[1,2,4,128]{3,2,1,0:T(4,128)S(1)}, u32[]{:S(2)}, u32[]{:S(2)}) collective-permute-start(f32[1,2,4,128]{3,2,1,0:T(4,128)S(1)} %bitcast.120), channel_id=1, source_target_pairs={{0,24},{8,16},{16,8},{24,0},{1,25},{9,17},{17,9},{25,1},{2,26},{10... | collective-permute-start | bytes 12296 | tf_op jit(solution)/shard_map/ppermute | solution.py:40
  46.6 0.6 collective-permute-done.17
  47.2 1.4 %collective-permute-done.16 = f32[1,2,4,128]{3,2,1,0:T(4,128)S(1)} collective-permute-done((f32[1,2,4,128]{3,2,1,0:T(4,128)S(1)}, f32[1,2,4,128]{3,2,1,0:T(4,128)S(1)}, u32[]{:S(2)}, u32[]{:S(2)}) %collective-permute-start.16) | collective-permute-done | bytes 4128 | tf_op jit(solution)/shard_map/ppermute | solution.py:40
  48.7 0.0 collective-permute-done.18
  48.7 1.3 %shard_map.68 = (f32[4,4,128,128]{3,2,1,0:T(8,128)S(1)}, bf16[4,128,48]{2,1,0:T(8,128)(2,1)S(1)}) custom-call(f32[3,2,2,4,128]{4,3,2,1,0:T(4,128)S(1)} %pad_maximum_fusion.4.mid_ref.all_refs_0_, f32[8,128]{1,0:T(8,128)S(1)} %get-tuple-element.107.all_refs_1_, f32[8,128]{1,0:T(8,128)S(1)} %get-tuple-element.106.all_refs_2_, ...), custom_call_target="tpu_custom_call" | custom-call | flops 29491200 | bytes 2359296 | tf_op jit(solution)/shard_map/pallas_call | solution.py:444
  50.0 0.1 collective-permute-start.19
  50.1 1.8 %shard_map.69.column_ref = f32[4,4,128,128]{3,2,1,0:T(8,128)S(1)} custom-call(f32[8,128]{1,0:T(8,128)S(1)} %bitcast.98, f32[8,128]{1,0:T(8,128)S(1)} %bitcast.100, bf16[48,1536]{1,0:T(8,128)(2,1)S(1)} %get-tuple-element.100.part_ref.all_refs_5_, bf16[48,1536]{1,0:T(8,128)(2,1)S(1)} %get-tuple-element.108.all_refs_6_.edge_ref, ...), custom_call_target="tpu_custom_call" | custom-call | flops 39321600 | bytes 3145728 | tf_op jit(solution)/shard_map/pallas_call | solution.py:444
  51.9 0.0 collective-permute-done.19
  51.9 1.0 %shard_map.70 = (f32[3,4,128]{2,1,0:T(4,128)S(1)}, f32[4,4,128]{2,1,0:T(4,128)S(1)}) custom-call(f32[3,2,2,4,128]{4,3,2,1,0:T(4,128)S(1)} %pad_maximum_fusion.4.mid_ref.all_refs_0_, f32[8,128]{1,0:T(8,128)S(1)} %bitcast.104, f32[8,128]{1,0:T(8,128)S(1)} %bitcast.103, bf16[48,1536]{1,0:T(8,128)(2,1)S(1)} %get-tuple-element.101.ghost_ref.all_refs_7_, ...), custom_call_target="tpu_custom_call" | custom-call | flops 19660800 | bytes 1572864 | tf_op jit(solution)/shard_map/pallas_call | solution.py:444
  52.9 1.5 %collective-permute-start.21 = (f32[1,2,2,4,128]{4,3,2,1,0:T(4,128)S(1)}, f32[1,2,2,4,128]{4,3,2,1,0:T(4,128)S(1)}, u32[]{:S(2)}, u32[]{:S(2)}) collective-permute-start(f32[1,2,2,4,128]{4,3,2,1,0:T(4,128)S(1)} %bitcast.110), channel_id=1, source_target_pairs={{0,8},{8,0},{16,24},{24,16},{1,9},{9,1},{17,25},{25,17},{2,10},{10... | collective-permute-start | bytes 24584 | tf_op jit(solution)/shard_map/ppermute | solution.py:39
  54.4 1.5 %collective-permute-start.20 = (f32[1,2,2,4,128]{4,3,2,1,0:T(4,128)S(1)}, f32[1,2,2,4,128]{4,3,2,1,0:T(4,128)S(1)}, u32[]{:S(2)}, u32[]{:S(2)}) collective-permute-start(f32[1,2,2,4,128]{4,3,2,1,0:T(4,128)S(1)} %bitcast.111), channel_id=1, source_target_pairs={{0,24},{8,16},{16,8},{24,0},{1,25},{9,17},{17,9},{25,1},{2,26},{10... | collective-permute-start | bytes 24584 | tf_op jit(solution)/shard_map/ppermute | solution.py:40
  55.9 0.7 collective-permute-done.21
  56.6 2.4 %collective-permute-done.20 = f32[1,2,2,4,128]{4,3,2,1,0:T(4,128)S(1)} collective-permute-done((f32[1,2,2,4,128]{4,3,2,1,0:T(4,128)S(1)}, f32[1,2,2,4,128]{4,3,2,1,0:T(4,128)S(1)}, u32[]{:S(2)}, u32[]{:S(2)}) %collective-permute-start.20) | collective-permute-done | bytes 8224 | tf_op jit(solution)/shard_map/ppermute | solution.py:40
  59.0 0.2 collective-permute-start.23
  59.2 2.5 %collective-permute-start.22 = (f32[3,2,2,4,128]{4,3,2,1,0:T(4,128)S(1)}, f32[3,2,2,4,128]{4,3,2,1,0:T(4,128)S(1)}, u32[]{:S(2)}, u32[]{:S(2)}) collective-permute-start(f32[3,2,2,4,128]{4,3,2,1,0:T(4,128)S(1)} %pad_maximum_fusion.5.mid_ref.all_refs_0_), channel_id=1, source_target_pairs={{0,3},{1,2},{2,1},{3,0},{4,7},{5,6},{6,5},{7,4},{8,11},{9,10},{10,... | collective-permute-start | bytes 73736 | tf_op jit(solution)/shard_map/ppermute | solution.py:40
  61.7 1.4 %collective-permute-done.23 = f32[3,2,2,4,128]{4,3,2,1,0:T(4,128)S(1)} collective-permute-done((f32[3,2,2,4,128]{4,3,2,1,0:T(4,128)S(1)}, f32[3,2,2,4,128]{4,3,2,1,0:T(4,128)S(1)}, u32[]{:S(2)}, u32[]{:S(2)}) %collective-permute-start.23) | collective-permute-done | bytes 24608 | tf_op jit(solution)/shard_map/ppermute | solution.py:39
  63.1 1.7 %collective-permute-done.22 = f32[3,2,2,4,128]{4,3,2,1,0:T(4,128)S(1)} collective-permute-done((f32[3,2,2,4,128]{4,3,2,1,0:T(4,128)S(1)}, f32[3,2,2,4,128]{4,3,2,1,0:T(4,128)S(1)}, u32[]{:S(2)}, u32[]{:S(2)}) %collective-permute-start.22) | collective-permute-done | bytes 24608 | tf_op jit(solution)/shard_map/ppermute | solution.py:40
  64.9 1.0 %shard_map.71 = (f32[4,128,128]{2,1,0:T(8,128)S(1)}, bf16[48,1536]{1,0:T(8,128)(2,1)S(1)}, f32[8,1536]{1,0:T(8,128)S(1)}, bf16[48,1536]{1,0:T(8,128)(2,1)S(1)}, ...) custom-call(f32[3,2,2,4,128]{4,3,2,1,0:T(4,128)S(1)} %pad_maximum_fusion.5.mid_ref.all_refs_0_, ...), custom_call_target="tpu_custom_call" | custom-call | flops 58982400 | bytes 4718592 | tf_op jit(solution)/shard_map/pallas_call | solution.py:444
  65.9 0.1 collective-permute-start.25
  65.9 1.3 %shard_map.72 = (f32[4,128,128]{2,1,0:T(8,128)S(1)}, f32[4,128,128]{2,1,0:T(8,128)S(1)}, bf16[48,1536]{1,0:T(8,128)(2,1)S(1)}, f32[8,1536]{1,0:T(8,128)S(1)}, bf16[4,128,48]{2,1,0:T(8,128)(2,1)S(1)}) custom-call(f32[3,2,2,4,128]{4,3,2,1,0:T(4,128)S(1)} %bitcast.75, f32[3,2,2,4,128]{4,3,2,1,0:T(4,128)S(1)} %bitcast.72, ...), custom_call_target="tpu_custom_call" | custom-call | flops 88473600 | bytes 7077888 | tf_op jit(solution)/shard_map/pallas_call | solution.py:444
  67.3 0.6 shard_map.73
  67.9 0.6 collective-permute-start.27
  68.5 2.4 %collective-permute-start.26 = (f32[1,2,4,128]{3,2,1,0:T(4,128)S(1)}, f32[1,2,4,128]{3,2,1,0:T(4,128)S(1)}, u32[]{:S(2)}, u32[]{:S(2)}) collective-permute-start(f32[1,2,4,128]{3,2,1,0:T(4,128)S(1)} %bitcast.114), channel_id=1, source_target_pairs={{0,24},{8,16},{16,8},{24,0},{1,25},{9,17},{17,9},{25,1},{2,26},{10... | collective-permute-start | bytes 12296 | tf_op jit(solution)/shard_map/ppermute | solution.py:40
  71.0 0.6 collective-permute-done.27
  71.6 1.4 %collective-permute-done.26 = f32[1,2,4,128]{3,2,1,0:T(4,128)S(1)} collective-permute-done((f32[1,2,4,128]{3,2,1,0:T(4,128)S(1)}, f32[1,2,4,128]{3,2,1,0:T(4,128)S(1)}, u32[]{:S(2)}, u32[]{:S(2)}) %collective-permute-start.26) | collective-permute-done | bytes 4128 | tf_op jit(solution)/shard_map/ppermute | solution.py:40
  73.1 1.3 %shard_map.74 = (f32[4,4,128,128]{3,2,1,0:T(8,128)S(1)}, bf16[4,128,48]{2,1,0:T(8,128)(2,1)S(1)}) custom-call(f32[3,2,2,4,128]{4,3,2,1,0:T(4,128)S(1)} %pad_maximum_fusion.5.mid_ref.all_refs_0_, f32[8,128]{1,0:T(8,128)S(1)} %get-tuple-element.130.all_refs_1_, f32[8,128]{1,0:T(8,128)S(1)} %get-tuple-element.129.all_refs_2_, ...), custom_call_target="tpu_custom_call" | custom-call | flops 29491200 | bytes 2359296 | tf_op jit(solution)/shard_map/pallas_call | solution.py:444
  74.4 0.1 collective-permute-start.29
  74.5 1.6 %shard_map.75.column_ref = f32[4,4,128,128]{3,2,1,0:T(8,128)S(1)} custom-call(f32[8,128]{1,0:T(8,128)S(1)} %bitcast.90, f32[8,128]{1,0:T(8,128)S(1)} %bitcast.92, bf16[48,1536]{1,0:T(8,128)(2,1)S(1)} %get-tuple-element.123.part_ref.all_refs_5_, bf16[48,1536]{1,0:T(8,128)(2,1)S(1)} %get-tuple-element.131.all_refs_6_.edge_ref, ...), custom_call_target="tpu_custom_call" | custom-call | flops 39321600 | bytes 3145728 | tf_op jit(solution)/shard_map/pallas_call | solution.py:444
  76.1 1.6 %shard_map.76 = (f32[3,4,128]{2,1,0:T(4,128)}, f32[3,4,128]{2,1,0:T(4,128)}) custom-call(f32[3,2,2,4,128]{4,3,2,1,0:T(4,128)S(1)} %pad_maximum_fusion.5.mid_ref.all_refs_0_, f32[8,128]{1,0:T(8,128)S(1)} %bitcast.106, f32[8,128]{1,0:T(8,128)S(1)} %bitcast.105, bf16[48,1536]{1,0:T(8,128)(2,1)S(1)} %get-tuple-element.124.ghost_ref.all_refs_7_, ...), custom_call_target="tpu_custom_call" | custom-call | flops 19660800 | bytes 1572864 | tf_op jit(solution)/shard_map/pallas_call | solution.py:444
  (45 shorter events, 0.2 us)
Async XLA Ops:
  1.5 4.7 %collective-permute-start.1 = (f32[1,2,2,4,128]{4,3,2,1,0:T(4,128)S(1)}, f32[1,2,2,4,128]{4,3,2,1,0:T(4,128)S(1)}, u32[]{:S(2)}, u32[]{:S(2)}) collective-permute-start(f32[1,2,2,4,128]{4,3,2,1,0:T(4,128)S(1)} %get-tuple-element.73), channel_id=1, source_target_pairs={{0,8},{8,0},{16,24},{24,16},{1,9},{9,1},{17,25},{25,17},{2,10},{10... | collective-permute-start | bytes 24584 | tf_op jit(solution)/shard_map/ppermute | solution.py:39
  4.5 4.5 %collective-permute-start = (f32[1,2,2,4,128]{4,3,2,1,0:T(4,128)S(1)}, f32[1,2,2,4,128]{4,3,2,1,0:T(4,128)S(1)}, u32[]{:S(2)}, u32[]{:S(2)}) collective-permute-start(f32[1,2,2,4,128]{4,3,2,1,0:T(4,128)S(1)} %get-tuple-element.73), channel_id=1, source_target_pairs={{0,24},{8,16},{16,8},{24,0},{1,25},{9,17},{17,9},{25,1},{2,26},{10... | collective-permute-start | bytes 24584 | tf_op jit(solution)/shard_map/ppermute | solution.py:40
  9.1 4.1 %collective-permute-start.3 = (f32[3,2,2,4,128]{4,3,2,1,0:T(4,128)S(1)}, f32[3,2,2,4,128]{4,3,2,1,0:T(4,128)S(1)}, u32[]{:S(2)}, u32[]{:S(2)}) collective-permute-start(f32[3,2,2,4,128]{4,3,2,1,0:T(4,128)S(1)} %pad_maximum_fusion.3.mid_ref.all_refs_0_), channel_id=1, source_target_pairs={{0,1},{1,0},{2,3},{3,2},{4,5},{5,4},{6,7},{7,6},{8,9},{9,8},{10,11... | collective-permute-start | bytes 73736 | tf_op jit(solution)/shard_map/ppermute | solution.py:39
  10.7 5.6 %collective-permute-start.2 = (f32[3,2,2,4,128]{4,3,2,1,0:T(4,128)S(1)}, f32[3,2,2,4,128]{4,3,2,1,0:T(4,128)S(1)}, u32[]{:S(2)}, u32[]{:S(2)}) collective-permute-start(f32[3,2,2,4,128]{4,3,2,1,0:T(4,128)S(1)} %pad_maximum_fusion.3.mid_ref.all_refs_0_), channel_id=1, source_target_pairs={{0,3},{1,2},{2,1},{3,0},{4,7},{5,6},{6,5},{7,4},{8,11},{9,10},{10,... | collective-permute-start | bytes 73736 | tf_op jit(solution)/shard_map/ppermute | solution.py:40
  13.2 3.2 %collective-permute-start.4 = (f32[3,2,2,4,128]{4,3,2,1,0:T(4,128)S(1)}, f32[3,2,2,4,128]{4,3,2,1,0:T(4,128)S(1)}, u32[]{:S(2)}, u32[]{:S(2)}) collective-permute-start(f32[3,2,2,4,128]{4,3,2,1,0:T(4,128)S(1)} %pad_maximum_fusion.3.mid_ref.all_refs_0_), channel_id=1, source_target_pairs={{0,4},{4,0},{1,5},{5,1},{2,6},{6,2},{3,7},{7,3},{8,12},{12,8},{9,1... | collective-permute-start | bytes 73736 | tf_op jit(solution)/shard_map/ppermute | solution.py:28
  17.4 1.4 %collective-permute-start.5 = (f32[3,2,4,4,128]{4,3,2,1,0:T(4,128)S(1)}, f32[3,2,4,4,128]{4,3,2,1,0:T(4,128)S(1)}, u32[]{:S(2)}, u32[]{:S(2)}) collective-permute-start(f32[3,2,4,4,128]{4,3,2,1,0:T(4,128)S(1)} %pad_maximum_fusion), channel_id=1, source_target_pairs={{0,4},{4,0},{1,5},{5,1},{2,6},{6,2},{3,7},{7,3},{8,12},{12,8},{9,1... | collective-permute-start | bytes 147464 | tf_op jit(solution)/shard_map/ppermute | solution.py:28
  19.4 3.7 %collective-permute-start.7 = (f32[1,2,4,128]{3,2,1,0:T(4,128)S(1)}, f32[1,2,4,128]{3,2,1,0:T(4,128)S(1)}, u32[]{:S(2)}, u32[]{:S(2)}) collective-permute-start(f32[1,2,4,128]{3,2,1,0:T(4,128)S(1)} %bitcast.116), channel_id=1, source_target_pairs={{0,8},{8,0},{16,24},{24,16},{1,9},{9,1},{17,25},{25,17},{2,10},{10... | collective-permute-start | bytes 12296 | tf_op jit(solution)/shard_map/ppermute | solution.py:39
  20.0 4.5 %collective-permute-start.6 = (f32[1,2,4,128]{3,2,1,0:T(4,128)S(1)}, f32[1,2,4,128]{3,2,1,0:T(4,128)S(1)}, u32[]{:S(2)}, u32[]{:S(2)}) collective-permute-start(f32[1,2,4,128]{3,2,1,0:T(4,128)S(1)} %bitcast.117), channel_id=1, source_target_pairs={{0,24},{8,16},{16,8},{24,0},{1,25},{9,17},{17,9},{25,1},{2,26},{10... | collective-permute-start | bytes 12296 | tf_op jit(solution)/shard_map/ppermute | solution.py:40
  22.5 2.1 %collective-permute-start.8 = (f32[1,2,4,128]{3,2,1,0:T(4,128)S(1)}, f32[1,2,4,128]{3,2,1,0:T(4,128)S(1)}, u32[]{:S(2)}, u32[]{:S(2)}) collective-permute-start(f32[1,2,4,128]{3,2,1,0:T(4,128)S(1)} %bitcast.118), channel_id=1, source_target_pairs={{0,4},{4,0},{1,5},{5,1},{2,6},{6,2},{3,7},{7,3},{8,12},{12,8},{9,1... | collective-permute-start | bytes 12296 | tf_op jit(solution)/shard_map/ppermute | solution.py:28
  25.9 1.7 %collective-permute-start.9 = (f32[2,2,4,128]{3,2,1,0:T(4,128)S(1)}, f32[2,2,4,128]{3,2,1,0:T(4,128)S(1)}, u32[]{:S(2)}, u32[]{:S(2)}) collective-permute-start(f32[2,2,4,128]{3,2,1,0:T(4,128)S(1)} %pad_maximum_fusion.6), channel_id=1, source_target_pairs={{0,4},{4,0},{1,5},{5,1},{2,6},{6,2},{3,7},{7,3},{8,12},{12,8},{9,1... | collective-permute-start | bytes 24584 | tf_op jit(solution)/shard_map/ppermute | solution.py:28
  28.6 3.7 %collective-permute-start.11 = (f32[1,2,2,4,128]{4,3,2,1,0:T(4,128)S(1)}, f32[1,2,2,4,128]{4,3,2,1,0:T(4,128)S(1)}, u32[]{:S(2)}, u32[]{:S(2)}) collective-permute-start(f32[1,2,2,4,128]{4,3,2,1,0:T(4,128)S(1)} %bitcast.107), channel_id=1, source_target_pairs={{0,8},{8,0},{16,24},{24,16},{1,9},{9,1},{17,25},{25,17},{2,10},{10... | collective-permute-start | bytes 24584 | tf_op jit(solution)/shard_map/ppermute | solution.py:39
  30.1 4.5 %collective-permute-start.10 = (f32[1,2,2,4,128]{4,3,2,1,0:T(4,128)S(1)}, f32[1,2,2,4,128]{4,3,2,1,0:T(4,128)S(1)}, u32[]{:S(2)}, u32[]{:S(2)}) collective-permute-start(f32[1,2,2,4,128]{4,3,2,1,0:T(4,128)S(1)} %bitcast.108), channel_id=1, source_target_pairs={{0,24},{8,16},{16,8},{24,0},{1,25},{9,17},{17,9},{25,1},{2,26},{10... | collective-permute-start | bytes 24584 | tf_op jit(solution)/shard_map/ppermute | solution.py:40
  34.7 4.1 %collective-permute-start.13 = (f32[3,2,2,4,128]{4,3,2,1,0:T(4,128)S(1)}, f32[3,2,2,4,128]{4,3,2,1,0:T(4,128)S(1)}, u32[]{:S(2)}, u32[]{:S(2)}) collective-permute-start(f32[3,2,2,4,128]{4,3,2,1,0:T(4,128)S(1)} %pad_maximum_fusion.4.mid_ref.all_refs_0_), channel_id=1, source_target_pairs={{0,1},{1,0},{2,3},{3,2},{4,5},{5,4},{6,7},{7,6},{8,9},{9,8},{10,11... | collective-permute-start | bytes 73736 | tf_op jit(solution)/shard_map/ppermute | solution.py:39
  34.8 5.7 %collective-permute-start.12 = (f32[3,2,2,4,128]{4,3,2,1,0:T(4,128)S(1)}, f32[3,2,2,4,128]{4,3,2,1,0:T(4,128)S(1)}, u32[]{:S(2)}, u32[]{:S(2)}) collective-permute-start(f32[3,2,2,4,128]{4,3,2,1,0:T(4,128)S(1)} %pad_maximum_fusion.4.mid_ref.all_refs_0_), channel_id=1, source_target_pairs={{0,3},{1,2},{2,1},{3,0},{4,7},{5,6},{6,5},{7,4},{8,11},{9,10},{10,... | collective-permute-start | bytes 73736 | tf_op jit(solution)/shard_map/ppermute | solution.py:40
  37.3 3.2 %collective-permute-start.14 = (f32[3,2,2,4,128]{4,3,2,1,0:T(4,128)S(1)}, f32[3,2,2,4,128]{4,3,2,1,0:T(4,128)S(1)}, u32[]{:S(2)}, u32[]{:S(2)}) collective-permute-start(f32[3,2,2,4,128]{4,3,2,1,0:T(4,128)S(1)} %pad_maximum_fusion.4.mid_ref.all_refs_0_), channel_id=1, source_target_pairs={{0,4},{4,0},{1,5},{5,1},{2,6},{6,2},{3,7},{7,3},{8,12},{12,8},{9,1... | collective-permute-start | bytes 73736 | tf_op jit(solution)/shard_map/ppermute | solution.py:28
  41.5 1.4 %collective-permute-start.15 = (f32[3,2,4,4,128]{4,3,2,1,0:T(4,128)S(1)}, f32[3,2,4,4,128]{4,3,2,1,0:T(4,128)S(1)}, u32[]{:S(2)}, u32[]{:S(2)}) collective-permute-start(f32[3,2,4,4,128]{4,3,2,1,0:T(4,128)S(1)} %pad_maximum_fusion.1), channel_id=1, source_target_pairs={{0,4},{4,0},{1,5},{5,1},{2,6},{6,2},{3,7},{7,3},{8,12},{12,8},{9,1... | collective-permute-start | bytes 147464 | tf_op jit(solution)/shard_map/ppermute | solution.py:28
  43.5 3.7 %collective-permute-start.17 = (f32[1,2,4,128]{3,2,1,0:T(4,128)S(1)}, f32[1,2,4,128]{3,2,1,0:T(4,128)S(1)}, u32[]{:S(2)}, u32[]{:S(2)}) collective-permute-start(f32[1,2,4,128]{3,2,1,0:T(4,128)S(1)} %bitcast.119), channel_id=1, source_target_pairs={{0,8},{8,0},{16,24},{24,16},{1,9},{9,1},{17,25},{25,17},{2,10},{10... | collective-permute-start | bytes 12296 | tf_op jit(solution)/shard_map/ppermute | solution.py:39
  44.2 4.5 %collective-permute-start.16 = (f32[1,2,4,128]{3,2,1,0:T(4,128)S(1)}, f32[1,2,4,128]{3,2,1,0:T(4,128)S(1)}, u32[]{:S(2)}, u32[]{:S(2)}) collective-permute-start(f32[1,2,4,128]{3,2,1,0:T(4,128)S(1)} %bitcast.120), channel_id=1, source_target_pairs={{0,24},{8,16},{16,8},{24,0},{1,25},{9,17},{17,9},{25,1},{2,26},{10... | collective-permute-start | bytes 12296 | tf_op jit(solution)/shard_map/ppermute | solution.py:40
  46.6 2.1 %collective-permute-start.18 = (f32[1,2,4,128]{3,2,1,0:T(4,128)S(1)}, f32[1,2,4,128]{3,2,1,0:T(4,128)S(1)}, u32[]{:S(2)}, u32[]{:S(2)}) collective-permute-start(f32[1,2,4,128]{3,2,1,0:T(4,128)S(1)} %bitcast.121), channel_id=1, source_target_pairs={{0,4},{4,0},{1,5},{5,1},{2,6},{6,2},{3,7},{7,3},{8,12},{12,8},{9,1... | collective-permute-start | bytes 12296 | tf_op jit(solution)/shard_map/ppermute | solution.py:28
  50.0 1.9 %collective-permute-start.19 = (f32[2,2,4,128]{3,2,1,0:T(4,128)S(1)}, f32[2,2,4,128]{3,2,1,0:T(4,128)S(1)}, u32[]{:S(2)}, u32[]{:S(2)}) collective-permute-start(f32[2,2,4,128]{3,2,1,0:T(4,128)S(1)} %pad_maximum_fusion.7), channel_id=1, source_target_pairs={{0,4},{4,0},{1,5},{5,1},{2,6},{6,2},{3,7},{7,3},{8,12},{12,8},{9,1... | collective-permute-start | bytes 24584 | tf_op jit(solution)/shard_map/ppermute | solution.py:28
  52.9 3.7 %collective-permute-start.21 = (f32[1,2,2,4,128]{4,3,2,1,0:T(4,128)S(1)}, f32[1,2,2,4,128]{4,3,2,1,0:T(4,128)S(1)}, u32[]{:S(2)}, u32[]{:S(2)}) collective-permute-start(f32[1,2,2,4,128]{4,3,2,1,0:T(4,128)S(1)} %bitcast.110), channel_id=1, source_target_pairs={{0,8},{8,0},{16,24},{24,16},{1,9},{9,1},{17,25},{25,17},{2,10},{10... | collective-permute-start | bytes 24584 | tf_op jit(solution)/shard_map/ppermute | solution.py:39
  54.4 4.5 %collective-permute-start.20 = (f32[1,2,2,4,128]{4,3,2,1,0:T(4,128)S(1)}, f32[1,2,2,4,128]{4,3,2,1,0:T(4,128)S(1)}, u32[]{:S(2)}, u32[]{:S(2)}) collective-permute-start(f32[1,2,2,4,128]{4,3,2,1,0:T(4,128)S(1)} %bitcast.111), channel_id=1, source_target_pairs={{0,24},{8,16},{16,8},{24,0},{1,25},{9,17},{17,9},{25,1},{2,26},{10... | collective-permute-start | bytes 24584 | tf_op jit(solution)/shard_map/ppermute | solution.py:40
  59.0 4.1 %collective-permute-start.23 = (f32[3,2,2,4,128]{4,3,2,1,0:T(4,128)S(1)}, f32[3,2,2,4,128]{4,3,2,1,0:T(4,128)S(1)}, u32[]{:S(2)}, u32[]{:S(2)}) collective-permute-start(f32[3,2,2,4,128]{4,3,2,1,0:T(4,128)S(1)} %pad_maximum_fusion.5.mid_ref.all_refs_0_), channel_id=1, source_target_pairs={{0,1},{1,0},{2,3},{3,2},{4,5},{5,4},{6,7},{7,6},{8,9},{9,8},{10,11... | collective-permute-start | bytes 73736 | tf_op jit(solution)/shard_map/ppermute | solution.py:39
  59.2 5.6 %collective-permute-start.22 = (f32[3,2,2,4,128]{4,3,2,1,0:T(4,128)S(1)}, f32[3,2,2,4,128]{4,3,2,1,0:T(4,128)S(1)}, u32[]{:S(2)}, u32[]{:S(2)}) collective-permute-start(f32[3,2,2,4,128]{4,3,2,1,0:T(4,128)S(1)} %pad_maximum_fusion.5.mid_ref.all_refs_0_), channel_id=1, source_target_pairs={{0,3},{1,2},{2,1},{3,0},{4,7},{5,6},{6,5},{7,4},{8,11},{9,10},{10,... | collective-permute-start | bytes 73736 | tf_op jit(solution)/shard_map/ppermute | solution.py:40
  61.7 3.2 %collective-permute-start.24 = (f32[3,2,2,4,128]{4,3,2,1,0:T(4,128)S(1)}, f32[3,2,2,4,128]{4,3,2,1,0:T(4,128)S(1)}, u32[]{:S(2)}, u32[]{:S(2)}) collective-permute-start(f32[3,2,2,4,128]{4,3,2,1,0:T(4,128)S(1)} %pad_maximum_fusion.5.mid_ref.all_refs_0_), channel_id=1, source_target_pairs={{0,4},{4,0},{1,5},{5,1},{2,6},{6,2},{3,7},{7,3},{8,12},{12,8},{9,1... | collective-permute-start | bytes 73736 | tf_op jit(solution)/shard_map/ppermute | solution.py:28
  65.9 1.4 %collective-permute-start.25 = (f32[3,2,4,4,128]{4,3,2,1,0:T(4,128)S(1)}, f32[3,2,4,4,128]{4,3,2,1,0:T(4,128)S(1)}, u32[]{:S(2)}, u32[]{:S(2)}) collective-permute-start(f32[3,2,4,4,128]{4,3,2,1,0:T(4,128)S(1)} %pad_maximum_fusion.2), channel_id=1, source_target_pairs={{0,4},{4,0},{1,5},{5,1},{2,6},{6,2},{3,7},{7,3},{8,12},{12,8},{9,1... | collective-permute-start | bytes 147464 | tf_op jit(solution)/shard_map/ppermute | solution.py:28
  67.9 3.7 %collective-permute-start.27 = (f32[1,2,4,128]{3,2,1,0:T(4,128)S(1)}, f32[1,2,4,128]{3,2,1,0:T(4,128)S(1)}, u32[]{:S(2)}, u32[]{:S(2)}) collective-permute-start(f32[1,2,4,128]{3,2,1,0:T(4,128)S(1)} %bitcast.113), channel_id=1, source_target_pairs={{0,8},{8,0},{16,24},{24,16},{1,9},{9,1},{17,25},{25,17},{2,10},{10... | collective-permute-start | bytes 12296 | tf_op jit(solution)/shard_map/ppermute | solution.py:39
  68.5 4.5 %collective-permute-start.26 = (f32[1,2,4,128]{3,2,1,0:T(4,128)S(1)}, f32[1,2,4,128]{3,2,1,0:T(4,128)S(1)}, u32[]{:S(2)}, u32[]{:S(2)}) collective-permute-start(f32[1,2,4,128]{3,2,1,0:T(4,128)S(1)} %bitcast.114), channel_id=1, source_target_pairs={{0,24},{8,16},{16,8},{24,0},{1,25},{9,17},{17,9},{25,1},{2,26},{10... | collective-permute-start | bytes 12296 | tf_op jit(solution)/shard_map/ppermute | solution.py:40
  71.0 2.1 %collective-permute-start.28 = (f32[1,2,4,128]{3,2,1,0:T(4,128)S(1)}, f32[1,2,4,128]{3,2,1,0:T(4,128)S(1)}, u32[]{:S(2)}, u32[]{:S(2)}) collective-permute-start(f32[1,2,4,128]{3,2,1,0:T(4,128)S(1)} %bitcast.115), channel_id=1, source_target_pairs={{0,4},{4,0},{1,5},{5,1},{2,6},{6,2},{3,7},{7,3},{8,12},{12,8},{9,1... | collective-permute-start | bytes 12296 | tf_op jit(solution)/shard_map/ppermute | solution.py:28
  74.4 1.7 %collective-permute-start.29 = (f32[2,2,4,128]{3,2,1,0:T(4,128)S(1)}, f32[2,2,4,128]{3,2,1,0:T(4,128)S(1)}, u32[]{:S(2)}, u32[]{:S(2)}) collective-permute-start(f32[2,2,4,128]{3,2,1,0:T(4,128)S(1)} %pad_maximum_fusion.8), channel_id=1, source_target_pairs={{0,4},{4,0},{1,5},{5,1},{2,6},{6,2},{3,7},{7,3},{8,12},{12,8},{9,1... | collective-permute-start | bytes 24584 | tf_op jit(solution)/shard_map/ppermute | solution.py:28

commit v5 on v4

--- a/solution.py
+++ b/solution.py
@@ -30,11 +30,10 @@
             lax.slice_in_dim(other, width, size, axis=dim),
             lax.slice_in_dim(other, 0, width, axis=dim),
         )
-    if count % 2:
+    if even is None or count % 2:
         below = lax.ppermute(tail, axis, [(i, (i + 1) % count) for i in range(count)])
         above = lax.ppermute(head, axis, [((i + 1) % count, i) for i in range(count)])
         return below, above
-    even = lax.axis_index(axis) % 2 == 0 if even is None else even
     first, second = (cells, cells) if size == width else (jnp.where(even, tail, head), jnp.where(even, head, tail))
     first = lax.ppermute(first, axis, [(i, i ^ 1) for i in range(count)])
     second = lax.ppermute(second, axis, [(i, (i - 1 if i % 2 == 0 else i + 1) % count) for i in range(count)])
@@ -453,9 +452,11 @@
             ),
         )(*operands)
 
-    even = {axis: lax.optimization_barrier(lax.axis_index(axis) % 2 == 0) for axis in ("gx", "gz")}
-
-    def evaluate(location, velocity, stage):
+    pairs = {axis: lax.optimization_barrier(lax.axis_index(axis) % 2 == 0) for axis in ("gx", "gz")}
+
+    rings = {"gx": None, "gz": None}
+
+    def evaluate(location, velocity, stage, even):
         mid = ring_halo(location, "gx", 0, 1, even["gx"])
         mid_below, mid_above = neighbours(mid, "gy", 1, 1)
         low, high = neighbours(mid, "gz", 2, 2, even["gz"])
@@ -536,8 +537,8 @@
         compiler_params=pltpu.CompilerParams(vmem_limit_bytes=GRANT),
         name="prepare",
     )(*arrays)
-    for stage in ("first", "middle", "last"):
-        velocity, moved = evaluate(location.reshape(cx, cy, cz, 4, slots), velocity, stage)
+    for sweep, stage in enumerate(("first", "middle", "last")):
+        velocity, moved = evaluate(location.reshape(cx, cy, cz, 4, slots), velocity, stage, pairs if sweep == 0 else rings)
         location = moved
     new_positions = moved
     return new_positions.reshape(positions.shape), velocity.reshape(positions.shape)

time: 77.9 us -> 75.9 us (0.974)
  starting transfers between devices: 29.6 us -> 26.4 us
  waiting for transfers between devices: 24.9 us -> 26.3 us
    ppermute x0 -> x12, waiting for transfers between devices: none -> 17.9 us  [the longest x6 13.1 us: neighbours(): lax.ppermute(tail, axis, [(i, (i + 1) % count) for i in range(count)])]
    ppermute x0 -> x12, starting transfers between devices: none -> 13.2 us  [the longest x6 6.88 us: neighbours(): lax.ppermute(tail, axis, [(i, (i + 1) % count) for i in range(count)])]
    ppermute x9 -> x3, starting transfers between devices: 19.3 us -> 6.39 us  [neighbours(): lax.ppermute(second, axis, [(i, (i - 1 if i % 2 == 0 else i + 1) % count)...]
    ppermute x9 -> x3, waiting for transfers between devices: 18.5 us -> 7.5 us  [neighbours(): lax.ppermute(second, axis, [(i, (i - 1 if i % 2 == 0 else i + 1) % count)...]
    ppermute x9 -> x3, waiting for transfers between devices: 6.33 us -> 0.79 us  [neighbours(): first = lax.ppermute(first, axis, [(i, i ^ 1) for i in range(count)])]
    ppermute x9 -> x3, starting transfers between devices: 9.87 us -> 5.27 us  [neighbours(): first = lax.ppermute(first, axis, [(i, i ^ 1) for i in range(count)])]
    ppermute x12, starting transfers between devices: 0.44 us -> 1.54 us  [neighbours(): other = lax.ppermute(cells, axis, [(0, 1), (1, 0)])]
  transfers between devices with their start and end apart: 30 -> 30, of which waited for: 17 -> 17; matrix products, arithmetic and copies ran while one was open for 0% -> 0% of each run, Pallas kernels for 11% -> 17%
where the time goes in v5:
time: 75.9 us; the launch traced here: 75.7 us
  starting transfers between devices  26.4 us (35%)
  waiting for transfers between devices  26.3 us (35%)
  Pallas kernels  21.8 us (29%)
  between operations  0.98 us (1%)
    pallas_call x18, Pallas kernels, call(): pl.pallas_call(kernel, out_shape=out_shape, in_specs=[vmem] * len(operand...  21 us
    ppermute x6, waiting for transfers between devices, neighbours(): lax.ppermute(tail, axis, [(i, (i + 1) % count) for i in range(count)])  13.1 us
    ppermute x3, waiting for transfers between devices, neighbours(): lax.ppermute(second, axis, [(i, (i - 1 if i % 2 == 0 else i + 1) % count)...  7.5 us
    ppermute x6, starting transfers between devices, neighbours(): lax.ppermute(tail, axis, [(i, (i + 1) % count) for i in range(count)])  6.88 us
    ppermute x3, starting transfers between devices, neighbours(): lax.ppermute(second, axis, [(i, (i - 1 if i % 2 == 0 else i + 1) % count)...  6.39 us
    ppermute x6, starting transfers between devices, neighbours(): lax.ppermute(head, axis, [((i + 1) % count, i) for i in range(count)])  6.35 us
    ppermute x3, starting transfers between devices, neighbours(): first = lax.ppermute(first, axis, [(i, i ^ 1) for i in range(count)])  5.27 us
    ppermute x6, waiting for transfers between devices, neighbours(): lax.ppermute(head, axis, [((i + 1) % count, i) for i in range(count)])  4.88 us
  transfers between devices with their start and end apart: 30, of which 17 were waited for; matrix products, arithmetic and copies ran while one was open for 0% of the time, Pallas kernels for 17%

profile of v5, /device:TPU:0, one launch (start us, length us, event | category | flops | bytes accessed | tf_op | source)
XLA Modules:
  0.0 75.7 jit_solution(8617196209122742641)
XLA Ops:
  0.6 0.8 %prepare.1 = (f32[1,2,2,4,128]{4,3,2,1,0:T(4,128)S(1)}, f32[3,4,128]{2,1,0:T(4,128)S(1)}) custom-call(f32[3,1,2,2,128]{4,3,2,1,0:T(2,128)} %pos_hbm.1, f32[3,1,2,2,128]{4,3,2,1,0:T(2,128)} %vel_hbm.1, s32[1,2,2,128]{3,2,1,0:T(2,128)} %species_hbm.1, s32[1,2,2]{2,1,0:T(2,128)} %counts_hbm.1), custom_call_target="tpu_custom_call" | custom-call | tf_op jit(solution)/shard_map/prepare/pallas_call | solution.py:531
  1.5 3.0 %collective-permute-start.1 = (f32[1,2,2,4,128]{4,3,2,1,0:T(4,128)S(1)}, f32[1,2,2,4,128]{4,3,2,1,0:T(4,128)S(1)}, u32[]{:S(2)}, u32[]{:S(2)}) collective-permute-start(f32[1,2,2,4,128]{4,3,2,1,0:T(4,128)S(1)} %get-tuple-element.73), channel_id=1, source_target_pairs={{0,8},{8,0},{16,24},{24,16},{1,9},{9,1},{17,25},{25,17},{2,10},{10... | collective-permute-start | bytes 24584 | tf_op jit(solution)/shard_map/ppermute | solution.py:38
  4.5 1.5 %collective-permute-start = (f32[1,2,2,4,128]{4,3,2,1,0:T(4,128)S(1)}, f32[1,2,2,4,128]{4,3,2,1,0:T(4,128)S(1)}, u32[]{:S(2)}, u32[]{:S(2)}) collective-permute-start(f32[1,2,2,4,128]{4,3,2,1,0:T(4,128)S(1)} %get-tuple-element.73), channel_id=1, source_target_pairs={{0,24},{8,16},{16,8},{24,0},{1,25},{9,17},{17,9},{25,1},{2,26},{10... | collective-permute-start | bytes 24584 | tf_op jit(solution)/shard_map/ppermute | solution.py:39
  6.0 0.1 collective-permute-done.1
  6.1 2.9 %collective-permute-done = f32[1,2,2,4,128]{4,3,2,1,0:T(4,128)S(1)} collective-permute-done((f32[1,2,2,4,128]{4,3,2,1,0:T(4,128)S(1)}, f32[1,2,2,4,128]{4,3,2,1,0:T(4,128)S(1)}, u32[]{:S(2)}, u32[]{:S(2)}) %collective-permute-start) | collective-permute-done | bytes 8224 | tf_op jit(solution)/shard_map/ppermute | solution.py:39
  9.1 1.6 %collective-permute-start.3 = (f32[3,2,2,4,128]{4,3,2,1,0:T(4,128)S(1)}, f32[3,2,2,4,128]{4,3,2,1,0:T(4,128)S(1)}, u32[]{:S(2)}, u32[]{:S(2)}) collective-permute-start(f32[3,2,2,4,128]{4,3,2,1,0:T(4,128)S(1)} %pad_maximum_fusion.3.mid_ref.all_refs_0_), channel_id=1, source_target_pairs={{0,1},{1,0},{2,3},{3,2},{4,5},{5,4},{6,7},{7,6},{8,9},{9,8},{10,11... | collective-permute-start | bytes 73736 | tf_op jit(solution)/shard_map/ppermute | solution.py:38
  10.7 2.5 %collective-permute-start.2 = (f32[3,2,2,4,128]{4,3,2,1,0:T(4,128)S(1)}, f32[3,2,2,4,128]{4,3,2,1,0:T(4,128)S(1)}, u32[]{:S(2)}, u32[]{:S(2)}) collective-permute-start(f32[3,2,2,4,128]{4,3,2,1,0:T(4,128)S(1)} %pad_maximum_fusion.3.mid_ref.all_refs_0_), channel_id=1, source_target_pairs={{0,3},{1,2},{2,1},{3,0},{4,7},{5,6},{6,5},{7,4},{8,11},{9,10},{10,... | collective-permute-start | bytes 73736 | tf_op jit(solution)/shard_map/ppermute | solution.py:39
  13.2 3.1 %collective-permute-done.2 = f32[3,2,2,4,128]{4,3,2,1,0:T(4,128)S(1)} collective-permute-done((f32[3,2,2,4,128]{4,3,2,1,0:T(4,128)S(1)}, f32[3,2,2,4,128]{4,3,2,1,0:T(4,128)S(1)}, u32[]{:S(2)}, u32[]{:S(2)}) %collective-permute-start.2) | collective-permute-done | bytes 24608 | tf_op jit(solution)/shard_map/ppermute | solution.py:39
  16.4 1.0 %shard_map.59 = (f32[4,128,128]{2,1,0:T(8,128)S(1)}, bf16[48,1536]{1,0:T(8,128)(2,1)S(1)}, f32[8,1536]{1,0:T(8,128)S(1)}, bf16[48,1536]{1,0:T(8,128)(2,1)S(1)}, ...) custom-call(f32[3,2,2,4,128]{4,3,2,1,0:T(4,128)S(1)} %pad_maximum_fusion.3.mid_ref.all_refs_0_, ...), custom_call_target="tpu_custom_call" | custom-call | flops 58982400 | bytes 4718592 | tf_op jit(solution)/shard_map/pallas_call | solution.py:443
  17.4 0.1 collective-permute-start.5
  17.4 1.3 %shard_map.60 = (f32[4,128,128]{2,1,0:T(8,128)S(1)}, f32[4,128,128]{2,1,0:T(8,128)S(1)}, bf16[48,1536]{1,0:T(8,128)(2,1)S(1)}, f32[8,1536]{1,0:T(8,128)S(1)}, bf16[4,128,48]{2,1,0:T(8,128)(2,1)S(1)}) custom-call(f32[3,2,2,4,128]{4,3,2,1,0:T(4,128)S(1)} %bitcast.51, f32[3,2,2,4,128]{4,3,2,1,0:T(4,128)S(1)} %bitcast.48, ...), custom_call_target="tpu_custom_call" | custom-call | flops 88473600 | bytes 7077888 | tf_op jit(solution)/shard_map/pallas_call | solution.py:443
  18.8 0.6 shard_map.61
  19.4 0.6 collective-permute-start.7
  20.0 2.4 %collective-permute-start.6 = (f32[1,2,4,128]{3,2,1,0:T(4,128)S(1)}, f32[1,2,4,128]{3,2,1,0:T(4,128)S(1)}, u32[]{:S(2)}, u32[]{:S(2)}) collective-permute-start(f32[1,2,4,128]{3,2,1,0:T(4,128)S(1)} %bitcast.74), channel_id=1, source_target_pairs={{0,24},{8,16},{16,8},{24,0},{1,25},{9,17},{17,9},{25,1},{2,26},{10... | collective-permute-start | bytes 12296 | tf_op jit(solution)/shard_map/ppermute | solution.py:39
  22.5 0.0 collective-permute-start.8
  22.5 0.6 collective-permute-done.7
  23.1 1.4 %collective-permute-done.6 = f32[1,2,4,128]{3,2,1,0:T(4,128)S(1)} collective-permute-done((f32[1,2,4,128]{3,2,1,0:T(4,128)S(1)}, f32[1,2,4,128]{3,2,1,0:T(4,128)S(1)}, u32[]{:S(2)}, u32[]{:S(2)}) %collective-permute-start.6) | collective-permute-done | bytes 4128 | tf_op jit(solution)/shard_map/ppermute | solution.py:39
  24.5 0.0 collective-permute-done.8
  24.6 1.3 %shard_map.62 = (f32[4,4,128,128]{3,2,1,0:T(8,128)S(1)}, bf16[4,128,48]{2,1,0:T(8,128)(2,1)S(1)}) custom-call(f32[3,2,2,4,128]{4,3,2,1,0:T(4,128)S(1)} %pad_maximum_fusion.3.mid_ref.all_refs_0_, f32[8,128]{1,0:T(8,128)S(1)} %get-tuple-element.84.all_refs_1_, f32[8,128]{1,0:T(8,128)S(1)} %get-tuple-element.83.all_refs_2_, ...), custom_call_target="tpu_custom_call" | custom-call | flops 29491200 | bytes 2359296 | tf_op jit(solution)/shard_map/pallas_call | solution.py:443
  25.9 0.1 collective-permute-start.9
  26.0 1.6 %shard_map.63.column_ref = f32[4,4,128,128]{3,2,1,0:T(8,128)S(1)} custom-call(f32[8,128]{1,0:T(8,128)S(1)} %bitcast.54, f32[8,128]{1,0:T(8,128)S(1)} %bitcast.56, bf16[48,1536]{1,0:T(8,128)(2,1)S(1)} %get-tuple-element.77.part_ref.all_refs_5_, bf16[48,1536]{1,0:T(8,128)(2,1)S(1)} %get-tuple-element.85.all_refs_6_.edge_ref, ...), custom_call_target="tpu_custom_call" | custom-call | flops 39321600 | bytes 3145728 | tf_op jit(solution)/shard_map/pallas_call | solution.py:443
  27.6 1.0 %shard_map.64 = (f32[3,4,128]{2,1,0:T(4,128)S(1)}, f32[4,4,128]{2,1,0:T(4,128)S(1)}) custom-call(f32[3,2,2,4,128]{4,3,2,1,0:T(4,128)S(1)} %pad_maximum_fusion.3.mid_ref.all_refs_0_, f32[8,128]{1,0:T(8,128)S(1)} %bitcast.62, f32[8,128]{1,0:T(8,128)S(1)} %bitcast.61, bf16[48,1536]{1,0:T(8,128)(2,1)S(1)} %get-tuple-element.78.ghost_ref.all_refs_7_, ...), custom_call_target="tpu_custom_call" | custom-call | flops 19660800 | bytes 1572864 | tf_op jit(solution)/shard_map/pallas_call | solution.py:443
  28.6 2.5 %collective-permute-start.11 = (f32[1,2,2,4,128]{4,3,2,1,0:T(4,128)S(1)}, f32[1,2,2,4,128]{4,3,2,1,0:T(4,128)S(1)}, u32[]{:S(2)}, u32[]{:S(2)}) collective-permute-start(f32[1,2,2,4,128]{4,3,2,1,0:T(4,128)S(1)} %bitcast.67), channel_id=1, source_target_pairs={{8,0},{16,8},{24,16},{0,24},{9,1},{17,9},{25,17},{1,25},{10,2},{18... | collective-permute-start | bytes 24584 | tf_op jit(solution)/shard_map/ppermute | solution.py:35
  31.0 1.4 %collective-permute-done.11 = f32[1,2,2,4,128]{4,3,2,1,0:T(4,128)S(1)} collective-permute-done((f32[1,2,2,4,128]{4,3,2,1,0:T(4,128)S(1)}, f32[1,2,2,4,128]{4,3,2,1,0:T(4,128)S(1)}, u32[]{:S(2)}, u32[]{:S(2)}) %collective-permute-start.11) | collective-permute-done | bytes 8224 | tf_op jit(solution)/shard_map/ppermute | solution.py:35
  32.4 3.2 %collective-permute-done.10 = f32[1,2,2,4,128]{4,3,2,1,0:T(4,128)S(1)} collective-permute-done((f32[1,2,2,4,128]{4,3,2,1,0:T(4,128)S(1)}, f32[1,2,2,4,128]{4,3,2,1,0:T(4,128)S(1)}, u32[]{:S(2)}, u32[]{:S(2)}) %collective-permute-start.10) | collective-permute-done | bytes 8224 | tf_op jit(solution)/shard_map/ppermute | solution.py:34
  35.6 0.1 collective-permute-start.14
  35.7 2.6 %collective-permute-start.13 = (f32[3,2,2,4,128]{4,3,2,1,0:T(4,128)S(1)}, f32[3,2,2,4,128]{4,3,2,1,0:T(4,128)S(1)}, u32[]{:S(2)}, u32[]{:S(2)}) collective-permute-start(f32[3,2,2,4,128]{4,3,2,1,0:T(4,128)S(1)} %pad_maximum_fusion.4.mid_ref.all_refs_0_), channel_id=1, source_target_pairs={{1,0},{2,1},{3,2},{0,3},{5,4},{6,5},{7,6},{4,7},{9,8},{10,9},{11,1... | collective-permute-start | bytes 73736 | tf_op jit(solution)/shard_map/ppermute | solution.py:35
  38.2 0.0 collective-permute-start.12
  38.2 0.0 collective-permute-done.14
  38.2 1.0 %shard_map.65 = (f32[4,128,128]{2,1,0:T(8,128)S(1)}, bf16[48,1536]{1,0:T(8,128)(2,1)S(1)}, f32[8,1536]{1,0:T(8,128)S(1)}, bf16[48,1536]{1,0:T(8,128)(2,1)S(1)}, ...) custom-call(f32[3,2,2,4,128]{4,3,2,1,0:T(4,128)S(1)} %pad_maximum_fusion.4.mid_ref.all_refs_0_, ...), custom_call_target="tpu_custom_call" | custom-call | flops 58982400 | bytes 4718592 | tf_op jit(solution)/shard_map/pallas_call | solution.py:443
  39.2 0.5 collective-permute-done.13.high_ref
  39.8 4.1 %collective-permute-done.12.low_ref = f32[3,2,2,4,128]{4,3,2,1,0:T(4,128)S(1)} collective-permute-done((f32[3,2,2,4,128]{4,3,2,1,0:T(4,128)S(1)}, f32[3,2,2,4,128]{4,3,2,1,0:T(4,128)S(1)}, u32[]{:S(2)}, u32[]{:S(2)}) %collective-permute-start.12) | collective-permute-done | bytes 24608 | tf_op jit(solution)/shard_map/ppermute | solution.py:34
  43.9 0.1 collective-permute-start.15
  44.0 1.3 %shard_map.66 = (f32[4,128,128]{2,1,0:T(8,128)S(1)}, f32[4,128,128]{2,1,0:T(8,128)S(1)}, bf16[48,1536]{1,0:T(8,128)(2,1)S(1)}, f32[8,1536]{1,0:T(8,128)S(1)}, bf16[4,128,48]{2,1,0:T(8,128)(2,1)S(1)}) custom-call(f32[3,2,2,4,128]{4,3,2,1,0:T(4,128)S(1)} %collective-permute-done.12.low_ref, f32[3,2,2,4,128]{4,3,2,1,0:T(4,128)S(1)} %collective-permute-done.13.high_ref, ...), custom_call_target="tpu_custom_call" | custom-call | flops 88473600 | bytes 7077888 | tf_op jit(solution)/shard_map/pallas_call | solution.py:443
  45.3 0.6 shard_map.67
  45.9 0.6 collective-permute-start.18
  46.5 0.0 collective-permute-start.17
  46.5 2.0 %collective-permute-start.16 = (f32[1,2,4,128]{3,2,1,0:T(4,128)S(1)}, f32[1,2,4,128]{3,2,1,0:T(4,128)S(1)}, u32[]{:S(2)}, u32[]{:S(2)}) collective-permute-start(f32[1,2,4,128]{3,2,1,0:T(4,128)S(1)} %bitcast.78), channel_id=1, source_target_pairs={{0,8},{8,16},{16,24},{24,0},{1,9},{9,17},{17,25},{25,1},{2,10},{10... | collective-permute-start | bytes 12296 | tf_op jit(solution)/shard_map/ppermute | solution.py:34
  48.5 1.3 %shard_map.68 = (f32[4,4,128,128]{3,2,1,0:T(8,128)S(1)}, bf16[4,128,48]{2,1,0:T(8,128)(2,1)S(1)}) custom-call(f32[3,2,2,4,128]{4,3,2,1,0:T(4,128)S(1)} %pad_maximum_fusion.4.mid_ref.all_refs_0_, f32[8,128]{1,0:T(8,128)S(1)} %get-tuple-element.107.all_refs_1_, f32[8,128]{1,0:T(8,128)S(1)} %get-tuple-element.106.all_refs_2_, ...), custom_call_target="tpu_custom_call" | custom-call | flops 29491200 | bytes 2359296 | tf_op jit(solution)/shard_map/pallas_call | solution.py:443
  49.8 0.3 collective-permute-done.17
  50.1 0.9 %collective-permute-done.16 = f32[1,2,4,128]{3,2,1,0:T(4,128)S(1)} collective-permute-done((f32[1,2,4,128]{3,2,1,0:T(4,128)S(1)}, f32[1,2,4,128]{3,2,1,0:T(4,128)S(1)}, u32[]{:S(2)}, u32[]{:S(2)}) %collective-permute-start.16) | collective-permute-done | bytes 4128 | tf_op jit(solution)/shard_map/ppermute | solution.py:34
  51.0 1.6 %shard_map.69.column_ref = f32[4,4,128,128]{3,2,1,0:T(8,128)S(1)} custom-call(f32[8,128]{1,0:T(8,128)S(1)} %bitcast.59, f32[8,128]{1,0:T(8,128)S(1)} %bitcast.57, bf16[48,1536]{1,0:T(8,128)(2,1)S(1)} %get-tuple-element.100.part_ref.all_refs_5_, bf16[48,1536]{1,0:T(8,128)(2,1)S(1)} %get-tuple-element.108.all_refs_6_.edge_ref, ...), custom_call_target="tpu_custom_call" | custom-call | flops 39321600 | bytes 3145728 | tf_op jit(solution)/shard_map/pallas_call | solution.py:443
  52.7 1.0 %shard_map.70 = (f32[3,4,128]{2,1,0:T(4,128)S(1)}, f32[4,4,128]{2,1,0:T(4,128)S(1)}) custom-call(f32[3,2,2,4,128]{4,3,2,1,0:T(4,128)S(1)} %pad_maximum_fusion.4.mid_ref.all_refs_0_, f32[8,128]{1,0:T(8,128)S(1)} %bitcast.64, f32[8,128]{1,0:T(8,128)S(1)} %bitcast.63, bf16[48,1536]{1,0:T(8,128)(2,1)S(1)} %get-tuple-element.101.ghost_ref.all_refs_7_, ...), custom_call_target="tpu_custom_call" | custom-call | flops 19660800 | bytes 1572864 | tf_op jit(solution)/shard_map/pallas_call | solution.py:443
  53.7 1.1 %collective-permute-start.21 = (f32[1,2,2,4,128]{4,3,2,1,0:T(4,128)S(1)}, f32[1,2,2,4,128]{4,3,2,1,0:T(4,128)S(1)}, u32[]{:S(2)}, u32[]{:S(2)}) collective-permute-start(f32[1,2,2,4,128]{4,3,2,1,0:T(4,128)S(1)} %bitcast.70), channel_id=1, source_target_pairs={{8,0},{16,8},{24,16},{0,24},{9,1},{17,9},{25,17},{1,25},{10,2},{18... | collective-permute-start | bytes 24584 | tf_op jit(solution)/shard_map/ppermute | solution.py:35
  54.8 1.0 %collective-permute-start.20 = (f32[1,2,2,4,128]{4,3,2,1,0:T(4,128)S(1)}, f32[1,2,2,4,128]{4,3,2,1,0:T(4,128)S(1)}, u32[]{:S(2)}, u32[]{:S(2)}) collective-permute-start(f32[1,2,2,4,128]{4,3,2,1,0:T(4,128)S(1)} %bitcast.71), channel_id=1, source_target_pairs={{0,8},{8,16},{16,24},{24,0},{1,9},{9,17},{17,25},{25,1},{2,10},{10... | collective-permute-start | bytes 24584 | tf_op jit(solution)/shard_map/ppermute | solution.py:34
  55.7 1.6 %collective-permute-done.21 = f32[1,2,2,4,128]{4,3,2,1,0:T(4,128)S(1)} collective-permute-done((f32[1,2,2,4,128]{4,3,2,1,0:T(4,128)S(1)}, f32[1,2,2,4,128]{4,3,2,1,0:T(4,128)S(1)}, u32[]{:S(2)}, u32[]{:S(2)}) %collective-permute-start.21) | collective-permute-done | bytes 8224 | tf_op jit(solution)/shard_map/ppermute | solution.py:35
  57.4 2.0 %collective-permute-done.20 = f32[1,2,2,4,128]{4,3,2,1,0:T(4,128)S(1)} collective-permute-done((f32[1,2,2,4,128]{4,3,2,1,0:T(4,128)S(1)}, f32[1,2,2,4,128]{4,3,2,1,0:T(4,128)S(1)}, u32[]{:S(2)}, u32[]{:S(2)}) %collective-permute-start.20) | collective-permute-done | bytes 8224 | tf_op jit(solution)/shard_map/ppermute | solution.py:34
  59.3 0.1 collective-permute-start.24
  59.4 0.1 collective-permute-start.23
  59.5 2.0 %collective-permute-start.22 = (f32[3,2,2,4,128]{4,3,2,1,0:T(4,128)S(1)}, f32[3,2,2,4,128]{4,3,2,1,0:T(4,128)S(1)}, u32[]{:S(2)}, u32[]{:S(2)}) collective-permute-start(f32[3,2,2,4,128]{4,3,2,1,0:T(4,128)S(1)} %pad_maximum_fusion.5.mid_ref.all_refs_0_), channel_id=1, source_target_pairs={{0,1},{1,2},{2,3},{3,0},{4,5},{5,6},{6,7},{7,4},{8,9},{9,10},{10,1... | collective-permute-start | bytes 73736 | tf_op jit(solution)/shard_map/ppermute | solution.py:34
  61.5 1.0 %shard_map.71 = (f32[4,128,128]{2,1,0:T(8,128)S(1)}, bf16[48,1536]{1,0:T(8,128)(2,1)S(1)}, f32[8,1536]{1,0:T(8,128)S(1)}, bf16[48,1536]{1,0:T(8,128)(2,1)S(1)}, ...) custom-call(f32[3,2,2,4,128]{4,3,2,1,0:T(4,128)S(1)} %pad_maximum_fusion.5.mid_ref.all_refs_0_, ...), custom_call_target="tpu_custom_call" | custom-call | flops 58982400 | bytes 4718592 | tf_op jit(solution)/shard_map/pallas_call | solution.py:443
  62.5 0.8 %collective-permute-done.23.high_ref = f32[3,2,2,4,128]{4,3,2,1,0:T(4,128)S(1)} collective-permute-done((f32[3,2,2,4,128]{4,3,2,1,0:T(4,128)S(1)}, f32[3,2,2,4,128]{4,3,2,1,0:T(4,128)S(1)}, u32[]{:S(2)}, u32[]{:S(2)}) %collective-permute-start.23) | collective-permute-done | bytes 24608 | tf_op jit(solution)/shard_map/ppermute | solution.py:35
  63.3 1.9 %collective-permute-done.22.low_ref = f32[3,2,2,4,128]{4,3,2,1,0:T(4,128)S(1)} collective-permute-done((f32[3,2,2,4,128]{4,3,2,1,0:T(4,128)S(1)}, f32[3,2,2,4,128]{4,3,2,1,0:T(4,128)S(1)}, u32[]{:S(2)}, u32[]{:S(2)}) %collective-permute-start.22) | collective-permute-done | bytes 24608 | tf_op jit(solution)/shard_map/ppermute | solution.py:34
  65.2 0.1 collective-permute-start.25
  65.2 1.3 %shard_map.72 = (f32[4,128,128]{2,1,0:T(8,128)S(1)}, f32[4,128,128]{2,1,0:T(8,128)S(1)}, bf16[48,1536]{1,0:T(8,128)(2,1)S(1)}, f32[8,1536]{1,0:T(8,128)S(1)}, bf16[4,128,48]{2,1,0:T(8,128)(2,1)S(1)}) custom-call(f32[3,2,2,4,128]{4,3,2,1,0:T(4,128)S(1)} %collective-permute-done.22.low_ref, f32[3,2,2,4,128]{4,3,2,1,0:T(4,128)S(1)} %collective-permute-done.23.high_ref, ...), custom_call_target="tpu_custom_call" | custom-call | flops 88473600 | bytes 7077888 | tf_op jit(solution)/shard_map/pallas_call | solution.py:443
  66.6 0.6 shard_map.73
  67.2 0.6 collective-permute-start.28
  67.8 0.1 collective-permute-start.27
  67.9 1.9 %collective-permute-start.26 = (f32[1,2,4,128]{3,2,1,0:T(4,128)S(1)}, f32[1,2,4,128]{3,2,1,0:T(4,128)S(1)}, u32[]{:S(2)}, u32[]{:S(2)}) collective-permute-start(f32[1,2,4,128]{3,2,1,0:T(4,128)S(1)} %bitcast.81), channel_id=1, source_target_pairs={{0,8},{8,16},{16,24},{24,0},{1,9},{9,17},{17,25},{25,1},{2,10},{10... | collective-permute-start | bytes 12296 | tf_op jit(solution)/shard_map/ppermute | solution.py:34
  69.8 1.3 %shard_map.74 = (f32[4,4,128,128]{3,2,1,0:T(8,128)S(1)}, bf16[4,128,48]{2,1,0:T(8,128)(2,1)S(1)}) custom-call(f32[3,2,2,4,128]{4,3,2,1,0:T(4,128)S(1)} %pad_maximum_fusion.5.mid_ref.all_refs_0_, f32[8,128]{1,0:T(8,128)S(1)} %get-tuple-element.130.all_refs_1_, f32[8,128]{1,0:T(8,128)S(1)} %get-tuple-element.129.all_refs_2_, ...), custom_call_target="tpu_custom_call" | custom-call | flops 29491200 | bytes 2359296 | tf_op jit(solution)/shard_map/pallas_call | solution.py:443
  71.1 0.3 collective-permute-done.27
  71.4 1.0 %collective-permute-done.26 = f32[1,2,4,128]{3,2,1,0:T(4,128)S(1)} collective-permute-done((f32[1,2,4,128]{3,2,1,0:T(4,128)S(1)}, f32[1,2,4,128]{3,2,1,0:T(4,128)S(1)}, u32[]{:S(2)}, u32[]{:S(2)}) %collective-permute-start.26) | collective-permute-done | bytes 4128 | tf_op jit(solution)/shard_map/ppermute | solution.py:34
  72.4 1.6 %shard_map.75.column_ref = f32[4,4,128,128]{3,2,1,0:T(8,128)S(1)} custom-call(f32[8,128]{1,0:T(8,128)S(1)} %bitcast.60, f32[8,128]{1,0:T(8,128)S(1)} %bitcast.58, bf16[48,1536]{1,0:T(8,128)(2,1)S(1)} %get-tuple-element.123.part_ref.all_refs_5_, bf16[48,1536]{1,0:T(8,128)(2,1)S(1)} %get-tuple-element.131.all_refs_6_.edge_ref, ...), custom_call_target="tpu_custom_call" | custom-call | flops 39321600 | bytes 3145728 | tf_op jit(solution)/shard_map/pallas_call | solution.py:443
  74.1 1.6 %shard_map.76 = (f32[3,4,128]{2,1,0:T(4,128)}, f32[3,4,128]{2,1,0:T(4,128)}) custom-call(f32[3,2,2,4,128]{4,3,2,1,0:T(4,128)S(1)} %pad_maximum_fusion.5.mid_ref.all_refs_0_, f32[8,128]{1,0:T(8,128)S(1)} %bitcast.66, f32[8,128]{1,0:T(8,128)S(1)} %bitcast.65, bf16[48,1536]{1,0:T(8,128)(2,1)S(1)} %get-tuple-element.124.ghost_ref.all_refs_7_, ...), custom_call_target="tpu_custom_call" | custom-call | flops 19660800 | bytes 1572864 | tf_op jit(solution)/shard_map/pallas_call | solution.py:443
  (39 shorter events, 0.2 us)
Async XLA Ops:
  1.5 4.7 %collective-permute-start.1 = (f32[1,2,2,4,128]{4,3,2,1,0:T(4,128)S(1)}, f32[1,2,2,4,128]{4,3,2,1,0:T(4,128)S(1)}, u32[]{:S(2)}, u32[]{:S(2)}) collective-permute-start(f32[1,2,2,4,128]{4,3,2,1,0:T(4,128)S(1)} %get-tuple-element.73), channel_id=1, source_target_pairs={{0,8},{8,0},{16,24},{24,16},{1,9},{9,1},{17,25},{25,17},{2,10},{10... | collective-permute-start | bytes 24584 | tf_op jit(solution)/shard_map/ppermute | solution.py:38
  4.5 4.5 %collective-permute-start = (f32[1,2,2,4,128]{4,3,2,1,0:T(4,128)S(1)}, f32[1,2,2,4,128]{4,3,2,1,0:T(4,128)S(1)}, u32[]{:S(2)}, u32[]{:S(2)}) collective-permute-start(f32[1,2,2,4,128]{4,3,2,1,0:T(4,128)S(1)} %get-tuple-element.73), channel_id=1, source_target_pairs={{0,24},{8,16},{16,8},{24,0},{1,25},{9,17},{17,9},{25,1},{2,26},{10... | collective-permute-start | bytes 24584 | tf_op jit(solution)/shard_map/ppermute | solution.py:39
  9.1 4.1 %collective-permute-start.3 = (f32[3,2,2,4,128]{4,3,2,1,0:T(4,128)S(1)}, f32[3,2,2,4,128]{4,3,2,1,0:T(4,128)S(1)}, u32[]{:S(2)}, u32[]{:S(2)}) collective-permute-start(f32[3,2,2,4,128]{4,3,2,1,0:T(4,128)S(1)} %pad_maximum_fusion.3.mid_ref.all_refs_0_), channel_id=1, source_target_pairs={{0,1},{1,0},{2,3},{3,2},{4,5},{5,4},{6,7},{7,6},{8,9},{9,8},{10,11... | collective-permute-start | bytes 73736 | tf_op jit(solution)/shard_map/ppermute | solution.py:38
  10.7 5.6 %collective-permute-start.2 = (f32[3,2,2,4,128]{4,3,2,1,0:T(4,128)S(1)}, f32[3,2,2,4,128]{4,3,2,1,0:T(4,128)S(1)}, u32[]{:S(2)}, u32[]{:S(2)}) collective-permute-start(f32[3,2,2,4,128]{4,3,2,1,0:T(4,128)S(1)} %pad_maximum_fusion.3.mid_ref.all_refs_0_), channel_id=1, source_target_pairs={{0,3},{1,2},{2,1},{3,0},{4,7},{5,6},{6,5},{7,4},{8,11},{9,10},{10,... | collective-permute-start | bytes 73736 | tf_op jit(solution)/shard_map/ppermute | solution.py:39
  13.2 3.2 %collective-permute-start.4 = (f32[3,2,2,4,128]{4,3,2,1,0:T(4,128)S(1)}, f32[3,2,2,4,128]{4,3,2,1,0:T(4,128)S(1)}, u32[]{:S(2)}, u32[]{:S(2)}) collective-permute-start(f32[3,2,2,4,128]{4,3,2,1,0:T(4,128)S(1)} %pad_maximum_fusion.3.mid_ref.all_refs_0_), channel_id=1, source_target_pairs={{0,4},{4,0},{1,5},{5,1},{2,6},{6,2},{3,7},{7,3},{8,12},{12,8},{9,1... | collective-permute-start | bytes 73736 | tf_op jit(solution)/shard_map/ppermute | solution.py:28
  17.4 1.4 %collective-permute-start.5 = (f32[3,2,4,4,128]{4,3,2,1,0:T(4,128)S(1)}, f32[3,2,4,4,128]{4,3,2,1,0:T(4,128)S(1)}, u32[]{:S(2)}, u32[]{:S(2)}) collective-permute-start(f32[3,2,4,4,128]{4,3,2,1,0:T(4,128)S(1)} %pad_maximum_fusion), channel_id=1, source_target_pairs={{0,4},{4,0},{1,5},{5,1},{2,6},{6,2},{3,7},{7,3},{8,12},{12,8},{9,1... | collective-permute-start | bytes 147464 | tf_op jit(solution)/shard_map/ppermute | solution.py:28
  19.4 3.7 %collective-permute-start.7 = (f32[1,2,4,128]{3,2,1,0:T(4,128)S(1)}, f32[1,2,4,128]{3,2,1,0:T(4,128)S(1)}, u32[]{:S(2)}, u32[]{:S(2)}) collective-permute-start(f32[1,2,4,128]{3,2,1,0:T(4,128)S(1)} %bitcast.73), channel_id=1, source_target_pairs={{0,8},{8,0},{16,24},{24,16},{1,9},{9,1},{17,25},{25,17},{2,10},{10... | collective-permute-start | bytes 12296 | tf_op jit(solution)/shard_map/ppermute | solution.py:38
  20.0 4.5 %collective-permute-start.6 = (f32[1,2,4,128]{3,2,1,0:T(4,128)S(1)}, f32[1,2,4,128]{3,2,1,0:T(4,128)S(1)}, u32[]{:S(2)}, u32[]{:S(2)}) collective-permute-start(f32[1,2,4,128]{3,2,1,0:T(4,128)S(1)} %bitcast.74), channel_id=1, source_target_pairs={{0,24},{8,16},{16,8},{24,0},{1,25},{9,17},{17,9},{25,1},{2,26},{10... | collective-permute-start | bytes 12296 | tf_op jit(solution)/shard_map/ppermute | solution.py:39
  22.5 2.1 %collective-permute-start.8 = (f32[1,2,4,128]{3,2,1,0:T(4,128)S(1)}, f32[1,2,4,128]{3,2,1,0:T(4,128)S(1)}, u32[]{:S(2)}, u32[]{:S(2)}) collective-permute-start(f32[1,2,4,128]{3,2,1,0:T(4,128)S(1)} %bitcast.75), channel_id=1, source_target_pairs={{0,4},{4,0},{1,5},{5,1},{2,6},{6,2},{3,7},{7,3},{8,12},{12,8},{9,1... | collective-permute-start | bytes 12296 | tf_op jit(solution)/shard_map/ppermute | solution.py:28
  25.9 1.7 %collective-permute-start.9 = (f32[2,2,4,128]{3,2,1,0:T(4,128)S(1)}, f32[2,2,4,128]{3,2,1,0:T(4,128)S(1)}, u32[]{:S(2)}, u32[]{:S(2)}) collective-permute-start(f32[2,2,4,128]{3,2,1,0:T(4,128)S(1)} %pad_maximum_fusion.6), channel_id=1, source_target_pairs={{0,4},{4,0},{1,5},{5,1},{2,6},{6,2},{3,7},{7,3},{8,12},{12,8},{9,1... | collective-permute-start | bytes 24584 | tf_op jit(solution)/shard_map/ppermute | solution.py:28
  28.6 3.8 %collective-permute-start.11 = (f32[1,2,2,4,128]{4,3,2,1,0:T(4,128)S(1)}, f32[1,2,2,4,128]{4,3,2,1,0:T(4,128)S(1)}, u32[]{:S(2)}, u32[]{:S(2)}) collective-permute-start(f32[1,2,2,4,128]{4,3,2,1,0:T(4,128)S(1)} %bitcast.67), channel_id=1, source_target_pairs={{8,0},{16,8},{24,16},{0,24},{9,1},{17,9},{25,17},{1,25},{10,2},{18... | collective-permute-start | bytes 24584 | tf_op jit(solution)/shard_map/ppermute | solution.py:35
  31.0 4.5 %collective-permute-start.10 = (f32[1,2,2,4,128]{4,3,2,1,0:T(4,128)S(1)}, f32[1,2,2,4,128]{4,3,2,1,0:T(4,128)S(1)}, u32[]{:S(2)}, u32[]{:S(2)}) collective-permute-start(f32[1,2,2,4,128]{4,3,2,1,0:T(4,128)S(1)} %bitcast.68), channel_id=1, source_target_pairs={{0,8},{8,16},{16,24},{24,0},{1,9},{9,17},{17,25},{25,1},{2,10},{10... | collective-permute-start | bytes 24584 | tf_op jit(solution)/shard_map/ppermute | solution.py:34
  35.6 2.6 %collective-permute-start.14 = (f32[3,2,2,4,128]{4,3,2,1,0:T(4,128)S(1)}, f32[3,2,2,4,128]{4,3,2,1,0:T(4,128)S(1)}, u32[]{:S(2)}, u32[]{:S(2)}) collective-permute-start(f32[3,2,2,4,128]{4,3,2,1,0:T(4,128)S(1)} %pad_maximum_fusion.4.mid_ref.all_refs_0_), channel_id=1, source_target_pairs={{0,4},{4,0},{1,5},{5,1},{2,6},{6,2},{3,7},{7,3},{8,12},{12,8},{9,1... | collective-permute-start | bytes 73736 | tf_op jit(solution)/shard_map/ppermute | solution.py:28
  35.7 4.1 %collective-permute-start.13 = (f32[3,2,2,4,128]{4,3,2,1,0:T(4,128)S(1)}, f32[3,2,2,4,128]{4,3,2,1,0:T(4,128)S(1)}, u32[]{:S(2)}, u32[]{:S(2)}) collective-permute-start(f32[3,2,2,4,128]{4,3,2,1,0:T(4,128)S(1)} %pad_maximum_fusion.4.mid_ref.all_refs_0_), channel_id=1, source_target_pairs={{1,0},{2,1},{3,2},{0,3},{5,4},{6,5},{7,6},{4,7},{9,8},{10,9},{11,1... | collective-permute-start | bytes 73736 | tf_op jit(solution)/shard_map/ppermute | solution.py:35
  38.2 5.6 %collective-permute-start.12 = (f32[3,2,2,4,128]{4,3,2,1,0:T(4,128)S(1)}, f32[3,2,2,4,128]{4,3,2,1,0:T(4,128)S(1)}, u32[]{:S(2)}, u32[]{:S(2)}) collective-permute-start(f32[3,2,2,4,128]{4,3,2,1,0:T(4,128)S(1)} %pad_maximum_fusion.4.mid_ref.all_refs_0_), channel_id=1, source_target_pairs={{0,1},{1,2},{2,3},{3,0},{4,5},{5,6},{6,7},{7,4},{8,9},{9,10},{10,1... | collective-permute-start | bytes 73736 | tf_op jit(solution)/shard_map/ppermute | solution.py:34
  43.9 1.4 %collective-permute-start.15 = (f32[3,2,4,4,128]{4,3,2,1,0:T(4,128)S(1)}, f32[3,2,4,4,128]{4,3,2,1,0:T(4,128)S(1)}, u32[]{:S(2)}, u32[]{:S(2)}) collective-permute-start(f32[3,2,4,4,128]{4,3,2,1,0:T(4,128)S(1)} %pad_maximum_fusion.1), channel_id=1, source_target_pairs={{0,4},{4,0},{1,5},{5,1},{2,6},{6,2},{3,7},{7,3},{8,12},{12,8},{9,1... | collective-permute-start | bytes 147464 | tf_op jit(solution)/shard_map/ppermute | solution.py:28
  45.9 2.6 %collective-permute-start.18 = (f32[1,2,4,128]{3,2,1,0:T(4,128)S(1)}, f32[1,2,4,128]{3,2,1,0:T(4,128)S(1)}, u32[]{:S(2)}, u32[]{:S(2)}) collective-permute-start(f32[1,2,4,128]{3,2,1,0:T(4,128)S(1)} %bitcast.76), channel_id=1, source_target_pairs={{0,4},{4,0},{1,5},{5,1},{2,6},{6,2},{3,7},{7,3},{8,12},{12,8},{9,1... | collective-permute-start | bytes 12296 | tf_op jit(solution)/shard_map/ppermute | solution.py:28
  46.5 3.6 %collective-permute-start.17 = (f32[1,2,4,128]{3,2,1,0:T(4,128)S(1)}, f32[1,2,4,128]{3,2,1,0:T(4,128)S(1)}, u32[]{:S(2)}, u32[]{:S(2)}) collective-permute-start(f32[1,2,4,128]{3,2,1,0:T(4,128)S(1)} %bitcast.77), channel_id=1, source_target_pairs={{8,0},{16,8},{24,16},{0,24},{9,1},{17,9},{25,17},{1,25},{10,2},{18... | collective-permute-start | bytes 12296 | tf_op jit(solution)/shard_map/ppermute | solution.py:35
  46.5 4.5 %collective-permute-start.16 = (f32[1,2,4,128]{3,2,1,0:T(4,128)S(1)}, f32[1,2,4,128]{3,2,1,0:T(4,128)S(1)}, u32[]{:S(2)}, u32[]{:S(2)}) collective-permute-start(f32[1,2,4,128]{3,2,1,0:T(4,128)S(1)} %bitcast.78), channel_id=1, source_target_pairs={{0,8},{8,16},{16,24},{24,0},{1,9},{9,17},{17,25},{25,1},{2,10},{10... | collective-permute-start | bytes 12296 | tf_op jit(solution)/shard_map/ppermute | solution.py:34
  51.0 1.6 %collective-permute-start.19 = (f32[2,2,4,128]{3,2,1,0:T(4,128)S(1)}, f32[2,2,4,128]{3,2,1,0:T(4,128)S(1)}, u32[]{:S(2)}, u32[]{:S(2)}) collective-permute-start(f32[2,2,4,128]{3,2,1,0:T(4,128)S(1)} %pad_maximum_fusion.7), channel_id=1, source_target_pairs={{0,4},{4,0},{1,5},{5,1},{2,6},{6,2},{3,7},{7,3},{8,12},{12,8},{9,1... | collective-permute-start | bytes 24584 | tf_op jit(solution)/shard_map/ppermute | solution.py:28
  53.7 3.7 %collective-permute-start.21 = (f32[1,2,2,4,128]{4,3,2,1,0:T(4,128)S(1)}, f32[1,2,2,4,128]{4,3,2,1,0:T(4,128)S(1)}, u32[]{:S(2)}, u32[]{:S(2)}) collective-permute-start(f32[1,2,2,4,128]{4,3,2,1,0:T(4,128)S(1)} %bitcast.70), channel_id=1, source_target_pairs={{8,0},{16,8},{24,16},{0,24},{9,1},{17,9},{25,17},{1,25},{10,2},{18... | collective-permute-start | bytes 24584 | tf_op jit(solution)/shard_map/ppermute | solution.py:35
  54.8 4.5 %collective-permute-start.20 = (f32[1,2,2,4,128]{4,3,2,1,0:T(4,128)S(1)}, f32[1,2,2,4,128]{4,3,2,1,0:T(4,128)S(1)}, u32[]{:S(2)}, u32[]{:S(2)}) collective-permute-start(f32[1,2,2,4,128]{4,3,2,1,0:T(4,128)S(1)} %bitcast.71), channel_id=1, source_target_pairs={{0,8},{8,16},{16,24},{24,0},{1,9},{9,17},{17,25},{25,1},{2,10},{10... | collective-permute-start | bytes 24584 | tf_op jit(solution)/shard_map/ppermute | solution.py:34
  59.3 2.2 %collective-permute-start.24 = (f32[3,2,2,4,128]{4,3,2,1,0:T(4,128)S(1)}, f32[3,2,2,4,128]{4,3,2,1,0:T(4,128)S(1)}, u32[]{:S(2)}, u32[]{:S(2)}) collective-permute-start(f32[3,2,2,4,128]{4,3,2,1,0:T(4,128)S(1)} %pad_maximum_fusion.5.mid_ref.all_refs_0_), channel_id=1, source_target_pairs={{0,4},{4,0},{1,5},{5,1},{2,6},{6,2},{3,7},{7,3},{8,12},{12,8},{9,1... | collective-permute-start | bytes 73736 | tf_op jit(solution)/shard_map/ppermute | solution.py:28
  59.4 3.9 %collective-permute-start.23 = (f32[3,2,2,4,128]{4,3,2,1,0:T(4,128)S(1)}, f32[3,2,2,4,128]{4,3,2,1,0:T(4,128)S(1)}, u32[]{:S(2)}, u32[]{:S(2)}) collective-permute-start(f32[3,2,2,4,128]{4,3,2,1,0:T(4,128)S(1)} %pad_maximum_fusion.5.mid_ref.all_refs_0_), channel_id=1, source_target_pairs={{1,0},{2,1},{3,2},{0,3},{5,4},{6,5},{7,6},{4,7},{9,8},{10,9},{11,1... | collective-permute-start | bytes 73736 | tf_op jit(solution)/shard_map/ppermute | solution.py:35
  59.5 5.7 %collective-permute-start.22 = (f32[3,2,2,4,128]{4,3,2,1,0:T(4,128)S(1)}, f32[3,2,2,4,128]{4,3,2,1,0:T(4,128)S(1)}, u32[]{:S(2)}, u32[]{:S(2)}) collective-permute-start(f32[3,2,2,4,128]{4,3,2,1,0:T(4,128)S(1)} %pad_maximum_fusion.5.mid_ref.all_refs_0_), channel_id=1, source_target_pairs={{0,1},{1,2},{2,3},{3,0},{4,5},{5,6},{6,7},{7,4},{8,9},{9,10},{10,1... | collective-permute-start | bytes 73736 | tf_op jit(solution)/shard_map/ppermute | solution.py:34
  65.2 1.4 %collective-permute-start.25 = (f32[3,2,4,4,128]{4,3,2,1,0:T(4,128)S(1)}, f32[3,2,4,4,128]{4,3,2,1,0:T(4,128)S(1)}, u32[]{:S(2)}, u32[]{:S(2)}) collective-permute-start(f32[3,2,4,4,128]{4,3,2,1,0:T(4,128)S(1)} %pad_maximum_fusion.2), channel_id=1, source_target_pairs={{0,4},{4,0},{1,5},{5,1},{2,6},{6,2},{3,7},{7,3},{8,12},{12,8},{9,1... | collective-permute-start | bytes 147464 | tf_op jit(solution)/shard_map/ppermute | solution.py:28
  67.2 2.6 %collective-permute-start.28 = (f32[1,2,4,128]{3,2,1,0:T(4,128)S(1)}, f32[1,2,4,128]{3,2,1,0:T(4,128)S(1)}, u32[]{:S(2)}, u32[]{:S(2)}) collective-permute-start(f32[1,2,4,128]{3,2,1,0:T(4,128)S(1)} %bitcast.79), channel_id=1, source_target_pairs={{0,4},{4,0},{1,5},{5,1},{2,6},{6,2},{3,7},{7,3},{8,12},{12,8},{9,1... | collective-permute-start | bytes 12296 | tf_op jit(solution)/shard_map/ppermute | solution.py:28
  67.8 3.6 %collective-permute-start.27 = (f32[1,2,4,128]{3,2,1,0:T(4,128)S(1)}, f32[1,2,4,128]{3,2,1,0:T(4,128)S(1)}, u32[]{:S(2)}, u32[]{:S(2)}) collective-permute-start(f32[1,2,4,128]{3,2,1,0:T(4,128)S(1)} %bitcast.80), channel_id=1, source_target_pairs={{8,0},{16,8},{24,16},{0,24},{9,1},{17,9},{25,17},{1,25},{10,2},{18... | collective-permute-start | bytes 12296 | tf_op jit(solution)/shard_map/ppermute | solution.py:35
  67.9 4.5 %collective-permute-start.26 = (f32[1,2,4,128]{3,2,1,0:T(4,128)S(1)}, f32[1,2,4,128]{3,2,1,0:T(4,128)S(1)}, u32[]{:S(2)}, u32[]{:S(2)}) collective-permute-start(f32[1,2,4,128]{3,2,1,0:T(4,128)S(1)} %bitcast.81), channel_id=1, source_target_pairs={{0,8},{8,16},{16,24},{24,0},{1,9},{9,17},{17,25},{25,1},{2,10},{10... | collective-permute-start | bytes 12296 | tf_op jit(solution)/shard_map/ppermute | solution.py:34
  72.4 1.6 %collective-permute-start.29 = (f32[2,2,4,128]{3,2,1,0:T(4,128)S(1)}, f32[2,2,4,128]{3,2,1,0:T(4,128)S(1)}, u32[]{:S(2)}, u32[]{:S(2)}) collective-permute-start(f32[2,2,4,128]{3,2,1,0:T(4,128)S(1)} %pad_maximum_fusion.8), channel_id=1, source_target_pairs={{0,4},{4,0},{1,5},{5,1},{2,6},{6,2},{3,7},{7,3},{8,12},{12,8},{9,1... | collective-permute-start | bytes 24584 | tf_op jit(solution)/shard_map/ppermute | solution.py:28

commit v6 on v4

--- a/solution.py
+++ b/solution.py
@@ -30,14 +30,13 @@
             lax.slice_in_dim(other, width, size, axis=dim),
             lax.slice_in_dim(other, 0, width, axis=dim),
         )
-    if count % 2:
+    if even is None or count % 2:
+        above = lax.ppermute(head, axis, [((i + 1) % count, i) for i in range(count)])
         below = lax.ppermute(tail, axis, [(i, (i + 1) % count) for i in range(count)])
-        above = lax.ppermute(head, axis, [((i + 1) % count, i) for i in range(count)])
         return below, above
-    even = lax.axis_index(axis) % 2 == 0 if even is None else even
     first, second = (cells, cells) if size == width else (jnp.where(even, tail, head), jnp.where(even, head, tail))
+    second = lax.ppermute(second, axis, [(i, (i - 1 if i % 2 == 0 else i + 1) % count) for i in range(count)])
     first = lax.ppermute(first, axis, [(i, i ^ 1) for i in range(count)])
-    second = lax.ppermute(second, axis, [(i, (i - 1 if i % 2 == 0 else i + 1) % count) for i in range(count)])
     return jnp.where(even, second, first), jnp.where(even, first, second)
 
 
@@ -453,12 +452,12 @@
             ),
         )(*operands)
 
-    even = {axis: lax.optimization_barrier(lax.axis_index(axis) % 2 == 0) for axis in ("gx", "gz")}
+    even = lax.optimization_barrier(lax.axis_index("gz") % 2 == 0)
 
     def evaluate(location, velocity, stage):
-        mid = ring_halo(location, "gx", 0, 1, even["gx"])
+        mid = ring_halo(location, "gx", 0, 1)
         mid_below, mid_above = neighbours(mid, "gy", 1, 1)
-        low, high = neighbours(mid, "gz", 2, 2, even["gz"])
+        low, high = neighbours(mid, "gz", 2, 2, even)
         inner, part, point, ghost, ghost_point, left = call(
             functools.partial(inner_density_kernel, own),
             [mid, mid_below, mid_above],
@@ -482,7 +481,7 @@
             [block("gedge")],
         )
         weights = weights.reshape(cx, cy, near, slots)
-        side_below, side_above = neighbours(weights, "gx", 0, 1, even["gx"])
+        side_below, side_above = neighbours(weights, "gx", 0, 1)
         weight_below, weight_above = neighbours(weights, "gy", 1, 1)
         column, left = call(
             functools.partial(column_force_kernel, own),

time: 77.9 us -> 74.8 us (0.960)
  starting transfers between devices: 29.6 us -> 25.9 us
  waiting for transfers between devices: 24.9 us -> 25.7 us
    ppermute x0 -> x12, waiting for transfers between devices: none -> 16.3 us  [the longest x6 11.2 us: neighbours(): lax.ppermute(tail, axis, [(i, (i + 1) % count) for i in range(count)])]
    ppermute x0 -> x12, starting transfers between devices: none -> 14.6 us  [the longest x6 8.04 us: neighbours(): lax.ppermute(tail, axis, [(i, (i + 1) % count) for i in range(count)])]
    ppermute x9 -> x3, starting transfers between devices: 19.3 us -> 7.55 us  [neighbours(): lax.ppermute(second, axis, [(i, (i - 1 if i % 2 == 0 else i + 1) % count)...]
    ppermute x9 -> x3, waiting for transfers between devices: 18.5 us -> 6.95 us  [neighbours(): lax.ppermute(second, axis, [(i, (i - 1 if i % 2 == 0 else i + 1) % count)...]
    ppermute x9 -> x3, starting transfers between devices: 9.87 us -> 1.85 us  [neighbours(): first = lax.ppermute(first, axis, [(i, i ^ 1) for i in range(count)])]
    ppermute x9 -> x3, waiting for transfers between devices: 6.33 us -> 2.42 us  [neighbours(): first = lax.ppermute(first, axis, [(i, i ^ 1) for i in range(count)])]
    ppermute x12, starting transfers between devices: 0.44 us -> 1.9 us  [neighbours(): other = lax.ppermute(cells, axis, [(0, 1), (1, 0)])]
  transfers between devices with their start and end apart: 30 -> 30, of which waited for: 17 -> 17; matrix products, arithmetic and copies ran while one was open for 0% -> 0% of each run, Pallas kernels for 11% -> 17%
where the time goes in v6:
time: 74.8 us; the launch traced here: 74.6 us
  starting transfers between devices  25.9 us (35%)
  waiting for transfers between devices  25.7 us (34%)
  Pallas kernels  21.8 us (29%)
  between operations  0.98 us (1%)
    pallas_call x18, Pallas kernels, call(): pl.pallas_call(kernel, out_shape=out_shape, in_specs=[vmem] * len(operand...  20.9 us
    ppermute x6, waiting for transfers between devices, neighbours(): lax.ppermute(tail, axis, [(i, (i + 1) % count) for i in range(count)])  11.2 us
    ppermute x6, starting transfers between devices, neighbours(): lax.ppermute(tail, axis, [(i, (i + 1) % count) for i in range(count)])  8.04 us
    ppermute x3, starting transfers between devices, neighbours(): lax.ppermute(second, axis, [(i, (i - 1 if i % 2 == 0 else i + 1) % count)...  7.55 us
    ppermute x3, waiting for transfers between devices, neighbours(): lax.ppermute(second, axis, [(i, (i - 1 if i % 2 == 0 else i + 1) % count)...  6.95 us
    ppermute x6, starting transfers between devices, neighbours(): lax.ppermute(head, axis, [((i + 1) % count, i) for i in range(count)])  6.6 us
    ppermute x6, waiting for transfers between devices, neighbours(): lax.ppermute(head, axis, [((i + 1) % count, i) for i in range(count)])  5.13 us
    ppermute x3, waiting for transfers between devices, neighbours(): first = lax.ppermute(first, axis, [(i, i ^ 1) for i in range(count)])  2.42 us
  transfers between devices with their start and end apart: 30, of which 17 were waited for; matrix products, arithmetic and copies ran while one was open for 0% of the time, Pallas kernels for 17%

profile of v6, /device:TPU:0, one launch (start us, length us, event | category | flops | bytes accessed | tf_op | source)
XLA Modules:
  0.0 74.6 jit_solution(14440099939971104239)
XLA Ops:
  0.6 0.8 %prepare.1 = (f32[1,2,2,4,128]{4,3,2,1,0:T(4,128)S(1)}, f32[3,4,128]{2,1,0:T(4,128)S(1)}) custom-call(f32[3,1,2,2,128]{4,3,2,1,0:T(2,128)} %pos_hbm.1, f32[3,1,2,2,128]{4,3,2,1,0:T(2,128)} %vel_hbm.1, s32[1,2,2,128]{3,2,1,0:T(2,128)} %species_hbm.1, s32[1,2,2]{2,1,0:T(2,128)} %counts_hbm.1), custom_call_target="tpu_custom_call" | custom-call | tf_op jit(solution)/shard_map/prepare/pallas_call | solution.py:529
  1.5 3.0 %collective-permute-start = (f32[1,2,2,4,128]{4,3,2,1,0:T(4,128)S(1)}, f32[1,2,2,4,128]{4,3,2,1,0:T(4,128)S(1)}, u32[]{:S(2)}, u32[]{:S(2)}) collective-permute-start(f32[1,2,2,4,128]{4,3,2,1,0:T(4,128)S(1)} %get-tuple-element.73), channel_id=1, source_target_pairs={{0,8},{8,16},{16,24},{24,0},{1,9},{9,17},{17,25},{25,1},{2,10},{10... | collective-permute-start | bytes 24584 | tf_op jit(solution)/shard_map/ppermute | solution.py:35
  4.5 1.0 %collective-permute-start.1 = (f32[1,2,2,4,128]{4,3,2,1,0:T(4,128)S(1)}, f32[1,2,2,4,128]{4,3,2,1,0:T(4,128)S(1)}, u32[]{:S(2)}, u32[]{:S(2)}) collective-permute-start(f32[1,2,2,4,128]{4,3,2,1,0:T(4,128)S(1)} %get-tuple-element.73), channel_id=1, source_target_pairs={{8,0},{16,8},{24,16},{0,24},{9,1},{17,9},{25,17},{1,25},{10,2},{18... | collective-permute-start | bytes 24584 | tf_op jit(solution)/shard_map/ppermute | solution.py:34
  5.5 1.6 %collective-permute-done = f32[1,2,2,4,128]{4,3,2,1,0:T(4,128)S(1)} collective-permute-done((f32[1,2,2,4,128]{4,3,2,1,0:T(4,128)S(1)}, f32[1,2,2,4,128]{4,3,2,1,0:T(4,128)S(1)}, u32[]{:S(2)}, u32[]{:S(2)}) %collective-permute-start) | collective-permute-done | bytes 8224 | tf_op jit(solution)/shard_map/ppermute | solution.py:35
  7.1 1.1 %collective-permute-done.1 = f32[1,2,2,4,128]{4,3,2,1,0:T(4,128)S(1)} collective-permute-done((f32[1,2,2,4,128]{4,3,2,1,0:T(4,128)S(1)}, f32[1,2,2,4,128]{4,3,2,1,0:T(4,128)S(1)}, u32[]{:S(2)}, u32[]{:S(2)}) %collective-permute-start.1) | collective-permute-done | bytes 8224 | tf_op jit(solution)/shard_map/ppermute | solution.py:34
  8.2 1.6 %collective-permute-start.3 = (f32[3,2,2,4,128]{4,3,2,1,0:T(4,128)S(1)}, f32[3,2,2,4,128]{4,3,2,1,0:T(4,128)S(1)}, u32[]{:S(2)}, u32[]{:S(2)}) collective-permute-start(f32[3,2,2,4,128]{4,3,2,1,0:T(4,128)S(1)} %constant_dynamic-update-slice_fusion.mid_ref.all_refs_0_), channel_id=1, source_target_pairs={{0,1},{1,0},{2,3},{3,2},{4,5},{5,4},{6,7},{7,6},{8,9},{9,8},{10,11... | collective-permute-start | bytes 73736 | tf_op jit(solution)/shard_map/ppermute | solution.py:39
  9.7 2.5 %collective-permute-start.2 = (f32[3,2,2,4,128]{4,3,2,1,0:T(4,128)S(1)}, f32[3,2,2,4,128]{4,3,2,1,0:T(4,128)S(1)}, u32[]{:S(2)}, u32[]{:S(2)}) collective-permute-start(f32[3,2,2,4,128]{4,3,2,1,0:T(4,128)S(1)} %constant_dynamic-update-slice_fusion.mid_ref.all_refs_0_), channel_id=1, source_target_pairs={{0,3},{1,2},{2,1},{3,0},{4,7},{5,6},{6,5},{7,4},{8,11},{9,10},{10,... | collective-permute-start | bytes 73736 | tf_op jit(solution)/shard_map/ppermute | solution.py:38
  12.2 0.0 collective-permute-start.4
  12.2 0.0 collective-permute-done.3
  12.2 3.1 %collective-permute-done.2 = f32[3,2,2,4,128]{4,3,2,1,0:T(4,128)S(1)} collective-permute-done((f32[3,2,2,4,128]{4,3,2,1,0:T(4,128)S(1)}, f32[3,2,2,4,128]{4,3,2,1,0:T(4,128)S(1)}, u32[]{:S(2)}, u32[]{:S(2)}) %collective-permute-start.2) | collective-permute-done | bytes 24608 | tf_op jit(solution)/shard_map/ppermute | solution.py:38
  15.4 0.0 collective-permute-done.4
  15.4 1.0 %shard_map.59 = (f32[4,128,128]{2,1,0:T(8,128)S(1)}, bf16[48,1536]{1,0:T(8,128)(2,1)S(1)}, f32[8,1536]{1,0:T(8,128)S(1)}, bf16[48,1536]{1,0:T(8,128)(2,1)S(1)}, ...) custom-call(f32[3,2,2,4,128]{4,3,2,1,0:T(4,128)S(1)} %constant_dynamic-update-slice_fusion.mid_ref.all_refs_0_, ...), custom_call_target="tpu_custom_call" | custom-call | flops 58982400 | bytes 4718592 | tf_op jit(solution)/shard_map/pallas_call | solution.py:443
  16.4 0.1 collective-permute-start.5
  16.5 1.3 %shard_map.60 = (f32[4,128,128]{2,1,0:T(8,128)S(1)}, f32[4,128,128]{2,1,0:T(8,128)S(1)}, bf16[48,1536]{1,0:T(8,128)(2,1)S(1)}, f32[8,1536]{1,0:T(8,128)S(1)}, bf16[4,128,48]{2,1,0:T(8,128)(2,1)S(1)}) custom-call(f32[3,2,2,4,128]{4,3,2,1,0:T(4,128)S(1)} %bitcast.57, f32[3,2,2,4,128]{4,3,2,1,0:T(4,128)S(1)} %bitcast.54, ...), custom_call_target="tpu_custom_call" | custom-call | flops 88473600 | bytes 7077888 | tf_op jit(solution)/shard_map/pallas_call | solution.py:443
  17.7 0.0 collective-permute-done.5
  17.8 0.6 shard_map.61
  18.4 0.6 collective-permute-start.8
  19.0 2.4 %collective-permute-start.7 = (f32[1,2,4,128]{3,2,1,0:T(4,128)S(1)}, f32[1,2,4,128]{3,2,1,0:T(4,128)S(1)}, u32[]{:S(2)}, u32[]{:S(2)}) collective-permute-start(f32[1,2,4,128]{3,2,1,0:T(4,128)S(1)} %bitcast.84), channel_id=1, source_target_pairs={{8,0},{16,8},{24,16},{0,24},{9,1},{17,9},{25,17},{1,25},{10,2},{18... | collective-permute-start | bytes 12296 | tf_op jit(solution)/shard_map/ppermute | solution.py:34
  21.3 0.0 collective-permute-start.6
  21.4 1.3 %shard_map.62 = (f32[4,4,128,128]{3,2,1,0:T(8,128)S(1)}, bf16[4,128,48]{2,1,0:T(8,128)(2,1)S(1)}) custom-call(f32[3,2,2,4,128]{4,3,2,1,0:T(4,128)S(1)} %constant_dynamic-update-slice_fusion.mid_ref.all_refs_0_, f32[8,128]{1,0:T(8,128)S(1)} %get-tuple-element.84.all_refs_1_, f32[8,128]{1,0:T(8,128)S(1)} %get-tuple-element.83.all_refs_2_, ...), custom_call_target="tpu_custom_call" | custom-call | flops 29491200 | bytes 2359296 | tf_op jit(solution)/shard_map/pallas_call | solution.py:443
  22.7 0.3 collective-permute-done.7
  23.0 2.9 %collective-permute-done.6 = f32[1,2,4,128]{3,2,1,0:T(4,128)S(1)} collective-permute-done((f32[1,2,4,128]{3,2,1,0:T(4,128)S(1)}, f32[1,2,4,128]{3,2,1,0:T(4,128)S(1)}, u32[]{:S(2)}, u32[]{:S(2)}) %collective-permute-start.6) | collective-permute-done | bytes 4128 | tf_op jit(solution)/shard_map/ppermute | solution.py:35
  25.9 1.6 %shard_map.63.column_ref = f32[4,4,128,128]{3,2,1,0:T(8,128)S(1)} custom-call(f32[8,128]{1,0:T(8,128)S(1)} %bitcast.68, f32[8,128]{1,0:T(8,128)S(1)} %bitcast.65, bf16[48,1536]{1,0:T(8,128)(2,1)S(1)} %get-tuple-element.77.part_ref.all_refs_5_, bf16[48,1536]{1,0:T(8,128)(2,1)S(1)} %get-tuple-element.85.all_refs_6_.edge_ref, ...), custom_call_target="tpu_custom_call" | custom-call | flops 39321600 | bytes 3145728 | tf_op jit(solution)/shard_map/pallas_call | solution.py:443
  27.5 1.0 %shard_map.64 = (f32[3,4,128]{2,1,0:T(4,128)S(1)}, f32[4,4,128]{2,1,0:T(4,128)S(1)}) custom-call(f32[3,2,2,4,128]{4,3,2,1,0:T(4,128)S(1)} %constant_dynamic-update-slice_fusion.mid_ref.all_refs_0_, f32[8,128]{1,0:T(8,128)S(1)} %bitcast.72, f32[8,128]{1,0:T(8,128)S(1)} %bitcast.71, bf16[48,1536]{1,0:T(8,128)(2,1)S(1)} %get-tuple-element.78.ghost_ref.all_refs_7_, ...), custom_call_target="tpu_custom_call" | custom-call | flops 19660800 | bytes 1572864 | tf_op jit(solution)/shard_map/pallas_call | solution.py:443
  28.5 0.1 collective-permute-start.11
  28.6 1.9 %collective-permute-start.10 = (f32[1,2,2,4,128]{4,3,2,1,0:T(4,128)S(1)}, f32[1,2,2,4,128]{4,3,2,1,0:T(4,128)S(1)}, u32[]{:S(2)}, u32[]{:S(2)}) collective-permute-start(f32[1,2,2,4,128]{4,3,2,1,0:T(4,128)S(1)} %bitcast.78), channel_id=1, source_target_pairs={{0,8},{8,16},{16,24},{24,0},{1,9},{9,17},{17,25},{25,1},{2,10},{10... | collective-permute-start | bytes 24584 | tf_op jit(solution)/shard_map/ppermute | solution.py:35
  30.5 1.6 %collective-permute-done.11 = f32[1,2,2,4,128]{4,3,2,1,0:T(4,128)S(1)} collective-permute-done((f32[1,2,2,4,128]{4,3,2,1,0:T(4,128)S(1)}, f32[1,2,2,4,128]{4,3,2,1,0:T(4,128)S(1)}, u32[]{:S(2)}, u32[]{:S(2)}) %collective-permute-start.11) | collective-permute-done | bytes 8224 | tf_op jit(solution)/shard_map/ppermute | solution.py:34
  32.2 1.0 %collective-permute-done.10 = f32[1,2,2,4,128]{4,3,2,1,0:T(4,128)S(1)} collective-permute-done((f32[1,2,2,4,128]{4,3,2,1,0:T(4,128)S(1)}, f32[1,2,2,4,128]{4,3,2,1,0:T(4,128)S(1)}, u32[]{:S(2)}, u32[]{:S(2)}) %collective-permute-start.10) | collective-permute-done | bytes 8224 | tf_op jit(solution)/shard_map/ppermute | solution.py:35
  33.2 0.1 collective-permute-start.13
  33.3 2.6 %collective-permute-start.12 = (f32[3,2,2,4,128]{4,3,2,1,0:T(4,128)S(1)}, f32[3,2,2,4,128]{4,3,2,1,0:T(4,128)S(1)}, u32[]{:S(2)}, u32[]{:S(2)}) collective-permute-start(f32[3,2,2,4,128]{4,3,2,1,0:T(4,128)S(1)} %pad_maximum_fusion.3.mid_ref.all_refs_0_), channel_id=1, source_target_pairs={{0,3},{1,2},{2,1},{3,0},{4,7},{5,6},{6,5},{7,4},{8,11},{9,10},{10,... | collective-permute-start | bytes 73736 | tf_op jit(solution)/shard_map/ppermute | solution.py:38
  35.8 1.2 %collective-permute-done.13 = f32[3,2,2,4,128]{4,3,2,1,0:T(4,128)S(1)} collective-permute-done((f32[3,2,2,4,128]{4,3,2,1,0:T(4,128)S(1)}, f32[3,2,2,4,128]{4,3,2,1,0:T(4,128)S(1)}, u32[]{:S(2)}, u32[]{:S(2)}) %collective-permute-start.13) | collective-permute-done | bytes 24608 | tf_op jit(solution)/shard_map/ppermute | solution.py:39
  37.1 1.9 %collective-permute-done.12 = f32[3,2,2,4,128]{4,3,2,1,0:T(4,128)S(1)} collective-permute-done((f32[3,2,2,4,128]{4,3,2,1,0:T(4,128)S(1)}, f32[3,2,2,4,128]{4,3,2,1,0:T(4,128)S(1)}, u32[]{:S(2)}, u32[]{:S(2)}) %collective-permute-start.12) | collective-permute-done | bytes 24608 | tf_op jit(solution)/shard_map/ppermute | solution.py:38
  39.0 1.0 %shard_map.65 = (f32[4,128,128]{2,1,0:T(8,128)S(1)}, bf16[48,1536]{1,0:T(8,128)(2,1)S(1)}, f32[8,1536]{1,0:T(8,128)S(1)}, bf16[48,1536]{1,0:T(8,128)(2,1)S(1)}, ...) custom-call(f32[3,2,2,4,128]{4,3,2,1,0:T(4,128)S(1)} %pad_maximum_fusion.3.mid_ref.all_refs_0_, ...), custom_call_target="tpu_custom_call" | custom-call | flops 58982400 | bytes 4718592 | tf_op jit(solution)/shard_map/pallas_call | solution.py:443
  40.0 0.1 collective-permute-start.15
  40.1 1.3 %shard_map.66 = (f32[4,128,128]{2,1,0:T(8,128)S(1)}, f32[4,128,128]{2,1,0:T(8,128)S(1)}, bf16[48,1536]{1,0:T(8,128)(2,1)S(1)}, f32[8,1536]{1,0:T(8,128)S(1)}, bf16[4,128,48]{2,1,0:T(8,128)(2,1)S(1)}) custom-call(f32[3,2,2,4,128]{4,3,2,1,0:T(4,128)S(1)} %bitcast.63, f32[3,2,2,4,128]{4,3,2,1,0:T(4,128)S(1)} %bitcast.60, ...), custom_call_target="tpu_custom_call" | custom-call | flops 88473600 | bytes 7077888 | tf_op jit(solution)/shard_map/pallas_call | solution.py:443
  41.4 0.6 shard_map.67
  42.0 0.6 collective-permute-start.18
  42.6 1.9 %collective-permute-start.17 = (f32[1,2,4,128]{3,2,1,0:T(4,128)S(1)}, f32[1,2,4,128]{3,2,1,0:T(4,128)S(1)}, u32[]{:S(2)}, u32[]{:S(2)}) collective-permute-start(f32[1,2,4,128]{3,2,1,0:T(4,128)S(1)} %bitcast.87), channel_id=1, source_target_pairs={{8,0},{16,8},{24,16},{0,24},{9,1},{17,9},{25,17},{1,25},{10,2},{18... | collective-permute-start | bytes 12296 | tf_op jit(solution)/shard_map/ppermute | solution.py:34
  44.5 0.1 collective-permute-start.16
  44.6 1.3 %shard_map.68 = (f32[4,4,128,128]{3,2,1,0:T(8,128)S(1)}, bf16[4,128,48]{2,1,0:T(8,128)(2,1)S(1)}) custom-call(f32[3,2,2,4,128]{4,3,2,1,0:T(4,128)S(1)} %pad_maximum_fusion.3.mid_ref.all_refs_0_, f32[8,128]{1,0:T(8,128)S(1)} %get-tuple-element.107.all_refs_1_, f32[8,128]{1,0:T(8,128)S(1)} %get-tuple-element.106.all_refs_2_, ...), custom_call_target="tpu_custom_call" | custom-call | flops 29491200 | bytes 2359296 | tf_op jit(solution)/shard_map/pallas_call | solution.py:443
  45.9 0.3 collective-permute-done.17
  46.2 2.8 %collective-permute-done.16 = f32[1,2,4,128]{3,2,1,0:T(4,128)S(1)} collective-permute-done((f32[1,2,4,128]{3,2,1,0:T(4,128)S(1)}, f32[1,2,4,128]{3,2,1,0:T(4,128)S(1)}, u32[]{:S(2)}, u32[]{:S(2)}) %collective-permute-start.16) | collective-permute-done | bytes 4128 | tf_op jit(solution)/shard_map/ppermute | solution.py:35
  49.1 1.6 %shard_map.69.column_ref = f32[4,4,128,128]{3,2,1,0:T(8,128)S(1)} custom-call(f32[8,128]{1,0:T(8,128)S(1)} %bitcast.69, f32[8,128]{1,0:T(8,128)S(1)} %bitcast.66, bf16[48,1536]{1,0:T(8,128)(2,1)S(1)} %get-tuple-element.100.part_ref.all_refs_5_, bf16[48,1536]{1,0:T(8,128)(2,1)S(1)} %get-tuple-element.108.all_refs_6_.edge_ref, ...), custom_call_target="tpu_custom_call" | custom-call | flops 39321600 | bytes 3145728 | tf_op jit(solution)/shard_map/pallas_call | solution.py:443
  50.7 1.0 %shard_map.70 = (f32[3,4,128]{2,1,0:T(4,128)S(1)}, f32[4,4,128]{2,1,0:T(4,128)S(1)}) custom-call(f32[3,2,2,4,128]{4,3,2,1,0:T(4,128)S(1)} %pad_maximum_fusion.3.mid_ref.all_refs_0_, f32[8,128]{1,0:T(8,128)S(1)} %bitcast.74, f32[8,128]{1,0:T(8,128)S(1)} %bitcast.73, bf16[48,1536]{1,0:T(8,128)(2,1)S(1)} %get-tuple-element.101.ghost_ref.all_refs_7_, ...), custom_call_target="tpu_custom_call" | custom-call | flops 19660800 | bytes 1572864 | tf_op jit(solution)/shard_map/pallas_call | solution.py:443
  51.7 0.1 collective-permute-start.21
  51.8 1.9 %collective-permute-start.20 = (f32[1,2,2,4,128]{4,3,2,1,0:T(4,128)S(1)}, f32[1,2,2,4,128]{4,3,2,1,0:T(4,128)S(1)}, u32[]{:S(2)}, u32[]{:S(2)}) collective-permute-start(f32[1,2,2,4,128]{4,3,2,1,0:T(4,128)S(1)} %bitcast.81), channel_id=1, source_target_pairs={{0,8},{8,16},{16,24},{24,0},{1,9},{9,17},{17,25},{25,1},{2,10},{10... | collective-permute-start | bytes 24584 | tf_op jit(solution)/shard_map/ppermute | solution.py:35
  53.8 1.6 %collective-permute-done.21 = f32[1,2,2,4,128]{4,3,2,1,0:T(4,128)S(1)} collective-permute-done((f32[1,2,2,4,128]{4,3,2,1,0:T(4,128)S(1)}, f32[1,2,2,4,128]{4,3,2,1,0:T(4,128)S(1)}, u32[]{:S(2)}, u32[]{:S(2)}) %collective-permute-start.21) | collective-permute-done | bytes 8224 | tf_op jit(solution)/shard_map/ppermute | solution.py:34
  55.4 1.0 %collective-permute-done.20 = f32[1,2,2,4,128]{4,3,2,1,0:T(4,128)S(1)} collective-permute-done((f32[1,2,2,4,128]{4,3,2,1,0:T(4,128)S(1)}, f32[1,2,2,4,128]{4,3,2,1,0:T(4,128)S(1)}, u32[]{:S(2)}, u32[]{:S(2)}) %collective-permute-start.20) | collective-permute-done | bytes 8224 | tf_op jit(solution)/shard_map/ppermute | solution.py:35
  56.4 0.2 collective-permute-start.23
  56.6 2.5 %collective-permute-start.22 = (f32[3,2,2,4,128]{4,3,2,1,0:T(4,128)S(1)}, f32[3,2,2,4,128]{4,3,2,1,0:T(4,128)S(1)}, u32[]{:S(2)}, u32[]{:S(2)}) collective-permute-start(f32[3,2,2,4,128]{4,3,2,1,0:T(4,128)S(1)} %pad_maximum_fusion.4.mid_ref.all_refs_0_), channel_id=1, source_target_pairs={{0,3},{1,2},{2,1},{3,0},{4,7},{5,6},{6,5},{7,4},{8,11},{9,10},{10,... | collective-permute-start | bytes 73736 | tf_op jit(solution)/shard_map/ppermute | solution.py:38
  59.1 1.2 %collective-permute-done.23 = f32[3,2,2,4,128]{4,3,2,1,0:T(4,128)S(1)} collective-permute-done((f32[3,2,2,4,128]{4,3,2,1,0:T(4,128)S(1)}, f32[3,2,2,4,128]{4,3,2,1,0:T(4,128)S(1)}, u32[]{:S(2)}, u32[]{:S(2)}) %collective-permute-start.23) | collective-permute-done | bytes 24608 | tf_op jit(solution)/shard_map/ppermute | solution.py:39
  60.3 1.9 %collective-permute-done.22 = f32[3,2,2,4,128]{4,3,2,1,0:T(4,128)S(1)} collective-permute-done((f32[3,2,2,4,128]{4,3,2,1,0:T(4,128)S(1)}, f32[3,2,2,4,128]{4,3,2,1,0:T(4,128)S(1)}, u32[]{:S(2)}, u32[]{:S(2)}) %collective-permute-start.22) | collective-permute-done | bytes 24608 | tf_op jit(solution)/shard_map/ppermute | solution.py:38
  62.3 1.0 %shard_map.71 = (f32[4,128,128]{2,1,0:T(8,128)S(1)}, bf16[48,1536]{1,0:T(8,128)(2,1)S(1)}, f32[8,1536]{1,0:T(8,128)S(1)}, bf16[48,1536]{1,0:T(8,128)(2,1)S(1)}, ...) custom-call(f32[3,2,2,4,128]{4,3,2,1,0:T(4,128)S(1)} %pad_maximum_fusion.4.mid_ref.all_refs_0_, ...), custom_call_target="tpu_custom_call" | custom-call | flops 58982400 | bytes 4718592 | tf_op jit(solution)/shard_map/pallas_call | solution.py:443
  63.2 0.1 collective-permute-start.25
  63.3 1.3 %shard_map.72 = (f32[4,128,128]{2,1,0:T(8,128)S(1)}, f32[4,128,128]{2,1,0:T(8,128)S(1)}, bf16[48,1536]{1,0:T(8,128)(2,1)S(1)}, f32[8,1536]{1,0:T(8,128)S(1)}, bf16[4,128,48]{2,1,0:T(8,128)(2,1)S(1)}) custom-call(f32[3,2,2,4,128]{4,3,2,1,0:T(4,128)S(1)} %bitcast.51, f32[3,2,2,4,128]{4,3,2,1,0:T(4,128)S(1)} %bitcast.48, ...), custom_call_target="tpu_custom_call" | custom-call | flops 88473600 | bytes 7077888 | tf_op jit(solution)/shard_map/pallas_call | solution.py:443
  64.6 0.6 shard_map.73
  65.3 0.6 collective-permute-start.28
  65.9 1.0 %collective-permute-start.27 = (f32[1,2,4,128]{3,2,1,0:T(4,128)S(1)}, f32[1,2,4,128]{3,2,1,0:T(4,128)S(1)}, u32[]{:S(2)}, u32[]{:S(2)}) collective-permute-start(f32[1,2,4,128]{3,2,1,0:T(4,128)S(1)} %bitcast.90), channel_id=1, source_target_pairs={{8,0},{16,8},{24,16},{0,24},{9,1},{17,9},{25,17},{1,25},{10,2},{18... | collective-permute-start | bytes 12296 | tf_op jit(solution)/shard_map/ppermute | solution.py:34
  66.9 1.0 %collective-permute-start.26 = (f32[1,2,4,128]{3,2,1,0:T(4,128)S(1)}, f32[1,2,4,128]{3,2,1,0:T(4,128)S(1)}, u32[]{:S(2)}, u32[]{:S(2)}) collective-permute-start(f32[1,2,4,128]{3,2,1,0:T(4,128)S(1)} %bitcast.91), channel_id=1, source_target_pairs={{0,8},{8,16},{16,24},{24,0},{1,9},{9,17},{17,25},{25,1},{2,10},{10... | collective-permute-start | bytes 12296 | tf_op jit(solution)/shard_map/ppermute | solution.py:35
  67.9 1.3 %shard_map.74 = (f32[4,4,128,128]{3,2,1,0:T(8,128)S(1)}, bf16[4,128,48]{2,1,0:T(8,128)(2,1)S(1)}) custom-call(f32[3,2,2,4,128]{4,3,2,1,0:T(4,128)S(1)} %pad_maximum_fusion.4.mid_ref.all_refs_0_, f32[8,128]{1,0:T(8,128)S(1)} %get-tuple-element.130.all_refs_1_, f32[8,128]{1,0:T(8,128)S(1)} %get-tuple-element.129.all_refs_2_, ...), custom_call_target="tpu_custom_call" | custom-call | flops 29491200 | bytes 2359296 | tf_op jit(solution)/shard_map/pallas_call | solution.py:443
  69.2 0.3 collective-permute-done.27
  69.5 1.9 %collective-permute-done.26 = f32[1,2,4,128]{3,2,1,0:T(4,128)S(1)} collective-permute-done((f32[1,2,4,128]{3,2,1,0:T(4,128)S(1)}, f32[1,2,4,128]{3,2,1,0:T(4,128)S(1)}, u32[]{:S(2)}, u32[]{:S(2)}) %collective-permute-start.26) | collective-permute-done | bytes 4128 | tf_op jit(solution)/shard_map/ppermute | solution.py:35
  71.4 1.6 %shard_map.75.column_ref = f32[4,4,128,128]{3,2,1,0:T(8,128)S(1)} custom-call(f32[8,128]{1,0:T(8,128)S(1)} %bitcast.70, f32[8,128]{1,0:T(8,128)S(1)} %bitcast.67, bf16[48,1536]{1,0:T(8,128)(2,1)S(1)} %get-tuple-element.123.part_ref.all_refs_5_, bf16[48,1536]{1,0:T(8,128)(2,1)S(1)} %get-tuple-element.131.all_refs_6_.edge_ref, ...), custom_call_target="tpu_custom_call" | custom-call | flops 39321600 | bytes 3145728 | tf_op jit(solution)/shard_map/pallas_call | solution.py:443
  73.0 1.6 %shard_map.76 = (f32[3,4,128]{2,1,0:T(4,128)}, f32[3,4,128]{2,1,0:T(4,128)}) custom-call(f32[3,2,2,4,128]{4,3,2,1,0:T(4,128)S(1)} %pad_maximum_fusion.4.mid_ref.all_refs_0_, f32[8,128]{1,0:T(8,128)S(1)} %bitcast.76, f32[8,128]{1,0:T(8,128)S(1)} %bitcast.75, bf16[48,1536]{1,0:T(8,128)(2,1)S(1)} %get-tuple-element.124.ghost_ref.all_refs_7_, ...), custom_call_target="tpu_custom_call" | custom-call | flops 19660800 | bytes 1572864 | tf_op jit(solution)/shard_map/pallas_call | solution.py:443
  (41 shorter events, 0.2 us)
Async XLA Ops:
  1.5 5.6 %collective-permute-start = (f32[1,2,2,4,128]{4,3,2,1,0:T(4,128)S(1)}, f32[1,2,2,4,128]{4,3,2,1,0:T(4,128)S(1)}, u32[]{:S(2)}, u32[]{:S(2)}) collective-permute-start(f32[1,2,2,4,128]{4,3,2,1,0:T(4,128)S(1)} %get-tuple-element.73), channel_id=1, source_target_pairs={{0,8},{8,16},{16,24},{24,0},{1,9},{9,17},{17,25},{25,1},{2,10},{10... | collective-permute-start | bytes 24584 | tf_op jit(solution)/shard_map/ppermute | solution.py:35
  4.5 3.7 %collective-permute-start.1 = (f32[1,2,2,4,128]{4,3,2,1,0:T(4,128)S(1)}, f32[1,2,2,4,128]{4,3,2,1,0:T(4,128)S(1)}, u32[]{:S(2)}, u32[]{:S(2)}) collective-permute-start(f32[1,2,2,4,128]{4,3,2,1,0:T(4,128)S(1)} %get-tuple-element.73), channel_id=1, source_target_pairs={{8,0},{16,8},{24,16},{0,24},{9,1},{17,9},{25,17},{1,25},{10,2},{18... | collective-permute-start | bytes 24584 | tf_op jit(solution)/shard_map/ppermute | solution.py:34
  8.2 4.1 %collective-permute-start.3 = (f32[3,2,2,4,128]{4,3,2,1,0:T(4,128)S(1)}, f32[3,2,2,4,128]{4,3,2,1,0:T(4,128)S(1)}, u32[]{:S(2)}, u32[]{:S(2)}) collective-permute-start(f32[3,2,2,4,128]{4,3,2,1,0:T(4,128)S(1)} %constant_dynamic-update-slice_fusion.mid_ref.all_refs_0_), channel_id=1, source_target_pairs={{0,1},{1,0},{2,3},{3,2},{4,5},{5,4},{6,7},{7,6},{8,9},{9,8},{10,11... | collective-permute-start | bytes 73736 | tf_op jit(solution)/shard_map/ppermute | solution.py:39
  9.7 5.6 %collective-permute-start.2 = (f32[3,2,2,4,128]{4,3,2,1,0:T(4,128)S(1)}, f32[3,2,2,4,128]{4,3,2,1,0:T(4,128)S(1)}, u32[]{:S(2)}, u32[]{:S(2)}) collective-permute-start(f32[3,2,2,4,128]{4,3,2,1,0:T(4,128)S(1)} %constant_dynamic-update-slice_fusion.mid_ref.all_refs_0_), channel_id=1, source_target_pairs={{0,3},{1,2},{2,1},{3,0},{4,7},{5,6},{6,5},{7,4},{8,11},{9,10},{10,... | collective-permute-start | bytes 73736 | tf_op jit(solution)/shard_map/ppermute | solution.py:38
  12.2 3.2 %collective-permute-start.4 = (f32[3,2,2,4,128]{4,3,2,1,0:T(4,128)S(1)}, f32[3,2,2,4,128]{4,3,2,1,0:T(4,128)S(1)}, u32[]{:S(2)}, u32[]{:S(2)}) collective-permute-start(f32[3,2,2,4,128]{4,3,2,1,0:T(4,128)S(1)} %constant_dynamic-update-slice_fusion.mid_ref.all_refs_0_), channel_id=1, source_target_pairs={{0,4},{4,0},{1,5},{5,1},{2,6},{6,2},{3,7},{7,3},{8,12},{12,8},{9,1... | collective-permute-start | bytes 73736 | tf_op jit(solution)/shard_map/ppermute | solution.py:28
  16.4 1.4 %collective-permute-start.5 = (f32[3,2,4,4,128]{4,3,2,1,0:T(4,128)S(1)}, f32[3,2,4,4,128]{4,3,2,1,0:T(4,128)S(1)}, u32[]{:S(2)}, u32[]{:S(2)}) collective-permute-start(f32[3,2,4,4,128]{4,3,2,1,0:T(4,128)S(1)} %pad_maximum_fusion), channel_id=1, source_target_pairs={{0,4},{4,0},{1,5},{5,1},{2,6},{6,2},{3,7},{7,3},{8,12},{12,8},{9,1... | collective-permute-start | bytes 147464 | tf_op jit(solution)/shard_map/ppermute | solution.py:28
  18.4 3.0 %collective-permute-start.8 = (f32[1,2,4,128]{3,2,1,0:T(4,128)S(1)}, f32[1,2,4,128]{3,2,1,0:T(4,128)S(1)}, u32[]{:S(2)}, u32[]{:S(2)}) collective-permute-start(f32[1,2,4,128]{3,2,1,0:T(4,128)S(1)} %bitcast.83), channel_id=1, source_target_pairs={{0,4},{4,0},{1,5},{5,1},{2,6},{6,2},{3,7},{7,3},{8,12},{12,8},{9,1... | collective-permute-start | bytes 12296 | tf_op jit(solution)/shard_map/ppermute | solution.py:28
  19.0 4.0 %collective-permute-start.7 = (f32[1,2,4,128]{3,2,1,0:T(4,128)S(1)}, f32[1,2,4,128]{3,2,1,0:T(4,128)S(1)}, u32[]{:S(2)}, u32[]{:S(2)}) collective-permute-start(f32[1,2,4,128]{3,2,1,0:T(4,128)S(1)} %bitcast.84), channel_id=1, source_target_pairs={{8,0},{16,8},{24,16},{0,24},{9,1},{17,9},{25,17},{1,25},{10,2},{18... | collective-permute-start | bytes 12296 | tf_op jit(solution)/shard_map/ppermute | solution.py:34
  21.3 4.5 %collective-permute-start.6 = (f32[1,2,4,128]{3,2,1,0:T(4,128)S(1)}, f32[1,2,4,128]{3,2,1,0:T(4,128)S(1)}, u32[]{:S(2)}, u32[]{:S(2)}) collective-permute-start(f32[1,2,4,128]{3,2,1,0:T(4,128)S(1)} %bitcast.85), channel_id=1, source_target_pairs={{0,8},{8,16},{16,24},{24,0},{1,9},{9,17},{17,25},{25,1},{2,10},{10... | collective-permute-start | bytes 12296 | tf_op jit(solution)/shard_map/ppermute | solution.py:35
  25.9 1.6 %collective-permute-start.9 = (f32[2,2,4,128]{3,2,1,0:T(4,128)S(1)}, f32[2,2,4,128]{3,2,1,0:T(4,128)S(1)}, u32[]{:S(2)}, u32[]{:S(2)}) collective-permute-start(f32[2,2,4,128]{3,2,1,0:T(4,128)S(1)} %pad_maximum_fusion.5), channel_id=1, source_target_pairs={{0,4},{4,0},{1,5},{5,1},{2,6},{6,2},{3,7},{7,3},{8,12},{12,8},{9,1... | collective-permute-start | bytes 24584 | tf_op jit(solution)/shard_map/ppermute | solution.py:28
  28.5 3.7 %collective-permute-start.11 = (f32[1,2,2,4,128]{4,3,2,1,0:T(4,128)S(1)}, f32[1,2,2,4,128]{4,3,2,1,0:T(4,128)S(1)}, u32[]{:S(2)}, u32[]{:S(2)}) collective-permute-start(f32[1,2,2,4,128]{4,3,2,1,0:T(4,128)S(1)} %bitcast.77), channel_id=1, source_target_pairs={{8,0},{16,8},{24,16},{0,24},{9,1},{17,9},{25,17},{1,25},{10,2},{18... | collective-permute-start | bytes 24584 | tf_op jit(solution)/shard_map/ppermute | solution.py:34
  28.6 4.6 %collective-permute-start.10 = (f32[1,2,2,4,128]{4,3,2,1,0:T(4,128)S(1)}, f32[1,2,2,4,128]{4,3,2,1,0:T(4,128)S(1)}, u32[]{:S(2)}, u32[]{:S(2)}) collective-permute-start(f32[1,2,2,4,128]{4,3,2,1,0:T(4,128)S(1)} %bitcast.78), channel_id=1, source_target_pairs={{0,8},{8,16},{16,24},{24,0},{1,9},{9,17},{17,25},{25,1},{2,10},{10... | collective-permute-start | bytes 24584 | tf_op jit(solution)/shard_map/ppermute | solution.py:35
  33.2 3.9 %collective-permute-start.13 = (f32[3,2,2,4,128]{4,3,2,1,0:T(4,128)S(1)}, f32[3,2,2,4,128]{4,3,2,1,0:T(4,128)S(1)}, u32[]{:S(2)}, u32[]{:S(2)}) collective-permute-start(f32[3,2,2,4,128]{4,3,2,1,0:T(4,128)S(1)} %pad_maximum_fusion.3.mid_ref.all_refs_0_), channel_id=1, source_target_pairs={{0,1},{1,0},{2,3},{3,2},{4,5},{5,4},{6,7},{7,6},{8,9},{9,8},{10,11... | collective-permute-start | bytes 73736 | tf_op jit(solution)/shard_map/ppermute | solution.py:39
  33.3 5.7 %collective-permute-start.12 = (f32[3,2,2,4,128]{4,3,2,1,0:T(4,128)S(1)}, f32[3,2,2,4,128]{4,3,2,1,0:T(4,128)S(1)}, u32[]{:S(2)}, u32[]{:S(2)}) collective-permute-start(f32[3,2,2,4,128]{4,3,2,1,0:T(4,128)S(1)} %pad_maximum_fusion.3.mid_ref.all_refs_0_), channel_id=1, source_target_pairs={{0,3},{1,2},{2,1},{3,0},{4,7},{5,6},{6,5},{7,4},{8,11},{9,10},{10,... | collective-permute-start | bytes 73736 | tf_op jit(solution)/shard_map/ppermute | solution.py:38
  35.8 3.1 %collective-permute-start.14 = (f32[3,2,2,4,128]{4,3,2,1,0:T(4,128)S(1)}, f32[3,2,2,4,128]{4,3,2,1,0:T(4,128)S(1)}, u32[]{:S(2)}, u32[]{:S(2)}) collective-permute-start(f32[3,2,2,4,128]{4,3,2,1,0:T(4,128)S(1)} %pad_maximum_fusion.3.mid_ref.all_refs_0_), channel_id=1, source_target_pairs={{0,4},{4,0},{1,5},{5,1},{2,6},{6,2},{3,7},{7,3},{8,12},{12,8},{9,1... | collective-permute-start | bytes 73736 | tf_op jit(solution)/shard_map/ppermute | solution.py:28
  40.0 1.4 %collective-permute-start.15 = (f32[3,2,4,4,128]{4,3,2,1,0:T(4,128)S(1)}, f32[3,2,4,4,128]{4,3,2,1,0:T(4,128)S(1)}, u32[]{:S(2)}, u32[]{:S(2)}) collective-permute-start(f32[3,2,4,4,128]{4,3,2,1,0:T(4,128)S(1)} %pad_maximum_fusion.1), channel_id=1, source_target_pairs={{0,4},{4,0},{1,5},{5,1},{2,6},{6,2},{3,7},{7,3},{8,12},{12,8},{9,1... | collective-permute-start | bytes 147464 | tf_op jit(solution)/shard_map/ppermute | solution.py:28
  42.0 2.6 %collective-permute-start.18 = (f32[1,2,4,128]{3,2,1,0:T(4,128)S(1)}, f32[1,2,4,128]{3,2,1,0:T(4,128)S(1)}, u32[]{:S(2)}, u32[]{:S(2)}) collective-permute-start(f32[1,2,4,128]{3,2,1,0:T(4,128)S(1)} %bitcast.86), channel_id=1, source_target_pairs={{0,4},{4,0},{1,5},{5,1},{2,6},{6,2},{3,7},{7,3},{8,12},{12,8},{9,1... | collective-permute-start | bytes 12296 | tf_op jit(solution)/shard_map/ppermute | solution.py:28
  42.6 3.6 %collective-permute-start.17 = (f32[1,2,4,128]{3,2,1,0:T(4,128)S(1)}, f32[1,2,4,128]{3,2,1,0:T(4,128)S(1)}, u32[]{:S(2)}, u32[]{:S(2)}) collective-permute-start(f32[1,2,4,128]{3,2,1,0:T(4,128)S(1)} %bitcast.87), channel_id=1, source_target_pairs={{8,0},{16,8},{24,16},{0,24},{9,1},{17,9},{25,17},{1,25},{10,2},{18... | collective-permute-start | bytes 12296 | tf_op jit(solution)/shard_map/ppermute | solution.py:34
  44.5 4.5 %collective-permute-start.16 = (f32[1,2,4,128]{3,2,1,0:T(4,128)S(1)}, f32[1,2,4,128]{3,2,1,0:T(4,128)S(1)}, u32[]{:S(2)}, u32[]{:S(2)}) collective-permute-start(f32[1,2,4,128]{3,2,1,0:T(4,128)S(1)} %bitcast.88), channel_id=1, source_target_pairs={{0,8},{8,16},{16,24},{24,0},{1,9},{9,17},{17,25},{25,1},{2,10},{10... | collective-permute-start | bytes 12296 | tf_op jit(solution)/shard_map/ppermute | solution.py:35
  49.0 1.6 %collective-permute-start.19 = (f32[2,2,4,128]{3,2,1,0:T(4,128)S(1)}, f32[2,2,4,128]{3,2,1,0:T(4,128)S(1)}, u32[]{:S(2)}, u32[]{:S(2)}) collective-permute-start(f32[2,2,4,128]{3,2,1,0:T(4,128)S(1)} %pad_maximum_fusion.6), channel_id=1, source_target_pairs={{0,4},{4,0},{1,5},{5,1},{2,6},{6,2},{3,7},{7,3},{8,12},{12,8},{9,1... | collective-permute-start | bytes 24584 | tf_op jit(solution)/shard_map/ppermute | solution.py:28
  51.7 3.7 %collective-permute-start.21 = (f32[1,2,2,4,128]{4,3,2,1,0:T(4,128)S(1)}, f32[1,2,2,4,128]{4,3,2,1,0:T(4,128)S(1)}, u32[]{:S(2)}, u32[]{:S(2)}) collective-permute-start(f32[1,2,2,4,128]{4,3,2,1,0:T(4,128)S(1)} %bitcast.80), channel_id=1, source_target_pairs={{8,0},{16,8},{24,16},{0,24},{9,1},{17,9},{25,17},{1,25},{10,2},{18... | collective-permute-start | bytes 24584 | tf_op jit(solution)/shard_map/ppermute | solution.py:34
  51.8 4.5 %collective-permute-start.20 = (f32[1,2,2,4,128]{4,3,2,1,0:T(4,128)S(1)}, f32[1,2,2,4,128]{4,3,2,1,0:T(4,128)S(1)}, u32[]{:S(2)}, u32[]{:S(2)}) collective-permute-start(f32[1,2,2,4,128]{4,3,2,1,0:T(4,128)S(1)} %bitcast.81), channel_id=1, source_target_pairs={{0,8},{8,16},{16,24},{24,0},{1,9},{9,17},{17,25},{25,1},{2,10},{10... | collective-permute-start | bytes 24584 | tf_op jit(solution)/shard_map/ppermute | solution.py:35
  56.4 3.9 %collective-permute-start.23 = (f32[3,2,2,4,128]{4,3,2,1,0:T(4,128)S(1)}, f32[3,2,2,4,128]{4,3,2,1,0:T(4,128)S(1)}, u32[]{:S(2)}, u32[]{:S(2)}) collective-permute-start(f32[3,2,2,4,128]{4,3,2,1,0:T(4,128)S(1)} %pad_maximum_fusion.4.mid_ref.all_refs_0_), channel_id=1, source_target_pairs={{0,1},{1,0},{2,3},{3,2},{4,5},{5,4},{6,7},{7,6},{8,9},{9,8},{10,11... | collective-permute-start | bytes 73736 | tf_op jit(solution)/shard_map/ppermute | solution.py:39
  56.6 5.6 %collective-permute-start.22 = (f32[3,2,2,4,128]{4,3,2,1,0:T(4,128)S(1)}, f32[3,2,2,4,128]{4,3,2,1,0:T(4,128)S(1)}, u32[]{:S(2)}, u32[]{:S(2)}) collective-permute-start(f32[3,2,2,4,128]{4,3,2,1,0:T(4,128)S(1)} %pad_maximum_fusion.4.mid_ref.all_refs_0_), channel_id=1, source_target_pairs={{0,3},{1,2},{2,1},{3,0},{4,7},{5,6},{6,5},{7,4},{8,11},{9,10},{10,... | collective-permute-start | bytes 73736 | tf_op jit(solution)/shard_map/ppermute | solution.py:38
  59.1 3.1 %collective-permute-start.24 = (f32[3,2,2,4,128]{4,3,2,1,0:T(4,128)S(1)}, f32[3,2,2,4,128]{4,3,2,1,0:T(4,128)S(1)}, u32[]{:S(2)}, u32[]{:S(2)}) collective-permute-start(f32[3,2,2,4,128]{4,3,2,1,0:T(4,128)S(1)} %pad_maximum_fusion.4.mid_ref.all_refs_0_), channel_id=1, source_target_pairs={{0,4},{4,0},{1,5},{5,1},{2,6},{6,2},{3,7},{7,3},{8,12},{12,8},{9,1... | collective-permute-start | bytes 73736 | tf_op jit(solution)/shard_map/ppermute | solution.py:28
  63.2 1.4 %collective-permute-start.25 = (f32[3,2,4,4,128]{4,3,2,1,0:T(4,128)S(1)}, f32[3,2,4,4,128]{4,3,2,1,0:T(4,128)S(1)}, u32[]{:S(2)}, u32[]{:S(2)}) collective-permute-start(f32[3,2,4,4,128]{4,3,2,1,0:T(4,128)S(1)} %pad_maximum_fusion.2), channel_id=1, source_target_pairs={{0,4},{4,0},{1,5},{5,1},{2,6},{6,2},{3,7},{7,3},{8,12},{12,8},{9,1... | collective-permute-start | bytes 147464 | tf_op jit(solution)/shard_map/ppermute | solution.py:28
  65.3 2.6 %collective-permute-start.28 = (f32[1,2,4,128]{3,2,1,0:T(4,128)S(1)}, f32[1,2,4,128]{3,2,1,0:T(4,128)S(1)}, u32[]{:S(2)}, u32[]{:S(2)}) collective-permute-start(f32[1,2,4,128]{3,2,1,0:T(4,128)S(1)} %bitcast.89), channel_id=1, source_target_pairs={{0,4},{4,0},{1,5},{5,1},{2,6},{6,2},{3,7},{7,3},{8,12},{12,8},{9,1... | collective-permute-start | bytes 12296 | tf_op jit(solution)/shard_map/ppermute | solution.py:28
  65.9 3.6 %collective-permute-start.27 = (f32[1,2,4,128]{3,2,1,0:T(4,128)S(1)}, f32[1,2,4,128]{3,2,1,0:T(4,128)S(1)}, u32[]{:S(2)}, u32[]{:S(2)}) collective-permute-start(f32[1,2,4,128]{3,2,1,0:T(4,128)S(1)} %bitcast.90), channel_id=1, source_target_pairs={{8,0},{16,8},{24,16},{0,24},{9,1},{17,9},{25,17},{1,25},{10,2},{18... | collective-permute-start | bytes 12296 | tf_op jit(solution)/shard_map/ppermute | solution.py:34
  66.9 4.5 %collective-permute-start.26 = (f32[1,2,4,128]{3,2,1,0:T(4,128)S(1)}, f32[1,2,4,128]{3,2,1,0:T(4,128)S(1)}, u32[]{:S(2)}, u32[]{:S(2)}) collective-permute-start(f32[1,2,4,128]{3,2,1,0:T(4,128)S(1)} %bitcast.91), channel_id=1, source_target_pairs={{0,8},{8,16},{16,24},{24,0},{1,9},{9,17},{17,25},{25,1},{2,10},{10... | collective-permute-start | bytes 12296 | tf_op jit(solution)/shard_map/ppermute | solution.py:35
  71.4 1.6 %collective-permute-start.29 = (f32[2,2,4,128]{3,2,1,0:T(4,128)S(1)}, f32[2,2,4,128]{3,2,1,0:T(4,128)S(1)}, u32[]{:S(2)}, u32[]{:S(2)}) collective-permute-start(f32[2,2,4,128]{3,2,1,0:T(4,128)S(1)} %pad_maximum_fusion.7), channel_id=1, source_target_pairs={{0,4},{4,0},{1,5},{5,1},{2,6},{6,2},{3,7},{7,3},{8,12},{12,8},{9,1... | collective-permute-start | bytes 24584 | tf_op jit(solution)/shard_map/ppermute | solution.py:28
